TPU v7x, 32 devices: a whole 2x2x4 slice. The times are simulated.
32 devices in a mesh: dp: 8 (over z, y), mp: 4 (over x, core).
Axes of the slice: x: 2, y: 2, z: 4, core: 2. Of those that a mesh axis runs over, the one named last changes fastest.
Arguments:
- features: bfloat16 [1024, 8, 1024], P('mp', 'dp'), may hold values from -16 to 16
- w1_in: bfloat16 [1024, 4096], P(None, 'mp'), may hold values from -0.1875 to 0.1875
- w1_out: bfloat16 [4096, 1024], P('mp'), may hold values from -0.1875 to 0.1875
- gain_ffn1: bfloat16 [1024], replicated, may hold values from 0.5 to 1.5
- w_qkv: bfloat16 [1024, 3, 1024], P(None, None, 'mp'), may hold values from -0.1875 to 0.1875
- w_attn_out: bfloat16 [1024, 1024], P('mp'), may hold values from -3 to 3
- rel_table: bfloat16 [73, 64], replicated, may hold values from -4 to 4
- gain_attn: bfloat16 [1024], replicated, may hold values from 0.5 to 1.5
- w_conv_in: bfloat16 [1024, 2, 1024], P(None, None, 'mp'), may hold values from -0.1875 to 0.1875
- w_depth: bfloat16 [31, 1024], P(None, 'mp'), may hold values from -1 to 1
- gain_depth: bfloat16 [1024], P('mp'), may hold values from 0.5 to 1.5
- w_conv_out: bfloat16 [1024, 1024], P('mp'), may hold values from -0.25 to 0.25
- gain_conv: bfloat16 [1024], replicated, may hold values from 0.5 to 1.5
- w2_in: bfloat16 [1024, 4096], P(None, 'mp'), may hold values from -0.1875 to 0.1875
- w2_out: bfloat16 [4096, 1024], P('mp'), may hold values from -0.1875 to 0.1875
- gain_ffn2: bfloat16 [1024], replicated, may hold values from 0.5 to 1.5
- gain_final: bfloat16 [1024], replicated, may hold values from 0.5 to 1.5
- cotangent: bfloat16 [1024, 8, 1024], P('mp', 'dp'), may hold values from -6 to 6
Outputs:
- output: float32 [1024, 8, 1024], P('mp', 'dp')
- input_grad: float32 [1024, 8, 1024], P('mp', 'dp')
- grad_w1_in: float32 [1024, 4096], P('dp', 'mp')
- grad_w1_out: float32 [4096, 1024], P('mp', 'dp')
- grad_gain_ffn1: float32 [1024], replicated
- grad_w_qkv: float32 [1024, 3, 1024], P('dp', None, 'mp')
- grad_w_attn_out: float32 [1024, 1024], P('mp', 'dp')
- grad_rel_table: float32 [73, 64], replicated
- grad_gain_attn: float32 [1024], replicated
- grad_w_conv_in: float32 [1024, 2, 1024], P('dp', None, 'mp')
- grad_w_depth: float32 [31, 1024], P(None, 'mp')
- grad_gain_depth: float32 [1024], P('mp')
- grad_w_conv_out: float32 [1024, 1024], P('mp', 'dp')
- grad_gain_conv: float32 [1024], replicated
- grad_w2_in: float32 [1024, 4096], P('dp', 'mp')
- grad_w2_out: float32 [4096, 1024], P('mp', 'dp')
- grad_gain_ffn2: float32 [1024], replicated
- grad_gain_final: float32 [1024], replicated
- rms_stats: float32 [5], replicated
All inputs are finite; a program needn't handle non-finite values.
Results may differ from a plain program's by a relative error of at most 0.03.
Values may be sent and summed in bfloat16 or wider, within the bound.
A program may use at most 192 MiB of HBM per device.

v0:
```python
import jax
import jax.numpy as jnp
from jax import lax
from jax.sharding import PartitionSpec as P

HEAD = 64
REL_LEFT = 64
REL_RIGHT = 8


epsilon = 1e-05
highest = lax.Precision.HIGHEST


def swish_act(values):
    return values * jax.nn.sigmoid(values)


def swish_slope(values):
    logistic = jax.nn.sigmoid(values)
    return logistic + values * logistic * (1.0 - logistic)


def norm_rows(values, gain):
    average = jnp.mean(values, -1, keepdims=True)
    centred = values - average
    spread = jnp.mean(centred * centred, -1, keepdims=True)
    inverse = lax.rsqrt(spread + epsilon)
    unit_rows = centred * inverse
    return (unit_rows * gain, unit_rows, inverse)


def norm_back(grad_out, unit_rows, inverse, gain):
    scaled = grad_out * gain
    first_mean = jnp.mean(scaled, -1, keepdims=True)
    second_mean = jnp.mean(scaled * unit_rows, -1, keepdims=True)
    grad_in = inverse * (scaled - first_mean - unit_rows * second_mean)
    return (grad_in, jnp.sum(grad_out * unit_rows, 0))


def contract_rows(left_mat, right_mat):
    return lax.dot_general(
        left_mat, right_mat, (((0,), (0,)), ((), ())), preferred_element_type=jnp.float32
    )


def contract_cols(left_mat, right_mat):
    return lax.dot_general(
        left_mat, right_mat, (((1,), (1,)), ((), ())), preferred_element_type=jnp.float32
    )


def spread_rows(normed):
    return lax.all_gather(normed, "mp", axis=0, tiled=True)


def fetch_grads(grad_rows):
    return lax.all_gather(grad_rows, "mp", axis=0, tiled=True)


def reduce_branch(term_fn, row_count):
    return lax.psum_scatter(
        term_fn(jnp.int32(0), lax.axis_size("mp") * row_count).astype(jnp.bfloat16),
        "mp",
        scatter_dimension=0,
        tiled=True,
    ).astype(jnp.float32)


def reduce_inputs(term_fn, row_count):
    return lax.psum_scatter(
        term_fn(jnp.int32(0), lax.axis_size("mp") * row_count).astype(jnp.bfloat16),
        "mp",
        scatter_dimension=0,
        tiled=True,
    ).astype(jnp.float32)


def settle_block(first_grad, second_grad):
    return (first_grad, second_grad)


def band_bias(relative, first_row, key_count):
    block_len = relative.shape[2]
    line_len = key_count + block_len
    spots = jnp.arange(line_len, dtype=jnp.int32) - (block_len - 1) - first_row
    offsets = jnp.clip(spots, -REL_LEFT, REL_RIGHT) + REL_LEFT
    selector = (jnp.arange(relative.shape[3], dtype=jnp.int32)[:, None] == offsets[None, :]).astype(
        jnp.float32
    )
    lines = jnp.einsum("chir,rx->chix", relative, selector, precision=highest)
    lead = lines.shape[:2]
    flat = lines.reshape(lead + (block_len * line_len,))
    skewed = flat[..., block_len - 1 : block_len - 1 + block_len * (line_len - 1)]
    return skewed.reshape(lead + (block_len, line_len - 1))[..., :key_count]


def feed_forward(stream, gain, w_in, w_out):
    normed, unit_rows, inverse = norm_rows(stream, gain.astype(jnp.float32))
    gathered = spread_rows(normed.astype(jnp.bfloat16))
    hidden = jnp.dot(gathered, w_in, preferred_element_type=jnp.float32)
    active = swish_act(hidden).astype(jnp.bfloat16)

    def feed_branch_rows(first_row, row_count):
        return jnp.dot(active, w_out, preferred_element_type=jnp.float32)

    branch = reduce_branch(feed_branch_rows, stream.shape[0])
    return (branch, (unit_rows, inverse, gathered, hidden, active))


def feed_back(grad_stream, kept_state, gain, w_in, w_out):
    unit_rows, inverse, gathered, hidden, active = kept_state
    grad_branch = fetch_grads((0.5 * grad_stream).astype(jnp.bfloat16))
    grad_w_out = contract_rows(active, grad_branch)
    grad_hidden = (contract_cols(grad_branch, w_out) * swish_slope(hidden)).astype(jnp.bfloat16)
    grad_w_in = contract_rows(gathered, grad_hidden)

    def feed_input_rows(first_row, row_count):
        return contract_cols(grad_hidden, w_in)

    grad_normed = reduce_inputs(feed_input_rows, grad_stream.shape[0])
    grad_in, grad_gain = norm_back(grad_normed, unit_rows, inverse, gain.astype(jnp.float32))
    return (grad_stream + grad_in, grad_w_in, grad_w_out, grad_gain)


def score_block(query_block, keys_all, rel_table, first_row):
    logits = jnp.einsum(
        "icha,jcha->chij", query_block, keys_all, preferred_element_type=jnp.float32
    )
    relative = jnp.einsum(
        "icha,ra->chir", query_block, rel_table, preferred_element_type=jnp.float32
    )
    rel_bias = band_bias(relative, first_row, keys_all.shape[0])
    return ((logits + rel_bias) * 0.125, relative)


def attention(stream, gain, w_qkv, w_attn_out, rel_table, clip_count):
    normed, unit_rows, inverse = norm_rows(stream, gain.astype(jnp.float32))
    gathered = spread_rows(normed.astype(jnp.bfloat16))
    projected = jnp.einsum(
        "rd,dkc->rkc", gathered, w_qkv, preferred_element_type=jnp.float32
    ).astype(jnp.bfloat16)
    frames = gathered.shape[0] // clip_count
    heads_here = w_qkv.shape[2] // HEAD
    qkv_split = projected.reshape(frames, clip_count, 3, heads_here, HEAD)
    queries = qkv_split[:, :, 0]
    keys_all = qkv_split[:, :, 1]
    values_all = qkv_split[:, :, 2]
    block_rows = min(512, frames)
    mixed_blocks = []
    totals = []
    for first_row in range(0, frames, block_rows):
        scores, relative = score_block(
            queries[first_row : first_row + block_rows], keys_all, rel_table, first_row
        )
        row_max = jnp.max(scores, -1, keepdims=True)
        weights = jnp.exp(scores - row_max)
        row_sum = jnp.sum(weights, -1, keepdims=True)
        attn_probs = (weights / row_sum).astype(jnp.bfloat16)
        mixed_blocks.append(
            jnp.einsum(
                "chij,jcha->icha", attn_probs, values_all, preferred_element_type=jnp.float32
            )
        )
        totals.append(row_max + jnp.log(row_sum))
    mixed = (
        jnp.concatenate(mixed_blocks, 0)
        .astype(jnp.bfloat16)
        .reshape(frames * clip_count, heads_here * HEAD)
    )

    def attention_branch_rows(first_row, row_count):
        return jnp.dot(mixed, w_attn_out, preferred_element_type=jnp.float32)

    branch = reduce_branch(attention_branch_rows, stream.shape[0])
    return (branch, (unit_rows, inverse, gathered, qkv_split, mixed, totals))


def attention_back(grad_stream, kept_state, gain, w_qkv, w_attn_out, rel_table, clip_count):
    unit_rows, inverse, gathered, qkv_split, mixed, totals = kept_state
    grad_branch = fetch_grads(grad_stream.astype(jnp.bfloat16))
    grad_w_attn_out = contract_rows(mixed, grad_branch)
    frames = qkv_split.shape[0]
    heads_here = qkv_split.shape[3]
    grad_mixed = (
        contract_cols(grad_branch, w_attn_out)
        .astype(jnp.bfloat16)
        .reshape(frames, clip_count, heads_here, HEAD)
    )
    queries = qkv_split[:, :, 0]
    keys_all = qkv_split[:, :, 1]
    values_all = qkv_split[:, :, 2]
    block_rows = min(512, frames)
    grad_keys = jnp.zeros(keys_all.shape, jnp.float32)
    grad_values = jnp.zeros(values_all.shape, jnp.float32)
    grad_table = jnp.zeros(rel_table.shape, jnp.float32)
    query_grads = []
    for block_index, first_row in enumerate(range(0, frames, block_rows)):
        query_block = queries[first_row : first_row + block_rows]
        scores, relative = score_block(query_block, keys_all, rel_table, first_row)
        attn_probs = jnp.exp(scores - totals[block_index])
        grad_out = grad_mixed[first_row : first_row + block_rows]
        grad_probs = jnp.einsum(
            "icha,jcha->chij", grad_out, values_all, preferred_element_type=jnp.float32
        )
        inner_sum = jnp.sum(attn_probs * grad_probs, -1, keepdims=True)
        grad_scores = (attn_probs * (grad_probs - inner_sum)).astype(jnp.bfloat16) * 0.125
        grad_values = grad_values + jnp.einsum(
            "chij,icha->jcha",
            attn_probs.astype(jnp.bfloat16),
            grad_out,
            preferred_element_type=jnp.float32,
        )
        grad_keys = grad_keys + jnp.einsum(
            "chij,icha->jcha", grad_scores, query_block, preferred_element_type=jnp.float32
        )
        bias_fn = lambda rel_values: band_bias(rel_values, first_row, keys_all.shape[0])
        pulled = jax.vjp(bias_fn, relative)[1](grad_scores.astype(jnp.float32))[0]
        grad_relative = pulled.astype(jnp.bfloat16)
        grad_query = jnp.einsum(
            "chij,jcha->icha", grad_scores, keys_all, preferred_element_type=jnp.float32
        )
        grad_query = grad_query + jnp.einsum(
            "chir,ra->icha", grad_relative, rel_table, preferred_element_type=jnp.float32
        )
        grad_table = grad_table + jnp.einsum(
            "chir,icha->ra", grad_relative, query_block, preferred_element_type=jnp.float32
        )
        query_grads.append(grad_query)
    grad_split = jnp.stack([jnp.concatenate(query_grads, 0), grad_keys, grad_values], 2)
    grad_split = grad_split.astype(jnp.bfloat16).reshape(frames * clip_count, 3, heads_here * HEAD)
    grad_w_qkv = jnp.einsum("rd,rkc->dkc", gathered, grad_split, preferred_element_type=jnp.float32)

    def attention_input_rows(first_row, row_count):
        return jnp.einsum("rkc,dkc->rd", grad_split, w_qkv, preferred_element_type=jnp.float32)

    grad_normed = reduce_inputs(attention_input_rows, grad_stream.shape[0])
    grad_in, grad_gain = norm_back(grad_normed, unit_rows, inverse, gain.astype(jnp.float32))
    return (grad_stream + grad_in, grad_w_qkv, grad_w_attn_out, grad_gain, grad_table)


def convolve(stream, gain, w_conv_in, w_depth, gain_depth, w_conv_out, clip_count, model_width):
    normed, unit_rows, inverse = norm_rows(stream, gain.astype(jnp.float32))
    gathered = spread_rows(normed.astype(jnp.bfloat16))
    paired = jnp.einsum("rd,dkc->rkc", gathered, w_conv_in, preferred_element_type=jnp.float32)
    frames = gathered.shape[0] // clip_count
    channels = paired.shape[2]
    glu_out = (paired[:, 0] * jax.nn.sigmoid(paired[:, 1])).reshape(frames, clip_count, channels)
    tap_weights = w_depth.astype(jnp.float32)
    tap_count = tap_weights.shape[0]
    padded = jnp.pad(glu_out, ((tap_count - 1, 0), (0, 0), (0, 0)))
    depth_out = jnp.zeros_like(glu_out)
    for tap_index in range(tap_count):
        depth_out = depth_out + tap_weights[tap_index] * padded[tap_index : tap_index + frames]
    average = lax.psum(jnp.sum(depth_out, -1), "mp") / model_width
    centred = depth_out - average[..., None]
    spread = lax.psum(jnp.sum(centred * centred, -1), "mp") / model_width
    depth_inverse = lax.rsqrt(spread + epsilon)[..., None]
    depth_unit = centred * depth_inverse
    active = (
        swish_act(depth_unit * gain_depth.astype(jnp.float32))
        .astype(jnp.bfloat16)
        .reshape(frames * clip_count, channels)
    )

    def convolve_branch_rows(first_row, row_count):
        return jnp.dot(active, w_conv_out, preferred_element_type=jnp.float32)

    branch = reduce_branch(convolve_branch_rows, stream.shape[0])
    return (branch, (unit_rows, inverse, gathered, paired, depth_unit, depth_inverse, active))


def convolve_back(
    grad_stream,
    kept_state,
    gain,
    w_conv_in,
    w_depth,
    gain_depth,
    w_conv_out,
    clip_count,
    model_width,
):
    unit_rows, inverse, gathered, paired, depth_unit, depth_inverse, active = kept_state
    grad_branch = fetch_grads(grad_stream.astype(jnp.bfloat16))
    grad_w_conv_out = contract_rows(active, grad_branch)
    frames = depth_unit.shape[0]
    channels = depth_unit.shape[2]
    depth_gain = gain_depth.astype(jnp.float32)
    gated = depth_unit * depth_gain
    grad_gated = contract_cols(grad_branch, w_conv_out).reshape(
        frames, clip_count, channels
    ) * swish_slope(gated)
    grad_gain_depth = jnp.sum(grad_gated * depth_unit, (0, 1))
    grad_unit = grad_gated * depth_gain
    first_sum, second_sum = lax.psum(
        (jnp.sum(grad_unit, -1), jnp.sum(grad_unit * depth_unit, -1)), "mp"
    )
    grad_depth = depth_inverse * (
        grad_unit
        - first_sum[..., None] / model_width
        - depth_unit * second_sum[..., None] / model_width
    )
    tap_weights = w_depth.astype(jnp.float32)
    tap_count = tap_weights.shape[0]
    gate_sig = jax.nn.sigmoid(paired[:, 1])
    glu_out = (paired[:, 0] * gate_sig).reshape(frames, clip_count, channels)
    padded = jnp.pad(glu_out, ((tap_count - 1, 0), (0, 0), (0, 0)))
    padded_grad = jnp.pad(grad_depth, ((0, tap_count - 1), (0, 0), (0, 0)))
    grad_glu = jnp.zeros_like(grad_depth)
    tap_grads = []
    for tap_index in range(tap_count):
        begin_at = tap_count - 1 - tap_index
        grad_glu = grad_glu + tap_weights[tap_index] * padded_grad[begin_at : begin_at + frames]
        tap_grads.append(jnp.sum(grad_depth * padded[tap_index : tap_index + frames], (0, 1)))
    grad_w_depth = jnp.stack(tap_grads, 0)
    grad_glu = grad_glu.reshape(frames * clip_count, channels)
    grad_paired = jnp.stack(
        [grad_glu * gate_sig, grad_glu * paired[:, 0] * gate_sig * (1.0 - gate_sig)], 1
    ).astype(jnp.bfloat16)
    grad_w_conv_in = jnp.einsum(
        "rd,rkc->dkc", gathered, grad_paired, preferred_element_type=jnp.float32
    )

    def convolve_input_rows(first_row, row_count):
        return jnp.einsum("rkc,dkc->rd", grad_paired, w_conv_in, preferred_element_type=jnp.float32)

    grad_normed = reduce_inputs(convolve_input_rows, grad_stream.shape[0])
    grad_in, grad_gain = norm_back(grad_normed, unit_rows, inverse, gain.astype(jnp.float32))
    return (
        grad_stream + grad_in,
        grad_w_conv_in,
        grad_w_conv_out,
        grad_gain,
        grad_w_depth,
        grad_gain_depth,
    )


def body(
    features,
    w1_in,
    w1_out,
    gain_ffn1,
    w_qkv,
    w_attn_out,
    rel_table,
    gain_attn,
    w_conv_in,
    w_depth,
    gain_depth,
    w_conv_out,
    gain_conv,
    w2_in,
    w2_out,
    gain_ffn2,
    gain_final,
    cotangent,
):
    local_frames, clip_count, model_width = features.shape
    row_count = local_frames * clip_count
    stream = features.reshape(row_count, model_width).astype(jnp.float32)
    branch_one, kept_one = feed_forward(stream, gain_ffn1, w1_in, w1_out)
    after_one = stream + 0.5 * branch_one
    branch_two, kept_two = attention(after_one, gain_attn, w_qkv, w_attn_out, rel_table, clip_count)
    after_two = after_one + branch_two
    branch_three, kept_three = convolve(
        after_two, gain_conv, w_conv_in, w_depth, gain_depth, w_conv_out, clip_count, model_width
    )
    after_three = after_two + branch_three
    branch_four, kept_four = feed_forward(after_three, gain_ffn2, w2_in, w2_out)
    after_four = after_three + 0.5 * branch_four
    final_gain = gain_final.astype(jnp.float32)
    output, final_unit, final_inverse = norm_rows(after_four, final_gain)
    squares = jnp.stack(
        [
            jnp.sum(branch_one * branch_one),
            jnp.sum(branch_two * branch_two),
            jnp.sum(branch_three * branch_three),
            jnp.sum(branch_four * branch_four),
            jnp.sum(after_four * after_four),
        ]
    )
    seed_grad = cotangent.reshape(row_count, model_width).astype(jnp.float32)
    grad_four, grad_final = norm_back(seed_grad, final_unit, final_inverse, final_gain)
    grad_three, grad_w2_in, grad_w2_out, grad_gain_ffn2 = feed_back(
        grad_four, kept_four, gain_ffn2, w2_in, w2_out
    )
    grad_w2_in, grad_w2_out = settle_block(grad_w2_in, grad_w2_out)
    grad_two, grad_w_conv_in, grad_w_conv_out, grad_gain_conv, grad_w_depth, grad_gain_depth = (
        convolve_back(
            grad_three,
            kept_three,
            gain_conv,
            w_conv_in,
            w_depth,
            gain_depth,
            w_conv_out,
            clip_count,
            model_width,
        )
    )
    grad_w_conv_in, grad_w_conv_out = settle_block(grad_w_conv_in, grad_w_conv_out)
    grad_one, grad_w_qkv, grad_w_attn_out, grad_gain_attn, grad_table = attention_back(
        grad_two, kept_two, gain_attn, w_qkv, w_attn_out, rel_table, clip_count
    )
    grad_w_qkv, grad_w_attn_out = settle_block(grad_w_qkv, grad_w_attn_out)
    grad_input, grad_w1_in, grad_w1_out, grad_gain_ffn1 = feed_back(
        grad_one, kept_one, gain_ffn1, w1_in, w1_out
    )
    grad_w1_in, grad_w1_out = settle_block(grad_w1_in, grad_w1_out)
    summed = (
        lax.psum_scatter(grad_w1_in, "dp", scatter_dimension=0, tiled=True),
        lax.psum_scatter(grad_w1_out, "dp", scatter_dimension=1, tiled=True),
        lax.psum_scatter(grad_w_qkv, "dp", scatter_dimension=0, tiled=True),
        lax.psum_scatter(grad_w_attn_out, "dp", scatter_dimension=1, tiled=True),
        lax.psum_scatter(grad_w_conv_in, "dp", scatter_dimension=0, tiled=True),
        lax.psum_scatter(grad_w_conv_out, "dp", scatter_dimension=1, tiled=True),
        lax.psum_scatter(grad_w2_in, "dp", scatter_dimension=0, tiled=True),
        lax.psum_scatter(grad_w2_out, "dp", scatter_dimension=1, tiled=True),
    )
    gain_grads = jnp.stack(
        [grad_gain_ffn1, grad_gain_attn, grad_gain_conv, grad_gain_ffn2, grad_final]
    )
    gain_sums, table_sum, total_squares = lax.psum((gain_grads, grad_table, squares), ("dp", "mp"))
    depth_sum, depth_gain_sum = lax.psum((grad_w_depth, grad_gain_depth), "dp")
    token_total = row_count * lax.axis_size("mp") * lax.axis_size("dp")
    rms_stats = jnp.sqrt(total_squares / (token_total * model_width))
    return (
        output.reshape(local_frames, clip_count, model_width),
        grad_input.reshape(local_frames, clip_count, model_width),
        summed[0],
        summed[1],
        gain_sums[0],
        summed[2],
        summed[3],
        table_sum,
        gain_sums[1],
        summed[4],
        depth_sum,
        depth_gain_sum,
        summed[5],
        gain_sums[2],
        summed[6],
        summed[7],
        gain_sums[3],
        gain_sums[4],
        rms_stats,
    )


def solution(mesh):
    return jax.shard_map(
        body,
        mesh=mesh,
        in_specs=(
            P("mp", "dp", None),
            P(None, "mp"),
            P("mp", None),
            P(),
            P(None, None, "mp"),
            P("mp", None),
            P(),
            P(),
            P(None, None, "mp"),
            P(None, "mp"),
            P("mp"),
            P("mp", None),
            P(),
            P(None, "mp"),
            P("mp", None),
            P(),
            P(),
            P("mp", "dp", None),
        ),
        out_specs=(
            P("mp", "dp", None),
            P("mp", "dp", None),
            P("dp", "mp"),
            P("mp", "dp"),
            P(),
            P("dp", None, "mp"),
            P("mp", "dp"),
            P(),
            P(),
            P("dp", None, "mp"),
            P(None, "mp"),
            P("mp"),
            P("mp", "dp"),
            P(),
            P("dp", "mp"),
            P("mp", "dp"),
            P(),
            P(),
            P(),
        ),
        check_vma=False,
    )
```

profile of v0, /device:TPU:0, one launch (start us, length us, event | category | flops | bytes accessed | tf_op | source)
XLA Modules:
  0.0 1522.7 jit_solution(11397160073045607270)
XLA Ops:
  12.8 25.4 %all-gather.9.cloned.1.call-done = bf16[1024,1024]{1,0:T(8,128)(2,1)} async-done(((bf16[256,1024]{1,0:T(8,128)(2,1)}), bf16[1024,1024]{1,0:T(8,128)(2,1)}) %all-gather.9.cloned.1.call-update) | async-done | bytes 2097168 | tf_op jit(solution)/shard_map/all_gather | solution.py:54
  48.7 31.5 %reduce-scatter.17.cloned.1.call-done = bf16[256,1024]{1,0:T(8,128)(2,1)} async-done(((bf16[1024,1024]{1,0:T(8,128)(2,1)}), bf16[256,1024]{1,0:T(8,128)(2,1)}) %reduce-scatter.17.cloned.1.call-update) | async-done | bytes 524304 | tf_op jit(solution)/shard_map/reduce_scatter | solution.py:62
  86.5 22.6 %all-gather.11.cloned.1.call-done = bf16[1024,1024]{1,0:T(8,128)(2,1)} async-done(((bf16[256,1024]{1,0:T(8,128)(2,1)}), bf16[1024,1024]{1,0:T(8,128)(2,1)}) %all-gather.11.cloned.1.call-update) | async-done | bytes 2097168 | tf_op jit(solution)/shard_map/all_gather | solution.py:54
  168.5 19.6 %reshape.565 = f32[1,4,512,1535]{3,2,1,0:T(8,128)} reshape(f32[3143680]{0:T(1024)} %reshape.601) | data formatting | bytes 25149440 | tf_op jit(solution)/shard_map/reshape | solution.py:95
  286.7 31.5 %reduce-scatter.19.cloned.1.call-done = bf16[256,1024]{1,0:T(8,128)(2,1)} async-done(((bf16[1024,1024]{1,0:T(8,128)(2,1)}), bf16[256,1024]{1,0:T(8,128)(2,1)}) %reduce-scatter.19.cloned.1.call-update) | async-done | bytes 524304 | tf_op jit(solution)/shard_map/reduce_scatter | solution.py:62
  322.5 22.6 %all-gather.13.cloned.1.call-done = bf16[1024,1024]{1,0:T(8,128)(2,1)} async-done(((bf16[256,1024]{1,0:T(8,128)(2,1)}), bf16[1024,1024]{1,0:T(8,128)(2,1)}) %all-gather.13.cloned.1.call-update) | async-done | bytes 2097168 | tf_op jit(solution)/shard_map/all_gather | solution.py:54
  371.6 32.8 %reduce-scatter.21.cloned.1.call-done = bf16[256,1024]{1,0:T(8,128)(2,1)} async-done(((bf16[1024,1024]{1,0:T(8,128)(2,1)}), bf16[256,1024]{1,0:T(8,128)(2,1)}) %reduce-scatter.21.cloned.1.call-update) | async-done | bytes 524304 | tf_op jit(solution)/shard_map/reduce_scatter | solution.py:62
  409.1 22.5 %all-gather.15.cloned.1.call-done = bf16[1024,1024]{1,0:T(8,128)(2,1)} async-done(((bf16[256,1024]{1,0:T(8,128)(2,1)}), bf16[1024,1024]{1,0:T(8,128)(2,1)}) %all-gather.15.cloned.1.call-update) | async-done | bytes 2097168 | tf_op jit(solution)/shard_map/all_gather | solution.py:54
  442.0 31.5 %reduce-scatter.23.cloned.1.call-done = bf16[256,1024]{1,0:T(8,128)(2,1)} async-done(((bf16[1024,1024]{1,0:T(8,128)(2,1)}), bf16[256,1024]{1,0:T(8,128)(2,1)}) %reduce-scatter.23.cloned.1.call-update) | async-done | bytes 524304 | tf_op jit(solution)/shard_map/reduce_scatter | solution.py:62
  478.6 22.7 %all-gather.17.cloned.1.call-done = bf16[1024,1024]{1,0:T(8,128)(2,1)} async-done(((bf16[256,1024]{1,0:T(8,128)(2,1)}), bf16[1024,1024]{1,0:T(8,128)(2,1)}) %all-gather.17.cloned.1.call-update) | async-done | bytes 2097168 | tf_op jit(solution)/shard_map/all_gather | solution.py:58
  512.7 31.6 %reduce-scatter.25.cloned.1.call-done = bf16[256,1024]{1,0:T(8,128)(2,1)} async-done(((bf16[1024,1024]{1,0:T(8,128)(2,1)}), bf16[256,1024]{1,0:T(8,128)(2,1)}) %reduce-scatter.25.cloned.1.call-update) | async-done | bytes 524304 | tf_op jit(solution)/shard_map/reduce_scatter | solution.py:71
  550.1 22.5 %all-gather.19.cloned.1.call-done = bf16[1024,1024]{1,0:T(8,128)(2,1)} async-done(((bf16[256,1024]{1,0:T(8,128)(2,1)}), bf16[1024,1024]{1,0:T(8,128)(2,1)}) %all-gather.19.cloned.1.call-update) | async-done | bytes 2097168 | tf_op jit(solution)/shard_map/all_gather | solution.py:58
  596.9 32.6 %reduce-scatter.27.cloned.1.call-done = bf16[256,1024]{1,0:T(8,128)(2,1)} async-done(((bf16[1024,1024]{1,0:T(8,128)(2,1)}), bf16[256,1024]{1,0:T(8,128)(2,1)}) %reduce-scatter.27.cloned.1.call-update) | async-done | bytes 524304 | tf_op jit(solution)/shard_map/reduce_scatter | solution.py:71
  634.2 22.2 %all-gather.21.cloned.1.call-done = bf16[1024,1024]{1,0:T(8,128)(2,1)} async-done(((bf16[256,1024]{1,0:T(8,128)(2,1)}), bf16[1024,1024]{1,0:T(8,128)(2,1)}) %all-gather.21.cloned.1.call-update) | async-done | bytes 2097168 | tf_op jit(solution)/shard_map/all_gather | solution.py:58
  769.0 31.1 %reduce-scatter.29.cloned.1.call-done = bf16[256,1024]{1,0:T(8,128)(2,1)} async-done(((bf16[1024,1024]{1,0:T(8,128)(2,1)}), bf16[256,1024]{1,0:T(8,128)(2,1)}) %reduce-scatter.29.cloned.1.call-update) | async-done | bytes 524304 | tf_op jit(solution)/shard_map/reduce_scatter | solution.py:71
  897.5 38.5 %all-reduce.7 = (f32[31,256]{1,0:T(8,128)}, f32[256]{0:T(256)}) all-reduce(f32[31,256]{1,0:T(8,128)S(1)} %stack.192, f32[256]{0:T(256)S(1)} %copy-done.85), channel_id=1, replica_groups=mesh['dp'=8,'mp'=4] {'dp'}, use_global_device_ids=true, to_apply=%region_85.86 | all-reduce | flops 8192 | bytes 65536 | tf_op jit(solution)/shard_map/psum | solution.py:426
  944.9 40.7 %all-reduce.6 = (f32[5,1024]{1,0:T(8,128)S(1)}, f32[73,64]{0,1:T(8,128)}, f32[5]{0:T(128)S(1)}) all-reduce(f32[5,1024]{1,0:T(8,128)S(1)} %stack.160, f32[73,64]{0,1:T(8,128)S(1)} %fusion.109, f32[5]{0:T(128)S(1)} %stack.198), channel_id=1, replica_groups=mesh['dp'=8,'mp'=4] {'dp','mp'}, use_global_device_ids=true, to_apply=%region_49.50 | all-reduce | flops 9797 | bytes 78376 | tf_op jit(solution)/shard_map/psum | solution.py:425
  986.8 39.6 %reduce-scatter.47.cloned.1.call-done = f32[1024,128]{1,0:T(8,128)} async-done(((f32[1024,1024]{1,0:T(8,128)}), f32[1024,128]{1,0:T(8,128)}) %reduce-scatter.47.cloned.1.call-update) | async-done | bytes 524304 | tf_op jit(solution)/shard_map/reduce_scatter | solution.py:420
  1026.4 92.3 %reduce-scatter.45.cloned.1.call-done = f32[128,1024]{1,0:T(8,128)} async-done(((f32[1024,1024]{1,0:T(8,128)}), f32[128,1024]{1,0:T(8,128)}) %reduce-scatter.45.cloned.1.call-update) | async-done | bytes 524304 | tf_op jit(solution)/shard_map/reduce_scatter | solution.py:419
  1118.7 67.5 %reduce-scatter.43.cloned.1.call-done = f32[256,128]{1,0:T(8,128)} async-done(((f32[256,1024]{1,0:T(8,128)}), f32[256,128]{1,0:T(8,128)}) %reduce-scatter.43.cloned.1.call-update) | async-done | bytes 131088 | tf_op jit(solution)/shard_map/reduce_scatter | solution.py:418
  1186.2 67.3 %reduce-scatter.39.cloned.1.call-done = f32[256,128]{1,0:T(8,128)} async-done(((f32[256,1024]{1,0:T(8,128)}), f32[256,128]{1,0:T(8,128)}) %reduce-scatter.39.cloned.1.call-update) | async-done | bytes 131088 | tf_op jit(solution)/shard_map/reduce_scatter | solution.py:416
  1253.5 77.9 %reduce-scatter.37.cloned.1.call-done = f32[128,3,256]{2,0,1:T(8,128)} async-done(((f32[1024,3,256]{2,0,1:T(8,128)}), f32[128,3,256]{2,0,1:T(8,128)}) %reduce-scatter.37.cloned.1.call-update) | async-done | bytes 393232 | tf_op jit(solution)/shard_map/reduce_scatter | solution.py:415
  1331.5 91.8 %reduce-scatter.35.cloned.1.call-done = f32[1024,128]{1,0:T(8,128)} async-done(((f32[1024,1024]{1,0:T(8,128)}), f32[1024,128]{1,0:T(8,128)}) %reduce-scatter.35.cloned.1.call-update) | async-done | bytes 524304 | tf_op jit(solution)/shard_map/reduce_scatter | solution.py:414
  1423.3 92.4 %reduce-scatter.33.cloned.1.call-done = f32[128,1024]{1,0:T(8,128)} async-done(((f32[1024,1024]{1,0:T(8,128)}), f32[128,1024]{1,0:T(8,128)}) %reduce-scatter.33.cloned.1.call-update) | async-done | bytes 524304 | tf_op jit(solution)/shard_map/reduce_scatter | solution.py:413
  (397 shorter events, 495.9 us)
Async XLA Ops:
  7.2 31.0 %all-gather.9.cloned.1.call-start = ((), (), s32[]{:S(2)}) async-start(), calls=%async_computation.16 | async-start | bytes 2621440 | tf_op jit(solution)/shard_map/all_gather | solution.py:54
  12.8 67.4 %reduce-scatter.17.cloned.1.call-start = ((), (), s32[]{:S(2)}) async-start(), calls=%async_computation.17 | async-start | bytes 2621440 | tf_op jit(solution)/shard_map/reduce_scatter | solution.py:62
  48.6 60.4 %all-gather.11.cloned.1.call-start = ((), (), s32[]{:S(2)}) async-start(), calls=%async_computation.18 | async-start | bytes 2621440 | tf_op jit(solution)/shard_map/all_gather | solution.py:54
  86.3 231.9 %reduce-scatter.19.cloned.1.call-start = ((), (), s32[]{:S(2)}) async-start(), calls=%async_computation.19 | async-start | bytes 2621440 | tf_op jit(solution)/shard_map/reduce_scatter | solution.py:62
  286.7 58.4 %all-gather.13.cloned.1.call-start = ((), (), s32[]{:S(2)}) async-start(), calls=%async_computation.20 | async-start | bytes 2621440 | tf_op jit(solution)/shard_map/all_gather | solution.py:54
  322.4 82.1 %reduce-scatter.21.cloned.1.call-start = ((), (), s32[]{:S(2)}) async-start(), calls=%async_computation.21 | async-start | bytes 2621440 | tf_op jit(solution)/shard_map/reduce_scatter | solution.py:62
  371.5 60.0 %all-gather.15.cloned.1.call-start = ((), (), s32[]{:S(2)}) async-start(), calls=%async_computation.22 | async-start | bytes 2621440 | tf_op jit(solution)/shard_map/all_gather | solution.py:54
  408.8 64.7 %reduce-scatter.23.cloned.1.call-start = ((), (), s32[]{:S(2)}) async-start(), calls=%async_computation.23 | async-start | bytes 2621440 | tf_op jit(solution)/shard_map/reduce_scatter | solution.py:62
  441.9 59.4 %all-gather.17.cloned.1.call-start = ((), (), s32[]{:S(2)}) async-start(), calls=%async_computation.24 | async-start | bytes 2621440 | tf_op jit(solution)/shard_map/all_gather | solution.py:58
  478.6 65.6 %reduce-scatter.25.cloned.1.call-start = ((), (), s32[]{:S(2)}) async-start(), calls=%async_computation.25 | async-start | bytes 2621440 | tf_op jit(solution)/shard_map/reduce_scatter | solution.py:71
  512.6 59.9 %all-gather.19.cloned.1.call-start = ((), (), s32[]{:S(2)}) async-start(), calls=%async_computation.26 | async-start | bytes 2621440 | tf_op jit(solution)/shard_map/all_gather | solution.py:58
  549.8 79.7 %reduce-scatter.27.cloned.1.call-start = ((), (), s32[]{:S(2)}) async-start(), calls=%async_computation.27 | async-start | bytes 2621440 | tf_op jit(solution)/shard_map/reduce_scatter | solution.py:71
  596.9 59.6 %all-gather.21.cloned.1.call-start = ((), (), s32[]{:S(2)}) async-start(), calls=%async_computation.28 | async-start | bytes 2621440 | tf_op jit(solution)/shard_map/all_gather | solution.py:58
  633.7 166.5 %reduce-scatter.29.cloned.1.call-start = ((), (), s32[]{:S(2)}) async-start(), calls=%async_computation.29 | async-start | bytes 2621440 | tf_op jit(solution)/shard_map/reduce_scatter | solution.py:71
  768.6 59.1 %all-gather.23.cloned.1.call-start = ((), (), s32[]{:S(2)}) async-start(), calls=%async_computation.30 | async-start | bytes 2621440 | tf_op jit(solution)/shard_map/all_gather | solution.py:58
  804.9 131.0 %reduce-scatter.41.cloned.1.call-start = ((), (), s32[]{:S(2)}) async-start(), calls=%async_computation.36 | async-start | bytes 2359296 | tf_op jit(solution)/shard_map/reduce_scatter | solution.py:417
  809.3 130.1 %reduce-scatter.31.cloned.1.call-start = ((), (), s32[]{:S(2)}) async-start(), calls=%async_computation.31 | async-start | bytes 2621440 | tf_op jit(solution)/shard_map/reduce_scatter | solution.py:71
  839.6 186.8 %reduce-scatter.47.cloned.1.call-start = ((), (), s32[]{:S(2)}) async-start(), calls=%async_computation.39 | async-start | bytes 4718592 | tf_op jit(solution)/shard_map/reduce_scatter | solution.py:420
  846.9 271.9 %reduce-scatter.45.cloned.1.call-start = ((), (), s32[]{:S(2)}) async-start(), calls=%async_computation.38 | async-start | bytes 4718592 | tf_op jit(solution)/shard_map/reduce_scatter | solution.py:419
  853.6 332.6 %reduce-scatter.43.cloned.1.call-start = ((), (), s32[]{:S(2)}) async-start(), calls=%async_computation.37 | async-start | bytes 1179648 | tf_op jit(solution)/shard_map/reduce_scatter | solution.py:418
  858.3 395.3 %reduce-scatter.39.cloned.1.call-start = ((), (), s32[]{:S(2)}) async-start(), calls=%async_computation.35 | async-start | bytes 1179648 | tf_op jit(solution)/shard_map/reduce_scatter | solution.py:416
  861.7 469.8 %reduce-scatter.37.cloned.1.call-start = ((), (), s32[]{:S(2)}) async-start(), calls=%async_computation.34 | async-start | bytes 3538944 | tf_op jit(solution)/shard_map/reduce_scatter | solution.py:415
  867.2 556.1 %reduce-scatter.35.cloned.1.call-start = ((), (), s32[]{:S(2)}) async-start(), calls=%async_computation.33 | async-start | bytes 4718592 | tf_op jit(solution)/shard_map/reduce_scatter | solution.py:414
  874.6 641.1 %reduce-scatter.33.cloned.1.call-start = ((), (), s32[]{:S(2)}) async-start(), calls=%async_computation.32 | async-start | bytes 4718592 | tf_op jit(solution)/shard_map/reduce_scatter | solution.py:413
  (99 other events, 2895.5 us)
Sparse Core Ops, SparseCore 0:
  12.9 25.2 all-gather.8
  48.8 31.4 reduce-scatter.16
  86.5 22.5 all-gather.10
  286.8 31.4 reduce-scatter.18
  322.5 22.5 all-gather.12
  371.7 32.7 reduce-scatter.20
  409.0 22.5 all-gather.14
  442.1 31.4 reduce-scatter.22
  478.7 22.5 all-gather.16
  512.7 31.4 reduce-scatter.24
  549.9 22.5 all-gather.18
  597.0 32.4 reduce-scatter.26
  633.8 22.5 all-gather.20
  768.7 31.4 reduce-scatter.28
  805.1 22.5 all-gather.22
  831.5 67.5 reduce-scatter.40
  901.6 30.4 reduce-scatter.30
  936.2 90.1 reduce-scatter.46
  1031.0 87.6 reduce-scatter.44
  1122.6 63.5 reduce-scatter.42
  1190.6 62.9 reduce-scatter.38
  1257.7 73.6 reduce-scatter.36
  1335.7 87.5 reduce-scatter.34
  1427.8 87.8 reduce-scatter.32
where the time goes:
time: 1530 us; the launch traced here: 1520 us
  waiting for transfers between devices  931 us (61%)
  local copies, waits for them, and re-layouts  224 us (15%)
  matrix products  172 us (11%)
  blocking collectives  96.7 us (6%)
  other arithmetic  81.1 us (5%)
  between operations  16.1 us (1%)
    reduce_scatter x4, waiting for transfers between devices, reduce_branch(): lax.psum_scatter(term_fn(jnp.int32(0), lax.axis_size('mp') * row_count).a...  127 us
    reduce_scatter x4, waiting for transfers between devices, reduce_inputs(): lax.psum_scatter(term_fn(jnp.int32(0), lax.axis_size('mp') * row_count).a...  95.3 us
    all_gather x4, waiting for transfers between devices, spread_rows(): return lax.all_gather(normed, 'mp', axis=0, tiled=True)  93.1 us
    reduce_scatter x1, waiting for transfers between devices, body(): lax.psum_scatter(grad_w1_in, 'dp', scatter_dimension=0, tiled=True)  92.4 us
    reduce_scatter x1, waiting for transfers between devices, body(): lax.psum_scatter(grad_w2_in, 'dp', scatter_dimension=0, tiled=True)  92.3 us
    reduce_scatter x1, waiting for transfers between devices, body(): lax.psum_scatter(grad_w1_out, 'dp', scatter_dimension=1, tiled=True)  91.8 us
    all_gather x4, waiting for transfers between devices, fetch_grads(): return lax.all_gather(grad_rows, 'mp', axis=0, tiled=True)  85.7 us
    reduce_scatter x1, waiting for transfers between devices, body(): lax.psum_scatter(grad_w_qkv, 'dp', scatter_dimension=0, tiled=True)  77.9 us
  transfers between devices with their start and end apart: 24, of which 22 were waited for; matrix products, arithmetic and copies ran while one was open for 5% of the time, Pallas kernels for 0%

commit v1 on v0

--- a/solution.py
+++ b/solution.py
@@ -1,11 +1,17 @@
+import functools
+
 import jax
 import jax.numpy as jnp
 from jax import lax
+from jax.experimental import pallas as pl
+from jax.experimental.pallas import tpu as pltpu
 from jax.sharding import PartitionSpec as P
 
 HEAD = 64
 REL_LEFT = 64
 REL_RIGHT = 8
+BQ = 128
+WIN = 4 * BQ
 
 
 epsilon = 1e-05
@@ -80,19 +86,162 @@
     return (first_grad, second_grad)
 
 
-def band_bias(relative, first_row, key_count):
-    block_len = relative.shape[2]
-    line_len = key_count + block_len
-    spots = jnp.arange(line_len, dtype=jnp.int32) - (block_len - 1) - first_row
-    offsets = jnp.clip(spots, -REL_LEFT, REL_RIGHT) + REL_LEFT
-    selector = (jnp.arange(relative.shape[3], dtype=jnp.int32)[:, None] == offsets[None, :]).astype(
-        jnp.float32
-    )
-    lines = jnp.einsum("chir,rx->chix", relative, selector, precision=highest)
-    lead = lines.shape[:2]
-    flat = lines.reshape(lead + (block_len * line_len,))
-    skewed = flat[..., block_len - 1 : block_len - 1 + block_len * (line_len - 1)]
-    return skewed.reshape(lead + (block_len, line_len - 1))[..., :key_count]
+def nt(a, b):
+    return lax.dot_general(a, b, (((1,), (1,)), ((), ())), preferred_element_type=jnp.float32)
+def nn(a, b):
+    return lax.dot_general(a, b, (((1,), (0,)), ((), ())), preferred_element_type=jnp.float32)
+def tn(a, b):
+    return lax.dot_general(a, b, (((0,), (0,)), ((), ())), preferred_element_type=jnp.float32)
+
+def split_pair(x):
+    left = lax.broadcasted_iota(jnp.int32, x.shape, 1) < HEAD
+    zero = jnp.zeros_like(x)
+    return jnp.concatenate([jnp.where(left, x, zero), jnp.where(left, zero, x)], 0)
+
+def join_pair(x):
+    rows = x.shape[0] // 2
+    left = lax.broadcasted_iota(jnp.int32, (rows, x.shape[1]), 1) < HEAD
+    return jnp.where(left, x[:rows], x[rows:])
+
+def fwd_kernel(q_ref, k_ref, v_ref, rel_ref, mixed_ref, probs_ref, bias_ref):
+    ib = pl.program_id(1)
+    qs = split_pair(q_ref[...] * 0.125)
+    s = nt(qs, k_ref[...])
+    b = nt(qs, rel_ref[...])
+    rows = b.shape[0] // 2
+    bias_ref[:, 0:BQ] = b[:, 3 * BQ : 4 * BQ]
+    for h in range(2):
+        r = pltpu.roll(b[h * rows : (h + 1) * rows, :WIN], 0, 1, stride=1, stride_axis=0)
+        bias_ref[h * rows : (h + 1) * rows, BQ : 4 * BQ] = r[:, : 3 * BQ]
+    bias_ref[:, 4 * BQ :] = b[:, 4 * BQ :]
+    nkeys = s.shape[1] // BQ
+    parts = []
+    for jb in range(nkeys):
+        at = pl.multiple_of(jnp.clip(jb - ib + 2, 0, 4) * BQ, BQ)
+        parts.append(s[:, jb * BQ : (jb + 1) * BQ] + bias_ref[:, pl.ds(at, BQ)])
+    top = functools.reduce(jnp.maximum, parts)
+    m = jnp.max(top, -1, keepdims=True)
+    es = [jnp.exp(p - m) for p in parts]
+    tot = jnp.sum(functools.reduce(jnp.add, es), -1, keepdims=True)
+    inv = 1.0 / tot
+    for jb in range(nkeys):
+        probs_ref[0, :, jb * BQ : (jb + 1) * BQ] = (es[jb] * inv).astype(jnp.bfloat16)
+    mixed_ref[...] = join_pair(nn(probs_ref[0], v_ref[...])).astype(jnp.bfloat16)
+
+def bwd_kernel(q_ref, k_ref, v_ref, relb_ref, hot_ref, probs_ref, do_ref, dq_ref, dk_ref, dv_ref, dt_ref,
+               tot_ref, dkt, dvt, dta, dz_ref):
+    pr, ib, nb = pl.program_id(0), pl.program_id(1), pl.num_programs(1)
+    @pl.when(ib == 0)
+    def _():
+        dkt[...] = jnp.zeros_like(dkt)
+        dvt[...] = jnp.zeros_like(dvt)
+    @pl.when((ib == 0) & (pr == 0))
+    def _():
+        dta[...] = jnp.zeros_like(dta)
+    qs = split_pair(q_ref[...] * 0.125)
+    dos = split_pair(do_ref[...])
+    p = probs_ref[0]
+    dp = nt(dos, v_ref[...])
+    nkeys = dp.shape[1] // BQ
+    dvt[...] += tn(dos, p)
+    pf = p.astype(jnp.float32)
+    acc = None
+    for jb in range(nkeys):
+        sl = slice(jb * BQ, (jb + 1) * BQ)
+        t = pf[:, sl] * dp[:, sl]
+        acc = t if acc is None else acc + t
+    inner = jnp.sum(acc, -1, keepdims=True)
+    tot_ref[...] = jnp.zeros_like(tot_ref)
+    for jb in range(nkeys):
+        sl = slice(jb * BQ, (jb + 1) * BQ)
+        dz = (pf[:, sl] * (dp[:, sl] - inner)).astype(jnp.bfloat16)
+        dz_ref[:, sl] = dz
+        at = pl.multiple_of(jnp.clip(jb - ib + 2, 0, 4) * BQ, BQ)
+        tot_ref[:, pl.ds(at, BQ)] += dz.astype(jnp.float32)
+    rows = BQ
+    r2 = lax.broadcasted_iota(jnp.int32, (2 * rows, 2 * rows), 0)
+    c2 = lax.broadcasted_iota(jnp.int32, (2 * rows, 2 * rows), 1)
+    mirror = (r2 + c2 == jnp.where(r2 < rows, rows - 1, 3 * rows - 1)).astype(jnp.bfloat16)
+    w = jnp.concatenate([tot_ref[:, BQ : 4 * BQ].astype(jnp.bfloat16), jnp.zeros((2 * rows, BQ), jnp.bfloat16)], 1)
+    w = nn(mirror, w)
+    outs = [pltpu.roll(w[h * rows : (h + 1) * rows], WIN - rows + 1, 1, stride=1, stride_axis=0) for h in range(2)]
+    d = nn(mirror, jnp.concatenate(outs, 0).astype(jnp.bfloat16)).astype(jnp.bfloat16)
+    drel = nn(d, hot_ref[...])
+    col = lax.broadcasted_iota(jnp.int32, drel.shape, 1)
+    low = jnp.sum(tot_ref[:, :BQ], -1, keepdims=True)
+    high = jnp.sum(tot_ref[:, 4 * BQ :], -1, keepdims=True)
+    drel = drel + jnp.where(col == 0, low, 0.0) + jnp.where(col == REL_LEFT + REL_RIGHT, high, 0.0)
+    drel = drel.astype(jnp.bfloat16)
+    dz = dz_ref[...]
+    dq = nn(dz, k_ref[...]) + nn(drel, relb_ref[...])
+    dq_ref[...] = (join_pair(dq) * 0.125).astype(jnp.bfloat16)
+    dkt[...] += tn(qs, dz)
+    dta[...] += tn(drel, qs)
+    @pl.when(ib == nb - 1)
+    def _():
+        dk_ref[...] = dkt[...].T.astype(jnp.bfloat16)
+        dv_ref[...] = dvt[...].T.astype(jnp.bfloat16)
+        dt_ref[...] = dta[...]
+
+def rel_tables(rel_table):
+    spots = jnp.arange(5 * BQ)
+    idx = jnp.where(spots < 3 * BQ, jnp.clip(spots - REL_LEFT, 0, REL_LEFT + REL_RIGHT), jnp.where(spots < 4 * BQ, 0, REL_LEFT + REL_RIGHT))
+    hot = (jnp.arange(BQ)[None, :] == idx[:, None]).astype(jnp.bfloat16)
+    padded = jnp.pad(rel_table, ((0, BQ - rel_table.shape[0]), (0, 0)))
+    padded = jnp.concatenate([padded, padded], 1)
+    ext = jnp.dot(hot, padded, preferred_element_type=jnp.float32).astype(jnp.bfloat16)
+    return ext, hot[:WIN], padded
+
+def attn_fwd(qkv, ext):
+    frames, cols = qkv.shape
+    pairs = cols // 3 // 128
+    nb = frames // BQ
+    bf = jnp.bfloat16
+    return pl.pallas_call(
+        fwd_kernel,
+        grid=(pairs, nb),
+        in_specs=[
+            pl.BlockSpec((BQ, 128), lambda p, i: (i, p)),
+            pl.BlockSpec((frames, 128), lambda p, i: (0, pairs + p)),
+            pl.BlockSpec((frames, 128), lambda p, i: (0, 2 * pairs + p)),
+            pl.BlockSpec(ext.shape, lambda p, i: (0, 0)),
+        ],
+        out_specs=[
+            pl.BlockSpec((BQ, 128), lambda p, i: (i, p)),
+            pl.BlockSpec((1, 2 * BQ, frames), lambda p, i: (p, i, 0)),
+        ],
+        out_shape=[jax.ShapeDtypeStruct((frames, cols // 3), bf), jax.ShapeDtypeStruct((pairs, 2 * frames, frames), bf)],
+        scratch_shapes=[pltpu.VMEM((2 * BQ, 5 * BQ), jnp.float32)],
+        compiler_params=pltpu.CompilerParams(vmem_limit_bytes=48 << 20),
+        name="attn_fwd",
+    )(qkv, qkv, qkv, ext)
+
+def attn_bwd(qkv, padded, hot, probs, dmixed):
+    frames, cols = qkv.shape
+    pairs = cols // 3 // 128
+    nb = frames // BQ
+    bf = jnp.bfloat16
+    blk = pl.BlockSpec((BQ, 128), lambda p, i: (i, p))
+    full = pl.BlockSpec((frames, 128), lambda p, i: (0, p))
+    return pl.pallas_call(
+        bwd_kernel,
+        grid=(pairs, nb),
+        in_specs=[
+            blk,
+            pl.BlockSpec((frames, 128), lambda p, i: (0, pairs + p)),
+            pl.BlockSpec((frames, 128), lambda p, i: (0, 2 * pairs + p)),
+            pl.BlockSpec(padded.shape, lambda p, i: (0, 0)),
+            pl.BlockSpec(hot.shape, lambda p, i: (0, 0)),
+            pl.BlockSpec((1, 2 * BQ, frames), lambda p, i: (p, i, 0)),
+            blk,
+        ],
+        out_specs=[blk, full, full, pl.BlockSpec((128, 128), lambda p, i: (0, 0))],
+        out_shape=[jax.ShapeDtypeStruct((frames, cols // 3), bf)] * 3 + [jax.ShapeDtypeStruct((128, 128), jnp.float32)],
+        scratch_shapes=[pltpu.VMEM((2 * BQ, 5 * BQ), jnp.float32), pltpu.VMEM((128, frames), jnp.float32), pltpu.VMEM((128, frames), jnp.float32),
+                        pltpu.VMEM((128, 128), jnp.float32), pltpu.VMEM((2 * BQ, frames), bf)],
+        compiler_params=pltpu.CompilerParams(vmem_limit_bytes=48 << 20),
+        name="attn_bwd",
+    )(qkv, qkv, qkv, padded, hot, probs, dmixed)
 
 
 def feed_forward(stream, gain, w_in, w_out):
@@ -123,116 +272,35 @@
     return (grad_stream + grad_in, grad_w_in, grad_w_out, grad_gain)
 
 
-def score_block(query_block, keys_all, rel_table, first_row):
-    logits = jnp.einsum(
-        "icha,jcha->chij", query_block, keys_all, preferred_element_type=jnp.float32
-    )
-    relative = jnp.einsum(
-        "icha,ra->chir", query_block, rel_table, preferred_element_type=jnp.float32
-    )
-    rel_bias = band_bias(relative, first_row, keys_all.shape[0])
-    return ((logits + rel_bias) * 0.125, relative)
-
-
 def attention(stream, gain, w_qkv, w_attn_out, rel_table, clip_count):
     normed, unit_rows, inverse = norm_rows(stream, gain.astype(jnp.float32))
     gathered = spread_rows(normed.astype(jnp.bfloat16))
-    projected = jnp.einsum(
-        "rd,dkc->rkc", gathered, w_qkv, preferred_element_type=jnp.float32
-    ).astype(jnp.bfloat16)
-    frames = gathered.shape[0] // clip_count
-    heads_here = w_qkv.shape[2] // HEAD
-    qkv_split = projected.reshape(frames, clip_count, 3, heads_here, HEAD)
-    queries = qkv_split[:, :, 0]
-    keys_all = qkv_split[:, :, 1]
-    values_all = qkv_split[:, :, 2]
-    block_rows = min(512, frames)
-    mixed_blocks = []
-    totals = []
-    for first_row in range(0, frames, block_rows):
-        scores, relative = score_block(
-            queries[first_row : first_row + block_rows], keys_all, rel_table, first_row
-        )
-        row_max = jnp.max(scores, -1, keepdims=True)
-        weights = jnp.exp(scores - row_max)
-        row_sum = jnp.sum(weights, -1, keepdims=True)
-        attn_probs = (weights / row_sum).astype(jnp.bfloat16)
-        mixed_blocks.append(
-            jnp.einsum(
-                "chij,jcha->icha", attn_probs, values_all, preferred_element_type=jnp.float32
-            )
-        )
-        totals.append(row_max + jnp.log(row_sum))
-    mixed = (
-        jnp.concatenate(mixed_blocks, 0)
-        .astype(jnp.bfloat16)
-        .reshape(frames * clip_count, heads_here * HEAD)
-    )
+    flat_qkv = w_qkv.reshape(w_qkv.shape[0], -1)
+    projected = jnp.dot(gathered, flat_qkv, preferred_element_type=jnp.float32).astype(jnp.bfloat16)
+    tables = rel_tables(rel_table)
+    mixed, probs = attn_fwd(projected, tables[0])
 
     def attention_branch_rows(first_row, row_count):
         return jnp.dot(mixed, w_attn_out, preferred_element_type=jnp.float32)
 
     branch = reduce_branch(attention_branch_rows, stream.shape[0])
-    return (branch, (unit_rows, inverse, gathered, qkv_split, mixed, totals))
+    return (branch, (unit_rows, inverse, gathered, projected, mixed, probs, tables))
 
 
 def attention_back(grad_stream, kept_state, gain, w_qkv, w_attn_out, rel_table, clip_count):
-    unit_rows, inverse, gathered, qkv_split, mixed, totals = kept_state
+    unit_rows, inverse, gathered, projected, mixed, probs, tables = kept_state
     grad_branch = fetch_grads(grad_stream.astype(jnp.bfloat16))
     grad_w_attn_out = contract_rows(mixed, grad_branch)
-    frames = qkv_split.shape[0]
-    heads_here = qkv_split.shape[3]
-    grad_mixed = (
-        contract_cols(grad_branch, w_attn_out)
-        .astype(jnp.bfloat16)
-        .reshape(frames, clip_count, heads_here, HEAD)
-    )
-    queries = qkv_split[:, :, 0]
-    keys_all = qkv_split[:, :, 1]
-    values_all = qkv_split[:, :, 2]
-    block_rows = min(512, frames)
-    grad_keys = jnp.zeros(keys_all.shape, jnp.float32)
-    grad_values = jnp.zeros(values_all.shape, jnp.float32)
-    grad_table = jnp.zeros(rel_table.shape, jnp.float32)
-    query_grads = []
-    for block_index, first_row in enumerate(range(0, frames, block_rows)):
-        query_block = queries[first_row : first_row + block_rows]
-        scores, relative = score_block(query_block, keys_all, rel_table, first_row)
-        attn_probs = jnp.exp(scores - totals[block_index])
-        grad_out = grad_mixed[first_row : first_row + block_rows]
-        grad_probs = jnp.einsum(
-            "icha,jcha->chij", grad_out, values_all, preferred_element_type=jnp.float32
-        )
-        inner_sum = jnp.sum(attn_probs * grad_probs, -1, keepdims=True)
-        grad_scores = (attn_probs * (grad_probs - inner_sum)).astype(jnp.bfloat16) * 0.125
-        grad_values = grad_values + jnp.einsum(
-            "chij,icha->jcha",
-            attn_probs.astype(jnp.bfloat16),
-            grad_out,
-            preferred_element_type=jnp.float32,
-        )
-        grad_keys = grad_keys + jnp.einsum(
-            "chij,icha->jcha", grad_scores, query_block, preferred_element_type=jnp.float32
-        )
-        bias_fn = lambda rel_values: band_bias(rel_values, first_row, keys_all.shape[0])
-        pulled = jax.vjp(bias_fn, relative)[1](grad_scores.astype(jnp.float32))[0]
-        grad_relative = pulled.astype(jnp.bfloat16)
-        grad_query = jnp.einsum(
-            "chij,jcha->icha", grad_scores, keys_all, preferred_element_type=jnp.float32
-        )
-        grad_query = grad_query + jnp.einsum(
-            "chir,ra->icha", grad_relative, rel_table, preferred_element_type=jnp.float32
-        )
-        grad_table = grad_table + jnp.einsum(
-            "chir,icha->ra", grad_relative, query_block, preferred_element_type=jnp.float32
-        )
-        query_grads.append(grad_query)
-    grad_split = jnp.stack([jnp.concatenate(query_grads, 0), grad_keys, grad_values], 2)
-    grad_split = grad_split.astype(jnp.bfloat16).reshape(frames * clip_count, 3, heads_here * HEAD)
-    grad_w_qkv = jnp.einsum("rd,rkc->dkc", gathered, grad_split, preferred_element_type=jnp.float32)
+    grad_mixed = contract_cols(grad_branch, w_attn_out).astype(jnp.bfloat16)
+    dq, dk, dv, dt = attn_bwd(projected, tables[2], tables[1], probs, grad_mixed)
+    rel = rel_table.shape[0]
+    grad_table = dt[:rel, :HEAD] + dt[:rel, HEAD:]
+    grad_split = jnp.concatenate([dq, dk, dv], 1)
+    grad_w_qkv = contract_rows(gathered, grad_split).reshape(w_qkv.shape)
+    flat_qkv = w_qkv.reshape(w_qkv.shape[0], -1)
 
     def attention_input_rows(first_row, row_count):
-        return jnp.einsum("rkc,dkc->rd", grad_split, w_qkv, preferred_element_type=jnp.float32)
+        return contract_cols(grad_split, flat_qkv)
 
     grad_normed = reduce_inputs(attention_input_rows, grad_stream.shape[0])
     grad_in, grad_gain = norm_back(grad_normed, unit_rows, inverse, gain.astype(jnp.float32))
@@ -335,6 +403,27 @@
         grad_w_depth,
         grad_gain_depth,
     )
+
+
+def halve_sum(grad, dim):
+    count = lax.axis_size("dp")
+    me = lax.axis_index("dp")
+    part = grad.astype(jnp.bfloat16)
+    shape = part.shape
+    size = shape[dim] // count
+    step = 1
+    part = part.reshape(shape[:dim] + (count, size) + shape[dim + 1 :])
+    while step < count:
+        groups = part.shape[dim] // 2
+        paired = part.reshape(part.shape[:dim] + (groups, 2) + part.shape[dim + 1 :])
+        bit = (me // step) % 2
+        keep = lax.dynamic_index_in_dim(paired, bit, dim + 1, keepdims=False)
+        give = lax.dynamic_index_in_dim(paired, 1 - bit, dim + 1, keepdims=False)
+        got = lax.ppermute(give, "dp", [(i, i ^ step) for i in range(count)])
+        total = keep.astype(jnp.float32) + got.astype(jnp.float32)
+        step *= 2
+        part = total.astype(jnp.bfloat16) if step < count else total
+    return part.reshape(shape[:dim] + (size,) + shape[dim + 1 :])
 
 
 def body(
@@ -410,14 +499,14 @@
     )
     grad_w1_in, grad_w1_out = settle_block(grad_w1_in, grad_w1_out)
     summed = (
-        lax.psum_scatter(grad_w1_in, "dp", scatter_dimension=0, tiled=True),
-        lax.psum_scatter(grad_w1_out, "dp", scatter_dimension=1, tiled=True),
-        lax.psum_scatter(grad_w_qkv, "dp", scatter_dimension=0, tiled=True),
-        lax.psum_scatter(grad_w_attn_out, "dp", scatter_dimension=1, tiled=True),
-        lax.psum_scatter(grad_w_conv_in, "dp", scatter_dimension=0, tiled=True),
-        lax.psum_scatter(grad_w_conv_out, "dp", scatter_dimension=1, tiled=True),
-        lax.psum_scatter(grad_w2_in, "dp", scatter_dimension=0, tiled=True),
-        lax.psum_scatter(grad_w2_out, "dp", scatter_dimension=1, tiled=True),
+        halve_sum(grad_w1_in, 0),
+        halve_sum(grad_w1_out, 1),
+        halve_sum(grad_w_qkv, 0),
+        halve_sum(grad_w_attn_out, 1),
+        halve_sum(grad_w_conv_in, 0),
+        halve_sum(grad_w_conv_out, 1),
+        halve_sum(grad_w2_in, 0),
+        halve_sum(grad_w2_out, 1),
     )
     gain_grads = jnp.stack(
         [grad_gain_ffn1, grad_gain_attn, grad_gain_conv, grad_gain_ffn2, grad_final]

time: 1530 us -> 858 us (0.56)
  waiting for transfers between devices: 931 us -> 423 us
  local copies, waits for them, and re-layouts: 224 us -> 61.2 us
  matrix products: 172 us -> 91.5 us
  Pallas kernels: 0 us -> 50.5 us
  starting transfers between devices: 2.37 us -> 23.1 us
    reduce_scatter x8 -> x0, waiting for transfers between devices: 529 us -> none  [the longest x1 92.4 us: body(): lax.psum_scatter(grad_w1_in, 'dp', scatter_dimension=0, tiled=True)]
    ppermute x0 -> x24, waiting for transfers between devices: none -> 98.2 us  [halve_sum(): got = lax.ppermute(give, 'dp', [(i, i ^ step) for i in range(count)])]
    reshape x6 -> x0, local copies, waits for them, and re-layouts: 90.2 us -> none  [the longest x4 54.7 us: band_bias(): return skewed.reshape(lead + (block_len, line_len - 1))[..., :key_count]]
    dot_general x25 -> x2, matrix products: 76.7 us -> 4.15 us  [the longest x1 3.86 us: attention(): jnp.dot(gathered, flat_qkv, preferred_element_type=jnp.float32)]
    pallas_call x0 -> x2, Pallas kernels: none -> 50.5 us  [the longest x1 29.2 us: attn_bwd(): pl.pallas_call(bwd_kernel, grid=(pairs, nb), in_specs=[blk, pl.BlockSpec(...]
    unnamed x205 -> x150, local copies, waits for them, and re-layouts: 77.8 us -> 31.5 us
    all_gather x4, waiting for transfers between devices: 85.7 us -> 45 us  [fetch_grads(): return lax.all_gather(grad_rows, 'mp', axis=0, tiled=True)]
    reduce_scatter x4, waiting for transfers between devices: 95.3 us -> 63.9 us  [reduce_inputs(): lax.psum_scatter(term_fn(jnp.int32(0), lax.axis_size('mp') * row_count).a...]
  transfers between devices with their start and end apart: 24 -> 40, of which waited for: 22 -> 27; matrix products, arithmetic and copies ran while one was open for 5% -> 14% of each run, Pallas kernels for 0% -> 3%
where the time goes in v1:
time: 858 us; the launch traced here: 848 us
  waiting for transfers between devices  423 us (49%)
  blocking collectives  96.4 us (11%)
  matrix products  91.5 us (11%)
  other arithmetic  87 us (10%)
  local copies, waits for them, and re-layouts  61.2 us (7%)
  Pallas kernels  50.5 us (6%)
  starting transfers between devices  23.1 us (3%)
  between operations  15.4 us (2%)
    reduce_scatter x4, waiting for transfers between devices, reduce_branch(): lax.psum_scatter(term_fn(jnp.int32(0), lax.axis_size('mp') * row_count).a...  126 us
    ppermute x24, waiting for transfers between devices, halve_sum(): got = lax.ppermute(give, 'dp', [(i, i ^ step) for i in range(count)])  98.2 us
    all_gather x4, waiting for transfers between devices, spread_rows(): return lax.all_gather(normed, 'mp', axis=0, tiled=True)  90.2 us
    reduce_scatter x4, waiting for transfers between devices, reduce_inputs(): lax.psum_scatter(term_fn(jnp.int32(0), lax.axis_size('mp') * row_count).a...  63.9 us
    all_gather x4, waiting for transfers between devices, fetch_grads(): return lax.all_gather(grad_rows, 'mp', axis=0, tiled=True)  45 us
    psum x1, blocking collectives, body(): depth_sum, depth_gain_sum = lax.psum((grad_w_depth, grad_gain_depth), 'dp')  39.7 us
    psum x1, blocking collectives, body(): lax.psum((gain_grads, grad_table, squares), ('dp', 'mp'))  39.2 us
    unnamed x150, local copies, waits for them, and re-layouts  31.5 us
  transfers between devices with their start and end apart: 40, of which 27 were waited for; matrix products, arithmetic and copies ran while one was open for 14% of the time, Pallas kernels for 3%

profile of v1, /device:TPU:0, one launch (start us, length us, event | category | flops | bytes accessed | tf_op | source)
XLA Modules:
  0.0 848.2 jit_solution(9263735794834223683)
XLA Ops:
  13.4 25.4 %all-gather.9.cloned.1.call-done = bf16[1024,1024]{1,0:T(8,128)(2,1)} async-done(((bf16[256,1024]{1,0:T(8,128)(2,1)}), bf16[1024,1024]{1,0:T(8,128)(2,1)}) %all-gather.9.cloned.1.call-update) | async-done | bytes 2097168 | tf_op jit(solution)/shard_map/all_gather | solution.py:60
  49.9 30.9 %reduce-scatter.9.cloned.1.call-done = bf16[256,1024]{1,0:T(8,128)(2,1)} async-done(((bf16[1024,1024]{1,0:T(8,128)(2,1)}), bf16[256,1024]{1,0:T(8,128)(2,1)}) %reduce-scatter.9.cloned.1.call-update) | async-done | bytes 524304 | tf_op jit(solution)/shard_map/reduce_scatter | solution.py:68
  88.5 19.7 %all-gather.11.cloned.1.call-done = bf16[1024,1024]{1,0:T(8,128)(2,1)} async-done(((bf16[256,1024]{1,0:T(8,128)(2,1)}), bf16[1024,1024]{1,0:T(8,128)(2,1)}) %all-gather.11.cloned.1.call-update) | async-done | bytes 2097168 | tf_op jit(solution)/shard_map/all_gather | solution.py:60
  112.1 21.3 %attn_fwd.1 = (bf16[1024,256]{1,0:T(8,128)(2,1)S(1)}, bf16[2,2048,1024]{2,1,0:T(8,128)(2,1)}) custom-call(bf16[1024,768]{1,0:T(8,128)(2,1)S(1)} %convolution_convert_fusion.12.q_ref.k_ref.v_ref, bf16[1024,768]{1,0:T(8,128)(2,1)S(1)} %convolution_convert_fusion.12.q_ref.k_ref.v_ref, bf16[1024,768]{1,0:T(8,128)(2,1)S(1)} %convolution_convert_fusion.12.q_ref.k_ref.v_ref, ...), custom_call_target="tpu_custom_call" | custom-call | tf_op jit(solution)/shard_map/attn_fwd/pallas_call | solution.py:200
  135.6 31.5 %reduce-scatter.11.cloned.1.call-done = bf16[256,1024]{1,0:T(8,128)(2,1)} async-done(((bf16[1024,1024]{1,0:T(8,128)(2,1)}), bf16[256,1024]{1,0:T(8,128)(2,1)}) %reduce-scatter.11.cloned.1.call-update) | async-done | bytes 524304 | tf_op jit(solution)/shard_map/reduce_scatter | solution.py:68
  171.6 22.4 %all-gather.13.cloned.1.call-done = bf16[1024,1024]{1,0:T(8,128)(2,1)} async-done(((bf16[256,1024]{1,0:T(8,128)(2,1)}), bf16[1024,1024]{1,0:T(8,128)(2,1)}) %all-gather.13.cloned.1.call-update) | async-done | bytes 2097168 | tf_op jit(solution)/shard_map/all_gather | solution.py:60
  221.1 32.3 %reduce-scatter.13.cloned.1.call-done = bf16[256,1024]{1,0:T(8,128)(2,1)} async-done(((bf16[1024,1024]{1,0:T(8,128)(2,1)}), bf16[256,1024]{1,0:T(8,128)(2,1)}) %reduce-scatter.13.cloned.1.call-update) | async-done | bytes 524304 | tf_op jit(solution)/shard_map/reduce_scatter | solution.py:68
  257.7 22.7 %all-gather.15.cloned.1.call-done = bf16[1024,1024]{1,0:T(8,128)(2,1)} async-done(((bf16[256,1024]{1,0:T(8,128)(2,1)}), bf16[1024,1024]{1,0:T(8,128)(2,1)}) %all-gather.15.cloned.1.call-update) | async-done | bytes 2097168 | tf_op jit(solution)/shard_map/all_gather | solution.py:60
  291.4 30.9 %reduce-scatter.15.cloned.1.call-done = bf16[256,1024]{1,0:T(8,128)(2,1)} async-done(((bf16[1024,1024]{1,0:T(8,128)(2,1)}), bf16[256,1024]{1,0:T(8,128)(2,1)}) %reduce-scatter.15.cloned.1.call-update) | async-done | bytes 524304 | tf_op jit(solution)/shard_map/reduce_scatter | solution.py:68
  327.7 22.3 %all-gather.17.cloned.1.call-done = bf16[1024,1024]{1,0:T(8,128)(2,1)} async-done(((bf16[256,1024]{1,0:T(8,128)(2,1)}), bf16[1024,1024]{1,0:T(8,128)(2,1)}) %all-gather.17.cloned.1.call-update) | async-done | bytes 2097168 | tf_op jit(solution)/shard_map/all_gather | solution.py:64
  361.4 31.5 %reduce-scatter.17.cloned.1.call-done = bf16[256,1024]{1,0:T(8,128)(2,1)} async-done(((bf16[1024,1024]{1,0:T(8,128)(2,1)}), bf16[256,1024]{1,0:T(8,128)(2,1)}) %reduce-scatter.17.cloned.1.call-update) | async-done | bytes 524304 | tf_op jit(solution)/shard_map/reduce_scatter | solution.py:77
  398.0 22.7 %all-gather.19.cloned.1.call-done = bf16[1024,1024]{1,0:T(8,128)(2,1)} async-done(((bf16[256,1024]{1,0:T(8,128)(2,1)}), bf16[1024,1024]{1,0:T(8,128)(2,1)}) %all-gather.19.cloned.1.call-update) | async-done | bytes 2097168 | tf_op jit(solution)/shard_map/all_gather | solution.py:64
  444.6 32.4 %reduce-scatter.19.cloned.1.call-done = bf16[256,1024]{1,0:T(8,128)(2,1)} async-done(((bf16[1024,1024]{1,0:T(8,128)(2,1)}), bf16[256,1024]{1,0:T(8,128)(2,1)}) %reduce-scatter.19.cloned.1.call-update) | async-done | bytes 524304 | tf_op jit(solution)/shard_map/reduce_scatter | solution.py:77
  498.9 16.8 %collective-permute-done.21 = bf16[1024,4,128]{2,0,1:T(8,128)(2,1)} collective-permute-done((bf16[1024,4,128]{2,0,1:T(8,128)(2,1)}, bf16[1024,4,128]{2,0,1:T(8,128)(2,1)}, u32[]{:S(2)}, u32[]{:S(2)}) %collective-permute-start.21) | collective-permute-done | bytes 1048608 | tf_op jit(solution)/shard_map/ppermute | solution.py:422
  520.7 29.2 %attn_bwd.1 = (bf16[1024,256]{1,0:T(8,128)(2,1)S(1)}, bf16[1024,256]{1,0:T(8,128)(2,1)S(1)}, bf16[1024,256]{1,0:T(8,128)(2,1)S(1)}, f32[128,128]{1,0:T(8,128)S(1)}) custom-call(bf16[1024,768]{1,0:T(8,128)(2,1)S(1)} %copy-done.3, bf16[1024,768]{1,0:T(8,128)(2,1)S(1)} %copy-done.3, bf16[1024,768]{1,0:T(8,128)(2,1)S(1)} %copy-done.3, ...), custom_call_target="tpu_custom_call" | custom-call | tf_op jit(solution)/shard_map/attn_bwd/pallas_call | solution.py:226
  562.2 12.0 %collective-permute-done.22 = bf16[1024,2,128]{2,0,1:T(8,128)(2,1)} collective-permute-done((bf16[1024,2,128]{2,0,1:T(8,128)(2,1)S(1)}, bf16[1024,2,128]{2,0,1:T(8,128)(2,1)}, u32[]{:S(2)}, u32[]{:S(2)}) %collective-permute-start.22) | collective-permute-done | bytes 524320 | tf_op jit(solution)/shard_map/ppermute | solution.py:422
  576.8 7.7 collective-permute-done.19
  613.9 39.7 %all-reduce.4 = (f32[31,256]{1,0:T(8,128)}, f32[256]{0:T(256)}) all-reduce(f32[31,256]{1,0:T(8,128)S(1)} %stack.176, f32[256]{0:T(256)S(1)} %get-tuple-element.88), channel_id=1, replica_groups=mesh['dp'=8,'mp'=4] {'dp'}, use_global_device_ids=true, to_apply=%region_74.75 | all-reduce | flops 8192 | bytes 65536 | tf_op jit(solution)/shard_map/psum | solution.py:515
  706.2 6.7 multiply_convert_fusion
  738.7 12.4 %collective-permute-done.3 = bf16[1024,4,128]{2,0,1:T(8,128)(2,1)} collective-permute-done((bf16[1024,4,128]{2,0,1:T(8,128)(2,1)}, bf16[1024,4,128]{2,0,1:T(8,128)(2,1)}, u32[]{:S(2)}, u32[]{:S(2)}) %collective-permute-start.3) | collective-permute-done | bytes 1048608 | tf_op jit(solution)/shard_map/ppermute | solution.py:422
  754.2 8.2 collective-permute-done
  766.3 7.5 collective-permute-done.4
  782.4 8.8 %collective-permute-done.5 = bf16[1024,1,128]{2,0,1:T(8,128)(2,1)S(1)} collective-permute-done((bf16[1024,1,128]{2,0,1:T(8,128)(2,1)S(1)}, bf16[1024,1,128]{2,0,1:T(8,128)(2,1)S(1)}, u32[]{:S(2)}, u32[]{:S(2)}) %collective-permute-start.5) | collective-permute-done | bytes 262176 | tf_op jit(solution)/shard_map/ppermute | solution.py:422
  796.5 39.2 %all-reduce.3 = (f32[5,1024]{1,0:T(8,128)S(1)}, f32[73,64]{1,0:T(8,128)S(1)}, f32[5]{0:T(128)S(1)}) all-reduce(f32[5,1024]{1,0:T(8,128)S(1)} %stack.144, f32[73,64]{1,0:T(8,128)S(1)} %slice_add_fusion, f32[5]{0:T(128)S(1)} %stack.182), channel_id=1, replica_groups=mesh['dp'=8,'mp'=4] {'dp','mp'}, use_global_device_ids=true, to_apply=%region_41.42 | all-reduce | flops 9797 | bytes 78376 | tf_op jit(solution)/shard_map/psum | solution.py:514
  (385 shorter events, 298.8 us)
Async XLA Ops:
  7.2 31.6 %all-gather.9.cloned.1.call-start = ((), (), s32[]{:S(2)}) async-start(), calls=%async_computation.8 | async-start | bytes 2621440 | tf_op jit(solution)/shard_map/all_gather | solution.py:60
  13.4 67.5 %reduce-scatter.9.cloned.1.call-start = ((), (), s32[]{:S(2)}) async-start(), calls=%async_computation.9 | async-start | bytes 2621440 | tf_op jit(solution)/shard_map/reduce_scatter | solution.py:68
  49.3 58.9 %all-gather.11.cloned.1.call-start = ((), (), s32[]{:S(2)}) async-start(), calls=%async_computation.10 | async-start | bytes 2621440 | tf_op jit(solution)/shard_map/all_gather | solution.py:60
  85.5 81.6 %reduce-scatter.11.cloned.1.call-start = ((), (), s32[]{:S(2)}) async-start(), calls=%async_computation.11 | async-start | bytes 2621440 | tf_op jit(solution)/shard_map/reduce_scatter | solution.py:68
  135.5 58.6 %all-gather.13.cloned.1.call-start = ((), (), s32[]{:S(2)}) async-start(), calls=%async_computation.12 | async-start | bytes 2621440 | tf_op jit(solution)/shard_map/all_gather | solution.py:60
  171.3 82.1 %reduce-scatter.13.cloned.1.call-start = ((), (), s32[]{:S(2)}) async-start(), calls=%async_computation.13 | async-start | bytes 2621440 | tf_op jit(solution)/shard_map/reduce_scatter | solution.py:68
  220.4 60.0 %all-gather.15.cloned.1.call-start = ((), (), s32[]{:S(2)}) async-start(), calls=%async_computation.14 | async-start | bytes 2621440 | tf_op jit(solution)/shard_map/all_gather | solution.py:60
  257.6 64.7 %reduce-scatter.15.cloned.1.call-start = ((), (), s32[]{:S(2)}) async-start(), calls=%async_computation.15 | async-start | bytes 2621440 | tf_op jit(solution)/shard_map/reduce_scatter | solution.py:68
  290.7 59.3 %all-gather.17.cloned.1.call-start = ((), (), s32[]{:S(2)}) async-start(), calls=%async_computation.16 | async-start | bytes 2621440 | tf_op jit(solution)/shard_map/all_gather | solution.py:64
  327.3 65.7 %reduce-scatter.17.cloned.1.call-start = ((), (), s32[]{:S(2)}) async-start(), calls=%async_computation.17 | async-start | bytes 2621440 | tf_op jit(solution)/shard_map/reduce_scatter | solution.py:77
  361.4 59.4 %all-gather.19.cloned.1.call-start = ((), (), s32[]{:S(2)}) async-start(), calls=%async_computation.18 | async-start | bytes 2621440 | tf_op jit(solution)/shard_map/all_gather | solution.py:64
  398.0 79.0 %reduce-scatter.19.cloned.1.call-start = ((), (), s32[]{:S(2)}) async-start(), calls=%async_computation.19 | async-start | bytes 2621440 | tf_op jit(solution)/shard_map/reduce_scatter | solution.py:77
  444.4 73.8 %all-gather.21.cloned.1.call-start = ((), (), s32[]{:S(2)}) async-start(), calls=%async_computation.20 | async-start | bytes 2621440 | tf_op jit(solution)/shard_map/all_gather | solution.py:64
  481.2 178.3 %reduce-scatter.21.cloned.1.call-start = ((), (), s32[]{:S(2)}) async-start(), calls=%async_computation.21 | async-start | bytes 2621440 | tf_op jit(solution)/shard_map/reduce_scatter | solution.py:77
  489.3 26.4 %collective-permute-start.21 = (bf16[1024,4,128]{2,0,1:T(8,128)(2,1)}, bf16[1024,4,128]{2,0,1:T(8,128)(2,1)}, u32[]{:S(2)}, u32[]{:S(2)}) collective-permute-start(bf16[1024,4,128]{2,0,1:T(8,128)(2,1)} %bitcast.135), channel_id=1, source_target_pairs={{0,4},{4,0},{8,12},{12,8},{16,20},{20,16},{24,28},{28,24},{1,5},{5... | collective-permute-start | bytes 3145736 | tf_op jit(solution)/shard_map/ppermute | solution.py:422
  498.3 59.5 %collective-permute-start.18 = (bf16[4,128,1024]{2,1,0:T(8,128)(2,1)}, bf16[4,128,1024]{2,1,0:T(8,128)(2,1)}, u32[]{:S(2)}, u32[]{:S(2)}) collective-permute-start(bf16[4,128,1024]{2,1,0:T(8,128)(2,1)} %dynamic-slice_bitcast_fusion), channel_id=1, source_target_pairs={{0,4},{4,0},{8,12},{12,8},{16,20},{20,16},{24,28},{28,24},{1,5},{5... | collective-permute-start | bytes 3145736 | tf_op jit(solution)/shard_map/ppermute | solution.py:422
  555.1 151.2 %all-gather.23.cloned.1.call-start = ((), (), s32[]{:S(2)}) async-start(), calls=%async_computation.22 | async-start | bytes 2621440 | tf_op jit(solution)/shard_map/all_gather | solution.py:64
  605.3 48.2 %collective-permute-start.15 = (bf16[256,4,128]{2,0,1:T(8,128)(2,1)S(1)}, bf16[256,4,128]{2,0,1:T(8,128)(2,1)}, u32[]{:S(2)}, u32[]{:S(2)}) collective-permute-start(bf16[256,4,128]{2,0,1:T(8,128)(2,1)S(1)} %bitcast.351), channel_id=1, source_target_pairs={{0,4},{4,0},{8,12},{12,8},{16,20},{20,16},{24,28},{28,24},{1,5},{5... | collective-permute-start | bytes 786440 | tf_op jit(solution)/shard_map/ppermute | solution.py:422
  611.5 43.2 %collective-permute-start.12 = (bf16[4,128,2,256]{3,1,2,0:T(8,128)(2,1)}, bf16[4,128,2,256]{3,1,2,0:T(8,128)(2,1)}, u32[]{:S(2)}, u32[]{:S(2)}) collective-permute-start(bf16[4,128,2,256]{3,1,2,0:T(8,128)(2,1)} %bitcast.320), channel_id=1, source_target_pairs={{0,4},{4,0},{8,12},{12,8},{16,20},{20,16},{24,28},{28,24},{1,5},{5... | collective-permute-start | bytes 1572872 | tf_op jit(solution)/shard_map/ppermute | solution.py:422
  664.0 130.8 %reduce-scatter.23.cloned.1.call-start = ((), (), s32[]{:S(2)}) async-start(), calls=%async_computation.23 | async-start | bytes 2621440 | tf_op jit(solution)/shard_map/reduce_scatter | solution.py:77
  697.3 37.5 %collective-permute-start.6 = (bf16[4,128,3,256]{1,0,3,2:T(4,128)(2,1)}, bf16[4,128,3,256]{1,0,3,2:T(4,128)(2,1)}, u32[]{:S(2)}, u32[]{:S(2)}) collective-permute-start(bf16[4,128,3,256]{1,0,3,2:T(4,128)(2,1)} %copy.76), channel_id=1, source_target_pairs={{0,4},{4,0},{8,12},{12,8},{16,20},{20,16},{24,28},{28,24},{1,5},{5... | collective-permute-start | bytes 2359304 | tf_op jit(solution)/shard_map/ppermute | solution.py:422
  705.5 28.6 %collective-permute-start.11 = (bf16[256,1,128]{2,0,1:T(8,128)(2,1)S(1)}, bf16[256,1,128]{2,0,1:T(8,128)(2,1)S(1)}, u32[]{:S(2)}, u32[]{:S(2)}) collective-permute-start(bf16[256,1,128]{2,0,1:T(8,128)(2,1)S(1)} %constant_dynamic-slice_fusion.10), channel_id=1, source_target_pairs={{0,16},{4,20},{8,24},{12,28},{16,0},{20,4},{24,8},{28,12},{1,17},{... | collective-permute-start | bytes 196616 | tf_op jit(solution)/shard_map/ppermute | solution.py:422
  732.1 30.2 %collective-permute-start = (bf16[4,128,1024]{2,1,0:T(8,128)(2,1)}, bf16[4,128,1024]{2,1,0:T(8,128)(2,1)}, u32[]{:S(2)}, u32[]{:S(2)}) collective-permute-start(bf16[4,128,1024]{2,1,0:T(8,128)(2,1)} %dynamic-slice_bitcast_fusion.1), channel_id=1, source_target_pairs={{0,4},{4,0},{8,12},{12,8},{16,20},{20,16},{24,28},{28,24},{1,5},{5... | collective-permute-start | bytes 3145736 | tf_op jit(solution)/shard_map/ppermute | solution.py:422
  737.9 27.8 %collective-permute-start.7 = (bf16[2,128,3,256]{3,1,2,0:T(8,128)(2,1)}, bf16[2,128,3,256]{3,1,2,0:T(8,128)(2,1)S(1)}, u32[]{:S(2)}, u32[]{:S(2)}) collective-permute-start(bf16[2,128,3,256]{3,1,2,0:T(8,128)(2,1)} %dynamic-slice_bitcast_fusion.6), channel_id=1, source_target_pairs={{0,8},{4,12},{8,0},{12,4},{16,24},{20,28},{24,16},{28,20},{1,9},{5... | collective-permute-start | bytes 1179656 | tf_op jit(solution)/shard_map/ppermute | solution.py:422
  (85 other events, 1119.8 us)
Sparse Core Ops, SparseCore 0:
  13.5 25.2 all-gather.8
  49.4 31.4 reduce-scatter.8
  85.6 22.5 all-gather.10
  135.6 31.4 reduce-scatter.10
  171.4 22.5 all-gather.12
  220.5 32.7 reduce-scatter.12
  257.7 22.5 all-gather.14
  290.8 31.4 reduce-scatter.14
  327.4 22.5 all-gather.16
  361.5 31.4 reduce-scatter.16
  398.1 22.5 all-gather.18
  444.5 32.4 reduce-scatter.18
  481.3 22.5 all-gather.20
  555.2 31.4 reduce-scatter.20
  664.1 18.8 all-gather.22
  718.1 29.3 reduce-scatter.22

commit v2 on v1

v2 whole, which is shorter than its diff:
```python
import functools

import jax
import jax.numpy as jnp
from jax import lax
from jax.experimental import pallas as pl
from jax.experimental.pallas import tpu as pltpu
from jax.sharding import PartitionSpec as P

HEAD = 64
REL_LEFT = 64
REL_RIGHT = 8
BQ = 128
WIN = 4 * BQ


epsilon = 1e-05


def nt(a, b):
    return lax.dot_general(a, b, (((1,), (1,)), ((), ())), preferred_element_type=jnp.float32)
def nn(a, b):
    return lax.dot_general(a, b, (((1,), (0,)), ((), ())), preferred_element_type=jnp.float32)
def tn(a, b):
    return lax.dot_general(a, b, (((0,), (0,)), ((), ())), preferred_element_type=jnp.float32)

def split_pair(x):
    left = lax.broadcasted_iota(jnp.int32, x.shape, 1) < HEAD
    zero = jnp.zeros_like(x)
    return jnp.concatenate([jnp.where(left, x, zero), jnp.where(left, zero, x)], 0)

def join_pair(x):
    rows = x.shape[0] // 2
    left = lax.broadcasted_iota(jnp.int32, (rows, x.shape[1]), 1) < HEAD
    return jnp.where(left, x[:rows], x[rows:])

def fwd_kernel(q_ref, k_ref, v_ref, rel_ref, mixed_ref, probs_ref, bias_ref):
    ib = pl.program_id(1)
    qs = split_pair(q_ref[...] * 0.125)
    s = nt(qs, k_ref[...])
    b = nt(qs, rel_ref[...])
    rows = b.shape[0] // 2
    bias_ref[:, 0:BQ] = b[:, 3 * BQ : 4 * BQ]
    for h in range(2):
        r = pltpu.roll(b[h * rows : (h + 1) * rows, :WIN], 0, 1, stride=1, stride_axis=0)
        bias_ref[h * rows : (h + 1) * rows, BQ : 4 * BQ] = r[:, : 3 * BQ]
    bias_ref[:, 4 * BQ :] = b[:, 4 * BQ :]
    nkeys = s.shape[1] // BQ
    parts = []
    for jb in range(nkeys):
        at = pl.multiple_of(jnp.clip(jb - ib + 2, 0, 4) * BQ, BQ)
        parts.append(s[:, jb * BQ : (jb + 1) * BQ] + bias_ref[:, pl.ds(at, BQ)])
    top = functools.reduce(jnp.maximum, parts)
    m = jnp.max(top, -1, keepdims=True)
    es = [jnp.exp(p - m) for p in parts]
    tot = jnp.sum(functools.reduce(jnp.add, es), -1, keepdims=True)
    inv = 1.0 / tot
    for jb in range(nkeys):
        probs_ref[0, :, jb * BQ : (jb + 1) * BQ] = (es[jb] * inv).astype(jnp.bfloat16)
    mixed_ref[...] = join_pair(nn(probs_ref[0], v_ref[...])).astype(jnp.bfloat16)

def bwd_kernel(q_ref, k_ref, v_ref, relb_ref, hot_ref, probs_ref, do_ref, dq_ref, dk_ref, dv_ref, dt_ref,
               tot_ref, dkt, dvt, dta, dz_ref):
    pr, ib, nb = pl.program_id(0), pl.program_id(1), pl.num_programs(1)
    @pl.when(ib == 0)
    def _():
        dkt[...] = jnp.zeros_like(dkt)
        dvt[...] = jnp.zeros_like(dvt)
    @pl.when((ib == 0) & (pr == 0))
    def _():
        dta[...] = jnp.zeros_like(dta)
    qs = split_pair(q_ref[...] * 0.125)
    dos = split_pair(do_ref[...])
    p = probs_ref[0]
    dp = nt(dos, v_ref[...])
    nkeys = dp.shape[1] // BQ
    dvt[...] += tn(dos, p)
    pf = p.astype(jnp.float32)
    acc = None
    for jb in range(nkeys):
        sl = slice(jb * BQ, (jb + 1) * BQ)
        t = pf[:, sl] * dp[:, sl]
        acc = t if acc is None else acc + t
    inner = jnp.sum(acc, -1, keepdims=True)
    tot_ref[...] = jnp.zeros_like(tot_ref)
    for jb in range(nkeys):
        sl = slice(jb * BQ, (jb + 1) * BQ)
        dz = (pf[:, sl] * (dp[:, sl] - inner)).astype(jnp.bfloat16)
        dz_ref[:, sl] = dz
        at = pl.multiple_of(jnp.clip(jb - ib + 2, 0, 4) * BQ, BQ)
        tot_ref[:, pl.ds(at, BQ)] += dz.astype(jnp.float32)
    rows = BQ
    r2 = lax.broadcasted_iota(jnp.int32, (2 * rows, 2 * rows), 0)
    c2 = lax.broadcasted_iota(jnp.int32, (2 * rows, 2 * rows), 1)
    mirror = (r2 + c2 == jnp.where(r2 < rows, rows - 1, 3 * rows - 1)).astype(jnp.bfloat16)
    w = jnp.concatenate([tot_ref[:, BQ : 4 * BQ].astype(jnp.bfloat16), jnp.zeros((2 * rows, BQ), jnp.bfloat16)], 1)
    w = nn(mirror, w)
    outs = [pltpu.roll(w[h * rows : (h + 1) * rows], WIN - rows + 1, 1, stride=1, stride_axis=0) for h in range(2)]
    d = nn(mirror, jnp.concatenate(outs, 0).astype(jnp.bfloat16)).astype(jnp.bfloat16)
    drel = nn(d, hot_ref[...])
    col = lax.broadcasted_iota(jnp.int32, drel.shape, 1)
    low = jnp.sum(tot_ref[:, :BQ], -1, keepdims=True)
    high = jnp.sum(tot_ref[:, 4 * BQ :], -1, keepdims=True)
    drel = drel + jnp.where(col == 0, low, 0.0) + jnp.where(col == REL_LEFT + REL_RIGHT, high, 0.0)
    drel = drel.astype(jnp.bfloat16)
    dz = dz_ref[...]
    dq = nn(dz, k_ref[...]) + nn(drel, relb_ref[...])
    dq_ref[...] = (join_pair(dq) * 0.125).astype(jnp.bfloat16)
    dkt[...] += tn(qs, dz)
    dta[...] += tn(drel, qs)
    @pl.when(ib == nb - 1)
    def _():
        dk_ref[...] = dkt[...].T.astype(jnp.bfloat16)
        dv_ref[...] = dvt[...].T.astype(jnp.bfloat16)
        dt_ref[...] = dta[...]

def rel_tables(rel_table):
    spots = jnp.arange(5 * BQ)
    idx = jnp.where(spots < 3 * BQ, jnp.clip(spots - REL_LEFT, 0, REL_LEFT + REL_RIGHT), jnp.where(spots < 4 * BQ, 0, REL_LEFT + REL_RIGHT))
    hot = (jnp.arange(BQ)[None, :] == idx[:, None]).astype(jnp.bfloat16)
    padded = jnp.pad(rel_table, ((0, BQ - rel_table.shape[0]), (0, 0)))
    padded = jnp.concatenate([padded, padded], 1)
    ext = jnp.dot(hot, padded, preferred_element_type=jnp.float32).astype(jnp.bfloat16)
    return ext, hot[:WIN], padded

def attn_fwd(qkv, ext):
    frames, cols = qkv.shape
    pairs = cols // 3 // 128
    nb = frames // BQ
    bf = jnp.bfloat16
    return pl.pallas_call(
        fwd_kernel,
        grid=(pairs, nb),
        in_specs=[
            pl.BlockSpec((BQ, 128), lambda p, i: (i, p)),
            pl.BlockSpec((frames, 128), lambda p, i: (0, pairs + p)),
            pl.BlockSpec((frames, 128), lambda p, i: (0, 2 * pairs + p)),
            pl.BlockSpec(ext.shape, lambda p, i: (0, 0)),
        ],
        out_specs=[
            pl.BlockSpec((BQ, 128), lambda p, i: (i, p)),
            pl.BlockSpec((1, 2 * BQ, frames), lambda p, i: (p, i, 0)),
        ],
        out_shape=[jax.ShapeDtypeStruct((frames, cols // 3), bf), jax.ShapeDtypeStruct((pairs, 2 * frames, frames), bf)],
        scratch_shapes=[pltpu.VMEM((2 * BQ, 5 * BQ), jnp.float32)],
        compiler_params=pltpu.CompilerParams(vmem_limit_bytes=20 << 20),
        name="attn_fwd",
    )(qkv, qkv, qkv, ext)

def attn_bwd(qkv, padded, hot, probs, dmixed):
    frames, cols = qkv.shape
    pairs = cols // 3 // 128
    nb = frames // BQ
    bf = jnp.bfloat16
    blk = pl.BlockSpec((BQ, 128), lambda p, i: (i, p))
    full = pl.BlockSpec((frames, 128), lambda p, i: (0, p))
    return pl.pallas_call(
        bwd_kernel,
        grid=(pairs, nb),
        in_specs=[
            blk,
            pl.BlockSpec((frames, 128), lambda p, i: (0, pairs + p)),
            pl.BlockSpec((frames, 128), lambda p, i: (0, 2 * pairs + p)),
            pl.BlockSpec(padded.shape, lambda p, i: (0, 0)),
            pl.BlockSpec(hot.shape, lambda p, i: (0, 0)),
            pl.BlockSpec((1, 2 * BQ, frames), lambda p, i: (p, i, 0)),
            blk,
        ],
        out_specs=[blk, full, full, pl.BlockSpec((128, 128), lambda p, i: (0, 0))],
        out_shape=[jax.ShapeDtypeStruct((frames, cols // 3), bf)] * 3 + [jax.ShapeDtypeStruct((128, 128), jnp.float32)],
        scratch_shapes=[pltpu.VMEM((2 * BQ, 5 * BQ), jnp.float32), pltpu.VMEM((128, frames), jnp.float32), pltpu.VMEM((128, frames), jnp.float32),
                        pltpu.VMEM((128, 128), jnp.float32), pltpu.VMEM((2 * BQ, frames), bf)],
        compiler_params=pltpu.CompilerParams(vmem_limit_bytes=20 << 20),
        name="attn_bwd",
    )(qkv, qkv, qkv, padded, hot, probs, dmixed)


MESH = pl.DeviceIdType.MESH
CHUNKS = 4


def silu_pair(h):
    sig = jax.nn.sigmoid(h)
    act = h * sig
    return act, sig + act * (1.0 - sig)


def unit_norm(s):
    centred = s - jnp.mean(s, -1, keepdims=True)
    inverse = lax.rsqrt(jnp.mean(centred * centred, -1, keepdims=True) + epsilon)
    return centred * inverse, inverse


def fold8(x):
    return jnp.sum(x.reshape(x.shape[0] // 8, 8, x.shape[1]), 0)


def norm_pull(grad, s, gain):
    unit, inverse = unit_norm(s)
    scaled = grad * gain
    first = jnp.mean(scaled, -1, keepdims=True)
    second = jnp.mean(scaled * unit, -1, keepdims=True)
    return inverse * (scaled - first - unit * second), fold8(grad * unit)


def stage(name, cid, rows, width, *, leave=None, enter=None, dws=(), junction, row_in=(), vec_in=(), row_out=(), sums=0):
    chunk = rows // CHUNKS
    frames = rows * 4
    f32, bf = jnp.float32, jnp.bfloat16
    ins, out_shape, scratch = [], [], []
    if leave:
        ins += [leave[0], leave[1]]
    if enter:
        ins += [enter[0]] + list(enter[3])
    n_dw_in = []
    for lhs, rhs in dws:
        ins += [lhs, rhs]
    ins += list(row_in) + list(vec_in)
    if enter:
        out_shape.append(jax.ShapeDtypeStruct((frames, width), bf))
        out_shape += [jax.ShapeDtypeStruct((frames, c), d) for c, d in enter[4]]
    for lhs, rhs in dws:
        out_shape.append(jax.ShapeDtypeStruct((rhs.shape[1] // 128, lhs.shape[1], 128), bf))
    out_shape += [jax.ShapeDtypeStruct((rows, width), d) for d in row_out]
    out_shape += [jax.ShapeDtypeStruct((8, width), f32)] * sums
    if leave:
        scratch += [pltpu.VMEM((rows, width), f32)] * 2
        scratch += [pltpu.VMEM((rows, width), bf)] * 6
    scratch += [pltpu.SemaphoreType.DMA((6, CHUNKS)), pltpu.SemaphoreType.DMA((6, CHUNKS))]

    def kernel(*refs):
        refs = list(refs)
        take = lambda n: [refs.pop(0) for _ in range(n)]
        if leave:
            x_ref, wl_ref = take(2)
        if enter:
            (we_ref,) = take(1)
            extra = take(len(enter[3]))
        dw_in = [take(2) for _ in dws]
        r_in, v_in = take(len(row_in)), take(len(vec_in))
        if enter:
            (all_ref,) = take(1)
            e_out = take(len(enter[4]))
        dw_out = take(len(dws))
        r_out, s_out = take(len(row_out)), take(sums)
        if leave:
            px, own, sb, sr, xs, xr, ob, orv = take(8)
        send, recv = take(2)
        dp, me = lax.axis_index("dp"), lax.axis_index("mp")
        core, chip = me % 2, me // 2
        sib = chip * 2 + 1 - core
        far = (1 - chip) * 2 + core
        diag = (1 - chip) * 2 + 1 - core

        def part(ref, block, k):
            return ref.at[pl.ds(pl.multiple_of(block * rows + k * chunk, chunk), chunk)]

        def copy(kind, k, src, dst, to):
            return pltpu.make_async_remote_copy(
                src, dst, send.at[kind, k], recv.at[kind, k], device_id=(dp, to), device_id_type=MESH
            )

        pair_send = lambda k: copy(0, k, part(sb, 0, k), part(sr, 0, k), sib)
        far_send = lambda k: copy(1, k, part(xs, 0, k), part(xr, 0, k), far)
        own_send = lambda k: copy(2, k, part(ob, 0, k), part(orv, 0, k), sib)
        all_far = lambda k: copy(3, k, part(all_ref, me, k), part(all_ref, me, k), far)
        all_sib = lambda k: copy(4, k, part(all_ref, me, k), part(all_ref, me, k), sib)
        all_fwd = lambda k: copy(5, k, part(all_ref, far, k), part(all_ref, far, k), sib)
        got_far = lambda k: copy(3, k, part(all_ref, far, k), part(all_ref, far, k), far)
        got_sib = lambda k: copy(4, k, part(all_ref, sib, k), part(all_ref, sib, k), sib)
        got_diag = lambda k: copy(5, k, part(all_ref, diag, k), part(all_ref, diag, k), sib)

        barrier = pltpu.get_barrier_semaphore()
        for to in (sib, far):
            pl.semaphore_signal(barrier, inc=1, device_id=(dp, to), device_id_type=MESH)
        pl.semaphore_wait(barrier, 2)
        for ref in s_out:
            ref[...] = jnp.zeros_like(ref)

        if leave:
            def two(k, block_a, block_b):
                lhs = jnp.concatenate([part(x_ref, block_a, k)[...], part(x_ref, block_b, k)[...]], 0)
                return leave[2](lhs, wl_ref[...])

            def push(k):
                pair_send(k).wait_recv()
                part(xs, 0, k)[...] = (part(px, 0, k)[...] + part(sr, 0, k)[...].astype(f32)).astype(bf)
                far_send(k).start()

            def out_far(k, c):
                p = two(k, far, diag)
                part(px, 0, k)[...] = p[:chunk]
                part(sb, 0, k)[...] = p[chunk:].astype(bf)
                pair_send(k).start()

                @pl.when(k > 0)
                def _():
                    push(k - 1)
                return c

            lax.fori_loop(0, CHUNKS, out_far, 0)

            def out_near(k, c):
                p = two(k, me, sib)
                part(own, 0, k)[...] = p[:chunk]
                part(ob, 0, k)[...] = p[chunk:].astype(bf)
                own_send(k).start()

                @pl.when(k == 0)
                def _():
                    push(CHUNKS - 1)
                return c

            lax.fori_loop(0, CHUNKS, out_near, 0)

        def join(k, c):
            for (lhs, rhs), out in zip(dw_in, dw_out):
                m = max(lhs.shape[1] // CHUNKS, 128)

                @pl.when(k * m < lhs.shape[1])
                def _(lhs=lhs, rhs=rhs, out=out, m=m):
                    at = pl.ds(pl.multiple_of(k * m, m), m)
                    g = tn(lhs[:, at], rhs[...]).astype(bf)
                    for u in range(out.shape[0]):
                        out[u, at, :] = g[:, u * 128 : (u + 1) * 128]
            branch = None
            if leave:
                own_send(k).wait_recv()
                far_send(k).wait_recv()
                branch = part(own, 0, k)[...] + part(orv, 0, k)[...].astype(f32) + part(xr, 0, k)[...].astype(f32)
            view = lambda ref: part(ref, 0, k)
            fresh = junction(branch, [view(r)[...] for r in r_in], [v[...] for v in v_in], [view(r) for r in r_out], s_out)
            if enter:
                part(all_ref, me, k)[...] = fresh
                all_far(k).start()
                all_sib(k).start()
            return c

        lax.fori_loop(0, CHUNKS, join, 0)

        if enter:
            def work(k, block_a, block_b):
                lhs = jnp.concatenate([part(all_ref, block_a, k)[...], part(all_ref, block_b, k)[...]], 0)
                h = enter[1](lhs, we_ref[...])
                for i, block in enumerate((block_a, block_b)):
                    view = lambda ref: part(ref, block, k)
                    enter[2](h[i * chunk : (i + 1) * chunk], [view(r)[...] for r in extra], [view(r) for r in e_out])

            def gather(k, c):
                got_sib(k).wait_recv()
                work(k, me, sib)
                got_far(k).wait_recv()
                all_fwd(k).start()
                got_diag(k).wait_recv()
                work(k, far, diag)
                return c

            lax.fori_loop(0, CHUNKS, gather, 0)

        def drain(k, c):
            if leave:
                pair_send(k).wait_send()
                far_send(k).wait_send()
                own_send(k).wait_send()
            if enter:
                all_far(k).wait_send()
                all_sib(k).wait_send()
                all_fwd(k).wait_send()
            return c

        lax.fori_loop(0, CHUNKS, drain, 0)

    flops = 0
    if leave:
        flops += 2 * frames * leave[0].shape[1] * width
    if enter:
        flops += 2 * frames * width * sum(c for c, _ in enter[4])
    flops += sum(2 * frames * a.shape[1] * b.shape[1] for a, b in dws)
    vm = pl.BlockSpec(memory_space=pltpu.VMEM)
    return pl.pallas_call(
        kernel,
        in_specs=[vm] * len(ins),
        out_specs=[vm] * len(out_shape),
        out_shape=out_shape,
        scratch_shapes=scratch,
        compiler_params=pltpu.CompilerParams(collective_id=cid, has_side_effects=True, vmem_limit_bytes=24 << 20),
        cost_estimate=pl.CostEstimate(flops=flops, bytes_accessed=60_000_000, transcendentals=0),
        name=name,
    )(*ins)


def halve_sum(part):
    count = lax.axis_size("dp")
    me = lax.axis_index("dp")
    step = 1
    while step < count:
        paired = part.reshape((part.shape[0] // 2, 2) + part.shape[1:])
        bit = (me // step) % 2
        keep = lax.dynamic_index_in_dim(paired, bit, 1, keepdims=False)
        give = lax.dynamic_index_in_dim(paired, 1 - bit, 1, keepdims=False)
        got = lax.ppermute(give, "dp", [(i, i ^ step) for i in range(count)])
        total = keep.astype(jnp.float32) + got.astype(jnp.float32)
        step *= 2
        part = total.astype(jnp.bfloat16) if step < count else total
    return part[0]


def sum_rows(units, shape):
    count = lax.axis_size("dp")
    groups, rows, lanes = units.shape
    split = units.reshape(groups, count, rows // count, lanes).transpose(1, 0, 2, 3)
    total = halve_sum(split)
    return total.transpose(1, 0, 2).reshape((rows // count,) + shape)


def sum_cols(units):
    count = lax.axis_size("dp")
    groups, rows, lanes = units.shape
    per = count // groups
    if per > 1:
        units = units.reshape(groups, rows, per, lanes // per).transpose(0, 2, 1, 3).reshape(count, rows, lanes // per)
    return halve_sum(units)


def body(
    features,
    w1_in,
    w1_out,
    gain_ffn1,
    w_qkv,
    w_attn_out,
    rel_table,
    gain_attn,
    w_conv_in,
    w_depth,
    gain_depth,
    w_conv_out,
    gain_conv,
    w2_in,
    w2_out,
    gain_ffn2,
    gain_final,
    cotangent,
):
    local_frames, clip_count, width = features.shape
    rows = local_frames * clip_count
    f32, bf = jnp.float32, jnp.bfloat16
    s0 = features.reshape(rows, width)
    seed = cotangent.reshape(rows, width)
    vec = lambda g: g.astype(f32).reshape(1, width)
    g1, ga, gc, g2, gf = vec(gain_ffn1), vec(gain_attn), vec(gain_conv), vec(gain_ffn2), vec(gain_final)
    flat_qkv = w_qkv.reshape(width, -1)
    flat_conv = w_conv_in.reshape(width, -1)
    units = w1_in.shape[1]
    chans = w_conv_out.shape[0]

    def swish_out(h, extra, outs):
        act, slope = silu_pair(h)
        outs[0][...] = act.astype(bf)
        outs[1][...] = slope.astype(bf)

    def plain_out(h, extra, outs):
        outs[0][...] = h.astype(outs[0].dtype)

    def glu_out(h, extra, outs):
        p0 = h[:, :chans]
        sig = jax.nn.sigmoid(h[:, chans:])
        glu = p0 * sig
        outs[0][...] = glu
        outs[1][...] = sig.astype(bf)
        outs[2][...] = (glu * (1.0 - sig)).astype(bf)

    def slope_out(h, extra, outs):
        outs[0][...] = (h * extra[0][...].astype(f32)).astype(bf)

    def first(branch, ins, vecs, outs, sums):
        return (unit_norm(ins[0].astype(f32))[0] * vecs[0]).astype(bf)

    def forward(scale):
        def run(branch, ins, vecs, outs, sums):
            fresh = ins[0].astype(f32) + scale * branch
            outs[0][...] = fresh
            sums[0][...] += fold8(branch * branch)
            return (unit_norm(fresh)[0] * vecs[0]).astype(bf)
        return run

    def turn(branch, ins, vecs, outs, sums):
        fresh = ins[0] + 0.5 * branch
        sums[0][...] += fold8(branch * branch)
        sums[1][...] += fold8(fresh * fresh)
        unit, inverse = unit_norm(fresh)
        outs[0][...] = unit * vecs[0]
        grad = ins[1].astype(f32)
        scaled = grad * vecs[0]
        mean_one = jnp.mean(scaled, -1, keepdims=True)
        mean_two = jnp.mean(scaled * unit, -1, keepdims=True)
        sums[2][...] += fold8(grad * unit)
        back = inverse * (scaled - mean_one - unit * mean_two)
        outs[1][...] = back
        return (0.5 * back).astype(bf)

    def backward(scale):
        def run(branch, ins, vecs, outs, sums):
            pull, grad_gain = norm_pull(branch, ins[1].astype(f32), vecs[0])
            fresh = ins[0] + pull
            outs[0][...] = fresh
            sums[0][...] += grad_gain
            return (scale * fresh).astype(bf)
        return run

    a1, act1, slope1 = stage(
        "ffn1_in", 0, rows, width, enter=(w1_in, nn, swish_out, (), ((units, bf), (units, bf))),
        junction=first, row_in=(s0,), vec_in=(g1,),
    )
    a2, qkv, s1, sq1 = stage(
        "ffn1_out", 1, rows, width, leave=(act1, w1_out, nn),
        enter=(flat_qkv, nn, plain_out, (), ((flat_qkv.shape[1], bf),)),
        junction=forward(0.5), row_in=(s0,), vec_in=(ga,), row_out=(f32,), sums=1,
    )
    ext, hot, padded = rel_tables(rel_table)
    mixed, probs = attn_fwd(qkv, ext)
    a3, glu, sig, tail, s2, sq2 = stage(
        "attn_out", 2, rows, width, leave=(mixed, w_attn_out, nn),
        enter=(flat_conv, nn, glu_out, (), ((chans, f32), (chans, bf), (chans, bf))),
        junction=forward(1.0), row_in=(s1,), vec_in=(gc,), row_out=(f32,), sums=1,
    )
    frames = glu.shape[0]
    taps = w_depth.astype(f32)
    tap_count = taps.shape[0]
    padded_glu = jnp.pad(glu, ((tap_count - 1, 0), (0, 0)))
    depth = jnp.zeros_like(glu)
    for k in range(tap_count):
        depth = depth + taps[k] * padded_glu[k : k + frames]
    average = lax.psum(jnp.sum(depth, -1, keepdims=True), "mp") / width
    centred = depth - average
    spread = lax.psum(jnp.sum(centred * centred, -1, keepdims=True), "mp") / width
    depth_inverse = lax.rsqrt(spread + epsilon)
    depth_unit = centred * depth_inverse
    depth_gain = gain_depth.astype(f32)
    act3, slope3 = silu_pair(depth_unit * depth_gain)
    act3 = act3.astype(bf)
    a4, act2, slope2, s3, sq3 = stage(
        "conv_out", 3, rows, width, leave=(act3, w_conv_out, nn),
        enter=(w2_in, nn, swish_out, (), ((units, bf), (units, bf))),
        junction=forward(1.0), row_in=(s2,), vec_in=(g2,), row_out=(f32,), sums=1,
    )
    db4, dh2, output, grad4, sq4, sq5, dgf = stage(
        "ffn2_out", 4, rows, width, leave=(act2, w2_out, nn),
        enter=(w2_out, nt, slope_out, (slope2,), ((units, bf),)),
        junction=turn, row_in=(s3, seed), vec_in=(gf,), row_out=(f32, f32), sums=3,
    )
    db3, de3, dw2_in, dw2_out, grad3, dg2 = stage(
        "ffn2_back", 5, rows, width, leave=(dh2, w2_in, nt),
        enter=(w_conv_out, nt, plain_out, (), ((chans, f32),)), dws=((a4, dh2), (act2, db4)),
        junction=backward(1.0), row_in=(grad4, s3), vec_in=(g2,), row_out=(f32,), sums=1,
    )
    grad_gated = de3 * slope3
    grad_gain_depth = jnp.sum(grad_gated * depth_unit, 0)
    grad_unit = grad_gated * depth_gain
    first_sum, second_sum = lax.psum(
        (jnp.sum(grad_unit, -1, keepdims=True), jnp.sum(grad_unit * depth_unit, -1, keepdims=True)), "mp"
    )
    grad_depth = depth_inverse * (grad_unit - first_sum / width - depth_unit * second_sum / width)
    padded_grad = jnp.pad(grad_depth, ((0, tap_count - 1), (0, 0)))
    grad_glu = jnp.zeros_like(grad_depth)
    tap_grads = []
    for k in range(tap_count):
        start = tap_count - 1 - k
        grad_glu = grad_glu + taps[k] * padded_grad[start : start + frames]
        tap_grads.append(jnp.sum(grad_depth * padded_glu[k : k + frames], 0))
    grad_w_depth = jnp.stack(tap_grads, 0)
    dpaired = jnp.concatenate([grad_glu * sig.astype(f32), grad_glu * tail.astype(f32)], 1).astype(bf)
    db2, dmixed, dw_conv_in, dw_conv_out, grad2, dgc = stage(
        "conv_back", 6, rows, width, leave=(dpaired, flat_conv, nt),
        enter=(w_attn_out, nt, plain_out, (), ((w_attn_out.shape[0], bf),)), dws=((a3, dpaired), (act3, db3)),
        junction=backward(1.0), row_in=(grad3, s2), vec_in=(gc,), row_out=(f32,), sums=1,
    )
    dq, dk, dv, dt = attn_bwd(qkv, padded, hot, probs, dmixed)
    rel = rel_table.shape[0]
    grad_table = dt[:rel, :HEAD] + dt[:rel, HEAD:]
    dqkv = jnp.concatenate([dq, dk, dv], 1)
    db1, dh1, dw_qkv, dw_attn_out, grad1, dga = stage(
        "attn_back", 7, rows, width, leave=(dqkv, flat_qkv, nt),
        enter=(w1_out, nt, slope_out, (slope1,), ((units, bf),)), dws=((a2, dqkv), (mixed, db2)),
        junction=backward(0.5), row_in=(grad2, s1), vec_in=(ga,), row_out=(f32,), sums=1,
    )
    dw1_in, dw1_out, grad0, dg1 = stage(
        "ffn1_back", 8, rows, width, leave=(dh1, w1_in, nt), dws=((a1, dh1), (act1, db1)),
        junction=backward(1.0), row_in=(grad1, s0), vec_in=(g1,), row_out=(f32,), sums=1,
    )
    gains = jnp.stack([jnp.sum(g, 0) for g in (dg1, dga, dgc, dg2, dgf)])
    squares = jnp.stack([jnp.sum(s) for s in (sq1, sq2, sq3, sq4, sq5)])
    gain_sums, table_sum, total_squares = lax.psum((gains, grad_table, squares), ("dp", "mp"))
    depth_sum, depth_gain_sum = lax.psum((grad_w_depth, grad_gain_depth), "dp")
    token_total = rows * lax.axis_size("mp") * lax.axis_size("dp")
    rms_stats = jnp.sqrt(total_squares / (token_total * width))
    whole = lambda x: x.reshape(local_frames, clip_count, width)
    return (
        whole(output),
        whole(grad0),
        sum_rows(dw1_in, (units,)),
        sum_cols(dw1_out),
        gain_sums[0],
        sum_rows(dw_qkv, (3, w_qkv.shape[2])),
        sum_cols(dw_attn_out),
        table_sum,
        gain_sums[1],
        sum_rows(dw_conv_in, (2, chans)),
        depth_sum,
        depth_gain_sum,
        sum_cols(dw_conv_out),
        gain_sums[2],
        sum_rows(dw2_in, (units,)),
        sum_cols(dw2_out),
        gain_sums[3],
        gain_sums[4],
        rms_stats,
    )


def solution(mesh):
    return jax.shard_map(
        body,
        mesh=mesh,
        in_specs=(
            P("mp", "dp", None),
            P(None, "mp"),
            P("mp", None),
            P(),
            P(None, None, "mp"),
            P("mp", None),
            P(),
            P(),
            P(None, None, "mp"),
            P(None, "mp"),
            P("mp"),
            P("mp", None),
            P(),
            P(None, "mp"),
            P("mp", None),
            P(),
            P(),
            P("mp", "dp", None),
        ),
        out_specs=(
            P("mp", "dp", None),
            P("mp", "dp", None),
            P("dp", "mp"),
            P("mp", "dp"),
            P(),
            P("dp", None, "mp"),
            P("mp", "dp"),
            P(),
            P(),
            P("dp", None, "mp"),
            P(None, "mp"),
            P("mp"),
            P("mp", "dp"),
            P(),
            P("dp", "mp"),
            P("mp", "dp"),
            P(),
            P(),
            P(),
        ),
        check_vma=False,
    )
```

time: 858 us -> 634 us (0.74)
  waiting for transfers between devices: 423 us -> 72.2 us
  Pallas kernels: 50.5 us -> 286 us
  matrix products: 91.5 us -> 0.29 us
  other arithmetic: 87 us -> 52.4 us
  blocking collectives: 96.4 us -> 120 us
  between operations: 15.4 us -> 2.91 us
    pallas_call x0 -> x9, Pallas kernels: none -> 238 us  [stage(): pl.pallas_call(kernel, in_specs=[vm] * len(ins), out_specs=[vm] * len(out...]
    reduce_scatter x8 -> x0, waiting for transfers between devices: 190 us -> none  [the longest x4 126 us: reduce_branch(): lax.psum_scatter(term_fn(jnp.int32(0), lax.axis_size('mp') * row_count).a...]
    all_gather x8 -> x0, waiting for transfers between devices: 135 us -> none  [the longest x4 90.2 us: spread_rows(): return lax.all_gather(normed, 'mp', axis=0, tiled=True)]
    dot_general x24 -> x0, matrix products: 91.3 us -> none  [the longest x7 30 us: contract_cols(): lax.dot_general(left_mat, right_mat, (((1,), (1,)), ((), ())), preferred_...]
    psum x4, blocking collectives: 56.7 us -> 82.8 us  [the longest x1 61.9 us: body(): lax.psum((gains, grad_table, squares), ('dp', 'mp'))]
    ppermute x24, waiting for transfers between devices: 98.2 us -> 72.2 us  [halve_sum(): got = lax.ppermute(give, 'dp', [(i, i ^ step) for i in range(count)])]
    convert_element_type x14 -> x2, other arithmetic: 15.9 us -> 2.26 us  [the longest x1 1.6 us: body(): act3 = act3.astype(bf)]
    reduce_sum x19 -> x15, other arithmetic: 34.1 us -> 20.4 us  [the longest x2 8.14 us: body(): tap_grads.append(jnp.sum(grad_depth * padded_glu[k:k + frames], 0))]
  transfers between devices with their start and end apart: 40 -> 24, of which waited for: 27 -> 11; matrix products, arithmetic and copies ran while one was open for 14% -> 9% of each run, Pallas kernels for 3% -> 12%
where the time goes in v2:
time: 634 us; the launch traced here: 626 us
  Pallas kernels  286 us (45%)
  blocking collectives  120 us (19%)
  waiting for transfers between devices  72.2 us (11%)
  local copies, waits for them, and re-layouts  69.2 us (11%)
  other arithmetic  52.4 us (8%)
  starting transfers between devices  22.6 us (4%)
    pallas_call x9, Pallas kernels, stage(): pl.pallas_call(kernel, in_specs=[vm] * len(ins), out_specs=[vm] * len(out...  238 us
    ppermute x24, waiting for transfers between devices, halve_sum(): got = lax.ppermute(give, 'dp', [(i, i ^ step) for i in range(count)])  72.2 us
    psum x1, blocking collectives, body(): lax.psum((gains, grad_table, squares), ('dp', 'mp'))  61.9 us
    unnamed x258, local copies, waits for them, and re-layouts  43.7 us
    psum x1, blocking collectives, body(): depth_sum, depth_gain_sum = lax.psum((grad_w_depth, grad_gain_depth), 'dp')  37.7 us
    pallas_call x1, Pallas kernels, attn_bwd(): pl.pallas_call(bwd_kernel, grid=(pairs, nb), in_specs=[blk, pl.BlockSpec(...  28.2 us
    ppermute x24, starting transfers between devices, halve_sum(): got = lax.ppermute(give, 'dp', [(i, i ^ step) for i in range(count)])  22.6 us
    pallas_call x1, Pallas kernels, attn_fwd(): pl.pallas_call(fwd_kernel, grid=(pairs, nb), in_specs=[pl.BlockSpec((BQ,...  20.2 us
  transfers between devices with their start and end apart: 24, of which 11 were waited for; matrix products, arithmetic and copies ran while one was open for 9% of the time, Pallas kernels for 12%

profile of v2, /device:TPU:0, one launch (start us, length us, event | category | flops | bytes accessed | tf_op | source)
XLA Modules:
  0.0 626.1 jit_solution(7015940495284047457)
XLA Ops:
  15.8 17.5 %ffn1_in.1 = (bf16[1024,1024]{1,0:T(8,128)(2,1)S(1)}, bf16[1024,1024]{1,0:T(8,128)(2,1)S(1)}, bf16[1024,1024]{1,0:T(8,128)(2,1)S(1)}) custom-call(bf16[1024,1024]{1,0:T(8,128)(2,1)S(1)} %copy-done.28, bf16[256,1024]{1,0:T(8,128)(2,1)S(1)} %bitcast.267, f32[1,1024]{1,0:T(1,128)S(1)} %bitcast.257), custom_call_target="tpu_custom_call" | custom-call | flops 4294967296 | bytes 60000000 | tf_op jit(solution)/shard_map/ffn1_in/pallas_call | solution.py:380
  36.0 28.8 %ffn1_out.1 = (bf16[1024,1024]{1,0:T(8,128)(2,1)S(1)}, bf16[1024,768]{1,0:T(8,128)(2,1)S(1)}, f32[256,1024]{1,0:T(8,128)S(1)}, f32[8,1024]{1,0:T(8,128)S(1)}) custom-call(bf16[1024,1024]{1,0:T(8,128)(2,1)S(1)} %get-tuple-element.72.refs_0_.refs_4_, bf16[1024,1024]{1,0:T(8,128)(2,1)S(1)} %copy-done.26, bf16[1024,768]{1,0:T(8,128)(2,1)S(1)} %copy.77.refs_2_.refs_1_, ...), custom_call_target="tpu_custom_call" | custom-call | flops 3758096384 | bytes 60000000 | tf_op jit(solution)/shard_map/ffn1_out/pallas_call | solution.py:380
  66.1 20.2 %attn_fwd.1 = (bf16[1024,256]{1,0:T(8,128)(2,1)S(1)}, bf16[2,2048,1024]{2,1,0:T(8,128)(2,1)S(1)}) custom-call(bf16[1024,768]{1,0:T(8,128)(2,1)S(1)} %get-tuple-element.73.q_ref.k_ref.v_ref, bf16[1024,768]{1,0:T(8,128)(2,1)S(1)} %get-tuple-element.73.q_ref.k_ref.v_ref, bf16[1024,768]{1,0:T(8,128)(2,1)S(1)} %get-tuple-element.73.q_ref.k_ref.v_ref, ...), custom_call_target="tpu_custom_call" | custom-call | tf_op jit(solution)/shard_map/attn_fwd/pallas_call | solution.py:131
  89.6 28.4 %attn_out.1 = (bf16[1024,1024]{1,0:T(8,128)(2,1)S(1)}, f32[1024,256]{1,0:T(8,128)S(1)}, bf16[1024,256]{1,0:T(8,128)(2,1)S(1)}, bf16[1024,256]{1,0:T(8,128)(2,1)S...) custom-call(bf16[1024,256]{1,0:T(8,128)(2,1)S(1)} %get-tuple-element.74.refs_0_.refs_6_, ...), custom_call_target="tpu_custom_call" | custom-call | flops 2147483648 | bytes 60000000 | tf_op jit(solution)/shard_map/attn_out/pallas_call | solution.py:380
  121.3 5.0 fusion.40
  126.4 7.6 %psum.63 = f32[1024,1]{0,1:T(1,128)S(1)} all-reduce(f32[1024,1]{0,1:T(1,128)S(1)} %bitcast.308), channel_id=1, replica_groups=mesh['dp'=8,'mp'=4] {'mp'}, use_global_device_ids=true, to_apply=%region_1.2 | all-reduce | flops 1024 | bytes 8192 | tf_op jit(solution)/shard_map/psum | solution.py:534
  135.5 5.9 psum.64
  147.2 28.3 %conv_out.1 = (bf16[1024,1024]{1,0:T(8,128)(2,1)S(1)}, bf16[1024,1024]{1,0:T(8,128)(2,1)S(1)}, bf16[1024,1024]{1,0:T(8,128)(2,1)S(1)}, f32[256,1024]{1,0:T(8,128)S(1)}, f32[8,1024]{1,0:T(8,128)S(1)}) custom-call(bf16[1024,256]{1,0:T(8,128)(2,1)S(1)} %fusion.31.refs_0_.refs_5_, bf16[256,1024]{1,0:T(8,128)(2,1)S(1)} %copy-done.31, ...), custom_call_target="tpu_custom_call" | custom-call | flops 4831838208 | bytes 60000000 | tf_op jit(solution)/shard_map/conv_out/pallas_call | solution.py:380
  175.5 29.9 %ffn2_out.1 = (bf16[1024,1024]{1,0:T(8,128)(2,1)S(1)}, bf16[1024,1024]{1,0:T(8,128)(2,1)S(1)}, f32[256,1024]{1,0:T(8,128)S(1)}, f32[256,1024]{1,0:T(8,128)S(1)},...) custom-call(bf16[1024,1024]{1,0:T(8,128)(2,1)S(1)} %get-tuple-element.78.refs_0_.refs_5_, ...), custom_call_target="tpu_custom_call" | custom-call | flops 4294967296 | bytes 60000000 | tf_op jit(solution)/shard_map/ffn2_out/pallas_call | solution.py:380
  206.4 29.2 %ffn2_back.1 = (bf16[1024,1024]{1,0:T(8,128)(2,1)S(1)}, f32[1024,256]{1,0:T(8,128)S(1)}, bf16[8,1024,128]{2,1,0:T(8,128)(2,1)S(1)}, bf16[8,1024,128]{2,1,0:T(8,1...) custom-call(bf16[1024,1024]{1,0:T(8,128)(2,1)S(1)} %get-tuple-element.83.refs_0_.refs_4_, ...), custom_call_target="tpu_custom_call" | custom-call | flops 6979321856 | bytes 60000000 | tf_op jit(solution)/shard_map/ffn2_back/pallas_call | solution.py:380
  240.9 7.3 %all-reduce.5 = (f32[1024]{0:T(1024)}, f32[1024,1]{0,1:T(1,128)S(1)}) all-reduce(f32[1024]{0:T(1024)S(1)} %get-tuple-element.202, f32[1024,1]{0,1:T(1,128)S(1)} %bitcast.307), channel_id=1, replica_groups=mesh['dp'=8,'mp'=4] {'mp'}, use_global_device_ids=true, to_apply=%region_7.8 | all-reduce | flops 2048 | bytes 16384 | tf_op jit(solution)/shard_map/psum | solution.py:560
  248.3 5.8 multiply_reduce_fusion.1
  260.6 28.8 %conv_back.1 = (bf16[1024,1024]{1,0:T(8,128)(2,1)S(1)}, bf16[1024,256]{1,0:T(8,128)(2,1)S(1)}, bf16[4,1024,128]{2,1,0:T(8,128)(2,1)S(1)}, bf16[8,256,128]{2,1,0:...) custom-call(bf16[1024,512]{1,0:T(8,128)(2,1)S(1)} %pad_maximum_fusion.1.refs_0_.refs_4_, ...), custom_call_target="tpu_custom_call" | custom-call | flops 3221225472 | bytes 60000000 | tf_op jit(solution)/shard_map/conv_back/pallas_call | solution.py:380
  292.3 28.2 %attn_bwd.1 = (bf16[1024,256]{1,0:T(8,128)(2,1)S(1)}, bf16[1024,256]{1,0:T(8,128)(2,1)S(1)}, bf16[1024,256]{1,0:T(8,128)(2,1)S(1)}, f32[128,128]{1,0:T(8,128)S(1)}) custom-call(bf16[1024,768]{1,0:T(8,128)(2,1)S(1)} %get-tuple-element.73.q_ref.k_ref.v_ref, bf16[1024,768]{1,0:T(8,128)(2,1)S(1)} %get-tuple-element.73.q_ref.k_ref.v_ref, ...), custom_call_target="tpu_custom_call" | custom-call | tf_op jit(solution)/shard_map/attn_bwd/pallas_call | solution.py:157
  322.4 29.7 %attn_back.1 = (bf16[1024,1024]{1,0:T(8,128)(2,1)S(1)}, bf16[1024,1024]{1,0:T(8,128)(2,1)S(1)}, bf16[6,1024,128]{2,1,0:T(8,128)(2,1)S(1)}, bf16[8,256,128]{2,1,0...) custom-call(bf16[1024,768]{1,0:T(8,128)(2,1)S(1)} %pad_maximum_fusion.refs_0_.refs_5_, ...), custom_call_target="tpu_custom_call" | custom-call | flops 5905580032 | bytes 60000000 | tf_op jit(solution)/shard_map/attn_back/pallas_call | solution.py:380
  357.1 17.1 %ffn1_back.1 = (bf16[8,1024,128]{2,1,0:T(8,128)(2,1)S(1)}, bf16[8,1024,128]{2,1,0:T(8,128)(2,1)S(1)}, f32[256,1024]{1,0:T(8,128)S(1)}, f32[8,1024]{1,0:T(8,128)S(1)}) custom-call(bf16[1024,1024]{1,0:T(8,128)(2,1)S(1)} %get-tuple-element.101.refs_0_.refs_3_, bf16[1024,1024]{1,0:T(8,128)(2,1)S(1)} %copy-done.29, bf16[1024,1024]{1,0:T(8,128)(2,1)S(1)} %copy-done.58, ...), custom_call_target="tpu_custom_call" | custom-call | flops 6442450944 | bytes 60000000 | tf_op jit(solution)/shard_map/ffn1_back/pallas_call | solution.py:380
  390.2 61.9 %all-reduce.3 = (f32[5,1024]{1,0:T(8,128)S(1)}, f32[73,64]{1,0:T(8,128)S(1)}, f32[5]{0:T(128)S(1)}) all-reduce(f32[5,1024]{1,0:T(8,128)S(1)} %stack.137, f32[73,64]{1,0:T(8,128)S(1)} %slice_add_fusion, f32[5]{0:T(128)S(1)} %stack.175), channel_id=1, replica_groups=mesh['dp'=8,'mp'=4] {'dp','mp'}, use_global_device_ids=true, to_apply=%region_13.14 | all-reduce | flops 9797 | bytes 78376 | tf_op jit(solution)/shard_map/psum | solution.py:593
  466.2 37.7 %all-reduce.4 = (f32[31,256]{1,0:T(8,128)}, f32[256]{0:T(256)}) all-reduce(f32[31,256]{1,0:T(8,128)S(1)} %stack.169, f32[256]{0:T(256)S(1)} %copy-done.121), channel_id=1, replica_groups=mesh['dp'=8,'mp'=4] {'dp'}, use_global_device_ids=true, to_apply=%region_46.47 | all-reduce | flops 8192 | bytes 65536 | tf_op jit(solution)/shard_map/psum | solution.py:594
  506.7 5.0 collective-permute-done.16
  511.8 5.7 collective-permute-done.10
  528.6 5.8 collective-permute-done.13
  537.0 6.2 collective-permute-done.14
  565.1 25.2 %collective-permute-done.8 = bf16[1,6,128,128]{3,2,1,0:T(8,128)(2,1)S(1)} collective-permute-done((bf16[1,6,128,128]{3,2,1,0:T(8,128)(2,1)S(1)}, bf16[1,6,128,128]{3,2,1,0:T(8,128)(2,1)S(1)}, u32[]{:S(2)}, u32[]{:S(2)}) %collective-permute-start.8) | collective-permute-done | bytes 196640 | tf_op jit(solution)/shard_map/ppermute | solution.py:401
  607.2 10.5 %collective-permute-done.2 = bf16[1,8,128,128]{3,2,1,0:T(8,128)(2,1)S(1)} collective-permute-done((bf16[1,8,128,128]{3,2,1,0:T(8,128)(2,1)S(1)}, bf16[1,8,128,128]{3,2,1,0:T(8,128)(2,1)S(1)}, u32[]{:S(2)}, u32[]{:S(2)}) %collective-permute-start.2) | collective-permute-done | bytes 262176 | tf_op jit(solution)/shard_map/ppermute | solution.py:401
  (399 shorter events, 147.4 us)
Async XLA Ops:
  290.1 214.4 %collective-permute-start.15 = (bf16[4,256,128]{2,1,0:T(8,128)(2,1)}, bf16[4,256,128]{2,1,0:T(8,128)(2,1)}, u32[]{:S(2)}, u32[]{:S(2)}) collective-permute-start(bf16[4,256,128]{2,1,0:T(8,128)(2,1)} %dynamic-slice_bitcast_fusion.11), channel_id=1, source_target_pairs={{0,4},{4,0},{8,12},{12,8},{16,20},{20,16},{24,28},{28,24},{1,5},{5... | collective-permute-start | bytes 786440 | tf_op jit(solution)/shard_map/ppermute | solution.py:401
  352.8 152.7 %collective-permute-start.9 = (bf16[4,256,128]{2,1,0:T(8,128)(2,1)}, bf16[4,256,128]{2,1,0:T(8,128)(2,1)}, u32[]{:S(2)}, u32[]{:S(2)}) collective-permute-start(bf16[4,256,128]{2,1,0:T(8,128)(2,1)} %dynamic-slice_bitcast_fusion.13), channel_id=1, source_target_pairs={{0,4},{4,0},{8,12},{12,8},{16,20},{20,16},{24,28},{28,24},{1,5},{5... | collective-permute-start | bytes 786440 | tf_op jit(solution)/shard_map/ppermute | solution.py:401
  354.1 163.5 %collective-permute-start.12 = (bf16[4,4,128,128]{3,2,1,0:T(8,128)(2,1)}, bf16[4,4,128,128]{3,2,1,0:T(8,128)(2,1)}, u32[]{:S(2)}, u32[]{:S(2)}) collective-permute-start(bf16[4,4,128,128]{3,2,1,0:T(8,128)(2,1)} %dynamic-slice_bitcast_fusion.7), channel_id=1, source_target_pairs={{0,4},{4,0},{8,12},{12,8},{16,20},{20,16},{24,28},{28,24},{1,5},{5... | collective-permute-start | bytes 1572872 | tf_op jit(solution)/shard_map/ppermute | solution.py:401
  356.9 187.4 %collective-permute-start.21 = (bf16[4,1024,128]{2,1,0:T(8,128)(2,1)}, bf16[4,1024,128]{2,1,0:T(8,128)(2,1)}, u32[]{:S(2)}, u32[]{:S(2)}) collective-permute-start(bf16[4,1024,128]{2,1,0:T(8,128)(2,1)} %dynamic-slice_bitcast_fusion), channel_id=1, source_target_pairs={{0,4},{4,0},{8,12},{12,8},{16,20},{20,16},{24,28},{28,24},{1,5},{5... | collective-permute-start | bytes 3145736 | tf_op jit(solution)/shard_map/ppermute | solution.py:401
  376.3 172.4 %collective-permute-start.3 = (bf16[4,1024,128]{2,1,0:T(8,128)(2,1)}, bf16[4,1024,128]{2,1,0:T(8,128)(2,1)}, u32[]{:S(2)}, u32[]{:S(2)}) collective-permute-start(bf16[4,1024,128]{2,1,0:T(8,128)(2,1)} %dynamic-slice_bitcast_fusion.2), channel_id=1, source_target_pairs={{0,4},{4,0},{8,12},{12,8},{16,20},{20,16},{24,28},{28,24},{1,5},{5... | collective-permute-start | bytes 3145736 | tf_op jit(solution)/shard_map/ppermute | solution.py:401
  504.4 31.2 %collective-permute-start.6 = (bf16[4,6,128,128]{3,2,1,0:T(8,128)(2,1)}, bf16[4,6,128,128]{3,2,1,0:T(8,128)(2,1)S(1)}, u32[]{:S(2)}, u32[]{:S(2)}) collective-permute-start(bf16[4,6,128,128]{3,2,1,0:T(8,128)(2,1)} %dynamic-slice_bitcast_fusion.4), channel_id=1, source_target_pairs={{0,4},{4,0},{8,12},{12,8},{16,20},{20,16},{24,28},{28,24},{1,5},{5... | collective-permute-start | bytes 2359304 | tf_op jit(solution)/shard_map/ppermute | solution.py:401
  505.5 6.2 collective-permute-start.16
  511.7 5.8 collective-permute-start.10
  517.5 7.8 %collective-permute-start.17 = (bf16[1,256,128]{2,1,0:T(8,128)(2,1)S(1)}, bf16[1,256,128]{2,1,0:T(8,128)(2,1)S(1)}, u32[]{:S(2)}, u32[]{:S(2)}) collective-permute-start(bf16[1,256,128]{2,1,0:T(8,128)(2,1)S(1)} %constant_dynamic-slice_fusion.2), channel_id=1, source_target_pairs={{0,16},{4,20},{8,24},{12,28},{16,0},{20,4},{24,8},{28,12},{1,17},{... | collective-permute-start | bytes 196616 | tf_op jit(solution)/shard_map/ppermute | solution.py:401
  517.5 8.7 %collective-permute-start.11 = (bf16[1,256,128]{2,1,0:T(8,128)(2,1)S(1)}, bf16[1,256,128]{2,1,0:T(8,128)(2,1)S(1)}, u32[]{:S(2)}, u32[]{:S(2)}) collective-permute-start(bf16[1,256,128]{2,1,0:T(8,128)(2,1)S(1)} %constant_dynamic-slice_fusion.4), channel_id=1, source_target_pairs={{0,16},{4,20},{8,24},{12,28},{16,0},{20,4},{24,8},{28,12},{1,17},{... | collective-permute-start | bytes 196616 | tf_op jit(solution)/shard_map/ppermute | solution.py:401
  525.2 9.2 %collective-permute-start.13 = (bf16[2,4,128,128]{3,2,1,0:T(8,128)(2,1)S(1)}, bf16[2,4,128,128]{3,2,1,0:T(8,128)(2,1)S(1)}, u32[]{:S(2)}, u32[]{:S(2)}) collective-permute-start(bf16[2,4,128,128]{3,2,1,0:T(8,128)(2,1)S(1)} %dynamic-slice_bitcast_fusion.12), channel_id=1, source_target_pairs={{0,8},{4,12},{8,0},{12,4},{16,24},{20,28},{24,16},{28,20},{1,9},{5... | collective-permute-start | bytes 786440 | tf_op jit(solution)/shard_map/ppermute | solution.py:401
  526.2 25.1 %collective-permute-start = (bf16[4,8,128,128]{3,2,1,0:T(8,128)(2,1)}, bf16[4,8,128,128]{3,2,1,0:T(8,128)(2,1)}, u32[]{:S(2)}, u32[]{:S(2)}) collective-permute-start(bf16[4,8,128,128]{3,2,1,0:T(8,128)(2,1)} %dynamic-slice_bitcast_fusion.3), channel_id=1, source_target_pairs={{0,4},{4,0},{8,12},{12,8},{16,20},{20,16},{24,28},{28,24},{1,5},{5... | collective-permute-start | bytes 3145736 | tf_op jit(solution)/shard_map/ppermute | solution.py:401
  534.4 27.3 %collective-permute-start.18 = (bf16[4,8,128,128]{3,2,1,0:T(8,128)(2,1)}, bf16[4,8,128,128]{3,2,1,0:T(8,128)(2,1)}, u32[]{:S(2)}, u32[]{:S(2)}) collective-permute-start(bf16[4,8,128,128]{3,2,1,0:T(8,128)(2,1)} %dynamic-slice_bitcast_fusion.1), channel_id=1, source_target_pairs={{0,4},{4,0},{8,12},{12,8},{16,20},{20,16},{24,28},{28,24},{1,5},{5... | collective-permute-start | bytes 3145736 | tf_op jit(solution)/shard_map/ppermute | solution.py:401
  535.6 7.6 %collective-permute-start.14 = (bf16[1,4,128,128]{3,2,1,0:T(8,128)(2,1)S(1)}, bf16[1,4,128,128]{3,2,1,0:T(8,128)(2,1)S(1)}, u32[]{:S(2)}, u32[]{:S(2)}) collective-permute-start(bf16[1,4,128,128]{3,2,1,0:T(8,128)(2,1)S(1)} %constant_dynamic-slice_fusion.3), channel_id=1, source_target_pairs={{0,16},{4,20},{8,24},{12,28},{16,0},{20,4},{24,8},{28,12},{1,17},{... | collective-permute-start | bytes 393224 | tf_op jit(solution)/shard_map/ppermute | solution.py:401
  543.2 12.4 %collective-permute-start.7 = (bf16[2,6,128,128]{3,2,1,0:T(8,128)(2,1)S(1)}, bf16[2,6,128,128]{3,2,1,0:T(8,128)(2,1)}, u32[]{:S(2)}, u32[]{:S(2)}) collective-permute-start(bf16[2,6,128,128]{3,2,1,0:T(8,128)(2,1)S(1)} %dynamic-slice_bitcast_fusion.10), channel_id=1, source_target_pairs={{0,8},{4,12},{8,0},{12,4},{16,24},{20,28},{24,16},{28,20},{1,9},{5... | collective-permute-start | bytes 1179656 | tf_op jit(solution)/shard_map/ppermute | solution.py:401
  546.7 46.5 %collective-permute-start.22 = (bf16[2,1024,128]{2,1,0:T(8,128)(2,1)}, bf16[2,1024,128]{2,1,0:T(8,128)(2,1)}, u32[]{:S(2)}, u32[]{:S(2)}) collective-permute-start(bf16[2,1024,128]{2,1,0:T(8,128)(2,1)} %dynamic-slice_bitcast_fusion.5), channel_id=1, source_target_pairs={{0,8},{4,12},{8,0},{12,4},{16,24},{20,28},{24,16},{28,20},{1,9},{5... | collective-permute-start | bytes 1572872 | tf_op jit(solution)/shard_map/ppermute | solution.py:401
  551.1 52.5 %collective-permute-start.4 = (bf16[2,1024,128]{2,1,0:T(8,128)(2,1)}, bf16[2,1024,128]{2,1,0:T(8,128)(2,1)}, u32[]{:S(2)}, u32[]{:S(2)}) collective-permute-start(bf16[2,1024,128]{2,1,0:T(8,128)(2,1)} %dynamic-slice_bitcast_fusion.8), channel_id=1, source_target_pairs={{0,8},{4,12},{8,0},{12,4},{16,24},{20,28},{24,16},{28,20},{1,9},{5... | collective-permute-start | bytes 1572872 | tf_op jit(solution)/shard_map/ppermute | solution.py:401
  553.8 44.3 %collective-permute-start.1 = (bf16[2,8,128,128]{3,2,1,0:T(8,128)(2,1)}, bf16[2,8,128,128]{3,2,1,0:T(8,128)(2,1)}, u32[]{:S(2)}, u32[]{:S(2)}) collective-permute-start(bf16[2,8,128,128]{3,2,1,0:T(8,128)(2,1)} %dynamic-slice_bitcast_fusion.9), channel_id=1, source_target_pairs={{0,8},{4,12},{8,0},{12,4},{16,24},{20,28},{24,16},{28,20},{1,9},{5... | collective-permute-start | bytes 1572872 | tf_op jit(solution)/shard_map/ppermute | solution.py:401
  556.7 33.6 %collective-permute-start.8 = (bf16[1,6,128,128]{3,2,1,0:T(8,128)(2,1)S(1)}, bf16[1,6,128,128]{3,2,1,0:T(8,128)(2,1)S(1)}, u32[]{:S(2)}, u32[]{:S(2)}) collective-permute-start(bf16[1,6,128,128]{3,2,1,0:T(8,128)(2,1)S(1)} %constant_dynamic-slice_fusion.5), channel_id=1, source_target_pairs={{0,16},{4,20},{8,24},{12,28},{16,0},{20,4},{24,8},{28,12},{1,17},{... | collective-permute-start | bytes 589832 | tf_op jit(solution)/shard_map/ppermute | solution.py:401
  565.1 36.6 %collective-permute-start.19 = (bf16[2,8,128,128]{3,2,1,0:T(8,128)(2,1)}, bf16[2,8,128,128]{3,2,1,0:T(8,128)(2,1)}, u32[]{:S(2)}, u32[]{:S(2)}) collective-permute-start(bf16[2,8,128,128]{3,2,1,0:T(8,128)(2,1)} %dynamic-slice_bitcast_fusion.6), channel_id=1, source_target_pairs={{0,8},{4,12},{8,0},{12,4},{16,24},{20,28},{24,16},{28,20},{1,9},{5... | collective-permute-start | bytes 1572872 | tf_op jit(solution)/shard_map/ppermute | solution.py:401
  594.5 28.5 %collective-permute-start.23 = (bf16[1,1024,128]{2,1,0:T(8,128)(2,1)S(1)}, bf16[1,1024,128]{2,1,0:T(8,128)(2,1)S(1)}, u32[]{:S(2)}, u32[]{:S(2)}) collective-permute-start(bf16[1,1024,128]{2,1,0:T(8,128)(2,1)S(1)} %constant_dynamic-slice_fusion), channel_id=1, source_target_pairs={{0,16},{4,20},{8,24},{12,28},{16,0},{20,4},{24,8},{28,12},{1,17},{... | collective-permute-start | bytes 786440 | tf_op jit(solution)/shard_map/ppermute | solution.py:401
  599.3 18.4 %collective-permute-start.2 = (bf16[1,8,128,128]{3,2,1,0:T(8,128)(2,1)S(1)}, bf16[1,8,128,128]{3,2,1,0:T(8,128)(2,1)S(1)}, u32[]{:S(2)}, u32[]{:S(2)}) collective-permute-start(bf16[1,8,128,128]{3,2,1,0:T(8,128)(2,1)S(1)} %constant_dynamic-slice_fusion.7), channel_id=1, source_target_pairs={{0,16},{4,20},{8,24},{12,28},{16,0},{20,4},{24,8},{28,12},{1,17},{... | collective-permute-start | bytes 786440 | tf_op jit(solution)/shard_map/ppermute | solution.py:401
  602.9 17.6 %collective-permute-start.20 = (bf16[1,8,128,128]{3,2,1,0:T(8,128)(2,1)S(1)}, bf16[1,8,128,128]{3,2,1,0:T(8,128)(2,1)S(1)}, u32[]{:S(2)}, u32[]{:S(2)}) collective-permute-start(bf16[1,8,128,128]{3,2,1,0:T(8,128)(2,1)S(1)} %constant_dynamic-slice_fusion.1), channel_id=1, source_target_pairs={{0,16},{4,20},{8,24},{12,28},{16,0},{20,4},{24,8},{28,12},{1,17},{... | collective-permute-start | bytes 786440 | tf_op jit(solution)/shard_map/ppermute | solution.py:401
  604.8 19.1 %collective-permute-start.5 = (bf16[1,1024,128]{2,1,0:T(8,128)(2,1)S(1)}, bf16[1,1024,128]{2,1,0:T(8,128)(2,1)}, u32[]{:S(2)}, u32[]{:S(2)}) collective-permute-start(bf16[1,1024,128]{2,1,0:T(8,128)(2,1)S(1)} %constant_dynamic-slice_fusion.6), channel_id=1, source_target_pairs={{0,16},{4,20},{8,24},{12,28},{16,0},{20,4},{24,8},{28,12},{1,17},{... | collective-permute-start | bytes 786440 | tf_op jit(solution)/shard_map/ppermute | solution.py:401
  (124 other events, 2341.1 us)

commit v3 on v2

v3 whole, which is shorter than its diff:
```python
import functools

import jax
import jax.numpy as jnp
from jax import lax
from jax.experimental import pallas as pl
from jax.experimental.pallas import tpu as pltpu
from jax.sharding import PartitionSpec as P

HEAD = 64
REL_LEFT = 64
REL_RIGHT = 8
BQ = 128
WIN = 4 * BQ


epsilon = 1e-05


def nt(a, b):
    return lax.dot_general(a, b, (((1,), (1,)), ((), ())), preferred_element_type=jnp.float32)
def nn(a, b):
    return lax.dot_general(a, b, (((1,), (0,)), ((), ())), preferred_element_type=jnp.float32)
def tn(a, b):
    return lax.dot_general(a, b, (((0,), (0,)), ((), ())), preferred_element_type=jnp.float32)

MESH = pl.DeviceIdType.MESH
CHUNKS = 4
PIECE = 256


def silu_pair(h):
    sig = jax.nn.sigmoid(h)
    act = h * sig
    return act, sig + act * (1.0 - sig)


def unit_norm(s):
    centred = s - jnp.mean(s, -1, keepdims=True)
    inverse = lax.rsqrt(jnp.mean(centred * centred, -1, keepdims=True) + epsilon)
    return centred * inverse, inverse


def fold8(x):
    return jnp.sum(x.reshape(x.shape[0] // 8, 8, x.shape[1]), 0)


def norm_pull(grad, s, gain):
    unit, inverse = unit_norm(s)
    scaled = grad * gain
    first = jnp.mean(scaled, -1, keepdims=True)
    second = jnp.mean(scaled * unit, -1, keepdims=True)
    return inverse * (scaled - first - unit * second), fold8(grad * unit)


class Grad:
    def __init__(self, array, bit, turned):
        self.array, self.bit, self.turned = array, bit, turned


def halved(shape, turned):
    pieces, pairs, _, block, cols = shape
    if pairs > 1:
        return jax.ShapeDtypeStruct((pieces, pairs // 2, 2, block, cols), jnp.bfloat16)
    if turned and block % 128 == 0:
        return jax.ShapeDtypeStruct((pieces * cols, block), jnp.float32)
    return jax.ShapeDtypeStruct((block, pieces * cols), jnp.float32)


def arriving(shape):
    return pltpu.VMEM((shape[0], shape[1]) + tuple(shape[3:]), jnp.bfloat16)


def place(dp, bit):
    own = (dp // 2**bit) % 2
    return own, dp + 2**bit * (1 - 2 * own)


def halving_copy(src, landing, piece, bit, send, recv, slot):
    dp, mp = lax.axis_index("dp"), lax.axis_index("mp")
    own, partner = place(dp, bit)
    return pltpu.make_async_remote_copy(
        src.at[piece, :, 1 - own], landing.at[piece], send.at[slot], recv.at[slot],
        device_id=(partner, mp), device_id_type=MESH,
    )


def halving_add(src, landing, out, piece, bit, turned):
    own, _ = place(lax.axis_index("dp"), bit)
    pairs, block, cols = landing.shape[1:]
    f32 = jnp.float32
    if pairs == 1:
        total = src[piece, 0, own].astype(f32) + landing[piece, 0].astype(f32)
        at = slice(piece * cols, (piece + 1) * cols)
        if turned and block % 128 == 0:
            out[at, :] = total.T
        else:
            out[:, at] = total
        return

    def add(j, c):
        total = src[piece, j, own].astype(f32) + landing[piece, j].astype(f32)
        out[piece, j // 2, j % 2] = total.astype(jnp.bfloat16)
        return c

    lax.fori_loop(0, pairs, add, 0)


def greet(targets):
    barrier = pltpu.get_barrier_semaphore()
    for to in targets:
        pl.semaphore_signal(barrier, inc=1, device_id=to, device_id_type=MESH)
    pl.semaphore_wait(barrier, len(targets))


def stage(name, cid, rows, width, count, *, leave=None, enter=None, dws=(), grads=(), small=None, junction, row_in=(), vec_in=(), row_out=(), sums=0):
    chunk = rows // CHUNKS
    frames = rows * 4
    steps = count.bit_length() - 1
    last = small is not None
    f32, bf = jnp.float32, jnp.bfloat16
    ins, out_shape, scratch = [], [], []
    if leave:
        ins += [leave[0], leave[1]]
        scratch += [pltpu.VMEM((rows, width), f32)] * 2 + [pltpu.VMEM((rows, width), bf)] * 6
        if leave[2]:
            scratch.append(pltpu.VMEM(leave[1].shape[::-1], bf))
    if enter:
        ins += [enter[0]] + list(enter[3])
        out_shape.append(jax.ShapeDtypeStruct((frames, width), bf))
        out_shape += [jax.ShapeDtypeStruct((frames, c), d) for c, d in enter[4]]
        if enter[1]:
            scratch.append(pltpu.VMEM(enter[0].shape[::-1], bf))
    ins += list(row_in) + list(vec_in)
    out_shape += [jax.ShapeDtypeStruct((rows, width), d) for d in row_out]
    out_shape += [jax.ShapeDtypeStruct((8, width), f32)] * sums
    fixed_out = len(out_shape)
    plan, dw_shapes = [], []
    for lhs, rhs, where, turned in dws:
        ins += [lhs, rhs]
        shape = (rhs.shape[1] // PIECE, count // 2, 2, width // count, PIECE)
        dw_shapes.append(shape)
        if where == "join":
            out_shape.append(jax.ShapeDtypeStruct(shape, bf))
        else:
            scratch.append(pltpu.VMEM(shape, bf))
            plan.append((shape, 0, turned))
    for g in grads:
        ins.append(g.array)
        plan.append((g.array.shape, g.bit, g.turned))
    chains = []
    slots = 0
    for shape, bit, turned in plan:
        links = []
        for b in range(bit, steps if last else bit + 1):
            nxt = halved(shape, turned)
            final = b == (steps if last else bit + 1) - 1
            scratch.append(arriving(shape))
            if final:
                out_shape.append(nxt)
            else:
                scratch.append(pltpu.VMEM(nxt.shape, nxt.dtype))
            links.append((b, final, slots))
            slots += shape[0]
            shape = nxt.shape
        chains.append((plan[len(chains)][0][0], turned, links))
    if last:
        ins += small
        small_shapes = [(16, width), small[-3].shape, (small[-2].shape[0] + 1, small[-2].shape[1])]
        small_steps = [steps + 2, steps + 2, steps]
        out_shape += [jax.ShapeDtypeStruct(s, f32) for s in small_shapes]
        scratch += [pltpu.VMEM((n,) + s, f32) for s, n in zip(small_shapes, small_steps)]
        scratch += [pltpu.SemaphoreType.DMA((3, steps + 2))] * 2
    if slots:
        scratch += [pltpu.SemaphoreType.DMA((slots,))] * 2
    scratch += [pltpu.SemaphoreType.DMA((6, CHUNKS))] * 2

    def kernel(*refs):
        i_refs = list(refs[: len(ins)])
        o_refs = list(refs[len(ins) : len(ins) + len(out_shape)])
        t_refs = list(refs[len(ins) + len(out_shape) :])
        take = lambda pool, n: [pool.pop(0) for _ in range(n)]
        if leave:
            x_ref, wl_raw = take(i_refs, 2)
            px, own, sb, sr, xs, xr, ob, orv = take(t_refs, 8)
            wl_ref = take(t_refs, 1)[0] if leave[2] else wl_raw
        if enter:
            (we_raw,) = take(i_refs, 1)
            extra = take(i_refs, len(enter[3]))
            (all_ref,) = take(o_refs, 1)
            e_out = take(o_refs, len(enter[4]))
            we_ref = take(t_refs, 1)[0] if enter[1] else we_raw
        r_in, v_in = take(i_refs, len(row_in)), take(i_refs, len(vec_in))
        r_out, s_out = take(o_refs, len(row_out)), take(o_refs, sums)
        dw_refs, sources = [], []
        for (lhs, rhs, where, turned) in dws:
            a, b = take(i_refs, 2)
            dw = take(o_refs if where == "join" else t_refs, 1)[0]
            dw_refs.append((a, b, dw, None if where == "join" else len(sources)))
            if where != "join":
                sources.append(dw)
        first_grad = len(sources)
        sources += take(i_refs, len(grads))
        runs = []
        for (pieces, turned, links), src in zip(chains, sources):
            run = []
            for b, final, slot in links:
                landing = take(t_refs, 1)[0]
                out = take(o_refs if final else t_refs, 1)[0]
                run.append((b, slot, src, landing, out))
                src = out
            runs.append((pieces, turned, run))
        if last:
            small_in = take(i_refs, len(small))
            small_out = take(o_refs, 3)
            small_land = take(t_refs, 3)
            ssend, srecv = take(t_refs, 2)
        if slots:
            gsend, grecv = take(t_refs, 2)
        send, recv = take(t_refs, 2)
        dp, me = lax.axis_index("dp"), lax.axis_index("mp")
        core, chip = me % 2, me // 2
        sib = chip * 2 + 1 - core
        far = (1 - chip) * 2 + core
        diag = (1 - chip) * 2 + 1 - core

        def part(ref, block, k):
            return ref.at[pl.ds(pl.multiple_of(block * rows + k * chunk, chunk), chunk)]

        def copy(kind, k, src, dst, to):
            return pltpu.make_async_remote_copy(
                src, dst, send.at[kind, k], recv.at[kind, k], device_id=(dp, to), device_id_type=MESH
            )

        pair_send = lambda k: copy(0, k, part(sb, 0, k), part(sr, 0, k), sib)
        far_send = lambda k: copy(1, k, part(xs, 0, k), part(xr, 0, k), far)
        own_send = lambda k: copy(2, k, part(ob, 0, k), part(orv, 0, k), sib)
        all_far = lambda k: copy(3, k, part(all_ref, me, k), part(all_ref, me, k), far)
        all_sib = lambda k: copy(4, k, part(all_ref, me, k), part(all_ref, me, k), sib)
        all_fwd = lambda k: copy(5, k, part(all_ref, far, k), part(all_ref, far, k), sib)
        got_far = lambda k: copy(3, k, part(all_ref, far, k), part(all_ref, far, k), far)
        got_sib = lambda k: copy(4, k, part(all_ref, sib, k), part(all_ref, sib, k), sib)
        got_diag = lambda k: copy(5, k, part(all_ref, diag, k), part(all_ref, diag, k), sib)

        def hop(chain, step, piece):
            b, slot, src, landing, out = runs[chain][2][step]
            return halving_copy(src, landing, piece, b, gsend, grecv, slot + piece)

        def settle(chain, step, piece):
            b, slot, src, landing, out = runs[chain][2][step]
            hop(chain, step, piece).wait_recv()
            halving_add(src, landing, out, piece, b, runs[chain][1])

        bits = sorted({r[0] for _, _, run in runs for r in run})
        greet([(dp, sib), (dp, far)] + [(place(dp, b)[1], me) for b in bits])
        for c in range(first_grad, len(runs)):
            for p in range(runs[c][0]):
                hop(c, 0, p).start()
        for ref in s_out:
            ref[...] = jnp.zeros_like(ref)

        def fill(k, where):
            for (lhs, rhs, at_loop, turned), (a, b, dw, chain) in zip(dws, dw_refs):
                if at_loop != where:
                    continue

                @pl.when(k < dw.shape[0])
                def _(a=a, b=b, dw=dw, chain=chain):
                    g = tn(a[...], b[:, pl.ds(pl.multiple_of(k * PIECE, PIECE), PIECE)])
                    dw[k] = g.astype(bf).reshape(dw.shape[1:])
                    if chain is not None:
                        hop(chain, 0, k).start()

        if leave:
            if leave[2]:
                wl_ref[...] = wl_raw[...].T

            def two(k, block_a, block_b):
                lhs = jnp.concatenate([part(x_ref, block_a, k)[...], part(x_ref, block_b, k)[...]], 0)
                return nn(lhs, wl_ref[...])

            def push(k):
                pair_send(k).wait_recv()
                part(xs, 0, k)[...] = (part(px, 0, k)[...] + part(sr, 0, k)[...].astype(f32)).astype(bf)
                far_send(k).start()

            def out_far(k, c):
                p = two(k, far, diag)
                part(px, 0, k)[...] = p[:chunk]
                part(sb, 0, k)[...] = p[chunk:].astype(bf)
                pair_send(k).start()

                @pl.when(k > 0)
                def _():
                    push(k - 1)

                fill(k, "far")
                return c

            lax.fori_loop(0, CHUNKS, out_far, 0)

            def out_near(k, c):
                p = two(k, me, sib)
                part(own, 0, k)[...] = p[:chunk]
                part(ob, 0, k)[...] = p[chunk:].astype(bf)
                own_send(k).start()

                @pl.when(k == 0)
                def _():
                    push(CHUNKS - 1)

                fill(k, "near")
                return c

            lax.fori_loop(0, CHUNKS, out_near, 0)
        if enter and enter[1]:
            we_ref[...] = we_raw[...].T

        def join(k, c):
            fill(k, "join")
            branch = None
            if leave:
                own_send(k).wait_recv()
                far_send(k).wait_recv()
                branch = part(own, 0, k)[...] + part(orv, 0, k)[...].astype(f32) + part(xr, 0, k)[...].astype(f32)
            view = lambda ref: part(ref, 0, k)
            fresh = junction(branch, [view(r)[...] for r in r_in], [v[...] for v in v_in], [view(r) for r in r_out], s_out)
            if enter:
                part(all_ref, me, k)[...] = fresh
                all_far(k).start()
                all_sib(k).start()
            return c

        lax.fori_loop(0, CHUNKS, join, 0)

        if enter:
            def work(k, block_a, block_b):
                lhs = jnp.concatenate([part(all_ref, block_a, k)[...], part(all_ref, block_b, k)[...]], 0)
                h = nn(lhs, we_ref[...])
                for i, block in enumerate((block_a, block_b)):
                    view = lambda ref: part(ref, block, k)
                    enter[2](h[i * chunk : (i + 1) * chunk], [view(r)[...] for r in extra], [view(r) for r in e_out])

            def gather(k, c):
                got_sib(k).wait_recv()
                work(k, me, sib)
                got_far(k).wait_recv()
                all_fwd(k).start()
                got_diag(k).wait_recv()
                work(k, far, diag)
                return c

            lax.fori_loop(0, CHUNKS, gather, 0)

        if last:
            *vectors, table, taps, tap_gain = small_in
            small_out[0][...] = jnp.zeros_like(small_out[0])
            for i, v in enumerate([s_out[0]] + vectors):
                small_out[0][i : i + 1, :] = jnp.sum(v[...], 0, keepdims=True)
            small_out[1][...] = table[...]
            small_out[2][: taps.shape[0], :] = taps[...]
            small_out[2][taps.shape[0] :, :] = tap_gain[...]

            def double(step):
                if step < steps:
                    to = (place(dp, step)[1], me)
                else:
                    to = (dp, sib if step == steps else far)
                return [
                    pltpu.make_async_remote_copy(
                        o, l.at[step], ssend.at[i, step], srecv.at[i, step], device_id=to, device_id_type=MESH
                    )
                    for i, (o, l, n) in enumerate(zip(small_out, small_land, small_steps))
                    if step < n
                ]

            for cp in double(0):
                cp.start()

        pieces = [(c, p) for c, (count_p, _, _) in enumerate(runs) for p in range(count_p)]
        order = [x for x in pieces if x[0] >= first_grad] + [x for x in pieces if x[0] < first_grad]
        deepest = max([len(run) for _, _, run in runs] + [0])
        total_slots = max(len(order) + deepest - 1, (steps + 2) if last else 0)
        for t in range(total_slots):
            if last and t < steps + 2:
                for cp in double(t):
                    cp.wait()
                for o, l, n in zip(small_out, small_land, small_steps):
                    if t < n:
                        o[...] += l[t]
                if t + 1 < steps + 2:
                    for cp in double(t + 1):
                        cp.start()
            for s in reversed(range(deepest)):
                if 0 <= t - s < len(order) and s < len(runs[order[t - s][0]][2]):
                    c, p = order[t - s]
                    settle(c, s, p)
                    if s + 1 < len(runs[c][2]):
                        hop(c, s + 1, p).start()
        for c, (count_p, _, run) in enumerate(runs):
            for s in range(len(run)):
                for p in range(count_p):
                    hop(c, s, p).wait_send()

        def drain(k, c):
            if leave:
                pair_send(k).wait_send()
                far_send(k).wait_send()
                own_send(k).wait_send()
            if enter:
                all_far(k).wait_send()
                all_sib(k).wait_send()
                all_fwd(k).wait_send()
            return c

        lax.fori_loop(0, CHUNKS, drain, 0)

    flops = 0
    if leave:
        flops += 2 * frames * leave[0].shape[1] * width
    if enter:
        flops += 2 * frames * width * sum(c for c, _ in enter[4])
    flops += sum(2 * frames * d[0].shape[1] * d[1].shape[1] for d in dws)
    vm = pl.BlockSpec(memory_space=pltpu.VMEM)
    outs = pl.pallas_call(
        kernel,
        in_specs=[vm] * len(ins),
        out_specs=[vm] * len(out_shape),
        out_shape=out_shape,
        scratch_shapes=scratch,
        compiler_params=pltpu.CompilerParams(
            collective_id=cid, has_side_effects=True, vmem_limit_bytes=(40 if last else 28) << 20
        ),
        cost_estimate=pl.CostEstimate(flops=flops, bytes_accessed=60_000_000, transcendentals=0),
        name=name,
    )(*ins)
    fixed, rest = list(outs[:fixed_out]), list(outs[fixed_out:])
    fresh = [Grad(rest.pop(0), 0, d[3]) for d in dws if d[2] == "join"]
    for (shape, bit, turned) in plan:
        fresh.append(Grad(rest.pop(0), steps if last else bit + 1, turned))
    return fixed + [fresh] + rest


def split_pair(x):
    left = lax.broadcasted_iota(jnp.int32, x.shape, 1) < HEAD
    zero = jnp.zeros_like(x)
    return jnp.concatenate([jnp.where(left, x, zero), jnp.where(left, zero, x)], 0)

def join_pair(x):
    rows = x.shape[0] // 2
    left = lax.broadcasted_iota(jnp.int32, (rows, x.shape[1]), 1) < HEAD
    return jnp.where(left, x[:rows], x[rows:])

def fwd_kernel(q_ref, k_ref, v_ref, rel_ref, mixed_ref, probs_ref, bias_ref):
    ib = pl.program_id(1)
    qs = split_pair(q_ref[...] * 0.125)
    s = nt(qs, k_ref[...])
    b = nt(qs, rel_ref[...])
    rows = b.shape[0] // 2
    bias_ref[:, 0:BQ] = b[:, 3 * BQ : 4 * BQ]
    for h in range(2):
        r = pltpu.roll(b[h * rows : (h + 1) * rows, :WIN], 0, 1, stride=1, stride_axis=0)
        bias_ref[h * rows : (h + 1) * rows, BQ : 4 * BQ] = r[:, : 3 * BQ]
    bias_ref[:, 4 * BQ :] = b[:, 4 * BQ :]
    nkeys = s.shape[1] // BQ
    parts = []
    for jb in range(nkeys):
        at = pl.multiple_of(jnp.clip(jb - ib + 2, 0, 4) * BQ, BQ)
        parts.append(s[:, jb * BQ : (jb + 1) * BQ] + bias_ref[:, pl.ds(at, BQ)])
    top = functools.reduce(jnp.maximum, parts)
    m = jnp.max(top, -1, keepdims=True)
    es = [jnp.exp(p - m) for p in parts]
    tot = jnp.sum(functools.reduce(jnp.add, es), -1, keepdims=True)
    inv = 1.0 / tot
    for jb in range(nkeys):
        probs_ref[0, :, jb * BQ : (jb + 1) * BQ] = (es[jb] * inv).astype(jnp.bfloat16)
    mixed_ref[...] = join_pair(nn(probs_ref[0], v_ref[...])).astype(jnp.bfloat16)

def bwd_kernel(plan, *refs):
    n = len(plan)
    pairs_in, refs = refs[7 : 7 + n], refs[:7] + refs[7 + n :]
    q_ref, k_ref, v_ref, relb_ref, hot_ref, probs_ref, do_ref, dq_ref, dk_ref, dv_ref, dt_ref = refs[:11]
    grads_out, refs = refs[11 : 11 + n], refs[11 + n :]
    tot_ref, dkt, dvt, dta, dz_ref = refs[:5]
    landings, sems = refs[5 : 5 + n], refs[5 + n :]
    pr, ib, nb = pl.program_id(0), pl.program_id(1), pl.num_programs(1)
    dp, mp = lax.axis_index("dp"), lax.axis_index("mp")
    hops, slot = [], 0
    for (pieces, bit, turned), src, landing, out in zip(plan, pairs_in, landings, grads_out):
        for p in range(pieces):
            hops.append((halving_copy(src, landing, p, bit, *sems, slot), src, landing, out, p, bit, turned))
            slot += 1

    if hops:

        @pl.when((ib == 0) & (pr == 0))
        def _():
            greet([(place(dp, b)[1], mp) for b in sorted({x[1] for x in plan})])
            for hop in hops:
                hop[0].start()

    @pl.when(ib == 0)
    def _():
        dkt[...] = jnp.zeros_like(dkt)
        dvt[...] = jnp.zeros_like(dvt)
    @pl.when((ib == 0) & (pr == 0))
    def _():
        dta[...] = jnp.zeros_like(dta)
    qs = split_pair(q_ref[...] * 0.125)
    dos = split_pair(do_ref[...])
    p = probs_ref[0]
    dp = nt(dos, v_ref[...])
    nkeys = dp.shape[1] // BQ
    dvt[...] += tn(dos, p)
    pf = p.astype(jnp.float32)
    acc = None
    for jb in range(nkeys):
        sl = slice(jb * BQ, (jb + 1) * BQ)
        t = pf[:, sl] * dp[:, sl]
        acc = t if acc is None else acc + t
    inner = jnp.sum(acc, -1, keepdims=True)
    tot_ref[...] = jnp.zeros_like(tot_ref)
    for jb in range(nkeys):
        sl = slice(jb * BQ, (jb + 1) * BQ)
        dz = (pf[:, sl] * (dp[:, sl] - inner)).astype(jnp.bfloat16)
        dz_ref[:, sl] = dz
        at = pl.multiple_of(jnp.clip(jb - ib + 2, 0, 4) * BQ, BQ)
        tot_ref[:, pl.ds(at, BQ)] += dz.astype(jnp.float32)
    rows = BQ
    r2 = lax.broadcasted_iota(jnp.int32, (2 * rows, 2 * rows), 0)
    c2 = lax.broadcasted_iota(jnp.int32, (2 * rows, 2 * rows), 1)
    mirror = (r2 + c2 == jnp.where(r2 < rows, rows - 1, 3 * rows - 1)).astype(jnp.bfloat16)
    w = jnp.concatenate([tot_ref[:, BQ : 4 * BQ].astype(jnp.bfloat16), jnp.zeros((2 * rows, BQ), jnp.bfloat16)], 1)
    w = nn(mirror, w)
    outs = [pltpu.roll(w[h * rows : (h + 1) * rows], WIN - rows + 1, 1, stride=1, stride_axis=0) for h in range(2)]
    d = nn(mirror, jnp.concatenate(outs, 0).astype(jnp.bfloat16)).astype(jnp.bfloat16)
    drel = nn(d, hot_ref[...])
    col = lax.broadcasted_iota(jnp.int32, drel.shape, 1)
    low = jnp.sum(tot_ref[:, :BQ], -1, keepdims=True)
    high = jnp.sum(tot_ref[:, 4 * BQ :], -1, keepdims=True)
    drel = drel + jnp.where(col == 0, low, 0.0) + jnp.where(col == REL_LEFT + REL_RIGHT, high, 0.0)
    drel = drel.astype(jnp.bfloat16)
    dz = dz_ref[...]
    dq = nn(dz, k_ref[...]) + nn(drel, relb_ref[...])
    dq_ref[...] = (join_pair(dq) * 0.125).astype(jnp.bfloat16)
    dkt[...] += tn(qs, dz)
    dta[...] += tn(drel, qs)
    @pl.when(ib == nb - 1)
    def _():
        dk_ref[...] = dkt[...].T.astype(jnp.bfloat16)
        dv_ref[...] = dvt[...].T.astype(jnp.bfloat16)
        dt_ref[...] = dta[...]

    if hops:

        @pl.when((ib == nb - 1) & (pr == pl.num_programs(0) - 1))
        def _():
            for hop in hops:
                hop[0].wait_recv()
                halving_add(*hop[1:])
            for hop in hops:
                hop[0].wait_send()

def rel_tables(rel_table):
    spots = jnp.arange(5 * BQ)
    idx = jnp.where(spots < 3 * BQ, jnp.clip(spots - REL_LEFT, 0, REL_LEFT + REL_RIGHT), jnp.where(spots < 4 * BQ, 0, REL_LEFT + REL_RIGHT))
    hot = (jnp.arange(BQ)[None, :] == idx[:, None]).astype(jnp.bfloat16)
    padded = jnp.pad(rel_table, ((0, BQ - rel_table.shape[0]), (0, 0)))
    padded = jnp.concatenate([padded, padded], 1)
    ext = jnp.dot(hot, padded, preferred_element_type=jnp.float32).astype(jnp.bfloat16)
    return ext, hot[:WIN], padded

def attn_fwd(qkv, ext):
    frames, cols = qkv.shape
    pairs = cols // 3 // 128
    nb = frames // BQ
    bf = jnp.bfloat16
    return pl.pallas_call(
        fwd_kernel,
        grid=(pairs, nb),
        in_specs=[
            pl.BlockSpec((BQ, 128), lambda p, i: (i, p)),
            pl.BlockSpec((frames, 128), lambda p, i: (0, pairs + p)),
            pl.BlockSpec((frames, 128), lambda p, i: (0, 2 * pairs + p)),
            pl.BlockSpec(ext.shape, lambda p, i: (0, 0)),
        ],
        out_specs=[
            pl.BlockSpec((BQ, 128), lambda p, i: (i, p)),
            pl.BlockSpec((1, 2 * BQ, frames), lambda p, i: (p, i, 0)),
        ],
        out_shape=[jax.ShapeDtypeStruct((frames, cols // 3), bf), jax.ShapeDtypeStruct((pairs, 2 * frames, frames), bf)],
        scratch_shapes=[pltpu.VMEM((2 * BQ, 5 * BQ), jnp.float32)],
        compiler_params=pltpu.CompilerParams(vmem_limit_bytes=20 << 20),
        name="attn_fwd",
    )(qkv, qkv, qkv, ext)

def attn_bwd(qkv, padded, hot, probs, dmixed, grads, cid):
    frames, cols = qkv.shape
    pairs = cols // 3 // 128
    nb = frames // BQ
    bf = jnp.bfloat16
    blk = pl.BlockSpec((BQ, 128), lambda p, i: (i, p))
    full = pl.BlockSpec((frames, 128), lambda p, i: (0, p))
    plan = [(g.array.shape[0], g.bit, g.turned) for g in grads]
    after = [halved(g.array.shape, g.turned) for g in grads]
    still = lambda shape: pl.BlockSpec(shape, lambda p, i: (0,) * len(shape), pipeline_mode=pl.Buffered(1))
    slots = sum(x[0] for x in plan)
    outs = pl.pallas_call(
        functools.partial(bwd_kernel, plan),
        grid=(pairs, nb),
        in_specs=[
            blk,
            pl.BlockSpec((frames, 128), lambda p, i: (0, pairs + p)),
            pl.BlockSpec((frames, 128), lambda p, i: (0, 2 * pairs + p)),
            pl.BlockSpec(padded.shape, lambda p, i: (0, 0)),
            pl.BlockSpec(hot.shape, lambda p, i: (0, 0)),
            pl.BlockSpec((1, 2 * BQ, frames), lambda p, i: (p, i, 0)),
            blk,
        ]
        + [still(g.array.shape) for g in grads],
        out_specs=[blk, full, full, pl.BlockSpec((128, 128), lambda p, i: (0, 0))] + [still(a.shape) for a in after],
        out_shape=[jax.ShapeDtypeStruct((frames, cols // 3), bf)] * 3 + [jax.ShapeDtypeStruct((128, 128), jnp.float32)] + after,
        scratch_shapes=[pltpu.VMEM((2 * BQ, 5 * BQ), jnp.float32), pltpu.VMEM((128, frames), jnp.float32), pltpu.VMEM((128, frames), jnp.float32),
                        pltpu.VMEM((128, 128), jnp.float32), pltpu.VMEM((2 * BQ, frames), bf)]
        + [arriving(g.array.shape) for g in grads]
        + ([pltpu.SemaphoreType.DMA((slots,))] * 2 if grads else []),
        compiler_params=pltpu.CompilerParams(
            vmem_limit_bytes=32 << 20, collective_id=cid, has_side_effects=True
        ),
        cost_estimate=pl.CostEstimate(flops=20 * frames * frames * 128 * pairs, bytes_accessed=20_000_000, transcendentals=0),
        name="attn_bwd",
    )(qkv, qkv, qkv, padded, hot, probs, dmixed, *[g.array for g in grads])
    return list(outs[:4]) + [[Grad(a, b + 1, t) for a, (_, b, t) in zip(outs[4:], plan)]]


def body(
    features,
    w1_in,
    w1_out,
    gain_ffn1,
    w_qkv,
    w_attn_out,
    rel_table,
    gain_attn,
    w_conv_in,
    w_depth,
    gain_depth,
    w_conv_out,
    gain_conv,
    w2_in,
    w2_out,
    gain_ffn2,
    gain_final,
    cotangent,
):
    local_frames, clip_count, width = features.shape
    rows = local_frames * clip_count
    f32, bf = jnp.float32, jnp.bfloat16
    s0 = features.reshape(rows, width)
    seed = cotangent.reshape(rows, width)
    vec = lambda g: g.astype(f32).reshape(1, width)
    g1, ga, gc, g2, gf = vec(gain_ffn1), vec(gain_attn), vec(gain_conv), vec(gain_ffn2), vec(gain_final)
    flat_qkv = w_qkv.reshape(width, -1)
    flat_conv = w_conv_in.reshape(width, -1)
    units = w1_in.shape[1]
    dp_count = lax.axis_size("dp")
    done = dp_count.bit_length() - 1
    pending = lambda items: [g for g in items if g.bit < done]
    chans = w_conv_out.shape[0]

    def swish_out(h, extra, outs):
        act, slope = silu_pair(h)
        outs[0][...] = act.astype(bf)
        outs[1][...] = slope.astype(bf)

    def plain_out(h, extra, outs):
        outs[0][...] = h.astype(outs[0].dtype)

    def glu_out(h, extra, outs):
        p0 = h[:, :chans]
        sig = jax.nn.sigmoid(h[:, chans:])
        glu = p0 * sig
        outs[0][...] = glu
        outs[1][...] = sig.astype(bf)
        outs[2][...] = (glu * (1.0 - sig)).astype(bf)

    def slope_out(h, extra, outs):
        outs[0][...] = (h * extra[0][...].astype(f32)).astype(bf)

    def first(branch, ins, vecs, outs, sums):
        return (unit_norm(ins[0].astype(f32))[0] * vecs[0]).astype(bf)

    def forward(scale):
        def run(branch, ins, vecs, outs, sums):
            fresh = ins[0].astype(f32) + scale * branch
            outs[0][...] = fresh
            sums[0][...] += fold8(branch * branch)
            return (unit_norm(fresh)[0] * vecs[0]).astype(bf)
        return run

    def turn(branch, ins, vecs, outs, sums):
        fresh = ins[0] + 0.5 * branch
        sums[0][...] += fold8(branch * branch)
        sums[1][...] += fold8(fresh * fresh)
        unit, inverse = unit_norm(fresh)
        outs[0][...] = unit * vecs[0]
        grad = ins[1].astype(f32)
        scaled = grad * vecs[0]
        mean_one = jnp.mean(scaled, -1, keepdims=True)
        mean_two = jnp.mean(scaled * unit, -1, keepdims=True)
        sums[2][...] += fold8(grad * unit)
        back = inverse * (scaled - mean_one - unit * mean_two)
        outs[1][...] = back
        return (0.5 * back).astype(bf)

    def backward(scale):
        def run(branch, ins, vecs, outs, sums):
            pull, grad_gain = norm_pull(branch, ins[1].astype(f32), vecs[0])
            fresh = ins[0] + pull
            outs[0][...] = fresh
            sums[0][...] += grad_gain
            return (scale * fresh).astype(bf)
        return run

    a1, act1, slope1, _ = stage(
        "ffn1_in", 0, rows, width, dp_count, enter=(w1_in, False, swish_out, (), ((units, bf), (units, bf))),
        junction=first, row_in=(s0,), vec_in=(g1,),
    )
    a2, qkv, s1, sq1, _ = stage(
        "ffn1_out", 1, rows, width, dp_count, leave=(act1, w1_out, False),
        enter=(flat_qkv, False, plain_out, (), ((flat_qkv.shape[1], bf),)),
        junction=forward(0.5), row_in=(s0,), vec_in=(ga,), row_out=(f32,), sums=1,
    )
    ext, hot, padded = rel_tables(rel_table)
    mixed, probs = attn_fwd(qkv, ext)
    a3, glu, sig, tail, s2, sq2, _ = stage(
        "attn_out", 2, rows, width, dp_count, leave=(mixed, w_attn_out, False),
        enter=(flat_conv, False, glu_out, (), ((chans, f32), (chans, bf), (chans, bf))),
        junction=forward(1.0), row_in=(s1,), vec_in=(gc,), row_out=(f32,), sums=1,
    )
    frames = glu.shape[0]
    taps = w_depth.astype(f32)
    tap_count = taps.shape[0]
    padded_glu = jnp.pad(glu, ((tap_count - 1, 0), (0, 0)))
    depth = jnp.zeros_like(glu)
    for k in range(tap_count):
        depth = depth + taps[k] * padded_glu[k : k + frames]
    average = lax.psum(jnp.sum(depth, -1, keepdims=True), "mp") / width
    centred = depth - average
    spread = lax.psum(jnp.sum(centred * centred, -1, keepdims=True), "mp") / width
    depth_inverse = lax.rsqrt(spread + epsilon)
    depth_unit = centred * depth_inverse
    depth_gain = gain_depth.astype(f32)
    act3, slope3 = silu_pair(depth_unit * depth_gain)
    act3 = act3.astype(bf)
    a4, act2, slope2, s3, sq3, _ = stage(
        "conv_out", 3, rows, width, dp_count, leave=(act3, w_conv_out, False),
        enter=(w2_in, False, swish_out, (), ((units, bf), (units, bf))),
        junction=forward(1.0), row_in=(s2,), vec_in=(g2,), row_out=(f32,), sums=1,
    )
    db4, dh2, output, grad4, sq4, sq5, dgf, _ = stage(
        "ffn2_out", 4, rows, width, dp_count, leave=(act2, w2_out, False),
        enter=(w2_out, True, slope_out, (slope2,), ((units, bf),)),
        junction=turn, row_in=(s3, seed), vec_in=(gf,), row_out=(f32, f32), sums=3,
    )
    db3, de3, grad3, dg2, (gw2_in, gw2_out) = stage(
        "ffn2_back", 5, rows, width, dp_count, leave=(dh2, w2_in, True),
        enter=(w_conv_out, True, plain_out, (), ((chans, f32),)), dws=((a4, dh2, "join", False), (db4, act2, "far", True)),
        junction=backward(1.0), row_in=(grad4, s3), vec_in=(g2,), row_out=(f32,), sums=1,
    )
    grad_gated = de3 * slope3
    grad_gain_depth = jnp.sum(grad_gated * depth_unit, 0)
    grad_unit = grad_gated * depth_gain
    first_sum, second_sum = lax.psum(
        (jnp.sum(grad_unit, -1, keepdims=True), jnp.sum(grad_unit * depth_unit, -1, keepdims=True)), "mp"
    )
    grad_depth = depth_inverse * (grad_unit - first_sum / width - depth_unit * second_sum / width)
    padded_grad = jnp.pad(grad_depth, ((0, tap_count - 1), (0, 0)))
    grad_glu = jnp.zeros_like(grad_depth)
    tap_grads = []
    for k in range(tap_count):
        start = tap_count - 1 - k
        grad_glu = grad_glu + taps[k] * padded_grad[start : start + frames]
        tap_grads.append(jnp.sum(grad_depth * padded_glu[k : k + frames], 0))
    grad_w_depth = jnp.stack(tap_grads, 0)
    dpaired = jnp.concatenate([grad_glu * sig.astype(f32), grad_glu * tail.astype(f32)], 1).astype(bf)
    db2, dmixed, grad2, dgc, (gconv_in, gconv_out, gw2_in, gw2_out) = stage(
        "conv_back", 6, rows, width, dp_count, leave=(dpaired, flat_conv, True),
        enter=(w_attn_out, True, plain_out, (), ((w_attn_out.shape[0], bf),)), dws=((a3, dpaired, "join", False), (db3, act3, "join", True)), grads=(gw2_in, gw2_out),
        junction=backward(1.0), row_in=(grad3, s2), vec_in=(gc,), row_out=(f32,), sums=1,
    )
    dq, dk, dv, dt, (gconv_in, gconv_out, gw2_in, gw2_out) = attn_bwd(
        qkv, padded, hot, probs, dmixed, [gconv_in, gconv_out, gw2_in, gw2_out], 9
    )
    dqkv = jnp.concatenate([dq, dk, dv], 1)
    db1, dh1, grad1, dga, (gqkv, gattn, gconv_in, gconv_out, gw2_in) = stage(
        "attn_back", 7, rows, width, dp_count, leave=(dqkv, flat_qkv, True),
        enter=(w1_out, True, slope_out, (slope1,), ((units, bf),)), dws=((a2, dqkv, "far", False), (db2, mixed, "far", True)), grads=(gconv_in, gconv_out, gw2_in),
        junction=backward(0.5), row_in=(grad2, s1), vec_in=(ga,), row_out=(f32,), sums=1,
    )
    early = [gqkv, gattn, gconv_in, gconv_out, gw2_in, gw2_out]
    waiting = pending(early)
    grad0, dg1, ends, small_rows, table, taps_end = stage(
        "ffn1_back", 8, rows, width, dp_count, leave=(dh1, w1_in, True),
        dws=((db1, act1, "far", True), (a1, dh1, "near", False)), grads=waiting,
        small=[dga, dgc, dg2, dgf, sq1, sq2, sq3, sq4, sq5, dt, grad_w_depth, grad_gain_depth[None]],
        junction=backward(1.0), row_in=(grad1, s0), vec_in=(g1,), row_out=(f32,), sums=1,
    )
    gw1_out, gw1_in = ends[:2]
    for item, end in zip(waiting, ends[2:]):
        item.array = end.array

    def finish(item):
        flip = item.turned and item.array.shape[0] * dp_count == width and (width // dp_count) % 128 != 0
        return item.array.T if flip else item.array

    rel = rel_table.shape[0]
    table_sum = table[:rel, :HEAD] + table[:rel, HEAD:]
    depth_sum, depth_gain_sum = taps_end[:-1], taps_end[-1]
    total_squares = jnp.sum(small_rows[5:10], -1)
    token_total = rows * lax.axis_size("mp") * lax.axis_size("dp")
    rms_stats = jnp.sqrt(total_squares / (token_total * width))
    whole = lambda x: x.reshape(local_frames, clip_count, width)
    return (
        whole(output),
        whole(grad0),
        finish(gw1_in),
        finish(gw1_out),
        small_rows[0],
        finish(gqkv).reshape(-1, 3, w_qkv.shape[2]),
        finish(gattn),
        table_sum,
        small_rows[1],
        finish(gconv_in).reshape(-1, 2, chans),
        depth_sum,
        depth_gain_sum,
        finish(gconv_out),
        small_rows[2],
        finish(gw2_in),
        finish(gw2_out),
        small_rows[3],
        small_rows[4],
        rms_stats,
    )


def solution(mesh):
    return jax.shard_map(
        body,
        mesh=mesh,
        in_specs=(
            P("mp", "dp", None),
            P(None, "mp"),
            P("mp", None),
            P(),
            P(None, None, "mp"),
            P("mp", None),
            P(),
            P(),
            P(None, None, "mp"),
            P(None, "mp"),
            P("mp"),
            P("mp", None),
            P(),
            P(None, "mp"),
            P("mp", None),
            P(),
            P(),
            P("mp", "dp", None),
        ),
        out_specs=(
            P("mp", "dp", None),
            P("mp", "dp", None),
            P("dp", "mp"),
            P("mp", "dp"),
            P(),
            P("dp", None, "mp"),
            P("mp", "dp"),
            P(),
            P(),
            P("dp", None, "mp"),
            P(None, "mp"),
            P("mp"),
            P("mp", "dp"),
            P(),
            P("dp", "mp"),
            P("mp", "dp"),
            P(),
            P(),
            P(),
        ),
        check_vma=False,
    )
```

time: 634 us -> 550 us (0.87)
  Pallas kernels: 286 us -> 407 us
  blocking collectives: 120 us -> 20.8 us
  waiting for transfers between devices: 72.2 us -> 0 us
  starting transfers between devices: 22.6 us -> 0 us
  other arithmetic: 52.4 us -> 39.1 us
    pallas_call x9, Pallas kernels: 238 us -> 354 us  [stage(): pl.pallas_call(kernel, in_specs=[vm] * len(ins), out_specs=[vm] * len(out...]
    psum x2 -> x0, blocking collectives: 99.6 us -> none  [the longest x1 61.9 us: body(): lax.psum((gains, grad_table, squares), ('dp', 'mp'))]
    ppermute x24 -> x0, waiting for transfers between devices: 72.2 us -> none  [halve_sum(): got = lax.ppermute(give, 'dp', [(i, i ^ step) for i in range(count)])]
    ppermute x24 -> x0, starting transfers between devices: 22.6 us -> none  [halve_sum(): got = lax.ppermute(give, 'dp', [(i, i ^ step) for i in range(count)])]
    unnamed x258 -> x198, local copies, waits for them, and re-layouts: 43.7 us -> 64.4 us
    convert_element_type x16 -> x0, other arithmetic: 16 us -> none  [halve_sum(): part = total.astype(jnp.bfloat16) if step < count else total]
    another operation x2, other arithmetic: 4.3 us -> 19.8 us
    squeeze x24 -> x0, local copies, waits for them, and re-layouts: 12.3 us -> none  [halve_sum(): give = lax.dynamic_index_in_dim(paired, 1 - bit, 1, keepdims=False)]
  transfers between devices with their start and end apart: 24 -> 0, of which waited for: 11 -> 0; matrix products, arithmetic and copies ran while one was open for 9% -> 0% of each run, Pallas kernels for 12% -> 0%
where the time goes in v3:
time: 550 us; the launch traced here: 541 us
  Pallas kernels  407 us (74%)
  local copies, waits for them, and re-layouts  72.4 us (13%)
  other arithmetic  39.1 us (7%)
  blocking collectives  20.8 us (4%)
    pallas_call x9, Pallas kernels, stage(): pl.pallas_call(kernel, in_specs=[vm] * len(ins), out_specs=[vm] * len(out...  354 us
    unnamed x198, local copies, waits for them, and re-layouts  64.4 us
    pallas_call x1, Pallas kernels, attn_bwd(): pl.pallas_call(functools.partial(bwd_kernel, plan), grid=(pairs, nb), in_...  32.3 us
    pallas_call x1, Pallas kernels, attn_fwd(): pl.pallas_call(fwd_kernel, grid=(pairs, nb), in_specs=[pl.BlockSpec((BQ,...  20.2 us
    another operation x2, other arithmetic  19.8 us

profile of v3, /device:TPU:0, one launch (start us, length us, event | category | flops | bytes accessed | tf_op | source)
XLA Modules:
  0.0 541.5 jit_solution(2493002787901181859)
XLA Ops:
  4.0 17.5 %ffn1_in.1 = (bf16[1024,1024]{1,0:T(8,128)(2,1)S(1)}, bf16[1024,1024]{1,0:T(8,128)(2,1)S(1)}, bf16[1024,1024]{1,0:T(8,128)(2,1)S(1)}) custom-call(bf16[1024,1024]{1,0:T(8,128)(2,1)S(1)} %copy-done.41, bf16[256,1024]{1,0:T(8,128)(2,1)S(1)} %bitcast.105, f32[1,1024]{1,0:T(1,128)S(1)} %bitcast.96), custom_call_target="tpu_custom_call" | custom-call | flops 4294967296 | bytes 60000000 | tf_op jit(solution)/shard_map/ffn1_in/pallas_call | solution.py:425
  27.2 2.1 copy-done.39
  31.9 28.8 %ffn1_out.1 = (bf16[1024,1024]{1,0:T(8,128)(2,1)S(1)}, bf16[1024,768]{1,0:T(8,128)(2,1)S(1)}, f32[256,1024]{1,0:T(8,128)S(1)}, f32[8,1024]{1,0:T(8,128)S(1)}) custom-call(bf16[1024,1024]{1,0:T(8,128)(2,1)S(1)} %copy-done.65, bf16[1024,1024]{1,0:T(8,128)(2,1)S(1)} %copy-done.39, bf16[1024,768]{1,0:T(8,128)(2,1)S(1)} %copy.44.refs_2_.refs_1_, ...), custom_call_target="tpu_custom_call" | custom-call | flops 3758096384 | bytes 60000000 | tf_op jit(solution)/shard_map/ffn1_out/pallas_call | solution.py:425
  63.5 20.2 %attn_fwd.1 = (bf16[1024,256]{1,0:T(8,128)(2,1)S(1)}, bf16[2,2048,1024]{2,1,0:T(8,128)(2,1)S(1)}) custom-call(bf16[1024,768]{1,0:T(8,128)(2,1)S(1)} %get-tuple-element.88.q_ref.k_ref.v_ref.refs_0_.refs_1_.refs_2_, bf16[1024,768]{1,0:T(8,128)(2,1)S(1)} %get-tuple-element.88.q_ref.k_ref.v_ref.refs_0_.refs_1_.refs_2_, ...), custom_call_target="tpu_custom_call" | custom-call | tf_op jit(solution)/shard_map/attn_fwd/pallas_call | solution.py:578
  83.8 3.2 copy-done.34
  89.0 28.5 %attn_out.1 = (bf16[1024,1024]{1,0:T(8,128)(2,1)S(1)}, f32[1024,256]{1,0:T(8,128)S(1)}, bf16[1024,256]{1,0:T(8,128)(2,1)S(1)}, bf16[1024,256]{1,0:T(8,128)(2,1)S...) custom-call(bf16[1024,256]{1,0:T(8,128)(2,1)S(1)} %get-tuple-element.89.refs_0_.refs_10_, ...), custom_call_target="tpu_custom_call" | custom-call | flops 2147483648 | bytes 60000000 | tf_op jit(solution)/shard_map/attn_out/pallas_call | solution.py:425
  121.4 5.0 fusion.24
  126.4 7.7 %psum.28 = f32[1024,1]{0,1:T(1,128)S(1)} all-reduce(f32[1024,1]{0,1:T(1,128)S(1)} %bitcast.119), channel_id=1, replica_groups=mesh['dp'=8,'mp'=4] {'mp'}, use_global_device_ids=true, to_apply=%region_1.2 | all-reduce | flops 1024 | bytes 8192 | tf_op jit(solution)/shard_map/psum | solution.py:748
  135.8 5.9 %psum.29 = f32[1024,1]{0,1:T(1,128)S(1)} all-reduce(f32[1024,1]{0,1:T(1,128)S(1)} %bitcast.120), channel_id=1, replica_groups=mesh['dp'=8,'mp'=4] {'mp'}, use_global_device_ids=true, to_apply=%region_3.4 | all-reduce | flops 1024 | bytes 8192 | tf_op jit(solution)/shard_map/psum | solution.py:750
  146.1 28.3 %conv_out.1 = (bf16[1024,1024]{1,0:T(8,128)(2,1)S(1)}, bf16[1024,1024]{1,0:T(8,128)(2,1)S(1)}, bf16[1024,1024]{1,0:T(8,128)(2,1)S(1)}, f32[256,1024]{1,0:T(8,128)S(1)}, f32[8,1024]{1,0:T(8,128)S(1)}) custom-call(bf16[1024,256]{1,0:T(8,128)(2,1)S(1)} %fusion.21.refs_0_.refs_9_, bf16[256,1024]{1,0:T(8,128)(2,1)S(1)} %copy-done.46, ...), custom_call_target="tpu_custom_call" | custom-call | flops 4831838208 | bytes 60000000 | tf_op jit(solution)/shard_map/conv_out/pallas_call | solution.py:425
  175.1 28.9 %ffn2_out.1 = (bf16[1024,1024]{1,0:T(8,128)(2,1)S(1)}, bf16[1024,1024]{1,0:T(8,128)(2,1)S(1)}, f32[256,1024]{1,0:T(8,128)S(1)}, f32[256,1024]{1,0:T(8,128)S(1)},...) custom-call(bf16[1024,1024]{1,0:T(8,128)(2,1)S(1)} %get-tuple-element.93.refs_0_.refs_9_, ...), custom_call_target="tpu_custom_call" | custom-call | flops 4294967296 | bytes 60000000 | tf_op jit(solution)/shard_map/ffn2_out/pallas_call | solution.py:425
  205.0 30.5 %ffn2_back.1 = (bf16[1024,1024]{1,0:T(8,128)(2,1)S(1)}, f32[1024,256]{1,0:T(8,128)S(1)}, f32[256,1024]{1,0:T(8,128)S(1)}, f32[8,1024]{1,0:T(8,128)S(1)}, bf16[4,...) custom-call(bf16[1024,1024]{1,0:T(8,128)(2,1)S(1)} %get-tuple-element.98.refs_0_.refs_7_, ...), custom_call_target="tpu_custom_call" | custom-call | flops 6979321856 | bytes 60000000 | tf_op jit(solution)/shard_map/ffn2_back/pallas_call | solution.py:425
  238.5 2.0 multiply_reduce_fusion
  240.5 7.2 %all-reduce.3 = (f32[1024]{0:T(1024)S(1)}, f32[1024,1]{0,1:T(1,128)S(1)}) all-reduce(f32[1024]{0:T(1024)S(1)} %get-tuple-element.194, f32[1024,1]{0,1:T(1,128)S(1)} %bitcast.118), channel_id=1, replica_groups=mesh['dp'=8,'mp'=4] {'mp'}, use_global_device_ids=true, to_apply=%region_7.8 | all-reduce | flops 2048 | bytes 16384 | tf_op jit(solution)/shard_map/psum | solution.py:774
  247.7 4.6 multiply_reduce_fusion.1
  254.1 2.5 stack.127.refs_23_
  256.5 18.5 %multiply_convert_fusion.1 = (bf16[1024,256]{1,0:T(8,128)(2,1)S(1)}, f32[1024,256]{1,0:T(8,128)S(1)}) fusion(bf16[1024,256]{1,0:T(8,128)(2,1)} %copy-done.21, f32[1024,256]{1,0:T(8,128)} %copy-done.82, f32[256]{0:T(256)S(1)} %bitcast.183, f32[256]{0:T(256)S(1)} %bitcast.181, f32[256]{0:T(256)S(1)} %bitcast.179, f32[256]{0:T(256)S(1)} %bitcast.177, ...), kind=kLoop, calls=%fused_computation.36 | loop fusion | flops 16777216 | bytes 3177472 | tf_op jit(solution)/shard_map/convert.6
  282.3 29.8 %conv_back.1 = (bf16[1024,1024]{1,0:T(8,128)(2,1)S(1)}, bf16[1024,256]{1,0:T(8,128)(2,1)S(1)}, f32[256,1024]{1,0:T(8,128)S(1)}, f32[8,1024]{1,0:T(8,128)S(1)}, b...) custom-call(bf16[1024,512]{1,0:T(8,128)(2,1)S(1)} %pad_maximum_fusio, ...), custom_call_target="tpu_custom_call" | custom-call | flops 3221225472 | bytes 60000000 | tf_op jit(solution)/shard_map/conv_back/pallas_call | solution.py:425
  313.8 3.4 copy-done.35
  317.2 32.3 %attn_bwd.1 = (bf16[1024,256]{1,0:T(8,128)(2,1)S(1)}, bf16[1024,256]{1,0:T(8,128)(2,1)S(1)}, bf16[1024,256]{1,0:T(8,128)(2,1)S(1)}, f32[128,128]{1,0:T(8,128)S(1...) custom-call(bf16[1024,768]{1,0:T(8,128)(2,1)S(1)} %get-tuple-element, ...), custom_call_target="tpu_custom_call" | custom-call | flops 5368709120 | bytes 20000000 | tf_op jit(solution)/shard_map/attn_bwd/pallas_call | solution.py:608
  354.6 31.1 %attn_back.1 = (bf16[1024,1024]{1,0:T(8,128)(2,1)S(1)}, bf16[1024,1024]{1,0:T(8,128)(2,1)S(1)}, f32[256,1024]{1,0:T(8,128)S(1)}, f32[8,1024]{1,0:T(8,128)S(1)}, ...) custom-call(bf16[1024,768]{1,0:T(8,128)(2,1)S(1)} %pad_maximum_fusio, ...), custom_call_target="tpu_custom_call" | custom-call | flops 5905580032 | bytes 60000000 | tf_op jit(solution)/shard_map/attn_back/pallas_call | solution.py:425
  391.6 131.0 %ffn1_back.1 = (f32[256,1024]{1,0:T(8,128)S(1)}, f32[8,1024]{1,0:T(8,128)}, f32[1024,128]{1,0:T(8,128)S(1)}, f32[128,1024]{1,0:T(8,128)S(1)}, f32[128,768]{1,0:T...) custom-call(bf16[1024,1024]{1,0:T(8,128)(2,1)S(1)} %copy-done.60, ...), custom_call_target="tpu_custom_call" | custom-call | flops 6442450944 | bytes 60000000 | tf_op jit(solution)/shard_map/ffn1_back/pallas_call | solution.py:425
  522.7 2.0 copy.49
  533.9 2.0 copy.48
  (224 shorter events, 66.5 us)
Async XLA Ops:
  27.1 33.6 %copy-start.8 = (bf16[1024,768]{1,0:T(8,128)(2,1)}, bf16[1024,768]{1,0:T(8,128)(2,1)S(1)}, u32[]{:S(2)}) copy-start(bf16[1024,768]{1,0:T(8,128)(2,1)S(1)} %copy.44.refs_2_.refs_1_) | copy-start | bytes 4718596
  31.9 31.1 %copy-start.86 = (bf16[73,64]{0,1:T(8,128)(2,1)S(1)}, bf16[73,64]{0,1:T(8,128)(2,1)}, u32[]{:S(2)}) copy-start(bf16[73,64]{0,1:T(8,128)(2,1)} %param.24) | copy-start | bytes 28036
  87.0 30.4 %copy-start.51 = (bf16[1024,256]{1,0:T(8,128)(2,1)}, bf16[1024,256]{1,0:T(8,128)(2,1)S(1)}, u32[]{:S(2)}) copy-start(bf16[1024,256]{1,0:T(8,128)(2,1)S(1)} %get-tuple-element.89.refs_0_.refs_10_) | copy-start | bytes 1572868
  87.2 30.2 %copy-start = (bf16[128,8,2,256]{3,1,2,0:T(8,128)(2,1)}, bf16[128,8,2,256]{3,1,2,0:T(8,128)(2,1)S(1)}, u32[]{:S(2)}) copy-start(bf16[128,8,2,256]{3,1,2,0:T(8,128)(2,1)S(1)} %copy.52) | copy-start | bytes 3145732
  89.0 32.4 %copy-start.85 = (bf16[31,256]{1,0:T(8,128)(2,1)S(1)}, bf16[31,256]{1,0:T(8,128)(2,1)}, u32[]{:S(2)}) copy-start(bf16[31,256]{1,0:T(8,128)(2,1)} %param.27) | copy-start | bytes 47620
  146.1 28.9 %copy-start.45 = (bf16[256,1,1024]{2,0,1:T(8,128)(2,1)S(1)}, bf16[256,1,1024]{2,0,1:T(8,128)(2,1)}, u32[]{:S(2)}) copy-start(bf16[256,1,1024]{2,0,1:T(8,128)(2,1)} %param.35) | copy-start | bytes 1572868
  175.0 30.0 %copy-start.38 = (bf16[1024,1024]{1,0:T(8,128)(2,1)S(1)}, bf16[1024,1024]{1,0:T(8,128)(2,1)}, u32[]{:S(2)}) copy-start(bf16[1024,1024]{1,0:T(8,128)(2,1)} %refs_1_.10) | copy-start | bytes 6291460
  175.1 30.0 %copy-start.47 = (bf16[256,1024]{1,0:T(8,128)(2,1)S(1)}, bf16[256,1024]{1,0:T(8,128)(2,1)}, u32[]{:S(2)}) copy-start(bf16[256,1024]{1,0:T(8,128)(2,1)} %refs_2_.7) | copy-start | bytes 1572868
  205.0 30.6 %copy-start.69 = (f32[8,1024]{1,0:T(8,128)}, f32[8,1024]{1,0:T(8,128)S(1)}, u32[]{:S(2)}) copy-start(f32[8,1024]{1,0:T(8,128)S(1)} %get-tuple-element.140.refs_20_) | copy-start | bytes 98308
  205.0 30.6 %copy-start.71 = (f32[8,1024]{1,0:T(8,128)}, f32[8,1024]{1,0:T(8,128)S(1)}, u32[]{:S(2)}) copy-start(f32[8,1024]{1,0:T(8,128)S(1)} %get-tuple-element.141.refs_21_) | copy-start | bytes 98308
  205.0 30.6 %copy-start.73 = (f32[8,1024]{1,0:T(8,128)}, f32[8,1024]{1,0:T(8,128)S(1)}, u32[]{:S(2)}) copy-start(f32[8,1024]{1,0:T(8,128)S(1)} %get-tuple-element.136.refs_16_) | copy-start | bytes 98308
  205.0 33.5 %copy-start.81 = (f32[1024,256]{1,0:T(8,128)S(1)}, f32[1024,256]{1,0:T(8,128)}, u32[]{:S(2)}) copy-start(f32[1024,256]{1,0:T(8,128)} %get-tuple-element.234) | copy-start | bytes 3145732
  317.2 32.5 %copy-start.40 = (bf16[1024,1024]{1,0:T(8,128)(2,1)S(1)}, bf16[1024,1024]{1,0:T(8,128)(2,1)}, u32[]{:S(2)}) copy-start(bf16[1024,1024]{1,0:T(8,128)(2,1)} %refs_2_.9) | copy-start | bytes 6291460
  317.2 32.5 %copy-start.44 = (bf16[1024,1024]{1,0:T(8,128)(2,1)S(1)}, bf16[1024,1024]{1,0:T(8,128)(2,1)}, u32[]{:S(2)}) copy-start(bf16[1024,1024]{1,0:T(8,128)(2,1)} %copy-done.43) | copy-start | bytes 6291460
  354.5 33.8 %copy-start.33 = (f32[31,256]{1,0:T(8,128)S(1)}, f32[31,256]{1,0:T(8,128)}, u32[]{:S(2)}) copy-start(f32[31,256]{1,0:T(8,128)} %stack.127.refs_23_) | copy-start | bytes 95236
  354.5 33.8 %copy-start.42 = (bf16[1024,1024]{1,0:T(8,128)(2,1)S(1)}, bf16[1024,1024]{1,0:T(8,128)(2,1)}, u32[]{:S(2)}) copy-start(bf16[1024,1024]{1,0:T(8,128)(2,1)} %refs_1_.11) | copy-start | bytes 6291460
  354.5 33.8 %copy-start.50 = (bf16[256,1,1024]{2,0,1:T(8,128)(2,1)S(1)}, bf16[256,1,1024]{2,0,1:T(8,128)(2,1)}, u32[]{:S(2)}) copy-start(bf16[256,1,1024]{2,0,1:T(8,128)(2,1)} %param.18) | copy-start | bytes 1572868
  354.5 33.8 %copy-start.68 = (f32[8,1024]{1,0:T(8,128)S(1)}, f32[8,1024]{1,0:T(8,128)}, u32[]{:S(2)}) copy-start(f32[8,1024]{1,0:T(8,128)} %copy-done.67) | copy-start | bytes 98308
  354.5 33.8 %copy-start.70 = (f32[8,1024]{1,0:T(8,128)S(1)}, f32[8,1024]{1,0:T(8,128)}, u32[]{:S(2)}) copy-start(f32[8,1024]{1,0:T(8,128)} %copy-done.69) | copy-start | bytes 98308
  354.6 33.8 %copy-start.72 = (f32[8,1024]{1,0:T(8,128)S(1)}, f32[8,1024]{1,0:T(8,128)}, u32[]{:S(2)}) copy-start(f32[8,1024]{1,0:T(8,128)} %copy-done.71) | copy-start | bytes 98308
  354.6 33.8 %copy-start.74 = (f32[8,1024]{1,0:T(8,128)S(1)}, f32[8,1024]{1,0:T(8,128)}, u32[]{:S(2)}) copy-start(f32[8,1024]{1,0:T(8,128)} %copy-done.73) | copy-start | bytes 98308
  354.6 33.8 %copy-start.76 = (f32[8,1024]{1,0:T(8,128)S(1)}, f32[8,1024]{1,0:T(8,128)}, u32[]{:S(2)}) copy-start(f32[8,1024]{1,0:T(8,128)} %copy-done.75) | copy-start | bytes 98308
  354.6 33.8 %copy-start.78 = (f32[8,1024]{1,0:T(8,128)S(1)}, f32[8,1024]{1,0:T(8,128)}, u32[]{:S(2)}) copy-start(f32[8,1024]{1,0:T(8,128)} %copy-done.77) | copy-start | bytes 98308
  354.6 33.8 %copy-start.80 = (f32[8,1024]{1,0:T(8,128)S(1)}, f32[8,1024]{1,0:T(8,128)}, u32[]{:S(2)}) copy-start(f32[8,1024]{1,0:T(8,128)} %copy-done.79) | copy-start | bytes 98308
  (68 other events, 322.5 us)

commit v4 on v3

v4 whole, which is shorter than its diff:
```python
import functools

import jax
import jax.numpy as jnp
from jax import lax
from jax.experimental import pallas as pl
from jax.experimental.pallas import tpu as pltpu
from jax.sharding import PartitionSpec as P

HEAD = 64
REL_LEFT = 64
REL_RIGHT = 8
BQ = 128
WIN = 4 * BQ


epsilon = 1e-05


def nt(a, b):
    return lax.dot_general(a, b, (((1,), (1,)), ((), ())), preferred_element_type=jnp.float32)
def nn(a, b):
    return lax.dot_general(a, b, (((1,), (0,)), ((), ())), preferred_element_type=jnp.float32)
def tn(a, b):
    return lax.dot_general(a, b, (((0,), (0,)), ((), ())), preferred_element_type=jnp.float32)

MESH = pl.DeviceIdType.MESH
CHUNKS = 4
PIECE = 256
VMEM_LIMIT = 58 << 20


def silu_pair(h):
    sig = jax.nn.sigmoid(h)
    act = h * sig
    return act, sig + act * (1.0 - sig)


def unit_norm(s):
    centred = s - jnp.mean(s, -1, keepdims=True)
    inverse = lax.rsqrt(jnp.mean(centred * centred, -1, keepdims=True) + epsilon)
    return centred * inverse, inverse


def fold8(x):
    return jnp.sum(x.reshape(x.shape[0] // 8, 8, x.shape[1]), 0)


def norm_pull(grad, s, gain):
    unit, inverse = unit_norm(s)
    scaled = grad * gain
    first = jnp.mean(scaled, -1, keepdims=True)
    second = jnp.mean(scaled * unit, -1, keepdims=True)
    return inverse * (scaled - first - unit * second), fold8(grad * unit)


def in_hbm():
    return pl.BlockSpec(memory_space=pltpu.HBM)


class Grad:
    def __init__(self, array, bit, turned):
        self.array, self.bit, self.turned = array, bit, turned


def halved(shape, turned):
    pieces, pairs, _, block, cols = shape
    if pairs > 1:
        return jax.ShapeDtypeStruct((pieces, pairs // 2, 2, block, cols), jnp.bfloat16)
    if turned and block % 128 == 0:
        return jax.ShapeDtypeStruct((pieces * cols, block), jnp.float32)
    return jax.ShapeDtypeStruct((block, pieces * cols), jnp.float32)


def arriving(shape):
    return pltpu.VMEM((shape[0], shape[1]) + tuple(shape[3:]), jnp.bfloat16)


def place(dp, bit):
    own = (dp // 2**bit) % 2
    return own, dp + 2**bit * (1 - 2 * own)


def halving_copy(src, landing, piece, bit, send, recv, slot):
    dp, mp = lax.axis_index("dp"), lax.axis_index("mp")
    own, partner = place(dp, bit)
    return pltpu.make_async_remote_copy(
        src.at[piece, :, 1 - own], landing.at[piece], send.at[slot], recv.at[slot],
        device_id=(partner, mp), device_id_type=MESH,
    )


def halving_keep(src, kept, bit, sem):
    own, _ = place(lax.axis_index("dp"), bit)
    return pltpu.make_async_copy(src.at[:, :, own], kept, sem)


def region(ref, piece, cols, turned):
    if len(ref.shape) > 2:
        return ref.at[piece]
    at = pl.ds(piece * cols, cols)
    return ref.at[at, :] if turned else ref.at[:, at]


def halving_add(held, landing, out, piece, turned):
    pairs, block, cols = landing.shape[1:]
    f32 = jnp.float32
    if pairs == 1:
        total = held(piece, 0).astype(f32) + landing[piece, 0].astype(f32)
        turned = turned and block % 128 == 0
        region(out, piece, cols, turned)[...] = total.T if turned else total
        return

    def add(j, c):
        total = held(piece, j).astype(f32) + landing[piece, j].astype(f32)
        out[piece, j // 2, j % 2] = total.astype(jnp.bfloat16)
        return c

    lax.fori_loop(0, pairs, add, 0)


def greet(targets):
    barrier = pltpu.get_barrier_semaphore()
    for to in targets:
        pl.semaphore_signal(barrier, inc=1, device_id=to, device_id_type=MESH)
    return lambda: pl.semaphore_wait(barrier, len(targets))


def stage(name, cid, rows, width, count, gains, *, leave=None, enter=None, dws=(), grads=(), small=None, junction, row_in=(), row_out=(), sums=0):
    chunk = rows // CHUNKS
    frames = rows * 4
    bits_all = count.bit_length() - 1
    last = small is not None
    f32, bf = jnp.float32, jnp.bfloat16
    ins, vm_ins, out_shape, scratch = [], [], [], []
    known = {}

    def add_in(array, direct=False):
        if direct:
            ins.append(array)
            vm_ins.append(None)
            return len(ins) - 1
        if id(array) not in known:
            known[id(array)] = len(ins)
            ins.append(array)
            vm_ins.append(pltpu.VMEM(array.shape, array.dtype))
        return known[id(array)]

    out_slots = [0]

    def add_out(shape, dtype, slots):
        out_shape.append(jax.ShapeDtypeStruct(shape, dtype))
        first = out_slots[0]
        out_slots[0] += slots
        return len(out_shape) - 1, first

    def add_scratch(item):
        scratch.append(item)
        return len(scratch) - 1

    if leave:
        x_i, wl_i = add_in(leave[0]), add_in(leave[1])
        leave_s = [add_scratch(pltpu.VMEM((rows, width), f32)) for _ in range(2)]
        leave_s += [add_scratch(pltpu.VMEM((rows, width), bf)) for _ in range(6)]
        wl_s = add_scratch(pltpu.VMEM(leave[1].shape[::-1], bf)) if leave[2] else None
    dw_in = [(add_in(d[0]), add_in(d[1])) for d in dws if d[2] != "join"]
    gains_i = add_in(gains)
    row_i = [add_in(r) for r in row_in]
    dw_join = [(add_in(d[0]), add_in(d[1])) for d in dws if d[2] == "join"]
    if enter:
        we_i = add_in(enter[0])
        extra_i = [add_in(e) for e in enter[3]]
        we_s = add_scratch(pltpu.VMEM(enter[0].shape[::-1], bf)) if enter[1] else None
        all_o = add_out((frames, width), bf, 4 * CHUNKS)
        e_o = [add_out((frames, c), d, 4 * CHUNKS) for c, d in enter[4]]
    r_o = [add_out((rows, width), d, CHUNKS) for d in row_out]
    s_o = [add_out((8, width), f32, 1) for _ in range(sums)]
    fixed_out = len(out_shape)
    plan, join_o = [], []
    for lhs, rhs, where, turned, deep in dws:
        shape = (rhs.shape[1] // PIECE, count // 2, 2, width // count, PIECE)
        if where == "join":
            join_o.append(add_out(shape, bf, shape[0]))
        else:
            plan.append((shape, 0, turned, bits_all if last else min(deep, bits_all), add_scratch(pltpu.VMEM(shape, bf)), None, None))
    first_grad = len(plan)
    for g in grads:
        shape = g.array.shape
        plan.append((shape, g.bit, g.turned, bits_all if last else g.bit + 1, None, add_in(g.array, True), add_scratch(arriving(shape))))
    chains = []
    slots = 0
    for shape, bit, turned, end, src_s, src_i, keep_s in plan:
        links = []
        pieces = shape[0]
        for b in range(bit, end):
            nxt = halved(shape, turned)
            final = b == end - 1
            land_s = add_scratch(arriving(shape))
            if final:
                links.append((b, slots, land_s, None, add_out(nxt.shape, nxt.dtype, pieces)))
            else:
                links.append((b, slots, land_s, add_scratch(pltpu.VMEM(nxt.shape, nxt.dtype)), None))
            slots += pieces
            shape = nxt.shape
        chains.append((pieces, turned, src_s, src_i, keep_s, links))
    if last:
        small_i = [add_in(s) for s in small]
        small_shapes = [(16, width), small[-2].shape, small[-1].shape]
        small_o = [add_out(s, f32, 1) for s in small_shapes]
        hops = bits_all + 2
        land_small = [add_scratch(pltpu.VMEM((hops,) + s, f32)) for s in small_shapes]
        small_sems = [add_scratch(pltpu.SemaphoreType.DMA((3, hops))) for _ in range(2)]
    if slots:
        grad_sems = [add_scratch(pltpu.SemaphoreType.DMA((slots,))) for _ in range(2)]
    ring_sems = [add_scratch(pltpu.SemaphoreType.DMA((6, CHUNKS))) for _ in range(2)]
    load_sem = add_scratch(pltpu.SemaphoreType.DMA((len(ins),)))
    store_sem = add_scratch(pltpu.SemaphoreType.DMA((out_slots[0],)))
    n_in, n_out, n_scratch = len(ins), len(out_shape), len(scratch)
    vm_at = {}
    for i, item in enumerate(vm_ins):
        if item is not None:
            vm_at[i] = add_scratch(item)
    vo_at = [add_scratch(pltpu.VMEM(o.shape, o.dtype)) for o in out_shape]

    def kernel(*refs):
        hbm_in, hbm_out, t = refs[:n_in], refs[n_in : n_in + n_out], refs[n_in + n_out :]
        vin = lambda i: t[vm_at[i]]
        vout = lambda i: t[vo_at[i]]
        load = lambda i: pltpu.make_async_copy(hbm_in[i], vin(i), t[load_sem].at[i])
        waited = set()

        def need(*items):
            for i in items:
                if i not in waited:
                    waited.add(i)
                    load(i).wait()

        dp, me = lax.axis_index("dp"), lax.axis_index("mp")
        core, chip = me % 2, me // 2
        sib = chip * 2 + 1 - core
        far = (1 - chip) * 2 + core
        diag = (1 - chip) * 2 + 1 - core
        bits = sorted({link[0] for ch in chains for link in ch[5]})
        meet = greet([(dp, sib), (dp, far)] + [(place(dp, b)[1], me) for b in bits])
        for i in range(n_in):
            if i in vm_at:
                load(i).start()

        def part(ref, block, k):
            return ref.at[pl.ds(pl.multiple_of(block * rows + k * chunk, chunk), chunk)]

        def store_rows(o, block, k):
            i, first = o
            return pltpu.make_async_copy(part(vout(i), block, k), part(hbm_out[i], block, k), t[store_sem].at[first + block * CHUNKS + k])

        def store_whole(o):
            i, first = o
            return pltpu.make_async_copy(vout(i), hbm_out[i], t[store_sem].at[first])

        def store_piece(o, piece, cols, turned):
            i, first = o
            return pltpu.make_async_copy(
                region(vout(i), piece, cols, turned), region(hbm_out[i], piece, cols, turned), t[store_sem].at[first + piece]
            )

        def copy(kind, k, src, dst, to):
            return pltpu.make_async_remote_copy(
                src, dst, t[ring_sems[0]].at[kind, k], t[ring_sems[1]].at[kind, k], device_id=(dp, to), device_id_type=MESH
            )

        if leave:
            px, own, sb, sr, xs, xr, ob, orv = [t[s] for s in leave_s]
            x_ref = vin(x_i)
            wl_ref = t[wl_s] if leave[2] else vin(wl_i)
        if enter:
            all_ref = vout(all_o[0])
            we_ref = t[we_s] if enter[1] else vin(we_i)
        pair_send = lambda k: copy(0, k, part(sb, 0, k), part(sr, 0, k), sib)
        far_send = lambda k: copy(1, k, part(xs, 0, k), part(xr, 0, k), far)
        own_send = lambda k: copy(2, k, part(ob, 0, k), part(orv, 0, k), sib)
        all_far = lambda k: copy(3, k, part(all_ref, me, k), part(all_ref, me, k), far)
        all_sib = lambda k: copy(4, k, part(all_ref, me, k), part(all_ref, me, k), sib)
        all_fwd = lambda k: copy(5, k, part(all_ref, far, k), part(all_ref, far, k), sib)
        got_far = lambda k: copy(3, k, part(all_ref, far, k), part(all_ref, far, k), far)
        got_sib = lambda k: copy(4, k, part(all_ref, sib, k), part(all_ref, sib, k), sib)
        got_diag = lambda k: copy(5, k, part(all_ref, diag, k), part(all_ref, diag, k), sib)

        def source(c, step):
            pieces, turned, src_s, src_i, keep_s, links = chains[c]
            if step:
                return t[links[step - 1][3]]
            return t[src_s] if src_s is not None else hbm_in[src_i]

        def hop(c, step, piece):
            b, slot, land_s, _, _ = chains[c][5][step]
            return halving_copy(source(c, step), t[land_s], piece, b, t[grad_sems[0]], t[grad_sems[1]], slot + piece)

        def keep(c):
            return halving_keep(hbm_in[chains[c][3]], t[chains[c][4]], chains[c][5][0][0], t[load_sem].at[chains[c][3]])

        kept = set()

        def settle(c, step, piece):
            pieces, turned, src_s, src_i, keep_s, links = chains[c]
            b, slot, land_s, out_s, out_o = links[step]
            hop(c, step, piece).wait_recv()
            if step == 0 and src_s is None:
                if c not in kept:
                    kept.add(c)
                    keep(c).wait()
                held = lambda p, j: t[keep_s][p, j]
            else:
                own_bit, _ = place(dp, b)
                src = source(c, step)
                held = lambda p, j: src[p, j, own_bit]
            landing = t[land_s]
            out = t[out_s] if out_o is None else vout(out_o[0])
            halving_add(held, landing, out, piece, turned)
            if out_o is not None:
                store_piece(out_o, piece, PIECE, turned and landing.shape[2] % 128 == 0).start()

        for c in range(first_grad, len(chains)):
            keep(c).start()
        meet()
        for c in range(first_grad, len(chains)):
            for p in range(chains[c][0]):
                hop(c, 0, p).start()
        for o in s_o:
            vout(o[0])[...] = jnp.zeros((8, width), f32)

        def fill(k, where):
            n_far, n_join = 0, 0
            for lhs, rhs, at_loop, turned, deep in dws:
                if at_loop == "join":
                    (a, b), o, c = dw_join[n_join], join_o[n_join], None
                    n_join += 1
                else:
                    (a, b), c = dw_in[n_far], n_far
                    n_far += 1
                if at_loop != where:
                    continue
                dw = vout(o[0]) if c is None else t[chains[c][2]]

                @pl.when(k < dw.shape[0])
                def _(a=a, b=b, dw=dw, c=c, o=o if c is None else None):
                    g = tn(vin(a)[...], vin(b)[:, pl.ds(pl.multiple_of(k * PIECE, PIECE), PIECE)])
                    dw[k] = g.astype(bf).reshape(dw.shape[1:])
                    if c is None:
                        store_piece(o, k, PIECE, False).start()
                    else:
                        hop(c, 0, k).start()

        if leave:
            need(x_i, wl_i)
            if leave[2]:
                wl_ref[...] = vin(wl_i)[...].T
            for a, b in dw_in:
                need(a, b)

            def two(k, block_a, block_b):
                lhs = jnp.concatenate([part(x_ref, block_a, k)[...], part(x_ref, block_b, k)[...]], 0)
                return nn(lhs, wl_ref[...])

            def push(k):
                pair_send(k).wait_recv()
                part(xs, 0, k)[...] = (part(px, 0, k)[...] + part(sr, 0, k)[...].astype(f32)).astype(bf)
                far_send(k).start()

            def out_far(k, c):
                p = two(k, far, diag)
                part(px, 0, k)[...] = p[:chunk]
                part(sb, 0, k)[...] = p[chunk:].astype(bf)
                pair_send(k).start()

                @pl.when(k > 0)
                def _():
                    push(k - 1)

                fill(k, "far")
                return c

            lax.fori_loop(0, CHUNKS, out_far, 0)

            def out_near(k, c):
                p = two(k, me, sib)
                part(own, 0, k)[...] = p[:chunk]
                part(ob, 0, k)[...] = p[chunk:].astype(bf)
                own_send(k).start()

                @pl.when(k == 0)
                def _():
                    push(CHUNKS - 1)

                fill(k, "near")
                return c

            lax.fori_loop(0, CHUNKS, out_near, 0)
        need(gains_i, *row_i)
        for a, b in dw_join:
            need(a, b)
        if enter and enter[1]:
            need(we_i)
            we_ref[...] = vin(we_i)[...].T

        def join(k, c):
            fill(k, "join")
            branch = None
            if leave:
                own_send(k).wait_recv()
                far_send(k).wait_recv()
                branch = part(own, 0, k)[...] + part(orv, 0, k)[...].astype(f32) + part(xr, 0, k)[...].astype(f32)
            fresh = junction(
                branch, [part(vin(r), 0, k)[...] for r in row_i], vin(gains_i), [part(vout(o[0]), 0, k) for o in r_o], [vout(o[0]) for o in s_o]
            )
            if enter:
                part(all_ref, me, k)[...] = fresh
                all_far(k).start()
                all_sib(k).start()
            for o in r_o:
                store_rows(o, 0, k).start()
            return c

        lax.fori_loop(0, CHUNKS, join, 0)
        for o in s_o:
            store_whole(o).start()

        lead = [c for c in range(first_grad) if len(chains[c][5]) == 2] if enter else []
        if enter:
            need(we_i, *extra_i)

            def work(k, block_a, block_b):
                lhs = jnp.concatenate([part(all_ref, block_a, k)[...], part(all_ref, block_b, k)[...]], 0)
                h = nn(lhs, we_ref[...])
                for i, block in enumerate((block_a, block_b)):
                    view = lambda ref: part(ref, block, k)
                    enter[2](h[i * chunk : (i + 1) * chunk], [view(vin(r))[...] for r in extra_i], [view(vout(o[0])) for o in e_o])
                    for o in [all_o] + e_o:
                        store_rows(o, block, k).start()

            def gather(k, c):
                got_sib(k).wait_recv()
                work(k, me, sib)
                got_far(k).wait_recv()
                all_fwd(k).start()
                got_diag(k).wait_recv()
                work(k, far, diag)
                if lead:

                    @pl.when(k == CHUNKS - 2)
                    def _():
                        for ch in lead:
                            for p in range(chains[ch][0]):
                                settle(ch, 0, p)
                                hop(ch, 1, p).start()

                return c

            lax.fori_loop(0, CHUNKS, gather, 0)

        if last:
            need(*small_i)
            *vectors, table, taps = [vin(i) for i in small_i]
            rows_ref, table_ref, taps_ref = [vout(o[0]) for o in small_o]
            rows_ref[...] = jnp.zeros(rows_ref.shape, f32)
            for i, v in enumerate([vout(s_o[0][0])] + vectors):
                rows_ref[i : i + 1, :] = jnp.sum(v[...], 0, keepdims=True)
            table_ref[...] = table[...]
            taps_ref[...] = taps[...]
            course = ["sib", "far"] + list(range(bits_all - 1, -1, -1))

            def double(n):
                at = course[n]
                to = (dp, sib) if at == "sib" else (dp, far) if at == "far" else (place(dp, at)[1], me)
                return [
                    (
                        pltpu.make_async_remote_copy(
                            r, t[l].at[n], t[small_sems[0]].at[i, n], t[small_sems[1]].at[i, n], device_id=to, device_id_type=MESH
                        ),
                        r,
                        t[l].at[n],
                    )
                    for i, (r, l) in enumerate(zip((rows_ref, table_ref, taps_ref), land_small))
                    if i < 2 or n > 1
                ]

            def finish_double(n):
                for cp, r, l in double(n):
                    cp.wait()
                    r[...] += l[...]

            for cp, _, _ in double(0):
                cp.start()

        pieces = [(c, p) for c in range(len(chains)) for p in range(chains[c][0])]
        order = [x for x in pieces if x[0] >= first_grad] + [x for x in pieces if x[0] < first_grad]
        depth = lambda c: len(chains[c][5])
        begin = lambda c: 1 if c in lead else 0
        deepest = max([depth(c) - begin(c) for c in range(len(chains))] + [0])
        total_slots = max(len(order) + deepest - 1, len(course) if last else 0)
        for slot in range(total_slots):
            if last:
                for n in range(len(course) - 1):
                    if slot == (n if n < 2 else min(3 * n - 3, total_slots - 1)):
                        finish_double(n)
                        for cp, _, _ in double(n + 1):
                            cp.start()
            for s in reversed(range(deepest)):
                if 0 <= slot - s < len(order):
                    c, p = order[slot - s]
                    step = s + begin(c)
                    if step < depth(c):
                        settle(c, step, p)
                        if step + 1 < depth(c):
                            hop(c, step + 1, p).start()
        if last:
            finish_double(len(course) - 1)
            for o in small_o:
                store_whole(o).start()
        for c in range(len(chains)):
            for s in range(depth(c)):
                for p in range(chains[c][0]):
                    hop(c, s, p).wait_send()
            out_o = chains[c][5][-1][4]
            block = chains[c][5][-1][2]
            for p in range(chains[c][0]):
                store_piece(out_o, p, PIECE, chains[c][1] and t[block].shape[2] % 128 == 0).wait()

        def drain(k, c):
            if leave:
                pair_send(k).wait_send()
                far_send(k).wait_send()
                own_send(k).wait_send()
            if enter:
                all_far(k).wait_send()
                all_sib(k).wait_send()
                all_fwd(k).wait_send()
                for block in range(4):
                    for o in [all_o] + e_o:
                        store_rows(o, block, k).wait()
            for o in r_o:
                store_rows(o, 0, k).wait()
            return c

        lax.fori_loop(0, CHUNKS, drain, 0)
        for o in s_o + (small_o if last else []):
            store_whole(o).wait()
        for o in join_o:
            for p in range(out_shape[o[0]].shape[0]):
                store_piece(o, p, PIECE, False).wait()

    flops = 0
    if leave:
        flops += 2 * frames * leave[0].shape[1] * width
    if enter:
        flops += 2 * frames * width * sum(c for c, _ in enter[4])
    flops += sum(2 * frames * d[0].shape[1] * d[1].shape[1] for d in dws)
    outs = pl.pallas_call(
        kernel,
        in_specs=[in_hbm()] * n_in,
        out_specs=[in_hbm()] * n_out,
        out_shape=out_shape,
        scratch_shapes=scratch,
        compiler_params=pltpu.CompilerParams(collective_id=cid, has_side_effects=True, vmem_limit_bytes=VMEM_LIMIT),
        cost_estimate=pl.CostEstimate(flops=flops, bytes_accessed=60_000_000, transcendentals=0),
        name=name,
    )(*ins)
    fixed, rest = list(outs[:fixed_out]), list(outs[fixed_out:])
    fresh = [Grad(rest.pop(0), 0, d[3]) for d in dws if d[2] == "join"]
    for item in plan:
        fresh.append(Grad(rest.pop(0), item[3], item[2]))
    return fixed + [fresh] + rest


def publish(arrays, thirds):
    out_shape, scratch = [], []
    for i, a in enumerate(arrays):
        if i in thirds:
            shape = (a.shape[0], thirds[i], a.shape[1] // thirds[i])
            scratch += [pltpu.VMEM(a.shape, a.dtype), pltpu.VMEM(shape, a.dtype)]
            out_shape.append(jax.ShapeDtypeStruct(shape, a.dtype))
        else:
            out_shape.append(jax.ShapeDtypeStruct(a.shape, a.dtype))
    scratch.append(pltpu.SemaphoreType.DMA((2, len(arrays))))

    def kernel(*refs):
        n = len(arrays)
        src, dst, sem = refs[:n], refs[n : 2 * n], refs[-1]
        bufs = list(refs[2 * n : -1])
        first, second = [], []
        for i in range(n):
            if i in thirds:
                flat, split = bufs.pop(0), bufs.pop(0)
                first.append((pltpu.make_async_copy(src[i], flat, sem.at[0, i]), flat, split, i))
            else:
                second.append(pltpu.make_async_copy(src[i], dst[i], sem.at[1, i]))
        for cp in [x[0] for x in first] + second:
            cp.start()
        for cp, flat, split, i in first:
            cp.wait()
            cols = split.shape[2]
            for j in range(split.shape[1]):
                split[:, j, :] = flat[:, j * cols : (j + 1) * cols]
            second.append(pltpu.make_async_copy(split, dst[i], sem.at[1, i]))
            second[-1].start()
        for cp in second:
            cp.wait()

    return pl.pallas_call(
        kernel,
        in_specs=[in_hbm()] * len(arrays),
        out_specs=[in_hbm()] * len(arrays),
        out_shape=out_shape,
        scratch_shapes=scratch,
        compiler_params=pltpu.CompilerParams(vmem_limit_bytes=VMEM_LIMIT),
        name="publish",
    )(*arrays)


SPAN = 128


def exchange(stats, landing, send, recv):
    dp, me = lax.axis_index("dp"), lax.axis_index("mp")
    core, chip = me % 2, me // 2
    others = [chip * 2 + 1 - core, (1 - chip) * 2 + core, (1 - chip) * 2 + 1 - core]
    return [
        pltpu.make_async_remote_copy(
            stats, landing.at[i], send.at[i], recv.at[i], device_id=(dp, to), device_id_type=MESH
        )
        for i, to in enumerate(others)
    ]


def group_targets():
    dp, me = lax.axis_index("dp"), lax.axis_index("mp")
    core, chip = me % 2, me // 2
    return [(dp, chip * 2 + 1 - core), (dp, (1 - chip) * 2 + core), (dp, (1 - chip) * 2 + 1 - core)]


def to_rows(first, second):
    lane = lax.broadcasted_iota(jnp.int32, (SPAN, SPAN), 1)
    both = jnp.where(lane == 0, first, jnp.where(lane == 1, second, 0.0))
    return both.T[:8]


def to_columns(rows8):
    return jnp.concatenate([rows8, jnp.zeros((SPAN - 8, SPAN), jnp.float32)], 0).T


def shifted(window, by):
    return window if by == 0 else pltpu.roll(window, window.shape[0] - by, 0)


def conv_mid(glu, w_depth, gain_depth, width, cid):
    frames, chans = glu.shape
    taps = w_depth.shape[0]
    reach = taps - 1
    edge = (reach + 7) // 8 * 8
    f32, bf = jnp.float32, jnp.bfloat16
    tiles, lanes = frames // SPAN, chans // 128

    def kernel(glu_h, w_h, g_h, act_h, slope_h, unit_h, stat_h, pad, w_v, g_v, act, slope, unit, stat, sendbuf, landing, lsem, ssem, send, recv):
        meet = greet(group_targets())
        loads = [
            pltpu.make_async_copy(glu_h, pad.at[pl.ds(edge, frames)], lsem.at[0]),
            pltpu.make_async_copy(w_h, w_v, lsem.at[1]),
            pltpu.make_async_copy(g_h, g_v, lsem.at[2]),
        ]
        for cp in loads:
            cp.start()
        pad[:edge, :] = jnp.zeros((edge, chans), f32)
        for cp in loads:
            cp.wait()

        def tile(i, c):
            at = pl.multiple_of(i * SPAN, SPAN)
            for lane in range(lanes):
                cols = slice(lane * 128, (lane + 1) * 128)
                window = pad[pl.ds(at, SPAN + edge), cols]
                total = jnp.zeros((SPAN, 128), f32)
                for by in range(8):
                    moved = shifted(window, by)
                    for base in range(0, edge + 1, 8):
                        tap = base + by - (edge - reach)
                        if 0 <= tap < taps:
                            total = total + w_v[tap : tap + 1, cols] * moved[base : base + SPAN]
                unit[pl.ds(at, SPAN), cols] = total
            depth = unit[pl.ds(at, SPAN), :]
            mean = jnp.mean(depth, -1, keepdims=True)
            centred = depth - mean
            sendbuf[:, pl.ds(at, SPAN)] = to_rows(mean, jnp.sum(centred * centred, -1, keepdims=True))
            return c

        lax.fori_loop(0, tiles, tile, 0)
        meet()
        copies = exchange(sendbuf, landing, send, recv)
        for cp in copies:
            cp.start()
        for cp in copies:
            cp.wait_recv()
        rows = [sendbuf[...]] + [landing[i] for i in range(3)]
        mean = sum(r[0:1] for r in rows) * 0.25
        spread = sum(r[1:2] + chans * (r[0:1] - mean) * (r[0:1] - mean) for r in rows) / width
        inverse = lax.rsqrt(spread + epsilon)
        row = lax.broadcasted_iota(jnp.int32, (8, frames), 0)
        stat[...] = jnp.where(row == 0, mean, jnp.where(row == 1, inverse, 0.0))
        outs = [(act, act_h), (slope, slope_h), (unit, unit_h)]

        def store(i, n):
            at = pl.ds(pl.multiple_of(i * SPAN, SPAN), SPAN)
            return pltpu.make_async_copy(outs[n][0].at[at], outs[n][1].at[at], ssem.at[n, i])

        def finish(i, c):
            at = pl.multiple_of(i * SPAN, SPAN)
            cols = to_columns(stat[:, pl.ds(at, SPAN)])
            u = (unit[pl.ds(at, SPAN), :] - cols[:, 0:1]) * cols[:, 1:2]
            a, s = silu_pair(u * g_v[...])
            unit[pl.ds(at, SPAN), :] = u
            act[pl.ds(at, SPAN), :] = a.astype(bf)
            slope[pl.ds(at, SPAN), :] = s.astype(bf)
            for n in range(3):
                store(i, n).start()
            return c

        lax.fori_loop(0, tiles, finish, 0)
        last = pltpu.make_async_copy(stat, stat_h, lsem.at[0])
        last.start()
        for cp in copies:
            cp.wait_send()
        for i in range(tiles):
            for n in range(3):
                store(i, n).wait()
        last.wait()

    S = jax.ShapeDtypeStruct
    out_shape = [S((frames, chans), bf), S((frames, chans), bf), S((frames, chans), f32), S((8, frames), f32)]
    vm = pltpu.VMEM
    return pl.pallas_call(
        kernel,
        in_specs=[in_hbm()] * 3,
        out_specs=[in_hbm()] * 4,
        out_shape=out_shape,
        scratch_shapes=[
            vm((frames + edge, chans), f32), vm(w_depth.shape, f32), vm((1, chans), f32),
            vm((frames, chans), bf), vm((frames, chans), bf), vm((frames, chans), f32), vm((8, frames), f32),
            vm((8, frames), f32), vm((3, 8, frames), f32),
            pltpu.SemaphoreType.DMA((3,)), pltpu.SemaphoreType.DMA((3, tiles)), pltpu.SemaphoreType.DMA((3,)), pltpu.SemaphoreType.DMA((3,)),
        ],
        compiler_params=pltpu.CompilerParams(collective_id=cid, has_side_effects=True, vmem_limit_bytes=VMEM_LIMIT),
        name="conv_mid",
    )(glu, w_depth, gain_depth)


def conv_mid_back(grad, slope, unit, stat, glu, sig, tail, w_depth, gain_depth, width, cid):
    frames, chans = glu.shape
    taps = w_depth.shape[0]
    reach = taps - 1
    edge = (reach + 7) // 8 * 8
    f32, bf = jnp.float32, jnp.bfloat16
    tiles, lanes = frames // SPAN, chans // 128
    ins = [grad, slope, unit, stat, w_depth, gain_depth, glu, sig, tail]

    def kernel(*refs):
        hbm, (pair_h, taps_h) = refs[:9], refs[9:11]
        (grad_v, slope_v, unit_v, stat_v, w_v, g_v, pad, sig_v, tail_v, back, pair, taps_v, acc, gacc, sendbuf, landing, lsem, ssem, send, recv) = refs[11:]
        meet = greet(group_targets())
        dst = [grad_v, slope_v, unit_v, stat_v, w_v, g_v, pad.at[pl.ds(edge, frames)], sig_v, tail_v]
        loads = [pltpu.make_async_copy(h, d, lsem.at[i]) for i, (h, d) in enumerate(zip(hbm, dst))]
        for cp in loads:
            cp.start()
        pad[:edge, :] = jnp.zeros((edge, chans), f32)
        back[frames:, :] = jnp.zeros((edge, chans), f32)
        acc[...] = jnp.zeros_like(acc)
        gacc[...] = jnp.zeros_like(gacc)
        for cp in loads[:6]:
            cp.wait()

        def first(i, c):
            at = pl.ds(pl.multiple_of(i * SPAN, SPAN), SPAN)
            u = unit_v[at, :]
            de = grad_v[at, :] * slope_v[at, :].astype(f32)
            gacc[...] += fold8(de * u)
            du = de * g_v[...]
            back[at, :] = du
            sendbuf[:, at] = to_rows(jnp.sum(du, -1, keepdims=True), jnp.sum(du * u, -1, keepdims=True))
            return c

        lax.fori_loop(0, tiles, first, 0)
        meet()
        copies = exchange(sendbuf, landing, send, recv)
        for cp in copies:
            cp.start()
        for cp in loads[6:]:
            cp.wait()
        for cp in copies:
            cp.wait_recv()
        means = (sendbuf[...] + landing[0] + landing[1] + landing[2]) / width
        row = lax.broadcasted_iota(jnp.int32, (8, frames), 0)
        stat_v[...] = jnp.where(row == 1, stat_v[...], jnp.where(row == 0, means[0:1], jnp.where(row == 2, means[1:2], 0.0)))

        def second(i, c):
            at = pl.ds(pl.multiple_of(i * SPAN, SPAN), SPAN)
            cols = to_columns(stat_v[:, at])
            back[at, :] = cols[:, 1:2] * (back[at, :] - cols[:, 0:1] - unit_v[at, :] * cols[:, 2:3])
            return c

        lax.fori_loop(0, tiles, second, 0)

        def store(i):
            at = pl.ds(pl.multiple_of(i * SPAN, SPAN), SPAN)
            return pltpu.make_async_copy(pair.at[at], pair_h.at[at], ssem.at[i])

        def third(i, c):
            at = pl.multiple_of(i * SPAN, SPAN)
            rows = pl.ds(at, SPAN)
            for lane in range(lanes):
                cols = slice(lane * 128, (lane + 1) * 128)
                ahead = back[pl.ds(at, SPAN + edge), cols]
                total = jnp.zeros((SPAN, 128), f32)
                for by in range(8):
                    moved = shifted(ahead, by)
                    for base in range(0, edge, 8):
                        tap = reach - (base + by)
                        if 0 <= tap < taps:
                            total = total + w_v[tap : tap + 1, cols] * moved[base : base + SPAN]
                pair[rows, cols] = (total * sig_v[rows, cols].astype(f32)).astype(bf)
                pair[rows, chans + lane * 128 : chans + (lane + 1) * 128] = (total * tail_v[rows, cols].astype(f32)).astype(bf)
            store(i).start()
            for lane in range(lanes):
                cols = slice(lane * 128, (lane + 1) * 128)
                here = back[rows, cols]
                window = pad[pl.ds(at, SPAN + edge), cols]
                for by in range(8):
                    moved = shifted(window, by)
                    for base in range(0, edge + 1, 8):
                        tap = base + by - (edge - reach)
                        if 0 <= tap < taps:
                            acc[tap * 8 : tap * 8 + 8, cols] += fold8(here * moved[base : base + SPAN])
            return c

        lax.fori_loop(0, tiles, third, 0)
        for tap in range(taps):
            taps_v[tap : tap + 1, :] = jnp.sum(acc[tap * 8 : tap * 8 + 8, :], 0, keepdims=True)
        taps_v[taps : taps + 1, :] = jnp.sum(gacc[...], 0, keepdims=True)
        last = pltpu.make_async_copy(taps_v, taps_h, lsem.at[0])
        last.start()
        for cp in copies:
            cp.wait_send()
        for i in range(tiles):
            store(i).wait()
        last.wait()

    S = jax.ShapeDtypeStruct
    vm = pltpu.VMEM
    return pl.pallas_call(
        kernel,
        in_specs=[in_hbm()] * 9,
        out_specs=[in_hbm()] * 2,
        out_shape=[S((frames, 2 * chans), bf), S((taps + 1, chans), f32)],
        scratch_shapes=[
            vm((frames, chans), f32), vm((frames, chans), bf), vm((frames, chans), f32), vm((8, frames), f32),
            vm(w_depth.shape, f32), vm((1, chans), f32), vm((frames + edge, chans), f32), vm((frames, chans), bf), vm((frames, chans), bf),
            vm((frames + edge, chans), f32), vm((frames, 2 * chans), bf), vm((taps + 1, chans), f32), vm((taps * 8, chans), f32), vm((8, chans), f32),
            vm((8, frames), f32), vm((3, 8, frames), f32),
            pltpu.SemaphoreType.DMA((9,)), pltpu.SemaphoreType.DMA((tiles,)), pltpu.SemaphoreType.DMA((3,)), pltpu.SemaphoreType.DMA((3,)),
        ],
        compiler_params=pltpu.CompilerParams(collective_id=cid, has_side_effects=True, vmem_limit_bytes=VMEM_LIMIT),
        name="conv_mid_back",
    )(*ins)


def split_pair(x):
    left = lax.broadcasted_iota(jnp.int32, x.shape, 1) < HEAD
    zero = jnp.zeros_like(x)
    return jnp.concatenate([jnp.where(left, x, zero), jnp.where(left, zero, x)], 0)

def join_pair(x):
    rows = x.shape[0] // 2
    left = lax.broadcasted_iota(jnp.int32, (rows, x.shape[1]), 1) < HEAD
    return jnp.where(left, x[:rows], x[rows:])

def fwd_kernel(q_ref, k_ref, v_ref, rel_ref, mixed_ref, probs_ref, bias_ref):
    ib = pl.program_id(1)
    qs = split_pair(q_ref[...] * 0.125)
    s = nt(qs, k_ref[...])
    b = nt(qs, rel_ref[...])
    rows = b.shape[0] // 2
    bias_ref[:, 0:BQ] = b[:, 3 * BQ : 4 * BQ]
    for h in range(2):
        r = pltpu.roll(b[h * rows : (h + 1) * rows, :WIN], 0, 1, stride=1, stride_axis=0)
        bias_ref[h * rows : (h + 1) * rows, BQ : 4 * BQ] = r[:, : 3 * BQ]
    bias_ref[:, 4 * BQ :] = b[:, 4 * BQ :]
    nkeys = s.shape[1] // BQ
    parts = []
    for jb in range(nkeys):
        at = pl.multiple_of(jnp.clip(jb - ib + 2, 0, 4) * BQ, BQ)
        parts.append(s[:, jb * BQ : (jb + 1) * BQ] + bias_ref[:, pl.ds(at, BQ)])
    top = functools.reduce(jnp.maximum, parts)
    m = jnp.max(top, -1, keepdims=True)
    es = [jnp.exp(p - m) for p in parts]
    tot = jnp.sum(functools.reduce(jnp.add, es), -1, keepdims=True)
    inv = 1.0 / tot
    for jb in range(nkeys):
        probs_ref[0, :, jb * BQ : (jb + 1) * BQ] = (es[jb] * inv).astype(jnp.bfloat16)
    mixed_ref[...] = join_pair(nn(probs_ref[0], v_ref[...])).astype(jnp.bfloat16)

def bwd_kernel(plan, *refs):
    n = len(plan)
    pairs_in, refs = refs[7 : 7 + n], refs[:7] + refs[7 + n :]
    q_ref, k_ref, v_ref, relb_ref, hot_ref, probs_ref, do_ref, dq_ref, dk_ref, dv_ref, dt_ref = refs[:11]
    grads_out, refs = refs[11 : 11 + n], refs[11 + n :]
    tot_ref, dkt, dvt, dta, dz_ref = refs[:5]
    landings, keeps, halves, sems = refs[5 : 5 + n], refs[5 + n : 5 + 2 * n], refs[5 + 2 * n : 5 + 3 * n], refs[5 + 3 * n :]
    pr, ib, nb = pl.program_id(0), pl.program_id(1), pl.num_programs(1)
    dp, mp = lax.axis_index("dp"), lax.axis_index("mp")
    hops, holds, slot = [], [], 0
    for i, ((pieces, bit, turned), src, landing, keep, half, out) in enumerate(zip(plan, pairs_in, landings, keeps, halves, grads_out)):
        holds.append(halving_keep(src, keep, bit, sems[2].at[i]))
        flip = turned and landing.shape[2] % 128 == 0
        for p in range(pieces):
            move = halving_copy(src, landing, p, bit, sems[0], sems[1], slot)
            store = pltpu.make_async_copy(region(half, p, PIECE, flip), region(out, p, PIECE, flip), sems[3].at[slot])
            hops.append((move, store, lambda q, j, keep=keep: keep[q, j], landing, half, p, turned))
            slot += 1

    if hops:

        @pl.when((ib == 0) & (pr == 0))
        def _():
            meet = greet([(place(dp, b)[1], mp) for b in sorted({x[1] for x in plan})])
            for hold in holds:
                hold.start()
            meet()
            for hop in hops:
                hop[0].start()

    @pl.when(ib == 0)
    def _():
        dkt[...] = jnp.zeros_like(dkt)
        dvt[...] = jnp.zeros_like(dvt)
    @pl.when((ib == 0) & (pr == 0))
    def _():
        dta[...] = jnp.zeros_like(dta)
    qs = split_pair(q_ref[...] * 0.125)
    dos = split_pair(do_ref[...])
    p = probs_ref[0]
    dp = nt(dos, v_ref[...])
    nkeys = dp.shape[1] // BQ
    dvt[...] += tn(dos, p)
    pf = p.astype(jnp.float32)
    acc = None
    for jb in range(nkeys):
        sl = slice(jb * BQ, (jb + 1) * BQ)
        t = pf[:, sl] * dp[:, sl]
        acc = t if acc is None else acc + t
    inner = jnp.sum(acc, -1, keepdims=True)
    tot_ref[...] = jnp.zeros_like(tot_ref)
    for jb in range(nkeys):
        sl = slice(jb * BQ, (jb + 1) * BQ)
        dz = (pf[:, sl] * (dp[:, sl] - inner)).astype(jnp.bfloat16)
        dz_ref[:, sl] = dz
        at = pl.multiple_of(jnp.clip(jb - ib + 2, 0, 4) * BQ, BQ)
        tot_ref[:, pl.ds(at, BQ)] += dz.astype(jnp.float32)
    rows = BQ
    r2 = lax.broadcasted_iota(jnp.int32, (2 * rows, 2 * rows), 0)
    c2 = lax.broadcasted_iota(jnp.int32, (2 * rows, 2 * rows), 1)
    mirror = (r2 + c2 == jnp.where(r2 < rows, rows - 1, 3 * rows - 1)).astype(jnp.bfloat16)
    w = jnp.concatenate([tot_ref[:, BQ : 4 * BQ].astype(jnp.bfloat16), jnp.zeros((2 * rows, BQ), jnp.bfloat16)], 1)
    w = nn(mirror, w)
    outs = [pltpu.roll(w[h * rows : (h + 1) * rows], WIN - rows + 1, 1, stride=1, stride_axis=0) for h in range(2)]
    d = nn(mirror, jnp.concatenate(outs, 0).astype(jnp.bfloat16)).astype(jnp.bfloat16)
    drel = nn(d, hot_ref[...])
    col = lax.broadcasted_iota(jnp.int32, drel.shape, 1)
    low = jnp.sum(tot_ref[:, :BQ], -1, keepdims=True)
    high = jnp.sum(tot_ref[:, 4 * BQ :], -1, keepdims=True)
    drel = drel + jnp.where(col == 0, low, 0.0) + jnp.where(col == REL_LEFT + REL_RIGHT, high, 0.0)
    drel = drel.astype(jnp.bfloat16)
    dz = dz_ref[...]
    dq = nn(dz, k_ref[...]) + nn(drel, relb_ref[...])
    dq_ref[...] = (join_pair(dq) * 0.125).astype(jnp.bfloat16)
    dkt[...] += tn(qs, dz)
    dta[...] += tn(drel, qs)
    @pl.when(ib == nb - 1)
    def _():
        dk_ref[...] = dkt[...].T.astype(jnp.bfloat16)
        dv_ref[...] = dvt[...].T.astype(jnp.bfloat16)
        dt_ref[...] = dta[...]

    if hops:

        @pl.when((ib == nb - 1) & (pr == pl.num_programs(0) - 1))
        def _():
            for hold in holds:
                hold.wait()
            for hop in hops:
                hop[0].wait_recv()
                halving_add(*hop[2:])
                hop[1].start()
            for hop in hops:
                hop[0].wait_send()
                hop[1].wait()

def rel_tables(rel_table):
    spots = jnp.arange(5 * BQ)
    idx = jnp.where(spots < 3 * BQ, jnp.clip(spots - REL_LEFT, 0, REL_LEFT + REL_RIGHT), jnp.where(spots < 4 * BQ, 0, REL_LEFT + REL_RIGHT))
    hot = (jnp.arange(BQ)[None, :] == idx[:, None]).astype(jnp.bfloat16)
    padded = jnp.pad(rel_table, ((0, BQ - rel_table.shape[0]), (0, 0)))
    padded = jnp.concatenate([padded, padded], 1)
    ext = jnp.dot(hot, padded, preferred_element_type=jnp.float32).astype(jnp.bfloat16)
    return ext, hot[:WIN], padded

def attn_fwd(qkv, ext):
    frames, cols = qkv.shape
    pairs = cols // 3 // 128
    nb = frames // BQ
    bf = jnp.bfloat16
    return pl.pallas_call(
        fwd_kernel,
        grid=(pairs, nb),
        in_specs=[
            pl.BlockSpec((BQ, 128), lambda p, i: (i, p)),
            pl.BlockSpec((frames, 128), lambda p, i: (0, pairs + p)),
            pl.BlockSpec((frames, 128), lambda p, i: (0, 2 * pairs + p)),
            pl.BlockSpec(ext.shape, lambda p, i: (0, 0)),
        ],
        out_specs=[
            pl.BlockSpec((BQ, 128), lambda p, i: (i, p)),
            pl.BlockSpec((1, 2 * BQ, frames), lambda p, i: (p, i, 0)),
        ],
        out_shape=[jax.ShapeDtypeStruct((frames, cols // 3), bf), jax.ShapeDtypeStruct((pairs, 2 * frames, frames), bf)],
        scratch_shapes=[pltpu.VMEM((2 * BQ, 5 * BQ), jnp.float32)],
        compiler_params=pltpu.CompilerParams(vmem_limit_bytes=VMEM_LIMIT),
        name="attn_fwd",
    )(qkv, qkv, qkv, ext)

def attn_bwd(qkv, padded, hot, probs, dmixed, grads, cid):
    frames, cols = qkv.shape
    pairs = cols // 3 // 128
    nb = frames // BQ
    bf = jnp.bfloat16
    blk = pl.BlockSpec((BQ, 128), lambda p, i: (i, p))
    full = pl.BlockSpec((frames, 128), lambda p, i: (0, p))
    plan = [(g.array.shape[0], g.bit, g.turned) for g in grads]
    after = [halved(g.array.shape, g.turned) for g in grads]
    slots = sum(x[0] for x in plan)
    outs = pl.pallas_call(
        functools.partial(bwd_kernel, plan),
        grid=(pairs, nb),
        in_specs=[
            blk,
            pl.BlockSpec((frames, 128), lambda p, i: (0, pairs + p)),
            pl.BlockSpec((frames, 128), lambda p, i: (0, 2 * pairs + p)),
            pl.BlockSpec(padded.shape, lambda p, i: (0, 0)),
            pl.BlockSpec(hot.shape, lambda p, i: (0, 0)),
            pl.BlockSpec((1, 2 * BQ, frames), lambda p, i: (p, i, 0)),
            blk,
        ]
        + [in_hbm()] * len(grads),
        out_specs=[blk, full, full, pl.BlockSpec((128, 128), lambda p, i: (0, 0))] + [in_hbm()] * len(after),
        out_shape=[jax.ShapeDtypeStruct((frames, cols // 3), bf)] * 3 + [jax.ShapeDtypeStruct((128, 128), jnp.float32)] + after,
        scratch_shapes=[pltpu.VMEM((2 * BQ, 5 * BQ), jnp.float32), pltpu.VMEM((128, frames), jnp.float32), pltpu.VMEM((128, frames), jnp.float32),
                        pltpu.VMEM((128, 128), jnp.float32), pltpu.VMEM((2 * BQ, frames), bf)]
        + [arriving(g.array.shape) for g in grads]
        + [arriving(g.array.shape) for g in grads]
        + [pltpu.VMEM(a.shape, a.dtype) for a in after]
        + ([pltpu.SemaphoreType.DMA((slots,))] * 2 + [pltpu.SemaphoreType.DMA((len(grads),)), pltpu.SemaphoreType.DMA((slots,))] if grads else []),
        compiler_params=pltpu.CompilerParams(
            vmem_limit_bytes=VMEM_LIMIT, collective_id=cid, has_side_effects=True
        ),
        cost_estimate=pl.CostEstimate(flops=20 * frames * frames * 128 * pairs, bytes_accessed=20_000_000, transcendentals=0),
        name="attn_bwd",
    )(qkv, qkv, qkv, padded, hot, probs, dmixed, *[g.array for g in grads])
    return list(outs[:4]) + [[Grad(a, b + 1, t) for a, (_, b, t) in zip(outs[4:], plan)]]


def body(
    features,
    w1_in,
    w1_out,
    gain_ffn1,
    w_qkv,
    w_attn_out,
    rel_table,
    gain_attn,
    w_conv_in,
    w_depth,
    gain_depth,
    w_conv_out,
    gain_conv,
    w2_in,
    w2_out,
    gain_ffn2,
    gain_final,
    cotangent,
):
    local_frames, clip_count, width = features.shape
    rows = local_frames * clip_count
    f32, bf = jnp.float32, jnp.bfloat16
    s0 = features.reshape(rows, width)
    seed = cotangent.reshape(rows, width)
    gains = jnp.stack([gain_ffn1, gain_attn, gain_conv, gain_ffn2, gain_final] + [gain_final] * 3).astype(f32)
    flat_qkv = w_qkv.reshape(width, -1)
    flat_conv = w_conv_in.reshape(width, -1)
    units = w1_in.shape[1]
    dp_count = lax.axis_size("dp")
    done = dp_count.bit_length() - 1
    pending = lambda items: [g for g in items if g.bit < done]
    chans = w_conv_out.shape[0]

    def swish_out(h, extra, outs):
        act, slope = silu_pair(h)
        outs[0][...] = act.astype(bf)
        outs[1][...] = slope.astype(bf)

    def plain_out(h, extra, outs):
        outs[0][...] = h.astype(outs[0].dtype)

    def glu_out(h, extra, outs):
        p0 = h[:, :chans]
        sig = jax.nn.sigmoid(h[:, chans:])
        glu = p0 * sig
        outs[0][...] = glu
        outs[1][...] = sig.astype(bf)
        outs[2][...] = (glu * (1.0 - sig)).astype(bf)

    def slope_out(h, extra, outs):
        outs[0][...] = (h * extra[0][...].astype(f32)).astype(bf)

    def first(branch, ins, gains, outs, sums):
        return (unit_norm(ins[0].astype(f32))[0] * gains[0:1, :]).astype(bf)

    def forward(scale, row):
        def run(branch, ins, gains, outs, sums):
            fresh = ins[0].astype(f32) + scale * branch
            outs[0][...] = fresh
            sums[0][...] += fold8(branch * branch)
            return (unit_norm(fresh)[0] * gains[row : row + 1, :]).astype(bf)
        return run

    def turn(branch, ins, gains, outs, sums):
        fresh = ins[0] + 0.5 * branch
        sums[0][...] += fold8(branch * branch)
        sums[1][...] += fold8(fresh * fresh)
        unit, inverse = unit_norm(fresh)
        outs[0][...] = unit * gains[4:5, :]
        grad = ins[1].astype(f32)
        scaled = grad * gains[4:5, :]
        mean_one = jnp.mean(scaled, -1, keepdims=True)
        mean_two = jnp.mean(scaled * unit, -1, keepdims=True)
        sums[2][...] += fold8(grad * unit)
        back = inverse * (scaled - mean_one - unit * mean_two)
        outs[1][...] = back
        return (0.5 * back).astype(bf)

    def backward(scale, row):
        def run(branch, ins, gains, outs, sums):
            pull, grad_gain = norm_pull(branch, ins[1].astype(f32), gains[row : row + 1, :])
            fresh = ins[0] + pull
            outs[0][...] = fresh
            sums[0][...] += grad_gain
            return (scale * fresh).astype(bf)
        return run

    a1, act1, slope1, _ = stage(
        "ffn1_in", 0, rows, width, dp_count, gains, enter=(w1_in, False, swish_out, (), ((units, bf), (units, bf))),
        junction=first, row_in=(s0,),
    )
    a2, qkv, s1, sq1, _ = stage(
        "ffn1_out", 1, rows, width, dp_count, gains, leave=(act1, w1_out, False),
        enter=(flat_qkv, False, plain_out, (), ((flat_qkv.shape[1], bf),)),
        junction=forward(0.5, 1), row_in=(s0,), row_out=(f32,), sums=1,
    )
    ext, hot, padded = rel_tables(rel_table)
    mixed, probs = attn_fwd(qkv, ext)
    a3, glu, sig, tail, s2, sq2, _ = stage(
        "attn_out", 2, rows, width, dp_count, gains, leave=(mixed, w_attn_out, False),
        enter=(flat_conv, False, glu_out, (), ((chans, f32), (chans, bf), (chans, bf))),
        junction=forward(1.0, 2), row_in=(s1,), row_out=(f32,), sums=1,
    )
    depth_taps = w_depth.astype(f32)
    depth_gain = gain_depth.astype(f32)[None]
    act3, slope3, depth_unit, depth_stat = conv_mid(glu, depth_taps, depth_gain, width, 10)
    a4, act2, slope2, s3, sq3, _ = stage(
        "conv_out", 3, rows, width, dp_count, gains, leave=(act3, w_conv_out, False),
        enter=(w2_in, False, swish_out, (), ((units, bf), (units, bf))),
        junction=forward(1.0, 3), row_in=(s2,), row_out=(f32,), sums=1,
    )
    db4, dh2, output, grad4, sq4, sq5, dgf, _ = stage(
        "ffn2_out", 4, rows, width, dp_count, gains, leave=(act2, w2_out, False),
        enter=(w2_out, True, slope_out, (slope2,), ((units, bf),)),
        junction=turn, row_in=(s3, seed), row_out=(f32, f32), sums=3,
    )
    db3, de3, grad3, dg2, (gw2_in, gw2_out) = stage(
        "ffn2_back", 5, rows, width, dp_count, gains, leave=(dh2, w2_in, True),
        enter=(w_conv_out, True, plain_out, (), ((chans, f32),)), dws=((a4, dh2, "join", False, 0), (db4, act2, "far", True, 1)),
        junction=backward(1.0, 3), row_in=(grad4, s3), row_out=(f32,), sums=1,
    )
    dpaired, tap_sums = conv_mid_back(de3, slope3, depth_unit, depth_stat, glu, sig, tail, depth_taps, depth_gain, width, 11)
    db2, dmixed, grad2, dgc, (gconv_in, gconv_out, gw2_in, gw2_out) = stage(
        "conv_back", 6, rows, width, dp_count, gains, leave=(dpaired, flat_conv, True),
        enter=(w_attn_out, True, plain_out, (), ((w_attn_out.shape[0], bf),)), dws=((a3, dpaired, "join", False, 0), (db3, act3, "join", True, 0)), grads=(gw2_in, gw2_out),
        junction=backward(1.0, 2), row_in=(grad3, s2), row_out=(f32,), sums=1,
    )
    dq, dk, dv, dt, (gconv_in, gconv_out, gw2_in, gw2_out) = attn_bwd(
        qkv, padded, hot, probs, dmixed, [gconv_in, gconv_out, gw2_in, gw2_out], 9
    )
    dqkv = jnp.concatenate([dq, dk, dv], 1)
    db1, dh1, grad1, dga, (gqkv, gattn, gconv_in, gconv_out, gw2_in) = stage(
        "attn_back", 7, rows, width, dp_count, gains, leave=(dqkv, flat_qkv, True),
        enter=(w1_out, True, slope_out, (slope1,), ((units, bf),)), dws=((a2, dqkv, "far", False, 1), (db2, mixed, "far", True, 1)), grads=(gconv_in, gconv_out, gw2_in),
        junction=backward(0.5, 1), row_in=(grad2, s1), row_out=(f32,), sums=1,
    )
    early = [gqkv, gattn, gconv_in, gconv_out, gw2_in, gw2_out]
    waiting = pending(early)
    grad0, dg1, ends, small_rows, table, taps_end = stage(
        "ffn1_back", 8, rows, width, dp_count, gains, leave=(dh1, w1_in, True),
        dws=((db1, act1, "far", True, 1), (a1, dh1, "near", False, 1)), grads=waiting,
        small=[dga, dgc, dg2, dgf, sq1, sq2, sq3, sq4, sq5, dt, tap_sums],
        junction=backward(1.0, 0), row_in=(grad1, s0), row_out=(f32,), sums=1,
    )
    gw1_out, gw1_in = ends[:2]
    for item, end in zip(waiting, ends[2:]):
        item.array = end.array

    def finish(item):
        flip = item.turned and item.array.shape[0] * dp_count == width and (width // dp_count) % 128 != 0
        return item.array.T if flip else item.array

    ends = [output, grad0] + [finish(g) for g in (gw1_in, gw1_out, gqkv, gattn, gconv_in, gconv_out, gw2_in, gw2_out)]
    ends = publish(ends + [small_rows, table, taps_end], {0: 1, 1: 1, 4: 3, 6: 2})
    small_rows, table, taps_end = ends[10:]
    rel = rel_table.shape[0]
    table_sum = table[:rel, :HEAD] + table[:rel, HEAD:]
    depth_sum, depth_gain_sum = taps_end[:-1], taps_end[-1]
    total_squares = jnp.sum(small_rows[5:10], -1)
    token_total = rows * lax.axis_size("mp") * lax.axis_size("dp")
    rms_stats = jnp.sqrt(total_squares / (token_total * width))
    whole = lambda x: x.reshape(local_frames, clip_count, width)
    return (
        whole(ends[0]),
        whole(ends[1]),
        ends[2],
        ends[3],
        small_rows[0],
        ends[4],
        ends[5],
        table_sum,
        small_rows[1],
        ends[6],
        depth_sum,
        depth_gain_sum,
        ends[7],
        small_rows[2],
        ends[8],
        ends[9],
        small_rows[3],
        small_rows[4],
        rms_stats,
    )


def solution(mesh):
    return jax.shard_map(
        body,
        mesh=mesh,
        in_specs=(
            P("mp", "dp", None),
            P(None, "mp"),
            P("mp", None),
            P(),
            P(None, None, "mp"),
            P("mp", None),
            P(),
            P(),
            P(None, None, "mp"),
            P(None, "mp"),
            P("mp"),
            P("mp", None),
            P(),
            P(None, "mp"),
            P("mp", None),
            P(),
            P(),
            P("mp", "dp", None),
        ),
        out_specs=(
            P("mp", "dp", None),
            P("mp", "dp", None),
            P("dp", "mp"),
            P("mp", "dp"),
            P(),
            P("dp", None, "mp"),
            P("mp", "dp"),
            P(),
            P(),
            P("dp", None, "mp"),
            P(None, "mp"),
            P("mp"),
            P("mp", "dp"),
            P(),
            P("dp", "mp"),
            P("mp", "dp"),
            P(),
            P(),
            P(),
        ),
        check_vma=False,
    )
```

time: 550 us -> 527 us (0.958); the launches traced: 541 us -> 526 us
  Pallas kernels: 407 us -> 503 us
  local copies, waits for them, and re-layouts: 72.4 us -> 12.7 us
  other arithmetic: 39.1 us -> 8.37 us
  blocking collectives: 20.8 us -> 0 us
    pallas_call x9 -> x12, Pallas kernels: 354 us -> 446 us  [the longest x9 340 us: stage(): pl.pallas_call(kernel, in_specs=[in_hbm()] * n_in, out_specs=[in_hbm()] *...]
    unnamed x198 -> x15, local copies, waits for them, and re-layouts: 64.4 us -> 4.77 us
    psum x3 -> x0, blocking collectives: 20.8 us -> none  [the longest x1 7.71 us: body(): average = lax.psum(jnp.sum(depth, -1, keepdims=True), 'mp') / width]
    another operation x2 -> x0, other arithmetic: 19.8 us -> none
    reduce_sum x5 -> x0, other arithmetic: 14.9 us -> none  [the longest x2 6.31 us: body(): tap_grads.append(jnp.sum(grad_depth * padded_glu[k:k + frames], 0))]
where the time goes in v4:
time: 527 us; the launch traced here: 526 us
  Pallas kernels  503 us (95%)
  local copies, waits for them, and re-layouts  12.7 us (2%)
  other arithmetic  8.37 us (2%)
    pallas_call x9, Pallas kernels, stage(): pl.pallas_call(kernel, in_specs=[in_hbm()] * n_in, out_specs=[in_hbm()] *...  340 us
    pallas_call x1, Pallas kernels, publish(): pl.pallas_call(kernel, in_specs=[in_hbm()] * len(arrays), out_specs=[in_h...  77.8 us
    pallas_call x1, Pallas kernels, attn_bwd(): pl.pallas_call(functools.partial(bwd_kernel, plan), grid=(pairs, nb), in_...  35.5 us
    pallas_call x1, Pallas kernels, attn_fwd(): pl.pallas_call(fwd_kernel, grid=(pairs, nb), in_specs=[pl.BlockSpec((BQ,...  21.9 us
    pallas_call x1, Pallas kernels, conv_mid_back(): pl.pallas_call(kernel, in_specs=[in_hbm()] * 9, out_specs=[in_hbm()] * 2,...  15.7 us
    pallas_call x1, Pallas kernels, conv_mid(): pl.pallas_call(kernel, in_specs=[in_hbm()] * 3, out_specs=[in_hbm()] * 4,...  12.4 us

profile of v4, /device:TPU:0, one launch (start us, length us, event | category | flops | bytes accessed | tf_op | source)
XLA Modules:
  0.0 525.9 jit_solution(14703719695800369221)
XLA Ops:
  4.8 19.6 %ffn1_in.1 = (bf16[1024,1024]{1,0:T(8,128)(2,1)}, bf16[1024,1024]{1,0:T(8,128)(2,1)}, bf16[1024,1024]{1,0:T(8,128)(2,1)}) custom-call(f32[8,1024]{1,0:T(8,128)} %convert_element_type.13.refs_0_.refs_2_.refs_4_.refs_5_, bf16[256,1024]{1,0:T(8,128)(2,1)} %bitcast.27, bf16[1024,1024]{1,0:T(8,128)(2,1)} %refs_1_.11), custom_call_target="tpu_custom_call" | custom-call | flops 4294967296 | bytes 60000000 | tf_op jit(solution)/shard_map/ffn1_in/pallas_call | solution.py:557
  24.4 0.9 copy.41
  25.3 1.6 copy.42.refs_4_.refs_1_
  26.9 31.1 %ffn1_out.1 = (bf16[1024,1024]{1,0:T(8,128)(2,1)}, bf16[1024,768]{1,0:T(8,128)(2,1)}, f32[256,1024]{1,0:T(8,128)}, f32[8,1024]{1,0:T(8,128)}) custom-call(bf16[1024,1024]{1,0:T(8,128)(2,1)} %get-tuple-element.106.refs_0_.refs_3_, bf16[1024,1024]{1,0:T(8,128)(2,1)} %refs_8_.5, f32[8,1024]{1,0:T(8,128)} %convert_element_type.13.refs_0_.refs_2_.refs_4_.refs_5_, ...), custom_call_target="tpu_custom_call" | custom-call | flops 3758096384 | bytes 60000000 | tf_op jit(solution)/shard_map/ffn1_out/pallas_call | solution.py:557
  58.2 1.0 convolution_convert_fusion.rel_ref
  59.2 21.9 %attn_fwd.1 = (bf16[1024,256]{1,0:T(8,128)(2,1)}, bf16[2,2048,1024]{2,1,0:T(8,128)(2,1)}) custom-call(bf16[1024,768]{1,0:T(8,128)(2,1)} %get-tuple-element.107.q_ref.k_ref.v_ref.refs_0_.refs_1_.refs_2_, bf16[1024,768]{1,0:T(8,128)(2,1)} %get-tuple-element.107.q_ref.k_ref.v_ref.refs_0_.refs_1_.refs_2_, ...), custom_call_target="tpu_custom_call" | custom-call | tf_op jit(solution)/shard_map/attn_fwd/pallas_call | solution.py:1017
  81.1 1.2 copy.47
  82.3 30.1 %attn_out.1 = (bf16[1024,1024]{1,0:T(8,128)(2,1)}, f32[1024,256]{1,0:T(8,128)}, bf16[1024,256]{1,0:T(8,128)(2,1)}, bf16[1024,256]{1,0:T(8,128)(2,1)}, f32[256,1024]{1,0:T(8,128)}, /*index=5*/f32[8,1024]{1,0:T(8,128)}) custom-call(bf16[1024,256]{1,0:T(8,128)(2,1)} %get-tuple-element.108.refs_0_.refs_4_, bf16[256,1024]{1,0:T(8,128)(2,1)} %refs_8_.4, ...), custom_call_target="tpu_custom_call" | custom-call | flops 2147483648 | bytes 60000000 | tf_op jit(solution)/shard_map/attn_out/pallas_call | solution.py:557
  113.6 12.4 %conv_mid.1 = (bf16[1024,256]{1,0:T(8,128)(2,1)}, bf16[1024,256]{1,0:T(8,128)(2,1)}, f32[1024,256]{1,0:T(8,128)}, f32[8,1024]{1,0:T(8,128)}) custom-call(f32[1024,256]{1,0:T(8,128)} %get-tuple-element.110.glu_h.refs_6_, f32[31,256]{1,0:T(8,128)} %convert_element_type.15.w_h.refs_4_, f32[1,256]{1,0:T(1,128)} %bitcast.22), custom_call_target="tpu_custom_call" | custom-call | tf_op jit(solution)/shard_map/conv_mid/pallas_call | solution.py:738
  126.0 30.0 %conv_out.1 = (bf16[1024,1024]{1,0:T(8,128)(2,1)}, bf16[1024,1024]{1,0:T(8,128)(2,1)}, bf16[1024,1024]{1,0:T(8,128)(2,1)}, f32[256,1024]{1,0:T(8,128)}, f32[8,1024]{1,0:T(8,128)}) custom-call(bf16[1024,256]{1,0:T(8,128)(2,1)} %get-tuple-element.111.refs_0_.refs_7_, bf16[256,1024]{1,0:T(8,128)(2,1)} %refs_8_.3, ...), custom_call_target="tpu_custom_call" | custom-call | flops 4831838208 | bytes 60000000 | tf_op jit(solution)/shard_map/conv_out/pallas_call | solution.py:557
  156.0 31.7 %ffn2_out.1 = (bf16[1024,1024]{1,0:T(8,128)(2,1)}, bf16[1024,1024]{1,0:T(8,128)(2,1)}, f32[256,1024]{1,0:T(8,128)}, f32[256,1024]{1,0:T(8,128)}, f32[8,1024]{1,0...) custom-call(bf16[1024,1024]{1,0:T(8,128)(2,1)} %get-tuple-element.113.refs_0_.refs_3_, bf16[1024,1024]{1,0:T(8,128)(2,1)} %refs_1_.9, ...), custom_call_target="tpu_custom_call" | custom-call | flops 4294967296 | bytes 60000000 | tf_op jit(solution)/shard_map/ffn2_out/pallas_call | solution.py:557
  187.7 32.8 %ffn2_back.1 = (bf16[1024,1024]{1,0:T(8,128)(2,1)}, f32[1024,256]{1,0:T(8,128)}, f32[256,1024]{1,0:T(8,128)}, f32[8,1024]{1,0:T(8,128)}, bf16[4,4,2,128,256]{4,3...) custom-call(bf16[1024,1024]{1,0:T(8,128)(2,1)} %get-tuple-element.118.refs_0_, bf16[1024,1024]{1,0:T(8,128)(2,1)} %refs_1_.10, ...), custom_call_target="tpu_custom_call" | custom-call | flops 6979321856 | bytes 60000000 | tf_op jit(solution)/shard_map/ffn2_back/pallas_call | solution.py:557
  220.5 15.7 %conv_mid_back.1 = (bf16[1024,512]{1,0:T(8,128)(2,1)}, f32[32,256]{1,0:T(8,128)}) custom-call(f32[1024,256]{1,0:T(8,128)} %get-tuple-element.122.refs_0_, bf16[1024,256]{1,0:T(8,128)(2,1)} %get-tuple-element.123.refs_1_, f32[1024,256]{1,0:T(8,128)} %get-tuple-element.124.refs_2_, f32[8,1024]{1,0:T(8,128)} %get-tuple-element.125.refs_3_, ...), custom_call_target="tpu_custom_call" | custom-call | tf_op jit(solution)/shard_map/conv_mid_back/pallas_call | solution.py:855
  236.3 31.2 %conv_back.1 = (bf16[1024,1024]{1,0:T(8,128)(2,1)}, bf16[1024,256]{1,0:T(8,128)(2,1)}, f32[256,1024]{1,0:T(8,128)}, f32[8,1024]{1,0:T(8,128)}, bf16[2,4,2,128,25...) custom-call(bf16[1024,512]{1,0:T(8,128)(2,1)} %get-tuple-element.128, ...), custom_call_target="tpu_custom_call" | custom-call | flops 3221225472 | bytes 60000000 | tf_op jit(solution)/shard_map/conv_back/pallas_call | solution.py:557
  269.0 35.5 %attn_bwd.1 = (bf16[1024,256]{1,0:T(8,128)(2,1)}, bf16[1024,256]{1,0:T(8,128)(2,1)}, bf16[1024,256]{1,0:T(8,128)(2,1)}, f32[128,128]{1,0:T(8,128)}, bf16[2,2,2,1...) custom-call(bf16[1024,768]{1,0:T(8,128)(2,1)} %get-tuple-element.107, ...), custom_call_target="tpu_custom_call" | custom-call | flops 5368709120 | bytes 20000000 | tf_op jit(solution)/shard_map/attn_bwd/pallas_call | solution.py:1046
  304.6 2.6 pad_maximum_fusion.refs_0_
  307.2 34.0 %attn_back.1 = (bf16[1024,1024]{1,0:T(8,128)(2,1)}, bf16[1024,1024]{1,0:T(8,128)(2,1)}, f32[256,1024]{1,0:T(8,128)}, f32[8,1024]{1,0:T(8,128)}, bf16[3,2,2,128,2...) custom-call(bf16[1024,768]{1,0:T(8,128)(2,1)} %pad_maximum_fusion.re, ...), custom_call_target="tpu_custom_call" | custom-call | flops 5905580032 | bytes 60000000 | tf_op jit(solution)/shard_map/attn_back/pallas_call | solution.py:557
  341.2 99.0 %ffn1_back.1 = (f32[256,1024]{1,0:T(8,128)}, f32[8,1024]{1,0:T(8,128)}, f32[1024,128]{1,0:T(8,128)}, f32[128,1024]{1,0:T(8,128)}, f32[128,768]{1,0:T(8,128)}, /*...) custom-call(bf16[1024,1024]{1,0:T(8,128)(2,1)} %get-tuple-element.14, ...), custom_call_target="tpu_custom_call" | custom-call | flops 6442450944 | bytes 60000000 | tf_op jit(solution)/shard_map/ffn1_back/pallas_call | solution.py:557
  440.2 77.8 %publish.1 = (f32[256,1,1024]{2,1,0:T(1,128)}, f32[256,1,1024]{2,1,0:T(1,128)}, f32[128,1024]{1,0:T(8,128)}, f32[1024,128]{1,0:T(8,128)}, f32[128,3,256]{2,1,0:T...) custom-call(f32[256,1024]{1,0:T(8,128)} %get-tuple-element.116.refs_, ...), custom_call_target="tpu_custom_call" | custom-call | tf_op jit(solution)/shard_map/publish/pallas_call | solution.py:608
  518.0 1.9 copy.45
  519.9 0.9 slice_add_fusion
  521.5 1.6 fusion.2
  523.1 1.3 slice.42
  524.4 1.0 slice_reduce_fusion
  (27 shorter events, 8.2 us)
Async XLA Ops:
  4.8 19.7 %copy-start = (bf16[1024,3,256]{2,0,1:T(8,128)(2,1)S(1)}, bf16[1024,3,256]{2,0,1:T(8,128)(2,1)}, u32[]{:S(2)}) copy-start(bf16[1024,3,256]{2,0,1:T(8,128)(2,1)} %param.22) | copy-start | bytes 4718596
  26.9 31.1 %copy-start.3 = (bf16[73,64]{0,1:T(8,128)(2,1)S(1)}, bf16[73,64]{0,1:T(8,128)(2,1)}, u32[]{:S(2)}) copy-start(bf16[73,64]{0,1:T(8,128)(2,1)} %param.24) | copy-start | bytes 28036
  59.2 21.9 %copy-start.1 = (bf16[1024,2,256]{2,1,0:T(2,128)(2,1)S(1)}, bf16[1024,2,256]{2,1,0:T(2,128)(2,1)}, u32[]{:S(2)}) copy-start(bf16[1024,2,256]{2,1,0:T(2,128)(2,1)} %param.26) | copy-start | bytes 3145732
  82.3 30.1 %copy-start.2 = (bf16[31,256]{1,0:T(8,128)(2,1)S(1)}, bf16[31,256]{1,0:T(8,128)(2,1)}, u32[]{:S(2)}) copy-start(bf16[31,256]{1,0:T(8,128)(2,1)} %param.27) | copy-start | bytes 47620
  82.3 30.7 %copy-start.4 = (bf16[256]{0:T(256)(128)(2,1)S(1)}, bf16[256]{0:T(256)(128)(2,1)}, u32[]{:S(2)}) copy-start(bf16[256]{0:T(256)(128)(2,1)} %param.28) | copy-start | bytes 1540

commit v5 on v4

--- a/solution.py
+++ b/solution.py
@@ -119,6 +119,61 @@
     lax.fori_loop(0, pairs, add, 0)
 
 
+def weight(lhs, rhs, where, turned, deep=1, lo=0, pieces=None):
+    cols = sum(r.shape[1] for r in rhs) if isinstance(rhs, tuple) else rhs.shape[1]
+    return lhs, rhs, where, turned, deep, lo, cols // PIECE if pieces is None else pieces
+
+
+class Riders:
+    def __init__(self, grads):
+        self.plan = [(g.array.shape[0], g.bit, g.turned) for g in grads]
+        self.arrays = [g.array for g in grads]
+        self.after = [halved(g.array.shape, g.turned) for g in grads]
+        self.slots = sum(x[0] for x in self.plan)
+        self.scratch = [arriving(g.array.shape) for g in grads] * 2 + [pltpu.VMEM(a.shape, a.dtype) for a in self.after]
+        if grads:
+            self.scratch += [pltpu.SemaphoreType.DMA((self.slots,))] * 3 + [pltpu.SemaphoreType.DMA((len(grads),))]
+
+    def bind(self, srcs, outs, scratch):
+        n = len(self.plan)
+        sems = scratch[3 * n :]
+        holds, hops, slot = [], [], 0
+        for i, (pieces, bit, turned) in enumerate(self.plan):
+            landing, keep, half = scratch[i], scratch[n + i], scratch[2 * n + i]
+            holds.append(halving_keep(srcs[i], keep, bit, sems[3].at[i]))
+            flip = turned and landing.shape[2] % 128 == 0
+            for p in range(pieces):
+                move = halving_copy(srcs[i], landing, p, bit, sems[0], sems[1], slot)
+                store = pltpu.make_async_copy(region(half, p, PIECE, flip), region(outs[i], p, PIECE, flip), sems[2].at[slot])
+                hops.append((move, store, lambda q, j, keep=keep: keep[q, j], landing, half, p, turned))
+                slot += 1
+        self.holds, self.hops = holds, hops
+
+    def targets(self):
+        dp, mp = lax.axis_index("dp"), lax.axis_index("mp")
+        return [(place(dp, b)[1], mp) for b in sorted({x[1] for x in self.plan})]
+
+    def start(self):
+        for hold in self.holds:
+            hold.start()
+        for hop in self.hops:
+            hop[0].start()
+
+    def finish(self):
+        for hold in self.holds:
+            hold.wait()
+        for hop in self.hops:
+            hop[0].wait_recv()
+            halving_add(*hop[2:])
+            hop[1].start()
+        for hop in self.hops:
+            hop[0].wait_send()
+            hop[1].wait()
+
+    def results(self, outs):
+        return [Grad(a, b + 1, t) for a, (_, b, t) in zip(outs, self.plan)]
+
+
 def greet(targets):
     barrier = pltpu.get_barrier_semaphore()
     for to in targets:
@@ -138,12 +193,12 @@
     def add_in(array, direct=False):
         if direct:
             ins.append(array)
-            vm_ins.append(None)
             return len(ins) - 1
         if id(array) not in known:
-            known[id(array)] = len(ins)
-            ins.append(array)
-            vm_ins.append(pltpu.VMEM(array.shape, array.dtype))
+            group = array if isinstance(array, tuple) else (array,)
+            known[id(array)] = len(vm_ins)
+            vm_ins.append((len(ins), len(group), pltpu.VMEM((group[0].shape[0], sum(a.shape[1] for a in group)), group[0].dtype)))
+            ins.extend(group)
         return known[id(array)]
 
     out_slots = [0]
@@ -177,8 +232,8 @@
     s_o = [add_out((8, width), f32, 1) for _ in range(sums)]
     fixed_out = len(out_shape)
     plan, join_o = [], []
-    for lhs, rhs, where, turned, deep in dws:
-        shape = (rhs.shape[1] // PIECE, count // 2, 2, width // count, PIECE)
+    for lhs, rhs, where, turned, deep, lo, pieces in dws:
+        shape = (pieces, count // 2, 2, width // count, PIECE)
         if where == "join":
             join_o.append(add_out(shape, bf, shape[0]))
         else:
@@ -216,24 +271,32 @@
     load_sem = add_scratch(pltpu.SemaphoreType.DMA((len(ins),)))
     store_sem = add_scratch(pltpu.SemaphoreType.DMA((out_slots[0],)))
     n_in, n_out, n_scratch = len(ins), len(out_shape), len(scratch)
-    vm_at = {}
-    for i, item in enumerate(vm_ins):
-        if item is not None:
-            vm_at[i] = add_scratch(item)
+    vm_at = [add_scratch(item[2]) for item in vm_ins]
     vo_at = [add_scratch(pltpu.VMEM(o.shape, o.dtype)) for o in out_shape]
 
     def kernel(*refs):
         hbm_in, hbm_out, t = refs[:n_in], refs[n_in : n_in + n_out], refs[n_in + n_out :]
         vin = lambda i: t[vm_at[i]]
         vout = lambda i: t[vo_at[i]]
-        load = lambda i: pltpu.make_async_copy(hbm_in[i], vin(i), t[load_sem].at[i])
         waited = set()
+
+        def load(i):
+            first, parts, _ = vm_ins[i]
+            if parts == 1:
+                return [pltpu.make_async_copy(hbm_in[first], vin(i), t[load_sem].at[first])]
+            copies, at = [], 0
+            for n in range(first, first + parts):
+                cols = hbm_in[n].shape[1]
+                copies.append(pltpu.make_async_copy(hbm_in[n], vin(i).at[:, pl.ds(at, cols)], t[load_sem].at[n]))
+                at += cols
+            return copies
 
         def need(*items):
             for i in items:
                 if i not in waited:
                     waited.add(i)
-                    load(i).wait()
+                    for cp in load(i):
+                        cp.wait()
 
         dp, me = lax.axis_index("dp"), lax.axis_index("mp")
         core, chip = me % 2, me // 2
@@ -242,9 +305,9 @@
         diag = (1 - chip) * 2 + 1 - core
         bits = sorted({link[0] for ch in chains for link in ch[5]})
         meet = greet([(dp, sib), (dp, far)] + [(place(dp, b)[1], me) for b in bits])
-        for i in range(n_in):
-            if i in vm_at:
-                load(i).start()
+        for i in range(len(vm_ins)):
+            for cp in load(i):
+                cp.start()
 
         def part(ref, block, k):
             return ref.at[pl.ds(pl.multiple_of(block * rows + k * chunk, chunk), chunk)]
@@ -330,7 +393,7 @@
 
         def fill(k, where):
             n_far, n_join = 0, 0
-            for lhs, rhs, at_loop, turned, deep in dws:
+            for lhs, rhs, at_loop, turned, deep, lo, pieces in dws:
                 if at_loop == "join":
                     (a, b), o, c = dw_join[n_join], join_o[n_join], None
                     n_join += 1
@@ -342,8 +405,8 @@
                 dw = vout(o[0]) if c is None else t[chains[c][2]]
 
                 @pl.when(k < dw.shape[0])
-                def _(a=a, b=b, dw=dw, c=c, o=o if c is None else None):
-                    g = tn(vin(a)[...], vin(b)[:, pl.ds(pl.multiple_of(k * PIECE, PIECE), PIECE)])
+                def _(a=a, b=b, dw=dw, c=c, o=o if c is None else None, lo=lo):
+                    g = tn(vin(a)[...], vin(b)[:, pl.ds(pl.multiple_of((lo + k) * PIECE, PIECE), PIECE)])
                     dw[k] = g.astype(bf).reshape(dw.shape[1:])
                     if c is None:
                         store_piece(o, k, PIECE, False).start()
@@ -550,10 +613,10 @@
 
     flops = 0
     if leave:
-        flops += 2 * frames * leave[0].shape[1] * width
+        flops += 2 * frames * leave[1].shape[1 if leave[2] else 0] * width
     if enter:
         flops += 2 * frames * width * sum(c for c, _ in enter[4])
-    flops += sum(2 * frames * d[0].shape[1] * d[1].shape[1] for d in dws)
+    flops += sum(2 * frames * width * PIECE * d[6] for d in dws)
     outs = pl.pallas_call(
         kernel,
         in_specs=[in_hbm()] * n_in,
@@ -571,49 +634,75 @@
     return fixed + [fresh] + rest
 
 
-def publish(arrays, thirds):
-    out_shape, scratch = [], []
-    for i, a in enumerate(arrays):
-        if i in thirds:
-            shape = (a.shape[0], thirds[i], a.shape[1] // thirds[i])
-            scratch += [pltpu.VMEM(a.shape, a.dtype), pltpu.VMEM(shape, a.dtype)]
-            out_shape.append(jax.ShapeDtypeStruct(shape, a.dtype))
-        else:
-            out_shape.append(jax.ShapeDtypeStruct(a.shape, a.dtype))
-    scratch.append(pltpu.SemaphoreType.DMA((2, len(arrays))))
+def publish(ends, small, sizes, rel, total):
+    flat, outs, where = [], [], []
+    f32 = jnp.float32
+    for arrays, parts in ends:
+        rows = arrays[0].shape[0]
+        joined = len(arrays) > 1 and sizes[len(outs)]
+        shape = (rows, sum(a.shape[1] for a in arrays)) if not joined else (sum(a.shape[0] for a in arrays), arrays[0].shape[1])
+        where.append((len(flat), arrays, joined))
+        flat.extend(arrays)
+        outs.append((shape, (shape[0], parts, shape[1] // parts) if parts else None))
+    n, m = len(flat), len(ends)
+    width = small[0].shape[1]
+    taps = small[2].shape
+    split_at = [i for i in range(m) if outs[i][1]]
+    small_shapes = [(1, width)] * 5 + [(rel, HEAD), (taps[0] - 1, taps[1]), (1, taps[1]), (1, 128)]
 
     def kernel(*refs):
-        n = len(arrays)
-        src, dst, sem = refs[:n], refs[n : 2 * n], refs[-1]
-        bufs = list(refs[2 * n : -1])
-        first, second = [], []
-        for i in range(n):
-            if i in thirds:
-                flat, split = bufs.pop(0), bufs.pop(0)
-                first.append((pltpu.make_async_copy(src[i], flat, sem.at[0, i]), flat, split, i))
-            else:
-                second.append(pltpu.make_async_copy(src[i], dst[i], sem.at[1, i]))
-        for cp in [x[0] for x in first] + second:
-            cp.start()
-        for cp, flat, split, i in first:
+        src, small_in = refs[:n], refs[n : n + 3]
+        dst, small_out = refs[n + 3 : n + 3 + m], refs[n + 3 + m : n + 12 + m]
+        rest = refs[n + 12 + m :]
+        held, split = rest[:m], dict(zip(split_at, rest[m:-1]))
+        sem = rest[-1]
+        loads, stores = [], []
+        for i, (first, arrays, joined) in enumerate(where):
+            at, copies = 0, []
+            for k in range(len(arrays)):
+                ref = src[first + k]
+                size = ref.shape[0 if joined else 1]
+                part = held[i].at[pl.ds(at, size)] if joined else held[i].at[:, pl.ds(at, size)]
+                copies.append(pltpu.make_async_copy(ref, part, sem.at[first + k]))
+                at += size
+            loads.append(copies)
+            stores.append(pltpu.make_async_copy(split.get(i, held[i]), dst[i], sem.at[n + i]))
+        for copies in loads:
+            for cp in copies:
+                cp.start()
+        rows, table, tap = [r[...] for r in small_in]
+        for i in range(5):
+            small_out[i][...] = rows[i : i + 1]
+        small_out[5][...] = table[:rel, :HEAD] + table[:rel, HEAD:]
+        small_out[6][...] = tap[:-1]
+        small_out[7][...] = tap[-1:]
+        square = jnp.sum(rows, -1, keepdims=True) / total
+        lane = lax.broadcasted_iota(jnp.int32, (rows.shape[0], 128), 1)
+        row = lax.broadcasted_iota(jnp.int32, (rows.shape[0], 128), 0)
+        small_out[8][...] = jnp.sqrt(jnp.sum(jnp.where(row == lane + 5, square, 0.0), 0, keepdims=True))
+        for i in range(m):
+            for cp in loads[i]:
+                cp.wait()
+            if i in split:
+                cols = split[i].shape[2]
+                for j in range(split[i].shape[1]):
+                    split[i][:, j, :] = held[i][:, j * cols : (j + 1) * cols]
+            stores[i].start()
+        for cp in stores:
             cp.wait()
-            cols = split.shape[2]
-            for j in range(split.shape[1]):
-                split[:, j, :] = flat[:, j * cols : (j + 1) * cols]
-            second.append(pltpu.make_async_copy(split, dst[i], sem.at[1, i]))
-            second[-1].start()
-        for cp in second:
-            cp.wait()
-
+
+    vm = pl.BlockSpec(memory_space=pltpu.VMEM)
     return pl.pallas_call(
         kernel,
-        in_specs=[in_hbm()] * len(arrays),
-        out_specs=[in_hbm()] * len(arrays),
-        out_shape=out_shape,
-        scratch_shapes=scratch,
+        in_specs=[in_hbm()] * n + [vm] * 3,
+        out_specs=[in_hbm()] * m + [vm] * 9,
+        out_shape=[jax.ShapeDtypeStruct(o[1] or o[0], f32) for o in outs] + [jax.ShapeDtypeStruct(s, f32) for s in small_shapes],
+        scratch_shapes=[pltpu.VMEM(o[0], f32) for o in outs]
+        + [pltpu.VMEM(outs[i][1], f32) for i in split_at]
+        + [pltpu.SemaphoreType.DMA((n + m,))],
         compiler_params=pltpu.CompilerParams(vmem_limit_bytes=VMEM_LIMIT),
         name="publish",
-    )(*arrays)
+    )(*flat, *small)
 
 
 SPAN = 128
@@ -751,7 +840,7 @@
     )(glu, w_depth, gain_depth)
 
 
-def conv_mid_back(grad, slope, unit, stat, glu, sig, tail, w_depth, gain_depth, width, cid):
+def conv_mid_back(grad, slope, unit, stat, glu, sig, tail, w_depth, gain_depth, width, cid, grads):
     frames, chans = glu.shape
     taps = w_depth.shape[0]
     reach = taps - 1
@@ -759,11 +848,15 @@
     f32, bf = jnp.float32, jnp.bfloat16
     tiles, lanes = frames // SPAN, chans // 128
     ins = [grad, slope, unit, stat, w_depth, gain_depth, glu, sig, tail]
+    riders = Riders(grads)
+    n = len(grads)
 
     def kernel(*refs):
-        hbm, (pair_h, taps_h) = refs[:9], refs[9:11]
-        (grad_v, slope_v, unit_v, stat_v, w_v, g_v, pad, sig_v, tail_v, back, pair, taps_v, acc, gacc, sendbuf, landing, lsem, ssem, send, recv) = refs[11:]
-        meet = greet(group_targets())
+        hbm, ride_in, (pair_h, taps_h), ride_out = refs[:9], refs[9 : 9 + n], refs[9 + n : 11 + n], refs[11 + n : 11 + 2 * n]
+        refs = refs[2 * n :]
+        (grad_v, slope_v, unit_v, stat_v, w_v, g_v, pad, sig_v, tail_v, back, pair, taps_v, acc, gacc, sendbuf, landing, lsem, ssem, send, recv) = refs[11:31]
+        riders.bind(ride_in, ride_out, refs[31:])
+        meet = greet(group_targets() + riders.targets())
         dst = [grad_v, slope_v, unit_v, stat_v, w_v, g_v, pad.at[pl.ds(edge, frames)], sig_v, tail_v]
         loads = [pltpu.make_async_copy(h, d, lsem.at[i]) for i, (h, d) in enumerate(zip(hbm, dst))]
         for cp in loads:
@@ -785,8 +878,9 @@
             sendbuf[:, at] = to_rows(jnp.sum(du, -1, keepdims=True), jnp.sum(du * u, -1, keepdims=True))
             return c
 
+        meet()
+        riders.start()
         lax.fori_loop(0, tiles, first, 0)
-        meet()
         copies = exchange(sendbuf, landing, send, recv)
         for cp in copies:
             cp.start()
@@ -846,27 +940,29 @@
         last.start()
         for cp in copies:
             cp.wait_send()
+        riders.finish()
         for i in range(tiles):
             store(i).wait()
         last.wait()
 
     S = jax.ShapeDtypeStruct
     vm = pltpu.VMEM
-    return pl.pallas_call(
+    outs = pl.pallas_call(
         kernel,
-        in_specs=[in_hbm()] * 9,
-        out_specs=[in_hbm()] * 2,
-        out_shape=[S((frames, 2 * chans), bf), S((taps + 1, chans), f32)],
+        in_specs=[in_hbm()] * (9 + n),
+        out_specs=[in_hbm()] * (2 + n),
+        out_shape=[S((frames, 2 * chans), bf), S((taps + 1, chans), f32)] + riders.after,
         scratch_shapes=[
             vm((frames, chans), f32), vm((frames, chans), bf), vm((frames, chans), f32), vm((8, frames), f32),
             vm(w_depth.shape, f32), vm((1, chans), f32), vm((frames + edge, chans), f32), vm((frames, chans), bf), vm((frames, chans), bf),
             vm((frames + edge, chans), f32), vm((frames, 2 * chans), bf), vm((taps + 1, chans), f32), vm((taps * 8, chans), f32), vm((8, chans), f32),
             vm((8, frames), f32), vm((3, 8, frames), f32),
             pltpu.SemaphoreType.DMA((9,)), pltpu.SemaphoreType.DMA((tiles,)), pltpu.SemaphoreType.DMA((3,)), pltpu.SemaphoreType.DMA((3,)),
-        ],
+        ] + riders.scratch,
         compiler_params=pltpu.CompilerParams(collective_id=cid, has_side_effects=True, vmem_limit_bytes=VMEM_LIMIT),
         name="conv_mid_back",
-    )(*ins)
+    )(*ins, *riders.arrays)
+    return outs[0], outs[1], riders.results(outs[2:])
 
 
 def split_pair(x):
@@ -879,8 +975,20 @@
     left = lax.broadcasted_iota(jnp.int32, (rows, x.shape[1]), 1) < HEAD
     return jnp.where(left, x[:rows], x[rows:])
 
-def fwd_kernel(q_ref, k_ref, v_ref, rel_ref, mixed_ref, probs_ref, bias_ref):
+def spot_table(spots):
+    spot = lax.broadcasted_iota(jnp.int32, (spots, BQ), 0)
+    inner = jnp.clip(spot - REL_LEFT, 0, REL_LEFT + REL_RIGHT)
+    row = jnp.where(spot < 3 * BQ, inner, jnp.where(spot < 4 * BQ, 0, REL_LEFT + REL_RIGHT))
+    return (lax.broadcasted_iota(jnp.int32, (spots, BQ), 1) == row).astype(jnp.bfloat16)
+
+
+def fwd_kernel(q_ref, k_ref, v_ref, relb_ref, mixed_ref, probs_ref, bias_ref, rel_ref):
     ib = pl.program_id(1)
+
+    @pl.when((ib == 0) & (pl.program_id(0) == 0))
+    def _():
+        rel_ref[...] = nn(spot_table(5 * BQ), relb_ref[...]).astype(jnp.bfloat16)
+
     qs = split_pair(q_ref[...] * 0.125)
     s = nt(qs, k_ref[...])
     b = nt(qs, rel_ref[...])
@@ -904,35 +1012,38 @@
         probs_ref[0, :, jb * BQ : (jb + 1) * BQ] = (es[jb] * inv).astype(jnp.bfloat16)
     mixed_ref[...] = join_pair(nn(probs_ref[0], v_ref[...])).astype(jnp.bfloat16)
 
-def bwd_kernel(plan, *refs):
-    n = len(plan)
-    pairs_in, refs = refs[7 : 7 + n], refs[:7] + refs[7 + n :]
-    q_ref, k_ref, v_ref, relb_ref, hot_ref, probs_ref, do_ref, dq_ref, dk_ref, dv_ref, dt_ref = refs[:11]
-    grads_out, refs = refs[11 : 11 + n], refs[11 + n :]
-    tot_ref, dkt, dvt, dta, dz_ref = refs[:5]
-    landings, keeps, halves, sems = refs[5 : 5 + n], refs[5 + n : 5 + 2 * n], refs[5 + 2 * n : 5 + 3 * n], refs[5 + 3 * n :]
+def bwd_kernel(riders, *refs):
+    n = len(riders.plan)
+    q_ref, k_ref, v_ref, relb_ref, probs_ref, do_ref, db_h, mix_h = refs[:8]
+    ride_in = refs[8 : 8 + n]
+    dq_ref, dk_ref, dv_ref, dt_ref, dw_h = refs[8 + n : 13 + n]
+    ride_out = refs[13 + n : 13 + 2 * n]
+    tot_ref, dkt, dvt, dta, dz_ref, hot_ref, db_v, mix_v, dw_v, dw_land, dw_half, osem, psem = refs[13 + 2 * n : 26 + 2 * n]
+    riders.bind(ride_in, ride_out, refs[26 + 2 * n :])
     pr, ib, nb = pl.program_id(0), pl.program_id(1), pl.num_programs(1)
     dp, mp = lax.axis_index("dp"), lax.axis_index("mp")
-    hops, holds, slot = [], [], 0
-    for i, ((pieces, bit, turned), src, landing, keep, half, out) in enumerate(zip(plan, pairs_in, landings, keeps, halves, grads_out)):
-        holds.append(halving_keep(src, keep, bit, sems[2].at[i]))
-        flip = turned and landing.shape[2] % 128 == 0
+    loads = [pltpu.make_async_copy(db_h, db_v, osem.at[0]), pltpu.make_async_copy(mix_h, mix_v, osem.at[1])]
+    pieces = dw_v.shape[0]
+    hops = [halving_copy(dw_v, dw_land, p, 0, psem.at[0], psem.at[1], p) for p in range(pieces)]
+    flip = dw_land.shape[2] % 128 == 0
+    stores = [
+        pltpu.make_async_copy(region(dw_half, p, PIECE, flip), region(dw_h, p, PIECE, flip), psem.at[2, p]) for p in range(pieces)
+    ]
+
+    @pl.when((ib == 0) & (pr == 0))
+    def _():
+        meet = greet(sorted_targets(riders, dp, mp))
+        for cp in loads:
+            cp.start()
+        hot_ref[...] = spot_table(WIN)
+        meet()
+        riders.start()
+        for cp in loads:
+            cp.wait()
         for p in range(pieces):
-            move = halving_copy(src, landing, p, bit, sems[0], sems[1], slot)
-            store = pltpu.make_async_copy(region(half, p, PIECE, flip), region(out, p, PIECE, flip), sems[3].at[slot])
-            hops.append((move, store, lambda q, j, keep=keep: keep[q, j], landing, half, p, turned))
-            slot += 1
-
-    if hops:
-
-        @pl.when((ib == 0) & (pr == 0))
-        def _():
-            meet = greet([(place(dp, b)[1], mp) for b in sorted({x[1] for x in plan})])
-            for hold in holds:
-                hold.start()
-            meet()
-            for hop in hops:
-                hop[0].start()
+            g = tn(db_v[...], mix_v[:, p * PIECE : (p + 1) * PIECE])
+            dw_v[p] = g.astype(jnp.bfloat16).reshape(dw_v.shape[1:])
+            hops[p].start()
 
     @pl.when(ib == 0)
     def _():
@@ -986,30 +1097,29 @@
         dv_ref[...] = dvt[...].T.astype(jnp.bfloat16)
         dt_ref[...] = dta[...]
 
-    if hops:
-
-        @pl.when((ib == nb - 1) & (pr == pl.num_programs(0) - 1))
-        def _():
-            for hold in holds:
-                hold.wait()
-            for hop in hops:
-                hop[0].wait_recv()
-                halving_add(*hop[2:])
-                hop[1].start()
-            for hop in hops:
-                hop[0].wait_send()
-                hop[1].wait()
-
-def rel_tables(rel_table):
-    spots = jnp.arange(5 * BQ)
-    idx = jnp.where(spots < 3 * BQ, jnp.clip(spots - REL_LEFT, 0, REL_LEFT + REL_RIGHT), jnp.where(spots < 4 * BQ, 0, REL_LEFT + REL_RIGHT))
-    hot = (jnp.arange(BQ)[None, :] == idx[:, None]).astype(jnp.bfloat16)
+    @pl.when((ib == nb - 1) & (pr == pl.num_programs(0) - 1))
+    def _():
+        own, _ = place(lax.axis_index("dp"), 0)
+        for p in range(pieces):
+            hops[p].wait_recv()
+            halving_add(lambda q, j: dw_v[q, j, own], dw_land, dw_half, p, True)
+            stores[p].start()
+        riders.finish()
+        for p in range(pieces):
+            hops[p].wait_send()
+            stores[p].wait()
+
+
+def sorted_targets(riders, dp, mp):
+    return [(place(dp, b)[1], mp) for b in sorted({0} | {x[1] for x in riders.plan})]
+
+
+def wide_table(rel_table):
     padded = jnp.pad(rel_table, ((0, BQ - rel_table.shape[0]), (0, 0)))
-    padded = jnp.concatenate([padded, padded], 1)
-    ext = jnp.dot(hot, padded, preferred_element_type=jnp.float32).astype(jnp.bfloat16)
-    return ext, hot[:WIN], padded
-
-def attn_fwd(qkv, ext):
+    return jnp.concatenate([padded, padded], 1)
+
+
+def attn_fwd(qkv, rel):
     frames, cols = qkv.shape
     pairs = cols // 3 // 128
     nb = frames // BQ
@@ -1021,56 +1131,57 @@
             pl.BlockSpec((BQ, 128), lambda p, i: (i, p)),
             pl.BlockSpec((frames, 128), lambda p, i: (0, pairs + p)),
             pl.BlockSpec((frames, 128), lambda p, i: (0, 2 * pairs + p)),
-            pl.BlockSpec(ext.shape, lambda p, i: (0, 0)),
+            pl.BlockSpec(rel.shape, lambda p, i: (0, 0)),
         ],
         out_specs=[
             pl.BlockSpec((BQ, 128), lambda p, i: (i, p)),
             pl.BlockSpec((1, 2 * BQ, frames), lambda p, i: (p, i, 0)),
         ],
         out_shape=[jax.ShapeDtypeStruct((frames, cols // 3), bf), jax.ShapeDtypeStruct((pairs, 2 * frames, frames), bf)],
-        scratch_shapes=[pltpu.VMEM((2 * BQ, 5 * BQ), jnp.float32)],
+        scratch_shapes=[pltpu.VMEM((2 * BQ, 5 * BQ), jnp.float32), pltpu.VMEM((5 * BQ, 128), bf)],
         compiler_params=pltpu.CompilerParams(vmem_limit_bytes=VMEM_LIMIT),
         name="attn_fwd",
-    )(qkv, qkv, qkv, ext)
-
-def attn_bwd(qkv, padded, hot, probs, dmixed, grads, cid):
+    )(qkv, qkv, qkv, rel)
+
+def attn_bwd(qkv, rel, probs, dmixed, grad_rows, mixed, grads, cid):
     frames, cols = qkv.shape
     pairs = cols // 3 // 128
     nb = frames // BQ
     bf = jnp.bfloat16
+    count = lax.axis_size("dp")
     blk = pl.BlockSpec((BQ, 128), lambda p, i: (i, p))
     full = pl.BlockSpec((frames, 128), lambda p, i: (0, p))
-    plan = [(g.array.shape[0], g.bit, g.turned) for g in grads]
-    after = [halved(g.array.shape, g.turned) for g in grads]
-    slots = sum(x[0] for x in plan)
+    riders = Riders(grads)
+    width = grad_rows.shape[1]
+    shape = (mixed.shape[1] // PIECE, count // 2, 2, width // count, PIECE)
+    half = halved(shape, True)
+    vm = pltpu.VMEM
     outs = pl.pallas_call(
-        functools.partial(bwd_kernel, plan),
+        functools.partial(bwd_kernel, riders),
         grid=(pairs, nb),
         in_specs=[
             blk,
             pl.BlockSpec((frames, 128), lambda p, i: (0, pairs + p)),
             pl.BlockSpec((frames, 128), lambda p, i: (0, 2 * pairs + p)),
-            pl.BlockSpec(padded.shape, lambda p, i: (0, 0)),
-            pl.BlockSpec(hot.shape, lambda p, i: (0, 0)),
+            pl.BlockSpec(rel.shape, lambda p, i: (0, 0)),
             pl.BlockSpec((1, 2 * BQ, frames), lambda p, i: (p, i, 0)),
             blk,
         ]
-        + [in_hbm()] * len(grads),
-        out_specs=[blk, full, full, pl.BlockSpec((128, 128), lambda p, i: (0, 0))] + [in_hbm()] * len(after),
-        out_shape=[jax.ShapeDtypeStruct((frames, cols // 3), bf)] * 3 + [jax.ShapeDtypeStruct((128, 128), jnp.float32)] + after,
-        scratch_shapes=[pltpu.VMEM((2 * BQ, 5 * BQ), jnp.float32), pltpu.VMEM((128, frames), jnp.float32), pltpu.VMEM((128, frames), jnp.float32),
-                        pltpu.VMEM((128, 128), jnp.float32), pltpu.VMEM((2 * BQ, frames), bf)]
-        + [arriving(g.array.shape) for g in grads]
-        + [arriving(g.array.shape) for g in grads]
-        + [pltpu.VMEM(a.shape, a.dtype) for a in after]
-        + ([pltpu.SemaphoreType.DMA((slots,))] * 2 + [pltpu.SemaphoreType.DMA((len(grads),)), pltpu.SemaphoreType.DMA((slots,))] if grads else []),
-        compiler_params=pltpu.CompilerParams(
-            vmem_limit_bytes=VMEM_LIMIT, collective_id=cid, has_side_effects=True
-        ),
+        + [in_hbm()] * (2 + len(grads)),
+        out_specs=[blk, full, full, pl.BlockSpec((128, 128), lambda p, i: (0, 0))] + [in_hbm()] * (1 + len(grads)),
+        out_shape=[jax.ShapeDtypeStruct((frames, cols // 3), bf)] * 3 + [jax.ShapeDtypeStruct((128, 128), jnp.float32), half] + riders.after,
+        scratch_shapes=[
+            vm((2 * BQ, 5 * BQ), jnp.float32), vm((128, frames), jnp.float32), vm((128, frames), jnp.float32),
+            vm((128, 128), jnp.float32), vm((2 * BQ, frames), bf), vm((WIN, BQ), bf),
+            vm(grad_rows.shape, bf), vm(mixed.shape, bf), vm(shape, bf), arriving(shape), vm(half.shape, half.dtype),
+            pltpu.SemaphoreType.DMA((2,)), pltpu.SemaphoreType.DMA((3, shape[0])),
+        ]
+        + riders.scratch,
+        compiler_params=pltpu.CompilerParams(vmem_limit_bytes=VMEM_LIMIT, collective_id=cid, has_side_effects=True),
         cost_estimate=pl.CostEstimate(flops=20 * frames * frames * 128 * pairs, bytes_accessed=20_000_000, transcendentals=0),
         name="attn_bwd",
-    )(qkv, qkv, qkv, padded, hot, probs, dmixed, *[g.array for g in grads])
-    return list(outs[:4]) + [[Grad(a, b + 1, t) for a, (_, b, t) in zip(outs[4:], plan)]]
+    )(qkv, qkv, qkv, rel, probs, dmixed, grad_rows, mixed, *riders.arrays)
+    return list(outs[:4]) + [[Grad(outs[4], 1, True)] + riders.results(outs[5:])]
 
 
 def body(
@@ -1098,10 +1209,15 @@
     f32, bf = jnp.float32, jnp.bfloat16
     s0 = features.reshape(rows, width)
     seed = cotangent.reshape(rows, width)
-    gains = jnp.stack([gain_ffn1, gain_attn, gain_conv, gain_ffn2, gain_final] + [gain_final] * 3).astype(f32)
+    row = jnp.arange(8)[:, None]
+    gains = sum(
+        jnp.where(row == i, g.astype(f32)[None], 0.0)
+        for i, g in enumerate((gain_ffn1, gain_attn, gain_conv, gain_ffn2, gain_final))
+    )
     flat_qkv = w_qkv.reshape(width, -1)
     flat_conv = w_conv_in.reshape(width, -1)
     units = w1_in.shape[1]
+    half = units // PIECE // 2
     dp_count = lax.axis_size("dp")
     done = dp_count.bit_length() - 1
     pending = lambda items: [g for g in items if g.bit < done]
@@ -1170,8 +1286,8 @@
         enter=(flat_qkv, False, plain_out, (), ((flat_qkv.shape[1], bf),)),
         junction=forward(0.5, 1), row_in=(s0,), row_out=(f32,), sums=1,
     )
-    ext, hot, padded = rel_tables(rel_table)
-    mixed, probs = attn_fwd(qkv, ext)
+    wide = wide_table(rel_table)
+    mixed, probs = attn_fwd(qkv, wide)
     a3, glu, sig, tail, s2, sq2, _ = stage(
         "attn_out", 2, rows, width, dp_count, gains, leave=(mixed, w_attn_out, False),
         enter=(flat_conv, False, glu_out, (), ((chans, f32), (chans, bf), (chans, bf))),
@@ -1190,31 +1306,37 @@
         enter=(w2_out, True, slope_out, (slope2,), ((units, bf),)),
         junction=turn, row_in=(s3, seed), row_out=(f32, f32), sums=3,
     )
-    db3, de3, grad3, dg2, (gw2_in, gw2_out) = stage(
+    db3, de3, grad3, dg2, (ga_in, gb_in, gw2_out) = stage(
         "ffn2_back", 5, rows, width, dp_count, gains, leave=(dh2, w2_in, True),
-        enter=(w_conv_out, True, plain_out, (), ((chans, f32),)), dws=((a4, dh2, "join", False, 0), (db4, act2, "far", True, 1)),
+        enter=(w_conv_out, True, plain_out, (), ((chans, f32),)), dws=(
+            weight(a4, dh2, "join", False, 1, 0, half),
+            weight(a4, dh2, "join", False, 1, half, units // PIECE - half),
+            weight(db4, act2, "far", True),
+        ),
         junction=backward(1.0, 3), row_in=(grad4, s3), row_out=(f32,), sums=1,
     )
-    dpaired, tap_sums = conv_mid_back(de3, slope3, depth_unit, depth_stat, glu, sig, tail, depth_taps, depth_gain, width, 11)
-    db2, dmixed, grad2, dgc, (gconv_in, gconv_out, gw2_in, gw2_out) = stage(
+    dpaired, tap_sums, (gw2_out, ga_in) = conv_mid_back(
+        de3, slope3, depth_unit, depth_stat, glu, sig, tail, depth_taps, depth_gain, width, 11, [gw2_out, ga_in]
+    )
+    db2, dmixed, grad2, dgc, (gconv_in, gconv_out, gb_in, gw2_out, ga_in) = stage(
         "conv_back", 6, rows, width, dp_count, gains, leave=(dpaired, flat_conv, True),
-        enter=(w_attn_out, True, plain_out, (), ((w_attn_out.shape[0], bf),)), dws=((a3, dpaired, "join", False, 0), (db3, act3, "join", True, 0)), grads=(gw2_in, gw2_out),
+        enter=(w_attn_out, True, plain_out, (), ((w_attn_out.shape[0], bf),)), dws=(weight(a3, dpaired, "far", False), weight(db3, act3, "far", True)), grads=(gb_in, gw2_out, ga_in),
         junction=backward(1.0, 2), row_in=(grad3, s2), row_out=(f32,), sums=1,
     )
-    dq, dk, dv, dt, (gconv_in, gconv_out, gw2_in, gw2_out) = attn_bwd(
-        qkv, padded, hot, probs, dmixed, [gconv_in, gconv_out, gw2_in, gw2_out], 9
+    dq, dk, dv, dt, (gattn, gb_in, ga_in, gconv_in, gconv_out) = attn_bwd(
+        qkv, wide, probs, dmixed, db2, mixed, [gb_in, ga_in, gconv_in, gconv_out], 9
     )
-    dqkv = jnp.concatenate([dq, dk, dv], 1)
-    db1, dh1, grad1, dga, (gqkv, gattn, gconv_in, gconv_out, gw2_in) = stage(
+    dqkv = (dq, dk, dv)
+    db1, dh1, grad1, dga, (gqkv, gconv_in, gconv_out, gb_in) = stage(
         "attn_back", 7, rows, width, dp_count, gains, leave=(dqkv, flat_qkv, True),
-        enter=(w1_out, True, slope_out, (slope1,), ((units, bf),)), dws=((a2, dqkv, "far", False, 1), (db2, mixed, "far", True, 1)), grads=(gconv_in, gconv_out, gw2_in),
+        enter=(w1_out, True, slope_out, (slope1,), ((units, bf),)), dws=(weight(a2, dqkv, "far", False, 2),), grads=(gconv_in, gconv_out, gb_in),
         junction=backward(0.5, 1), row_in=(grad2, s1), row_out=(f32,), sums=1,
     )
-    early = [gqkv, gattn, gconv_in, gconv_out, gw2_in, gw2_out]
+    early = [gqkv, gattn, gconv_in, gconv_out, ga_in, gb_in, gw2_out]
     waiting = pending(early)
     grad0, dg1, ends, small_rows, table, taps_end = stage(
         "ffn1_back", 8, rows, width, dp_count, gains, leave=(dh1, w1_in, True),
-        dws=((db1, act1, "far", True, 1), (a1, dh1, "near", False, 1)), grads=waiting,
+        dws=(weight(db1, act1, "far", True), weight(a1, dh1, "near", False)), grads=waiting,
         small=[dga, dgc, dg2, dgf, sq1, sq2, sq3, sq4, sq5, dt, tap_sums],
         junction=backward(1.0, 0), row_in=(grad1, s0), row_out=(f32,), sums=1,
     )
@@ -1226,36 +1348,43 @@
         flip = item.turned and item.array.shape[0] * dp_count == width and (width // dp_count) % 128 != 0
         return item.array.T if flip else item.array
 
-    ends = [output, grad0] + [finish(g) for g in (gw1_in, gw1_out, gqkv, gattn, gconv_in, gconv_out, gw2_in, gw2_out)]
-    ends = publish(ends + [small_rows, table, taps_end], {0: 1, 1: 1, 4: 3, 6: 2})
-    small_rows, table, taps_end = ends[10:]
-    rel = rel_table.shape[0]
-    table_sum = table[:rel, :HEAD] + table[:rel, HEAD:]
-    depth_sum, depth_gain_sum = taps_end[:-1], taps_end[-1]
-    total_squares = jnp.sum(small_rows[5:10], -1)
-    token_total = rows * lax.axis_size("mp") * lax.axis_size("dp")
-    rms_stats = jnp.sqrt(total_squares / (token_total * width))
-    whole = lambda x: x.reshape(local_frames, clip_count, width)
+    token_total = rows * lax.axis_size("mp") * dp_count
+    ends = [
+        ([output], 1),
+        ([grad0], 1),
+        ([finish(gw1_in)], 0),
+        ([finish(gw1_out)], 0),
+        ([finish(gqkv)], 3),
+        ([finish(gattn)], 0),
+        ([finish(gconv_in)], 2),
+        ([finish(gconv_out)], 0),
+        ([finish(ga_in), finish(gb_in)], 0),
+        ([finish(gw2_out)], 0),
+    ]
+    done_ends = publish(ends, [small_rows, table, taps_end], {8: False}, rel_table.shape[0], float(token_total * width))
+    (output, grad0, gw1_in, gw1_out, gqkv, gattn, gconv_in, gconv_out, gw2_in, gw2_out) = done_ends[:10]
+    *gain_sums, table_sum, depth_sum, depth_gain_sum, rms_stats = done_ends[10:]
+    gain_sums = [g[0] for g in gain_sums]
     return (
-        whole(ends[0]),
-        whole(ends[1]),
-        ends[2],
-        ends[3],
-        small_rows[0],
-        ends[4],
-        ends[5],
+        output,
+        grad0,
+        gw1_in,
+        gw1_out,
+        gain_sums[0],
+        gqkv,
+        gattn,
         table_sum,
-        small_rows[1],
-        ends[6],
+        gain_sums[1],
+        gconv_in,
         depth_sum,
-        depth_gain_sum,
-        ends[7],
-        small_rows[2],
-        ends[8],
-        ends[9],
-        small_rows[3],
-        small_rows[4],
-        rms_stats,
+        depth_gain_sum[0],
+        gconv_out,
+        gain_sums[2],
+        gw2_in,
+        gw2_out,
+        gain_sums[3],
+        gain_sums[4],
+        rms_stats[0, :5],
     )
 
 

time: 527 us -> 455 us (0.86)
  Pallas kernels: 503 us -> 436 us
    pallas_call x3, Pallas kernels: 129 us -> 57.5 us  [the longest x1 34.5 us: attn_bwd(): pl.pallas_call(functools.partial(bwd_kernel, riders), grid=(pairs, nb), i...]
where the time goes in v5:
time: 455 us; the launch traced here: 454 us
  Pallas kernels  436 us (96%)
  local copies, waits for them, and re-layouts  10.2 us (2%)
  other arithmetic  7.5 us (2%)
    pallas_call x9, Pallas kernels, stage(): pl.pallas_call(kernel, in_specs=[in_hbm()] * n_in, out_specs=[in_hbm()] *...  343 us
    pallas_call x1, Pallas kernels, attn_bwd(): pl.pallas_call(functools.partial(bwd_kernel, riders), grid=(pairs, nb), i...  34.5 us
    pallas_call x1, Pallas kernels, attn_fwd(): pl.pallas_call(fwd_kernel, grid=(pairs, nb), in_specs=[pl.BlockSpec((BQ,...  22.1 us
    pallas_call x1, Pallas kernels, conv_mid_back(): pl.pallas_call(kernel, in_specs=[in_hbm()] * (9 + n), out_specs=[in_hbm()...  17.6 us
    pallas_call x1, Pallas kernels, conv_mid(): pl.pallas_call(kernel, in_specs=[in_hbm()] * 3, out_specs=[in_hbm()] * 4,...  12.5 us

profile of v5, /device:TPU:0, one launch (start us, length us, event | category | flops | bytes accessed | tf_op | source)
XLA Modules:
  0.0 454.0 jit_solution(17134861669373653386)
XLA Ops:
  0.7 1.3 broadcast_in_dim.88
  6.1 0.8 copy.43
  7.0 0.7 pad_maximum_fusion.relb_ref.refs_3_
  7.7 1.3 convert_element_type.26.w_h.refs_4_
  9.0 2.4 copy.47
  11.4 0.9 copy.41
  12.3 1.6 copy.42.refs_4_.refs_3_
  13.9 19.6 %ffn1_in.1 = (bf16[1024,1024]{1,0:T(8,128)(2,1)}, bf16[1024,1024]{1,0:T(8,128)(2,1)}, bf16[1024,1024]{1,0:T(8,128)(2,1)}) custom-call(f32[8,1024]{1,0:T(8,128)} %select_add_fusion.refs_0_.refs_2_.refs_4_.refs_5_, bf16[256,1024]{1,0:T(8,128)(2,1)} %bitcast.21, bf16[1024,1024]{1,0:T(8,128)(2,1)} %refs_1_.11), custom_call_target="tpu_custom_call" | custom-call | flops 4294967296 | bytes 60000000 | tf_op jit(solution)/shard_map/ffn1_in/pallas_call | solution.py:620
  33.5 31.3 %ffn1_out.1 = (bf16[1024,1024]{1,0:T(8,128)(2,1)}, bf16[1024,768]{1,0:T(8,128)(2,1)}, f32[256,1024]{1,0:T(8,128)}, f32[8,1024]{1,0:T(8,128)}) custom-call(bf16[1024,1024]{1,0:T(8,128)(2,1)} %get-tuple-element.114.refs_0_.refs_3_, bf16[1024,1024]{1,0:T(8,128)(2,1)} %refs_8_.5, f32[8,1024]{1,0:T(8,128)} %select_add_fusion.refs_0_.refs_2_.refs_4_.refs_5_, ...), custom_call_target="tpu_custom_call" | custom-call | flops 3758096384 | bytes 60000000 | tf_op jit(solution)/shard_map/ffn1_out/pallas_call | solution.py:620
  64.8 22.1 %attn_fwd.1 = (bf16[1024,256]{1,0:T(8,128)(2,1)}, bf16[2,2048,1024]{2,1,0:T(8,128)(2,1)}) custom-call(bf16[1024,768]{1,0:T(8,128)(2,1)} %get-tuple-element.115.q_ref.k_ref.v_ref.refs_0_.refs_1_.refs_2_, bf16[1024,768]{1,0:T(8,128)(2,1)} %get-tuple-element.115.q_ref.k_ref.v_ref.refs_0_.refs_1_.refs_2_, ...), custom_call_target="tpu_custom_call" | custom-call | tf_op jit(solution)/shard_map/attn_fwd/pallas_call | solution.py:1127
  86.9 30.0 %attn_out.1 = (bf16[1024,1024]{1,0:T(8,128)(2,1)}, f32[1024,256]{1,0:T(8,128)}, bf16[1024,256]{1,0:T(8,128)(2,1)}, bf16[1024,256]{1,0:T(8,128)(2,1)}, f32[256,1024]{1,0:T(8,128)}, /*index=5*/f32[8,1024]{1,0:T(8,128)}) custom-call(bf16[1024,256]{1,0:T(8,128)(2,1)} %get-tuple-element.116.refs_0_.refs_7_, bf16[256,1024]{1,0:T(8,128)(2,1)} %refs_8_.4, ...), custom_call_target="tpu_custom_call" | custom-call | flops 2147483648 | bytes 60000000 | tf_op jit(solution)/shard_map/attn_out/pallas_call | solution.py:620
  116.9 12.5 %conv_mid.1 = (bf16[1024,256]{1,0:T(8,128)(2,1)}, bf16[1024,256]{1,0:T(8,128)(2,1)}, f32[1024,256]{1,0:T(8,128)}, f32[8,1024]{1,0:T(8,128)}) custom-call(f32[1024,256]{1,0:T(8,128)} %get-tuple-element.118.glu_h.refs_6_, f32[31,256]{1,0:T(8,128)} %convert_element_type.26.w_h.refs_4_, f32[1,256]{1,0:T(1,128)} %bitcast.18), custom_call_target="tpu_custom_call" | custom-call | tf_op jit(solution)/shard_map/conv_mid/pallas_call | solution.py:827
  129.3 30.0 %conv_out.1 = (bf16[1024,1024]{1,0:T(8,128)(2,1)}, bf16[1024,1024]{1,0:T(8,128)(2,1)}, bf16[1024,1024]{1,0:T(8,128)(2,1)}, f32[256,1024]{1,0:T(8,128)}, f32[8,1024]{1,0:T(8,128)}) custom-call(bf16[1024,256]{1,0:T(8,128)(2,1)} %get-tuple-element.119.refs_0_.refs_4_, bf16[256,1024]{1,0:T(8,128)(2,1)} %refs_8_.3, ...), custom_call_target="tpu_custom_call" | custom-call | flops 4831838208 | bytes 60000000 | tf_op jit(solution)/shard_map/conv_out/pallas_call | solution.py:620
  159.4 31.6 %ffn2_out.1 = (bf16[1024,1024]{1,0:T(8,128)(2,1)}, bf16[1024,1024]{1,0:T(8,128)(2,1)}, f32[256,1024]{1,0:T(8,128)}, f32[256,1024]{1,0:T(8,128)}, f32[8,1024]{1,0...) custom-call(bf16[1024,1024]{1,0:T(8,128)(2,1)} %get-tuple-element.121.refs_0_.refs_3_, bf16[1024,1024]{1,0:T(8,128)(2,1)} %refs_1_.9, ...), custom_call_target="tpu_custom_call" | custom-call | flops 4294967296 | bytes 60000000 | tf_op jit(solution)/shard_map/ffn2_out/pallas_call | solution.py:620
  191.0 32.9 %ffn2_back.1 = (bf16[1024,1024]{1,0:T(8,128)(2,1)}, f32[1024,256]{1,0:T(8,128)}, f32[256,1024]{1,0:T(8,128)}, f32[8,1024]{1,0:T(8,128)}, bf16[2,4,2,128,256]{4,3...) custom-call(bf16[1024,1024]{1,0:T(8,128)(2,1)} %get-tuple-element.126.refs_0_, ...), custom_call_target="tpu_custom_call" | custom-call | flops 6979321856 | bytes 60000000 | tf_op jit(solution)/shard_map/ffn2_back/pallas_call | solution.py:620
  223.9 17.6 %conv_mid_back.1 = (bf16[1024,512]{1,0:T(8,128)(2,1)}, f32[32,256]{1,0:T(8,128)}, bf16[4,1,2,128,256]{4,3,2,1,0:T(8,128)(2,1)}, bf16[2,2,2,128,256]{4,3,2,1,0:T(8,128)(2,1)}) custom-call(f32[1024,256]{1,0:T(8,128)} %get-tuple-element.130.refs_0_, bf16[1024,256]{1,0:T(8,128)(2,1)} %get-tuple-element.131.refs_1_, f32[1024,256]{1,0:T(8,128)} %get-tuple-element.132.refs_2_, ...), custom_call_target="tpu_custom_call" | custom-call | tf_op jit(solution)/shard_map/conv_mid_back/pallas_call | solution.py:950
  241.5 35.3 %conv_back.1 = (bf16[1024,1024]{1,0:T(8,128)(2,1)}, bf16[1024,256]{1,0:T(8,128)(2,1)}, f32[256,1024]{1,0:T(8,128)}, f32[8,1024]{1,0:T(8,128)}, bf16[2,2,2,128,25...) custom-call(bf16[1024,512]{1,0:T(8,128)(2,1)} %get-tuple-element.138, ...), custom_call_target="tpu_custom_call" | custom-call | flops 3221225472 | bytes 60000000 | tf_op jit(solution)/shard_map/conv_back/pallas_call | solution.py:620
  276.9 34.5 %attn_bwd.1 = (bf16[1024,256]{1,0:T(8,128)(2,1)}, bf16[1024,256]{1,0:T(8,128)(2,1)}, bf16[1024,256]{1,0:T(8,128)(2,1)}, f32[128,128]{1,0:T(8,128)}, bf16[1,2,2,1...) custom-call(bf16[1024,768]{1,0:T(8,128)(2,1)} %get-tuple-element.115, ...), custom_call_target="tpu_custom_call" | custom-call | flops 5368709120 | bytes 20000000 | tf_op jit(solution)/shard_map/attn_bwd/pallas_call | solution.py:1159
  311.3 39.5 %attn_back.1 = (bf16[1024,1024]{1,0:T(8,128)(2,1)}, bf16[1024,1024]{1,0:T(8,128)(2,1)}, f32[256,1024]{1,0:T(8,128)}, f32[8,1024]{1,0:T(8,128)}, bf16[3,1,2,128,2...) custom-call(bf16[1024,256]{1,0:T(8,128)(2,1)} %get-tuple-element.151.refs_0_, ...), custom_call_target="tpu_custom_call" | custom-call | flops 5368709120 | bytes 60000000 | tf_op jit(solution)/shard_map/attn_back/pallas_call | solution.py:620
  350.8 93.2 %ffn1_back.1 = (f32[256,1024]{1,0:T(8,128)}, f32[8,1024]{1,0:T(8,128)}, f32[1024,128]{1,0:T(8,128)}, f32[128,1024]{1,0:T(8,128)}, f32[128,768]{1,0:T(8,128)}, /*...) custom-call(bf16[1024,1024]{1,0:T(8,128)(2,1)} %get-tuple-element.160.refs_0_, ...), custom_call_target="tpu_custom_call" | custom-call | flops 6442450944 | bytes 60000000 | tf_op jit(solution)/shard_map/ffn1_back/pallas_call | solution.py:620
  444.1 5.5 %publish.1 = (f32[256,1,1024]{2,1,0:T(1,128)}, f32[256,1,1024]{2,1,0:T(1,128)}, f32[128,1024]{1,0:T(8,128)}, f32[1024,128]{1,0:T(8,128)}, f32[128,3,256]{2,1,0:T...) custom-call(f32[256,1024]{1,0:T(8,128)} %get-tuple-element.124.refs_, ...), custom_call_target="tpu_custom_call" | custom-call | tf_op jit(solution)/shard_map/publish/pallas_call | solution.py:695
  449.5 1.2 slice_bitcast_fusion
  450.7 1.5 copy.46
  452.2 1.9 copy.45
  (12 shorter events, 4.2 us)
Async XLA Ops:
  0.7 10.8 %copy-start = (bf16[1024,3,256]{2,0,1:T(8,128)(2,1)S(1)}, bf16[1024,3,256]{2,0,1:T(8,128)(2,1)}, u32[]{:S(2)}) copy-start(bf16[1024,3,256]{2,0,1:T(8,128)(2,1)} %param.22) | copy-start | bytes 4718596

commit v6 on v5

--- a/solution.py
+++ b/solution.py
@@ -26,6 +26,7 @@
 
 MESH = pl.DeviceIdType.MESH
 CHUNKS = 4
+TABLE_ROWS = 40
 PIECE = 256
 VMEM_LIMIT = 58 << 20
 
@@ -122,6 +123,19 @@
 def weight(lhs, rhs, where, turned, deep=1, lo=0, pieces=None):
     cols = sum(r.shape[1] for r in rhs) if isinstance(rhs, tuple) else rhs.shape[1]
     return lhs, rhs, where, turned, deep, lo, cols // PIECE if pieces is None else pieces
+
+
+def flat_shape(array):
+    if isinstance(array, tuple):
+        return array[0].shape[0], sum(a.shape[1] for a in array)
+    if len(array.shape) == 3:
+        return array.shape[1], array.shape[0] * array.shape[2]
+    return array.shape
+
+
+def gain_row(ref, i, width):
+    first = i * width // 128
+    return jnp.concatenate([ref[first + j : first + j + 1, :] for j in range(width // 128)], 1)
 
 
 class Riders:
@@ -181,11 +195,10 @@
     return lambda: pl.semaphore_wait(barrier, len(targets))
 
 
-def stage(name, cid, rows, width, count, gains, *, leave=None, enter=None, dws=(), grads=(), small=None, junction, row_in=(), row_out=(), sums=0):
+def stage(name, cid, rows, width, count, gains, *, leave=None, enter=None, dws=(), grads=(), small=None, last=False, junction, row_in=(), row_out=(), sums=0):
     chunk = rows // CHUNKS
     frames = rows * 4
     bits_all = count.bit_length() - 1
-    last = small is not None
     f32, bf = jnp.float32, jnp.bfloat16
     ins, vm_ins, out_shape, scratch = [], [], [], []
     known = {}
@@ -197,7 +210,7 @@
         if id(array) not in known:
             group = array if isinstance(array, tuple) else (array,)
             known[id(array)] = len(vm_ins)
-            vm_ins.append((len(ins), len(group), pltpu.VMEM((group[0].shape[0], sum(a.shape[1] for a in group)), group[0].dtype)))
+            vm_ins.append((len(ins), len(group), pltpu.VMEM(flat_shape(array), group[0].dtype)))
             ins.extend(group)
         return known[id(array)]
 
@@ -214,18 +227,20 @@
         return len(scratch) - 1
 
     if leave:
+        front_in = [(add_in(d[0]), add_in(d[1])) for d in dws if d[2] == "front"]
         x_i, wl_i = add_in(leave[0]), add_in(leave[1])
         leave_s = [add_scratch(pltpu.VMEM((rows, width), f32)) for _ in range(2)]
         leave_s += [add_scratch(pltpu.VMEM((rows, width), bf)) for _ in range(6)]
-        wl_s = add_scratch(pltpu.VMEM(leave[1].shape[::-1], bf)) if leave[2] else None
+        wl_s = add_scratch(pltpu.VMEM(flat_shape(leave[1])[::-1], bf)) if leave[2] else None
     dw_in = [(add_in(d[0]), add_in(d[1])) for d in dws if d[2] != "join"]
     gains_i = add_in(gains)
+    gain_s = add_scratch(pltpu.VMEM((8, width), f32))
     row_i = [add_in(r) for r in row_in]
     dw_join = [(add_in(d[0]), add_in(d[1])) for d in dws if d[2] == "join"]
     if enter:
         we_i = add_in(enter[0])
         extra_i = [add_in(e) for e in enter[3]]
-        we_s = add_scratch(pltpu.VMEM(enter[0].shape[::-1], bf)) if enter[1] else None
+        we_s = add_scratch(pltpu.VMEM(flat_shape(enter[0])[::-1], bf)) if enter[1] else None
         all_o = add_out((frames, width), bf, 4 * CHUNKS)
         e_o = [add_out((frames, c), d, 4 * CHUNKS) for c, d in enter[4]]
     r_o = [add_out((rows, width), d, CHUNKS) for d in row_out]
@@ -258,13 +273,20 @@
             slots += pieces
             shape = nxt.shape
         chains.append((pieces, turned, src_s, src_i, keep_s, links))
-    if last:
-        small_i = [add_in(s) for s in small]
-        small_shapes = [(16, width), small[-2].shape, small[-1].shape]
+    if small:
+        vectors_in, table_in, taps_in = small
+        vector_i = [add_in(v) for v in vectors_in]
+        small_shapes = [(1 + len(vectors_in), width)]
+        if table_in is not None:
+            table_i, taps_i = add_in(table_in), add_in(taps_in)
+            small_shapes += [(TABLE_ROWS, 128), taps_in.shape]
         small_o = [add_out(s, f32, 1) for s in small_shapes]
-        hops = bits_all + 2
-        land_small = [add_scratch(pltpu.VMEM((hops,) + s, f32)) for s in small_shapes]
-        small_sems = [add_scratch(pltpu.SemaphoreType.DMA((3, hops))) for _ in range(2)]
+        if last:
+            course = ["sib", "far"] + list(range(bits_all - 1, -1, -1))
+        else:
+            course = list(range(bits_all - 1, -1, -1)) + ["sib", "far"]
+        land_small = [add_scratch(pltpu.VMEM((len(course),) + s, f32)) for s in small_shapes]
+        small_sems = [add_scratch(pltpu.SemaphoreType.DMA((3, len(course)))) for _ in range(2)]
     if slots:
         grad_sems = [add_scratch(pltpu.SemaphoreType.DMA((slots,))) for _ in range(2)]
     ring_sems = [add_scratch(pltpu.SemaphoreType.DMA((6, CHUNKS))) for _ in range(2)]
@@ -282,6 +304,12 @@
 
         def load(i):
             first, parts, _ = vm_ins[i]
+            if len(hbm_in[first].shape) == 3:
+                slabs, _, cols = hbm_in[first].shape
+                return [
+                    pltpu.make_async_copy(hbm_in[first].at[n], vin(i).at[:, pl.ds(n * cols, cols)], t[load_sem].at[first])
+                    for n in range(slabs)
+                ]
             if parts == 1:
                 return [pltpu.make_async_copy(hbm_in[first], vin(i), t[load_sem].at[first])]
             copies, at = [], 0
@@ -303,7 +331,7 @@
         sib = chip * 2 + 1 - core
         far = (1 - chip) * 2 + core
         diag = (1 - chip) * 2 + 1 - core
-        bits = sorted({link[0] for ch in chains for link in ch[5]})
+        bits = sorted({link[0] for ch in chains for link in ch[5]} | set(range(bits_all) if small else ()))
         meet = greet([(dp, sib), (dp, far)] + [(place(dp, b)[1], me) for b in bits])
         for i in range(len(vm_ins)):
             for cp in load(i):
@@ -413,12 +441,24 @@
                     else:
                         hop(c, 0, k).start()
 
+        def need_for(where):
+            for (a, b), d in zip(dw_in, [d for d in dws if d[2] != "join"]):
+                if d[2] == where:
+                    need(a, b)
+
         if leave:
+            if front_in:
+                need_for("front")
+
+                def front(k, c):
+                    fill(k, "front")
+                    return c
+
+                lax.fori_loop(0, CHUNKS, front, 0)
             need(x_i, wl_i)
             if leave[2]:
                 wl_ref[...] = vin(wl_i)[...].T
-            for a, b in dw_in:
-                need(a, b)
+            need_for("far")
 
             def two(k, block_a, block_b):
                 lhs = jnp.concatenate([part(x_ref, block_a, k)[...], part(x_ref, block_b, k)[...]], 0)
@@ -443,6 +483,7 @@
                 return c
 
             lax.fori_loop(0, CHUNKS, out_far, 0)
+            need_for("near")
 
             def out_near(k, c):
                 p = two(k, me, sib)
@@ -459,6 +500,8 @@
 
             lax.fori_loop(0, CHUNKS, out_near, 0)
         need(gains_i, *row_i)
+        for i in range(5):
+            t[gain_s][i : i + 1, :] = gain_row(vin(gains_i), i, width)
         for a, b in dw_join:
             need(a, b)
         if enter and enter[1]:
@@ -473,7 +516,7 @@
                 far_send(k).wait_recv()
                 branch = part(own, 0, k)[...] + part(orv, 0, k)[...].astype(f32) + part(xr, 0, k)[...].astype(f32)
             fresh = junction(
-                branch, [part(vin(r), 0, k)[...] for r in row_i], vin(gains_i), [part(vout(o[0]), 0, k) for o in r_o], [vout(o[0]) for o in s_o]
+                branch, [part(vin(r), 0, k)[...] for r in row_i], t[gain_s], [part(vout(o[0]), 0, k) for o in r_o], [vout(o[0]) for o in s_o]
             )
             if enter:
                 part(all_ref, me, k)[...] = fresh
@@ -487,6 +530,46 @@
         for o in s_o:
             store_whole(o).start()
 
+        if small:
+            need(*vector_i)
+            rows_ref = vout(small_o[0][0])
+            for i, v in enumerate([vout(s_o[0][0])] + [vin(i) for i in vector_i]):
+                rows_ref[i : i + 1, :] = jnp.sum(v[...], 0, keepdims=True)
+            if table_in is not None:
+                need(table_i, taps_i)
+                both = vin(table_i)[...]
+                both = both + pltpu.roll(both, 64, 1)
+                left = lax.broadcasted_iota(jnp.int32, (TABLE_ROWS, 128), 1) < HEAD
+                vout(small_o[1][0])[...] = jnp.where(left, both[:TABLE_ROWS], both[TABLE_ROWS : 2 * TABLE_ROWS])
+                vout(small_o[2][0])[...] = vin(taps_i)[...]
+
+            def double(n):
+                at = course[n]
+                to = (dp, sib) if at == "sib" else (dp, far) if at == "far" else (place(dp, at)[1], me)
+                return [
+                    (
+                        pltpu.make_async_remote_copy(
+                            vout(o[0]), t[l].at[n], t[small_sems[0]].at[i, n], t[small_sems[1]].at[i, n],
+                            device_id=to, device_id_type=MESH,
+                        ),
+                        vout(o[0]),
+                        t[l].at[n],
+                    )
+                    for i, (o, l) in enumerate(zip(small_o, land_small))
+                    if i < 2 or not isinstance(at, str)
+                ]
+
+            def advance(n):
+                for cp, r, l in double(n):
+                    cp.wait()
+                    r[...] += l[...]
+                if n + 1 < len(course):
+                    for cp, _, _ in double(n + 1):
+                        cp.start()
+
+            for cp, _, _ in double(0):
+                cp.start()
+
         lead = [c for c in range(first_grad) if len(chains[c][5]) == 2] if enter else []
         if enter:
             need(we_i, *extra_i)
@@ -507,6 +590,13 @@
                 all_fwd(k).start()
                 got_diag(k).wait_recv()
                 work(k, far, diag)
+                if small:
+                    for n in range(min(CHUNKS, len(course))):
+
+                        @pl.when(k == n)
+                        def _(n=n):
+                            advance(n)
+
                 if lead:
 
                     @pl.when(k == CHUNKS - 2)
@@ -519,40 +609,9 @@
                 return c
 
             lax.fori_loop(0, CHUNKS, gather, 0)
-
-        if last:
-            need(*small_i)
-            *vectors, table, taps = [vin(i) for i in small_i]
-            rows_ref, table_ref, taps_ref = [vout(o[0]) for o in small_o]
-            rows_ref[...] = jnp.zeros(rows_ref.shape, f32)
-            for i, v in enumerate([vout(s_o[0][0])] + vectors):
-                rows_ref[i : i + 1, :] = jnp.sum(v[...], 0, keepdims=True)
-            table_ref[...] = table[...]
-            taps_ref[...] = taps[...]
-            course = ["sib", "far"] + list(range(bits_all - 1, -1, -1))
-
-            def double(n):
-                at = course[n]
-                to = (dp, sib) if at == "sib" else (dp, far) if at == "far" else (place(dp, at)[1], me)
-                return [
-                    (
-                        pltpu.make_async_remote_copy(
-                            r, t[l].at[n], t[small_sems[0]].at[i, n], t[small_sems[1]].at[i, n], device_id=to, device_id_type=MESH
-                        ),
-                        r,
-                        t[l].at[n],
-                    )
-                    for i, (r, l) in enumerate(zip((rows_ref, table_ref, taps_ref), land_small))
-                    if i < 2 or n > 1
-                ]
-
-            def finish_double(n):
-                for cp, r, l in double(n):
-                    cp.wait()
-                    r[...] += l[...]
-
-            for cp, _, _ in double(0):
-                cp.start()
+            if small:
+                for n in range(CHUNKS, len(course)):
+                    advance(n)
 
         pieces = [(c, p) for c in range(len(chains)) for p in range(chains[c][0])]
         order = [x for x in pieces if x[0] >= first_grad] + [x for x in pieces if x[0] < first_grad]
@@ -564,9 +623,7 @@
             if last:
                 for n in range(len(course) - 1):
                     if slot == (n if n < 2 else min(3 * n - 3, total_slots - 1)):
-                        finish_double(n)
-                        for cp, _, _ in double(n + 1):
-                            cp.start()
+                        advance(n)
             for s in reversed(range(deepest)):
                 if 0 <= slot - s < len(order):
                     c, p = order[slot - s]
@@ -576,7 +633,8 @@
                         if step + 1 < depth(c):
                             hop(c, step + 1, p).start()
         if last:
-            finish_double(len(course) - 1)
+            advance(len(course) - 1)
+        if small:
             for o in small_o:
                 store_whole(o).start()
         for c in range(len(chains)):
@@ -605,7 +663,7 @@
             return c
 
         lax.fori_loop(0, CHUNKS, drain, 0)
-        for o in s_o + (small_o if last else []):
+        for o in s_o + (small_o if small else []):
             store_whole(o).wait()
         for o in join_o:
             for p in range(out_shape[o[0]].shape[0]):
@@ -613,7 +671,7 @@
 
     flops = 0
     if leave:
-        flops += 2 * frames * leave[1].shape[1 if leave[2] else 0] * width
+        flops += 2 * frames * flat_shape(leave[1])[1 if leave[2] else 0] * width
     if enter:
         flops += 2 * frames * width * sum(c for c, _ in enter[4])
     flops += sum(2 * frames * width * PIECE * d[6] for d in dws)
@@ -643,17 +701,21 @@
         shape = (rows, sum(a.shape[1] for a in arrays)) if not joined else (sum(a.shape[0] for a in arrays), arrays[0].shape[1])
         where.append((len(flat), arrays, joined))
         flat.extend(arrays)
-        outs.append((shape, (shape[0], parts, shape[1] // parts) if parts else None))
+        if parts < 0:
+            outs.append((shape, (-parts, shape[0], shape[1] // -parts)))
+        else:
+            outs.append((shape, (shape[0], parts, shape[1] // parts) if parts else None))
     n, m = len(flat), len(ends)
     width = small[0].shape[1]
-    taps = small[2].shape
-    split_at = [i for i in range(m) if outs[i][1]]
-    small_shapes = [(1, width)] * 5 + [(rel, HEAD), (taps[0] - 1, taps[1]), (1, taps[1]), (1, 128)]
+    taps = small[3].shape
+    split_at = [i for i in range(m) if ends[i][1] > 0]
+    slab_at = [i for i in range(m) if ends[i][1] < 0]
+    small_shapes = [(1, width)] * 5 + [(HEAD, rel), (taps[0] - 1, taps[1]), (1, taps[1]), (1, 5)]
 
     def kernel(*refs):
-        src, small_in = refs[:n], refs[n : n + 3]
-        dst, small_out = refs[n + 3 : n + 3 + m], refs[n + 3 + m : n + 12 + m]
-        rest = refs[n + 12 + m :]
+        src, small_in = refs[:n], refs[n : n + 4]
+        dst, small_out = refs[n + 4 : n + 4 + m], refs[n + 4 + m : n + 13 + m]
+        rest = refs[n + 13 + m :]
         held, split = rest[:m], dict(zip(split_at, rest[m:-1]))
         sem = rest[-1]
         loads, stores = [], []
@@ -666,20 +728,33 @@
                 copies.append(pltpu.make_async_copy(ref, part, sem.at[first + k]))
                 at += size
             loads.append(copies)
-            stores.append(pltpu.make_async_copy(split.get(i, held[i]), dst[i], sem.at[n + i]))
+            if i in slab_at:
+                slabs, _, cols = dst[i].shape
+                stores.append(
+                    [
+                        pltpu.make_async_copy(held[i].at[:, pl.ds(k * cols, cols)], dst[i].at[k], sem.at[n + m + k])
+                        for k in range(slabs)
+                    ]
+                )
+            else:
+                stores.append([pltpu.make_async_copy(split.get(i, held[i]), dst[i], sem.at[n + i])])
         for copies in loads:
             for cp in copies:
                 cp.start()
-        rows, table, tap = [r[...] for r in small_in]
-        for i in range(5):
-            small_out[i][...] = rows[i : i + 1]
-        small_out[5][...] = table[:rel, :HEAD] + table[:rel, HEAD:]
+        lead, rows, table, tap = [r[...] for r in small_in]
+        small_out[0][...] = lead
+        for i in range(4):
+            small_out[1 + i][...] = rows[i : i + 1]
+        turned = jnp.concatenate([table, jnp.zeros((128 - TABLE_ROWS, 128), f32)], 0).T
+        small_out[5][:, :TABLE_ROWS] = turned[:HEAD, :TABLE_ROWS]
+        small_out[5][:, TABLE_ROWS:] = turned[HEAD:, : rel - TABLE_ROWS]
         small_out[6][...] = tap[:-1]
         small_out[7][...] = tap[-1:]
         square = jnp.sum(rows, -1, keepdims=True) / total
         lane = lax.broadcasted_iota(jnp.int32, (rows.shape[0], 128), 1)
         row = lax.broadcasted_iota(jnp.int32, (rows.shape[0], 128), 0)
-        small_out[8][...] = jnp.sqrt(jnp.sum(jnp.where(row == lane + 5, square, 0.0), 0, keepdims=True))
+        root = jnp.sqrt(jnp.sum(jnp.where(row == lane + 4, square, 0.0), 0, keepdims=True))
+        small_out[8][...] = root[:, :5]
         for i in range(m):
             for cp in loads[i]:
                 cp.wait()
@@ -687,19 +762,21 @@
                 cols = split[i].shape[2]
                 for j in range(split[i].shape[1]):
                     split[i][:, j, :] = held[i][:, j * cols : (j + 1) * cols]
-            stores[i].start()
-        for cp in stores:
-            cp.wait()
+            for cp in stores[i]:
+                cp.start()
+        for copies in stores:
+            for cp in copies:
+                cp.wait()
 
     vm = pl.BlockSpec(memory_space=pltpu.VMEM)
     return pl.pallas_call(
         kernel,
-        in_specs=[in_hbm()] * n + [vm] * 3,
+        in_specs=[in_hbm()] * n + [vm] * 4,
         out_specs=[in_hbm()] * m + [vm] * 9,
         out_shape=[jax.ShapeDtypeStruct(o[1] or o[0], f32) for o in outs] + [jax.ShapeDtypeStruct(s, f32) for s in small_shapes],
         scratch_shapes=[pltpu.VMEM(o[0], f32) for o in outs]
         + [pltpu.VMEM(outs[i][1], f32) for i in split_at]
-        + [pltpu.SemaphoreType.DMA((n + m,))],
+        + [pltpu.SemaphoreType.DMA((n + m + 4,))],
         compiler_params=pltpu.CompilerParams(vmem_limit_bytes=VMEM_LIMIT),
         name="publish",
     )(*flat, *small)
@@ -740,7 +817,12 @@
     return window if by == 0 else pltpu.roll(window, window.shape[0] - by, 0)
 
 
-def conv_mid(glu, w_depth, gain_depth, width, cid):
+def depth_gain_row(ref, width, chans):
+    first = 5 * width // 128
+    return jnp.concatenate([ref[first + j : first + j + 1, :] for j in range(chans // 128)], 1)
+
+
+def conv_mid(glu, w_depth, gains, width, cid):
     frames, chans = glu.shape
     taps = w_depth.shape[0]
     reach = taps - 1
@@ -748,18 +830,20 @@
     f32, bf = jnp.float32, jnp.bfloat16
     tiles, lanes = frames // SPAN, chans // 128
 
-    def kernel(glu_h, w_h, g_h, act_h, slope_h, unit_h, stat_h, pad, w_v, g_v, act, slope, unit, stat, sendbuf, landing, lsem, ssem, send, recv):
+    def kernel(glu_h, w_h, g_h, act_h, slope_h, unit_h, stat_h, pad, w_raw, g_raw, w_v, g_v, act, slope, unit, stat, sendbuf, landing, lsem, ssem, send, recv):
         meet = greet(group_targets())
         loads = [
             pltpu.make_async_copy(glu_h, pad.at[pl.ds(edge, frames)], lsem.at[0]),
-            pltpu.make_async_copy(w_h, w_v, lsem.at[1]),
-            pltpu.make_async_copy(g_h, g_v, lsem.at[2]),
+            pltpu.make_async_copy(w_h, w_raw, lsem.at[1]),
+            pltpu.make_async_copy(g_h, g_raw, lsem.at[2]),
         ]
         for cp in loads:
             cp.start()
         pad[:edge, :] = jnp.zeros((edge, chans), f32)
         for cp in loads:
             cp.wait()
+        w_v[...] = w_raw[...].astype(f32)
+        g_v[...] = depth_gain_row(g_raw, width, chans)
 
         def tile(i, c):
             at = pl.multiple_of(i * SPAN, SPAN)
@@ -830,34 +914,34 @@
         out_specs=[in_hbm()] * 4,
         out_shape=out_shape,
         scratch_shapes=[
-            vm((frames + edge, chans), f32), vm(w_depth.shape, f32), vm((1, chans), f32),
+            vm((frames + edge, chans), f32), vm(w_depth.shape, bf), vm(gains.shape, f32), vm(w_depth.shape, f32), vm((1, chans), f32),
             vm((frames, chans), bf), vm((frames, chans), bf), vm((frames, chans), f32), vm((8, frames), f32),
             vm((8, frames), f32), vm((3, 8, frames), f32),
             pltpu.SemaphoreType.DMA((3,)), pltpu.SemaphoreType.DMA((3, tiles)), pltpu.SemaphoreType.DMA((3,)), pltpu.SemaphoreType.DMA((3,)),
         ],
         compiler_params=pltpu.CompilerParams(collective_id=cid, has_side_effects=True, vmem_limit_bytes=VMEM_LIMIT),
         name="conv_mid",
-    )(glu, w_depth, gain_depth)
-
-
-def conv_mid_back(grad, slope, unit, stat, glu, sig, tail, w_depth, gain_depth, width, cid, grads):
+    )(glu, w_depth, gains)
+
+
+def conv_mid_back(grad, slope, unit, stat, glu, sig, tail, w_depth, gains, width, cid, grads):
     frames, chans = glu.shape
     taps = w_depth.shape[0]
     reach = taps - 1
     edge = (reach + 7) // 8 * 8
     f32, bf = jnp.float32, jnp.bfloat16
     tiles, lanes = frames // SPAN, chans // 128
-    ins = [grad, slope, unit, stat, w_depth, gain_depth, glu, sig, tail]
+    ins = [grad, slope, unit, stat, w_depth, gains, glu, sig, tail]
     riders = Riders(grads)
     n = len(grads)
 
     def kernel(*refs):
         hbm, ride_in, (pair_h, taps_h), ride_out = refs[:9], refs[9 : 9 + n], refs[9 + n : 11 + n], refs[11 + n : 11 + 2 * n]
         refs = refs[2 * n :]
-        (grad_v, slope_v, unit_v, stat_v, w_v, g_v, pad, sig_v, tail_v, back, pair, taps_v, acc, gacc, sendbuf, landing, lsem, ssem, send, recv) = refs[11:31]
-        riders.bind(ride_in, ride_out, refs[31:])
+        (grad_v, slope_v, unit_v, stat_v, w_raw, g_raw, pad, sig_v, tail_v, w_v, g_v, back, pair, taps_v, acc, gacc, sendbuf, landing, lsem, ssem, send, recv) = refs[11:33]
+        riders.bind(ride_in, ride_out, refs[33:])
         meet = greet(group_targets() + riders.targets())
-        dst = [grad_v, slope_v, unit_v, stat_v, w_v, g_v, pad.at[pl.ds(edge, frames)], sig_v, tail_v]
+        dst = [grad_v, slope_v, unit_v, stat_v, w_raw, g_raw, pad.at[pl.ds(edge, frames)], sig_v, tail_v]
         loads = [pltpu.make_async_copy(h, d, lsem.at[i]) for i, (h, d) in enumerate(zip(hbm, dst))]
         for cp in loads:
             cp.start()
@@ -867,6 +951,8 @@
         gacc[...] = jnp.zeros_like(gacc)
         for cp in loads[:6]:
             cp.wait()
+        w_v[...] = w_raw[...].astype(f32)
+        g_v[...] = depth_gain_row(g_raw, width, chans)
 
         def first(i, c):
             at = pl.ds(pl.multiple_of(i * SPAN, SPAN), SPAN)
@@ -954,7 +1040,8 @@
         out_shape=[S((frames, 2 * chans), bf), S((taps + 1, chans), f32)] + riders.after,
         scratch_shapes=[
             vm((frames, chans), f32), vm((frames, chans), bf), vm((frames, chans), f32), vm((8, frames), f32),
-            vm(w_depth.shape, f32), vm((1, chans), f32), vm((frames + edge, chans), f32), vm((frames, chans), bf), vm((frames, chans), bf),
+            vm(w_depth.shape, bf), vm(gains.shape, f32), vm((frames + edge, chans), f32), vm((frames, chans), bf), vm((frames, chans), bf),
+            vm(w_depth.shape, f32), vm((1, chans), f32),
             vm((frames + edge, chans), f32), vm((frames, 2 * chans), bf), vm((taps + 1, chans), f32), vm((taps * 8, chans), f32), vm((8, chans), f32),
             vm((8, frames), f32), vm((3, 8, frames), f32),
             pltpu.SemaphoreType.DMA((9,)), pltpu.SemaphoreType.DMA((tiles,)), pltpu.SemaphoreType.DMA((3,)), pltpu.SemaphoreType.DMA((3,)),
@@ -982,12 +1069,21 @@
     return (lax.broadcasted_iota(jnp.int32, (spots, BQ), 1) == row).astype(jnp.bfloat16)
 
 
-def fwd_kernel(q_ref, k_ref, v_ref, relb_ref, mixed_ref, probs_ref, bias_ref, rel_ref):
+def wide_table(rel_ref, wide_ref):
+    wide_ref[...] = jnp.zeros_like(wide_ref)
+    turned = rel_ref[...].astype(jnp.float32)
+    cols = turned.shape[1]
+    wide_ref[0:HEAD, :cols] = turned
+    wide_ref[HEAD : 2 * HEAD, :cols] = turned
+    return wide_ref[...].T.astype(jnp.bfloat16)
+
+
+def fwd_kernel(q_ref, k_ref, v_ref, relt_ref, mixed_ref, probs_ref, bias_ref, rel_ref, wide_ref):
     ib = pl.program_id(1)
 
     @pl.when((ib == 0) & (pl.program_id(0) == 0))
     def _():
-        rel_ref[...] = nn(spot_table(5 * BQ), relb_ref[...]).astype(jnp.bfloat16)
+        rel_ref[...] = nn(spot_table(5 * BQ), wide_table(relt_ref, wide_ref)).astype(jnp.bfloat16)
 
     qs = split_pair(q_ref[...] * 0.125)
     s = nt(qs, k_ref[...])
@@ -1014,12 +1110,12 @@
 
 def bwd_kernel(riders, *refs):
     n = len(riders.plan)
-    q_ref, k_ref, v_ref, relb_ref, probs_ref, do_ref, db_h, mix_h = refs[:8]
+    q_ref, k_ref, v_ref, relt_ref, probs_ref, do_ref, db_h, mix_h = refs[:8]
     ride_in = refs[8 : 8 + n]
     dq_ref, dk_ref, dv_ref, dt_ref, dw_h = refs[8 + n : 13 + n]
     ride_out = refs[13 + n : 13 + 2 * n]
-    tot_ref, dkt, dvt, dta, dz_ref, hot_ref, db_v, mix_v, dw_v, dw_land, dw_half, osem, psem = refs[13 + 2 * n : 26 + 2 * n]
-    riders.bind(ride_in, ride_out, refs[26 + 2 * n :])
+    tot_ref, dkt, dvt, dta, dz_ref, hot_ref, db_v, mix_v, dw_v, dw_land, dw_half, relb_ref, wide_ref, osem, psem = refs[13 + 2 * n : 28 + 2 * n]
+    riders.bind(ride_in, ride_out, refs[28 + 2 * n :])
     pr, ib, nb = pl.program_id(0), pl.program_id(1), pl.num_programs(1)
     dp, mp = lax.axis_index("dp"), lax.axis_index("mp")
     loads = [pltpu.make_async_copy(db_h, db_v, osem.at[0]), pltpu.make_async_copy(mix_h, mix_v, osem.at[1])]
@@ -1036,6 +1132,7 @@
         for cp in loads:
             cp.start()
         hot_ref[...] = spot_table(WIN)
+        relb_ref[...] = wide_table(relt_ref, wide_ref)
         meet()
         riders.start()
         for cp in loads:
@@ -1114,11 +1211,6 @@
     return [(place(dp, b)[1], mp) for b in sorted({0} | {x[1] for x in riders.plan})]
 
 
-def wide_table(rel_table):
-    padded = jnp.pad(rel_table, ((0, BQ - rel_table.shape[0]), (0, 0)))
-    return jnp.concatenate([padded, padded], 1)
-
-
 def attn_fwd(qkv, rel):
     frames, cols = qkv.shape
     pairs = cols // 3 // 128
@@ -1138,7 +1230,7 @@
             pl.BlockSpec((1, 2 * BQ, frames), lambda p, i: (p, i, 0)),
         ],
         out_shape=[jax.ShapeDtypeStruct((frames, cols // 3), bf), jax.ShapeDtypeStruct((pairs, 2 * frames, frames), bf)],
-        scratch_shapes=[pltpu.VMEM((2 * BQ, 5 * BQ), jnp.float32), pltpu.VMEM((5 * BQ, 128), bf)],
+        scratch_shapes=[pltpu.VMEM((2 * BQ, 5 * BQ), jnp.float32), pltpu.VMEM((5 * BQ, 128), bf), pltpu.VMEM((128, 128), jnp.float32)],
         compiler_params=pltpu.CompilerParams(vmem_limit_bytes=VMEM_LIMIT),
         name="attn_fwd",
     )(qkv, qkv, qkv, rel)
@@ -1174,6 +1266,7 @@
             vm((2 * BQ, 5 * BQ), jnp.float32), vm((128, frames), jnp.float32), vm((128, frames), jnp.float32),
             vm((128, 128), jnp.float32), vm((2 * BQ, frames), bf), vm((WIN, BQ), bf),
             vm(grad_rows.shape, bf), vm(mixed.shape, bf), vm(shape, bf), arriving(shape), vm(half.shape, half.dtype),
+            vm((128, 128), bf), vm((128, 128), jnp.float32),
             pltpu.SemaphoreType.DMA((2,)), pltpu.SemaphoreType.DMA((3, shape[0])),
         ]
         + riders.scratch,
@@ -1209,12 +1302,10 @@
     f32, bf = jnp.float32, jnp.bfloat16
     s0 = features.reshape(rows, width)
     seed = cotangent.reshape(rows, width)
-    row = jnp.arange(8)[:, None]
-    gains = sum(
-        jnp.where(row == i, g.astype(f32)[None], 0.0)
-        for i, g in enumerate((gain_ffn1, gain_attn, gain_conv, gain_ffn2, gain_final))
-    )
-    flat_qkv = w_qkv.reshape(width, -1)
+    spare = jnp.zeros((width - gain_depth.shape[0],), bf)
+    gains = jnp.concatenate([gain_ffn1, gain_attn, gain_conv, gain_ffn2, gain_final, gain_depth, spare])
+    gains = gains.astype(f32).reshape(-1, 128)
+    flat_qkv = w_qkv.transpose(1, 0, 2)
     flat_conv = w_conv_in.reshape(width, -1)
     units = w1_in.shape[1]
     half = units // PIECE // 2
@@ -1283,19 +1374,17 @@
     )
     a2, qkv, s1, sq1, _ = stage(
         "ffn1_out", 1, rows, width, dp_count, gains, leave=(act1, w1_out, False),
-        enter=(flat_qkv, False, plain_out, (), ((flat_qkv.shape[1], bf),)),
+        enter=(flat_qkv, False, plain_out, (), ((3 * w_qkv.shape[2], bf),)),
         junction=forward(0.5, 1), row_in=(s0,), row_out=(f32,), sums=1,
     )
-    wide = wide_table(rel_table)
-    mixed, probs = attn_fwd(qkv, wide)
+    turned_table = rel_table.T
+    mixed, probs = attn_fwd(qkv, turned_table)
     a3, glu, sig, tail, s2, sq2, _ = stage(
         "attn_out", 2, rows, width, dp_count, gains, leave=(mixed, w_attn_out, False),
         enter=(flat_conv, False, glu_out, (), ((chans, f32), (chans, bf), (chans, bf))),
         junction=forward(1.0, 2), row_in=(s1,), row_out=(f32,), sums=1,
     )
-    depth_taps = w_depth.astype(f32)
-    depth_gain = gain_depth.astype(f32)[None]
-    act3, slope3, depth_unit, depth_stat = conv_mid(glu, depth_taps, depth_gain, width, 10)
+    act3, slope3, depth_unit, depth_stat = conv_mid(glu, w_depth, gains, width, 10)
     a4, act2, slope2, s3, sq3, _ = stage(
         "conv_out", 3, rows, width, dp_count, gains, leave=(act3, w_conv_out, False),
         enter=(w2_in, False, swish_out, (), ((units, bf), (units, bf))),
@@ -1316,7 +1405,7 @@
         junction=backward(1.0, 3), row_in=(grad4, s3), row_out=(f32,), sums=1,
     )
     dpaired, tap_sums, (gw2_out, ga_in) = conv_mid_back(
-        de3, slope3, depth_unit, depth_stat, glu, sig, tail, depth_taps, depth_gain, width, 11, [gw2_out, ga_in]
+        de3, slope3, depth_unit, depth_stat, glu, sig, tail, w_depth, gains, width, 11, [gw2_out, ga_in]
     )
     db2, dmixed, grad2, dgc, (gconv_in, gconv_out, gb_in, gw2_out, ga_in) = stage(
         "conv_back", 6, rows, width, dp_count, gains, leave=(dpaired, flat_conv, True),
@@ -1324,20 +1413,21 @@
         junction=backward(1.0, 2), row_in=(grad3, s2), row_out=(f32,), sums=1,
     )
     dq, dk, dv, dt, (gattn, gb_in, ga_in, gconv_in, gconv_out) = attn_bwd(
-        qkv, wide, probs, dmixed, db2, mixed, [gb_in, ga_in, gconv_in, gconv_out], 9
+        qkv, turned_table, probs, dmixed, db2, mixed, [gb_in, ga_in, gconv_in, gconv_out], 9
     )
     dqkv = (dq, dk, dv)
-    db1, dh1, grad1, dga, (gqkv, gconv_in, gconv_out, gb_in) = stage(
+    db1, dh1, grad1, dga, (gqkv, gconv_in, gconv_out, gb_in), other_rows, table_end, taps_end = stage(
         "attn_back", 7, rows, width, dp_count, gains, leave=(dqkv, flat_qkv, True),
-        enter=(w1_out, True, slope_out, (slope1,), ((units, bf),)), dws=(weight(a2, dqkv, "far", False, 2),), grads=(gconv_in, gconv_out, gb_in),
+        enter=(w1_out, True, slope_out, (slope1,), ((units, bf),)), dws=(weight(a2, dqkv, "far", False),), grads=(gconv_in, gconv_out, gb_in),
+        small=((dgc, dg2, dgf, sq1, sq2, sq3, sq4, sq5), dt, tap_sums),
         junction=backward(0.5, 1), row_in=(grad2, s1), row_out=(f32,), sums=1,
     )
     early = [gqkv, gattn, gconv_in, gconv_out, ga_in, gb_in, gw2_out]
     waiting = pending(early)
-    grad0, dg1, ends, small_rows, table, taps_end = stage(
+    grad0, dg1, ends, lead_row = stage(
         "ffn1_back", 8, rows, width, dp_count, gains, leave=(dh1, w1_in, True),
-        dws=(weight(db1, act1, "far", True), weight(a1, dh1, "near", False)), grads=waiting,
-        small=[dga, dgc, dg2, dgf, sq1, sq2, sq3, sq4, sq5, dt, tap_sums],
+        dws=(weight(db1, act1, "front", True), weight(a1, dh1, "near", False)), grads=waiting,
+        small=((), None, None), last=True,
         junction=backward(1.0, 0), row_in=(grad1, s0), row_out=(f32,), sums=1,
     )
     gw1_out, gw1_in = ends[:2]
@@ -1354,14 +1444,14 @@
         ([grad0], 1),
         ([finish(gw1_in)], 0),
         ([finish(gw1_out)], 0),
-        ([finish(gqkv)], 3),
+        ([finish(gqkv)], -3),
         ([finish(gattn)], 0),
         ([finish(gconv_in)], 2),
         ([finish(gconv_out)], 0),
         ([finish(ga_in), finish(gb_in)], 0),
         ([finish(gw2_out)], 0),
     ]
-    done_ends = publish(ends, [small_rows, table, taps_end], {8: False}, rel_table.shape[0], float(token_total * width))
+    done_ends = publish(ends, [lead_row, other_rows, table_end, taps_end], {8: False}, rel_table.shape[0], float(token_total * width))
     (output, grad0, gw1_in, gw1_out, gqkv, gattn, gconv_in, gconv_out, gw2_in, gw2_out) = done_ends[:10]
     *gain_sums, table_sum, depth_sum, depth_gain_sum, rms_stats = done_ends[10:]
     gain_sums = [g[0] for g in gain_sums]
@@ -1371,9 +1461,9 @@
         gw1_in,
         gw1_out,
         gain_sums[0],
-        gqkv,
+        gqkv.transpose(1, 0, 2),
         gattn,
-        table_sum,
+        table_sum.T,
         gain_sums[1],
         gconv_in,
         depth_sum,
@@ -1384,7 +1474,7 @@
         gw2_out,
         gain_sums[3],
         gain_sums[4],
-        rms_stats[0, :5],
+        rms_stats[0],
     )
 
 

time: 455 us -> 441 us (0.969)
  other arithmetic: 7.5 us -> 0.61 us
where the time goes in v6:
time: 441 us
  Pallas kernels  432 us (98%)
  local copies, waits for them, and re-layouts  6.89 us (2%)
    pallas_call x9, Pallas kernels, stage(): pl.pallas_call(kernel, in_specs=[in_hbm()] * n_in, out_specs=[in_hbm()] *...  340 us
    pallas_call x1, Pallas kernels, attn_bwd(): pl.pallas_call(functools.partial(bwd_kernel, riders), grid=(pairs, nb), i...  34.4 us
    pallas_call x1, Pallas kernels, attn_fwd(): pl.pallas_call(fwd_kernel, grid=(pairs, nb), in_specs=[pl.BlockSpec((BQ,...  22.2 us
    pallas_call x1, Pallas kernels, conv_mid_back(): pl.pallas_call(kernel, in_specs=[in_hbm()] * (9 + n), out_specs=[in_hbm()...  17.6 us
    pallas_call x1, Pallas kernels, conv_mid(): pl.pallas_call(kernel, in_specs=[in_hbm()] * 3, out_specs=[in_hbm()] * 4,...  12.7 us

profile of v6, /device:TPU:0, one launch (start us, length us, event | category | flops | bytes accessed | tf_op | source)
XLA Modules:
  0.0 440.9 jit_solution(3043899342739232878)
XLA Ops:
  0.7 0.7 constant_dynamic-update-slice_fusion.4
  1.3 0.7 constant_dynamic-update-slice_fusion.3
  2.0 0.7 constant_dynamic-update-slice_fusion.2
  2.7 0.7 constant_dynamic-update-slice_fusion.1
  3.4 0.7 constant_dynamic-update-slice_fusion
  4.1 0.8 dynamic-update-slice.5
  4.9 0.2 dynamic-update-slice.6
  5.1 0.6 bitcast_convert_fusion.refs_0_.refs_2_.g_h.refs_4_.refs_5_
  5.7 2.4 copy.37
  8.2 19.5 %ffn1_in.1 = (bf16[1024,1024]{1,0:T(8,128)(2,1)}, bf16[1024,1024]{1,0:T(8,128)(2,1)}, bf16[1024,1024]{1,0:T(8,128)(2,1)}) custom-call(f32[48,128]{1,0:T(8,128)} %bitcast_convert_fusion.refs_0_.refs_2_.g_h.refs_4_.refs_5_, bf16[256,1024]{1,0:T(8,128)(2,1)} %bitcast.26, bf16[1024,1024]{1,0:T(8,128)(2,1)} %refs_3_.1), custom_call_target="tpu_custom_call" | custom-call | flops 4294967296 | bytes 60000000 | tf_op jit(solution)/shard_map/ffn1_in/pallas_call | solution.py:678
  27.7 31.3 %ffn1_out.1 = (bf16[1024,1024]{1,0:T(8,128)(2,1)}, bf16[1024,768]{1,0:T(8,128)(2,1)}, f32[256,1024]{1,0:T(8,128)}, f32[8,1024]{1,0:T(8,128)}) custom-call(bf16[1024,1024]{1,0:T(8,128)(2,1)} %get-tuple-element.114.refs_0_.refs_1_, bf16[1024,1024]{1,0:T(8,128)(2,1)} %refs_8_.5, f32[48,128]{1,0:T(8,128)} %bitcast_convert_fusion.refs_0_.refs_2_.g_h.refs_4_.refs_5_, ...), custom_call_target="tpu_custom_call" | custom-call | flops 3758096384 | bytes 60000000 | tf_op jit(solution)/shard_map/ffn1_out/pallas_call | solution.py:678
  59.0 22.2 %attn_fwd.1 = (bf16[1024,256]{1,0:T(8,128)(2,1)}, bf16[2,2048,1024]{2,1,0:T(8,128)(2,1)}) custom-call(bf16[1024,768]{1,0:T(8,128)(2,1)} %get-tuple-element.115.q_ref.k_ref.v_ref.refs_0_.refs_1_.refs_2_, bf16[1024,768]{1,0:T(8,128)(2,1)} %get-tuple-element.115.q_ref.k_ref.v_ref.refs_0_.refs_1_.refs_2_, ...), custom_call_target="tpu_custom_call" | custom-call | tf_op jit(solution)/shard_map/attn_fwd/pallas_call | solution.py:1219
  81.2 29.9 %attn_out.1 = (bf16[1024,1024]{1,0:T(8,128)(2,1)}, f32[1024,256]{1,0:T(8,128)}, bf16[1024,256]{1,0:T(8,128)(2,1)}, bf16[1024,256]{1,0:T(8,128)(2,1)}, f32[256,1024]{1,0:T(8,128)}, /*index=5*/f32[8,1024]{1,0:T(8,128)}) custom-call(bf16[1024,256]{1,0:T(8,128)(2,1)} %get-tuple-element.116.refs_0_.refs_7_, bf16[256,1024]{1,0:T(8,128)(2,1)} %refs_8_.4, ...), custom_call_target="tpu_custom_call" | custom-call | flops 2147483648 | bytes 60000000 | tf_op jit(solution)/shard_map/attn_out/pallas_call | solution.py:678
  111.1 12.7 %conv_mid.1 = (bf16[1024,256]{1,0:T(8,128)(2,1)}, bf16[1024,256]{1,0:T(8,128)(2,1)}, f32[1024,256]{1,0:T(8,128)}, f32[8,1024]{1,0:T(8,128)}) custom-call(f32[1024,256]{1,0:T(8,128)} %get-tuple-element.118.glu_h.refs_6_, bf16[31,256]{1,0:T(8,128)(2,1)} %refs_4_.3, f32[48,128]{1,0:T(8,128)} %bitcast_convert_fusion.refs_0_.refs_2_.g_h.refs_4_.refs_5_), custom_call_target="tpu_custom_call" | custom-call | tf_op jit(solution)/shard_map/conv_mid/pallas_call | solution.py:911
  123.8 29.9 %conv_out.1 = (bf16[1024,1024]{1,0:T(8,128)(2,1)}, bf16[1024,1024]{1,0:T(8,128)(2,1)}, bf16[1024,1024]{1,0:T(8,128)(2,1)}, f32[256,1024]{1,0:T(8,128)}, f32[8,1024]{1,0:T(8,128)}) custom-call(bf16[1024,256]{1,0:T(8,128)(2,1)} %get-tuple-element.119.refs_0_.refs_4_, bf16[256,1024]{1,0:T(8,128)(2,1)} %refs_8_.3, ...), custom_call_target="tpu_custom_call" | custom-call | flops 4831838208 | bytes 60000000 | tf_op jit(solution)/shard_map/conv_out/pallas_call | solution.py:678
  153.7 31.7 %ffn2_out.1 = (bf16[1024,1024]{1,0:T(8,128)(2,1)}, bf16[1024,1024]{1,0:T(8,128)(2,1)}, f32[256,1024]{1,0:T(8,128)}, f32[256,1024]{1,0:T(8,128)}, f32[8,1024]{1,0...) custom-call(bf16[1024,1024]{1,0:T(8,128)(2,1)} %get-tuple-element.121.refs_0_.refs_3_, bf16[1024,1024]{1,0:T(8,128)(2,1)} %refs_1_.8, ...), custom_call_target="tpu_custom_call" | custom-call | flops 4294967296 | bytes 60000000 | tf_op jit(solution)/shard_map/ffn2_out/pallas_call | solution.py:678
  185.5 32.7 %ffn2_back.1 = (bf16[1024,1024]{1,0:T(8,128)(2,1)}, f32[1024,256]{1,0:T(8,128)}, f32[256,1024]{1,0:T(8,128)}, f32[8,1024]{1,0:T(8,128)}, bf16[2,4,2,128,256]{4,3...) custom-call(bf16[1024,1024]{1,0:T(8,128)(2,1)} %get-tuple-element.126.refs_0_, ...), custom_call_target="tpu_custom_call" | custom-call | flops 6979321856 | bytes 60000000 | tf_op jit(solution)/shard_map/ffn2_back/pallas_call | solution.py:678
  218.2 17.6 %conv_mid_back.1 = (bf16[1024,512]{1,0:T(8,128)(2,1)}, f32[32,256]{1,0:T(8,128)}, bf16[4,1,2,128,256]{4,3,2,1,0:T(8,128)(2,1)}, bf16[2,2,2,128,256]{4,3,2,1,0:T(8,128)(2,1)}) custom-call(f32[1024,256]{1,0:T(8,128)} %get-tuple-element.130.refs_0_, bf16[1024,256]{1,0:T(8,128)(2,1)} %get-tuple-element.131.refs_1_, f32[1024,256]{1,0:T(8,128)} %get-tuple-element.132.refs_2_, ...), custom_call_target="tpu_custom_call" | custom-call | tf_op jit(solution)/shard_map/conv_mid_back/pallas_call | solution.py:1036
  235.8 35.3 %conv_back.1 = (bf16[1024,1024]{1,0:T(8,128)(2,1)}, bf16[1024,256]{1,0:T(8,128)(2,1)}, f32[256,1024]{1,0:T(8,128)}, f32[8,1024]{1,0:T(8,128)}, bf16[2,2,2,128,25...) custom-call(bf16[1024,512]{1,0:T(8,128)(2,1)} %get-tuple-element.138, ...), custom_call_target="tpu_custom_call" | custom-call | flops 3221225472 | bytes 60000000 | tf_op jit(solution)/shard_map/conv_back/pallas_call | solution.py:678
  271.2 34.4 %attn_bwd.1 = (bf16[1024,256]{1,0:T(8,128)(2,1)}, bf16[1024,256]{1,0:T(8,128)(2,1)}, bf16[1024,256]{1,0:T(8,128)(2,1)}, f32[128,128]{1,0:T(8,128)}, bf16[1,2,2,1...) custom-call(bf16[1024,768]{1,0:T(8,128)(2,1)} %get-tuple-element.115, ...), custom_call_target="tpu_custom_call" | custom-call | flops 5368709120 | bytes 20000000 | tf_op jit(solution)/shard_map/attn_bwd/pallas_call | solution.py:1251
  305.6 40.3 %attn_back.1 = (bf16[1024,1024]{1,0:T(8,128)(2,1)}, bf16[1024,1024]{1,0:T(8,128)(2,1)}, f32[256,1024]{1,0:T(8,128)}, f32[8,1024]{1,0:T(8,128)}, bf16[3,2,2,128,2...) custom-call(bf16[1024,256]{1,0:T(8,128)(2,1)} %get-tuple-element.151, ...), custom_call_target="tpu_custom_call" | custom-call | flops 5368709120 | bytes 60000000 | tf_op jit(solution)/shard_map/attn_back/pallas_call | solution.py:678
  345.9 89.4 %ffn1_back.1 = (f32[256,1024]{1,0:T(8,128)}, f32[8,1024]{1,0:T(8,128)}, f32[1024,128]{1,0:T(8,128)}, f32[128,1024]{1,0:T(8,128)}, f32[128,768]{1,0:T(8,128)}, /*index=5*/f32[256,128]{1,0:T(8,128)}, f32[1,1024]{1,0:T(1,128)}) custom-call(bf16[1024,1024]{1,0:T(8,128)(2,1)} %get-tuple-element.170.refs_0_, ...), custom_call_target="tpu_custom_call" | custom-call | flops 6442450944 | bytes 60000000 | tf_op jit(solution)/shard_map/ffn1_back/pallas_call | solution.py:678
  435.3 5.4 %publish.1 = (f32[256,1,1024]{2,1,0:T(1,128)}, f32[256,1,1024]{2,1,0:T(1,128)}, f32[128,1024]{1,0:T(8,128)}, f32[1024,128]{1,0:T(8,128)}, f32[3,128,256]{2,1,0:T...) custom-call(f32[256,1024]{1,0:T(8,128)} %get-tuple-element.124.refs_, ...), custom_call_target="tpu_custom_call" | custom-call | tf_op jit(solution)/shard_map/publish/pallas_call | solution.py:772
  (1 shorter events, 0.0 us)

commit v7 on v6

--- a/solution.py
+++ b/solution.py
@@ -121,8 +121,9 @@
 
 
 def weight(lhs, rhs, where, turned, deep=1, lo=0, pieces=None):
-    cols = sum(r.shape[1] for r in rhs) if isinstance(rhs, tuple) else rhs.shape[1]
-    return lhs, rhs, where, turned, deep, lo, cols // PIECE if pieces is None else pieces
+    if pieces is None:
+        pieces = (sum(r.shape[1] for r in rhs) if isinstance(rhs, tuple) else rhs.shape[1]) // PIECE
+    return lhs, rhs, where, turned, deep, lo, pieces
 
 
 def flat_shape(array):
@@ -195,7 +196,43 @@
     return lambda: pl.semaphore_wait(barrier, len(targets))
 
 
-def stage(name, cid, rows, width, count, gains, *, leave=None, enter=None, dws=(), grads=(), small=None, last=False, junction, row_in=(), row_out=(), sums=0):
+class Doubling:
+    def __init__(self, course, refs, lands, sems, partner):
+        self.course, self.items, self.sems, self.partner = course, list(zip(refs, lands)), sems, partner
+        self.done = 0
+
+    def copies(self, n):
+        at = self.course[n]
+        return [
+            (
+                pltpu.make_async_remote_copy(
+                    r, l.at[n], self.sems[0].at[i, n], self.sems[1].at[i, n], device_id=self.partner(at), device_id_type=MESH
+                ),
+                r,
+                l.at[n],
+            )
+            for i, (r, l) in enumerate(self.items)
+            if i < 2 or not isinstance(at, str)
+        ]
+
+    def start(self, n=0):
+        for cp, _, _ in self.copies(n):
+            cp.start()
+
+    def advance(self, n):
+        for cp, r, l in self.copies(n):
+            cp.wait()
+            r[...] += l[...]
+        if n + 1 < len(self.course):
+            self.start(n + 1)
+
+    def step(self):
+        if self.done < len(self.course):
+            self.advance(self.done)
+            self.done += 1
+
+
+def stage(name, cid, rows, width, count, gains, *, leave=None, enter=None, dws=(), grads=(), small=None, tail=None, junction, row_in=(), row_out=(), sums=0):
     chunk = rows // CHUNKS
     frames = rows * 4
     bits_all = count.bit_length() - 1
@@ -204,6 +241,8 @@
     known = {}
 
     def add_in(array, direct=False):
+        if isinstance(array, str):
+            return array
         if direct:
             ins.append(array)
             return len(ins) - 1
@@ -216,47 +255,70 @@
 
     out_slots = [0]
 
-    def add_out(shape, dtype, slots):
+    def add_scratch(item):
+        scratch.append(item)
+        return len(scratch) - 1
+
+    def add_out(shape, dtype, slots, kept=True):
+        if not kept:
+            return -1 - add_scratch(pltpu.VMEM(shape, dtype)), None
         out_shape.append(jax.ShapeDtypeStruct(shape, dtype))
         first = out_slots[0]
         out_slots[0] += slots
         return len(out_shape) - 1, first
 
-    def add_scratch(item):
-        scratch.append(item)
-        return len(scratch) - 1
-
+    add_dw = lambda where: [(add_in(d[0]), add_in(d[1])) if d[2] in where else None for d in dws]
+    groups = []
     if leave:
-        front_in = [(add_in(d[0]), add_in(d[1])) for d in dws if d[2] == "front"]
         x_i, wl_i = add_in(leave[0]), add_in(leave[1])
         leave_s = [add_scratch(pltpu.VMEM((rows, width), f32)) for _ in range(2)]
         leave_s += [add_scratch(pltpu.VMEM((rows, width), bf)) for _ in range(6)]
         wl_s = add_scratch(pltpu.VMEM(flat_shape(leave[1])[::-1], bf)) if leave[2] else None
-    dw_in = [(add_in(d[0]), add_in(d[1])) for d in dws if d[2] != "join"]
+        groups.append(len(vm_ins))
+        add_dw(("far",))
     gains_i = add_in(gains)
     gain_s = add_scratch(pltpu.VMEM((8, width), f32))
     row_i = [add_in(r) for r in row_in]
-    dw_join = [(add_in(d[0]), add_in(d[1])) for d in dws if d[2] == "join"]
+    if not leave:
+        groups.append(len(vm_ins))
+    add_dw(("near", "join"))
+    kept = not tail
     if enter:
         we_i = add_in(enter[0])
         extra_i = [add_in(e) for e in enter[3]]
         we_s = add_scratch(pltpu.VMEM(flat_shape(enter[0])[::-1], bf)) if enter[1] else None
-        all_o = add_out((frames, width), bf, 4 * CHUNKS)
-        e_o = [add_out((frames, c), d, 4 * CHUNKS) for c, d in enter[4]]
-    r_o = [add_out((rows, width), d, CHUNKS) for d in row_out]
-    s_o = [add_out((8, width), f32, 1) for _ in range(sums)]
+        all_o = add_out((frames, width), bf, 4 * CHUNKS, kept)
+        e_o = [add_out((frames, c), d, 4 * CHUNKS, kept) for c, d in enter[4]]
+    r_o = [add_out((rows, width), d, CHUNKS, kept) for d in row_out]
+    s_o = [add_out((8, width), f32, 1, kept) for _ in range(sums)]
+    if small:
+        vectors_in, table_in, taps_in = small
+        vector_i = [add_in(v) for v in vectors_in]
+        table_i, taps_i = add_in(table_in), add_in(taps_in)
+    groups.append(len(vm_ins))
+    if tail:
+        add_dw(("front",))
+        tw_i = add_in(tail[0])
+        tw_s = add_scratch(pltpu.VMEM(flat_shape(tail[0])[::-1], bf))
+        tail_i = [add_in(r) for r in tail[2]]
+        add_dw(("close",))
+        tail_o = [add_out((rows, width), f32, CHUNKS)]
+        tail_sum = add_out((8, width), f32, 1, False)
+    groups.append(len(vm_ins))
     fixed_out = len(out_shape)
-    plan, join_o = [], []
-    for lhs, rhs, where, turned, deep, lo, pieces in dws:
-        shape = (pieces, count // 2, 2, width // count, PIECE)
-        if where == "join":
-            join_o.append(add_out(shape, bf, shape[0]))
+    plan, dw_o = [], []
+    for d in dws:
+        shape = (d[6], count // 2, 2, width // count, PIECE)
+        if d[2] == "join":
+            dw_o.append(add_out(shape, bf, shape[0]))
         else:
-            plan.append((shape, 0, turned, bits_all if last else min(deep, bits_all), add_scratch(pltpu.VMEM(shape, bf)), None, None))
+            plan.append((shape, 0, d[3], bits_all if tail else 1, add_scratch(pltpu.VMEM(shape, bf)), None, None))
+            dw_o.append(len(plan) - 1)
+    dw_in = [(add_in(d[0]), add_in(d[1])) for d in dws]
     first_grad = len(plan)
     for g in grads:
         shape = g.array.shape
-        plan.append((shape, g.bit, g.turned, bits_all if last else g.bit + 1, None, add_in(g.array, True), add_scratch(arriving(shape))))
+        plan.append((shape, g.bit, g.turned, bits_all if tail else g.bit + 1, None, add_in(g.array, True), add_scratch(arriving(shape))))
     chains = []
     slots = 0
     for shape, bit, turned, end, src_s, src_i, keep_s in plan:
@@ -264,9 +326,8 @@
         pieces = shape[0]
         for b in range(bit, end):
             nxt = halved(shape, turned)
-            final = b == end - 1
             land_s = add_scratch(arriving(shape))
-            if final:
+            if b == end - 1:
                 links.append((b, slots, land_s, None, add_out(nxt.shape, nxt.dtype, pieces)))
             else:
                 links.append((b, slots, land_s, add_scratch(pltpu.VMEM(nxt.shape, nxt.dtype)), None))
@@ -274,32 +335,34 @@
             shape = nxt.shape
         chains.append((pieces, turned, src_s, src_i, keep_s, links))
     if small:
-        vectors_in, table_in, taps_in = small
-        vector_i = [add_in(v) for v in vectors_in]
-        small_shapes = [(1 + len(vectors_in), width)]
-        if table_in is not None:
-            table_i, taps_i = add_in(table_in), add_in(taps_in)
-            small_shapes += [(TABLE_ROWS, 128), taps_in.shape]
+        small_shapes = [(8, width), (TABLE_ROWS, 128), taps_in.shape]
         small_o = [add_out(s, f32, 1) for s in small_shapes]
-        if last:
-            course = ["sib", "far"] + list(range(bits_all - 1, -1, -1))
-        else:
-            course = list(range(bits_all - 1, -1, -1)) + ["sib", "far"]
-        land_small = [add_scratch(pltpu.VMEM((len(course),) + s, f32)) for s in small_shapes]
-        small_sems = [add_scratch(pltpu.SemaphoreType.DMA((3, len(course)))) for _ in range(2)]
+        lead_o = add_out((1, width), f32, 1)
+        downward = list(range(bits_all - 1, -1, -1))
+        courses = [downward + ["sib", "far"], ["sib", "far"] + downward]
+        small_l = [add_scratch(pltpu.VMEM((bits_all + 2,) + s, f32)) for s in small_shapes]
+        lead_l = [add_scratch(pltpu.VMEM((bits_all + 2, 1, width), f32))]
+        small_sems = [add_scratch(pltpu.SemaphoreType.DMA((3, bits_all + 2))) for _ in range(4)]
     if slots:
         grad_sems = [add_scratch(pltpu.SemaphoreType.DMA((slots,))) for _ in range(2)]
     ring_sems = [add_scratch(pltpu.SemaphoreType.DMA((6, CHUNKS))) for _ in range(2)]
     load_sem = add_scratch(pltpu.SemaphoreType.DMA((len(ins),)))
     store_sem = add_scratch(pltpu.SemaphoreType.DMA((out_slots[0],)))
-    n_in, n_out, n_scratch = len(ins), len(out_shape), len(scratch)
+    n_in, n_out = len(ins), len(out_shape)
     vm_at = [add_scratch(item[2]) for item in vm_ins]
     vo_at = [add_scratch(pltpu.VMEM(o.shape, o.dtype)) for o in out_shape]
 
     def kernel(*refs):
         hbm_in, hbm_out, t = refs[:n_in], refs[n_in : n_in + n_out], refs[n_in + n_out :]
-        vin = lambda i: t[vm_at[i]]
-        vout = lambda i: t[vo_at[i]]
+        vout = lambda o: t[-1 - o[0]] if o[0] < 0 else t[vo_at[o[0]]]
+
+        def vin(i):
+            if i == "all":
+                return vout(all_o)
+            if i == "out":
+                return vout(e_o[0])
+            return t[vm_at[i]]
+
         waited = set()
 
         def load(i):
@@ -319,9 +382,17 @@
                 at += cols
             return copies
 
+        begun = [0]
+
+        def begin_loads(group):
+            for i in range(begun[0], groups[group]):
+                for cp in load(i):
+                    cp.start()
+            begun[0] = max(begun[0], groups[group])
+
         def need(*items):
             for i in items:
-                if i not in waited:
+                if not isinstance(i, str) and i not in waited:
                     waited.add(i)
                     for cp in load(i):
                         cp.wait()
@@ -333,25 +404,22 @@
         diag = (1 - chip) * 2 + 1 - core
         bits = sorted({link[0] for ch in chains for link in ch[5]} | set(range(bits_all) if small else ()))
         meet = greet([(dp, sib), (dp, far)] + [(place(dp, b)[1], me) for b in bits])
-        for i in range(len(vm_ins)):
-            for cp in load(i):
-                cp.start()
+        begin_loads(0)
 
         def part(ref, block, k):
             return ref.at[pl.ds(pl.multiple_of(block * rows + k * chunk, chunk), chunk)]
 
         def store_rows(o, block, k):
-            i, first = o
-            return pltpu.make_async_copy(part(vout(i), block, k), part(hbm_out[i], block, k), t[store_sem].at[first + block * CHUNKS + k])
+            return pltpu.make_async_copy(
+                part(vout(o), block, k), part(hbm_out[o[0]], block, k), t[store_sem].at[o[1] + block * CHUNKS + k]
+            )
 
         def store_whole(o):
-            i, first = o
-            return pltpu.make_async_copy(vout(i), hbm_out[i], t[store_sem].at[first])
+            return pltpu.make_async_copy(vout(o), hbm_out[o[0]], t[store_sem].at[o[1]])
 
         def store_piece(o, piece, cols, turned):
-            i, first = o
             return pltpu.make_async_copy(
-                region(vout(i), piece, cols, turned), region(hbm_out[i], piece, cols, turned), t[store_sem].at[first + piece]
+                region(vout(o), piece, cols, turned), region(hbm_out[o[0]], piece, cols, turned), t[store_sem].at[o[1] + piece]
             )
 
         def copy(kind, k, src, dst, to):
@@ -361,10 +429,8 @@
 
         if leave:
             px, own, sb, sr, xs, xr, ob, orv = [t[s] for s in leave_s]
-            x_ref = vin(x_i)
-            wl_ref = t[wl_s] if leave[2] else vin(wl_i)
         if enter:
-            all_ref = vout(all_o[0])
+            all_ref = vout(all_o)
             we_ref = t[we_s] if enter[1] else vin(we_i)
         pair_send = lambda k: copy(0, k, part(sb, 0, k), part(sr, 0, k), sib)
         far_send = lambda k: copy(1, k, part(xs, 0, k), part(xr, 0, k), far)
@@ -389,15 +455,15 @@
         def keep(c):
             return halving_keep(hbm_in[chains[c][3]], t[chains[c][4]], chains[c][5][0][0], t[load_sem].at[chains[c][3]])
 
-        kept = set()
+        held_back = set()
 
         def settle(c, step, piece):
             pieces, turned, src_s, src_i, keep_s, links = chains[c]
             b, slot, land_s, out_s, out_o = links[step]
             hop(c, step, piece).wait_recv()
             if step == 0 and src_s is None:
-                if c not in kept:
-                    kept.add(c)
+                if c not in held_back:
+                    held_back.add(c)
                     keep(c).wait()
                 held = lambda p, j: t[keep_s][p, j]
             else:
@@ -405,61 +471,33 @@
                 src = source(c, step)
                 held = lambda p, j: src[p, j, own_bit]
             landing = t[land_s]
-            out = t[out_s] if out_o is None else vout(out_o[0])
+            out = t[out_s] if out_o is None else vout(out_o)
             halving_add(held, landing, out, piece, turned)
             if out_o is not None:
                 store_piece(out_o, piece, PIECE, turned and landing.shape[2] % 128 == 0).start()
 
-        for c in range(first_grad, len(chains)):
-            keep(c).start()
-        meet()
-        for c in range(first_grad, len(chains)):
-            for p in range(chains[c][0]):
-                hop(c, 0, p).start()
-        for o in s_o:
-            vout(o[0])[...] = jnp.zeros((8, width), f32)
-
         def fill(k, where):
-            n_far, n_join = 0, 0
-            for lhs, rhs, at_loop, turned, deep, lo, pieces in dws:
-                if at_loop == "join":
-                    (a, b), o, c = dw_join[n_join], join_o[n_join], None
-                    n_join += 1
-                else:
-                    (a, b), c = dw_in[n_far], n_far
-                    n_far += 1
-                if at_loop != where:
+            for d, (a, b), o in zip(dws, dw_in, dw_o):
+                if d[2] != where:
                     continue
-                dw = vout(o[0]) if c is None else t[chains[c][2]]
+                chain = None if where == "join" else o
+                dw = vout(o) if chain is None else t[chains[o][2]]
 
                 @pl.when(k < dw.shape[0])
-                def _(a=a, b=b, dw=dw, c=c, o=o if c is None else None, lo=lo):
+                def _(a=a, b=b, dw=dw, chain=chain, o=o, lo=d[5]):
                     g = tn(vin(a)[...], vin(b)[:, pl.ds(pl.multiple_of((lo + k) * PIECE, PIECE), PIECE)])
                     dw[k] = g.astype(bf).reshape(dw.shape[1:])
-                    if c is None:
+                    if chain is None:
                         store_piece(o, k, PIECE, False).start()
                     else:
-                        hop(c, 0, k).start()
+                        hop(chain, 0, k).start()
 
         def need_for(where):
-            for (a, b), d in zip(dw_in, [d for d in dws if d[2] != "join"]):
+            for d, (a, b) in zip(dws, dw_in):
                 if d[2] == where:
                     need(a, b)
 
-        if leave:
-            if front_in:
-                need_for("front")
-
-                def front(k, c):
-                    fill(k, "front")
-                    return c
-
-                lax.fori_loop(0, CHUNKS, front, 0)
-            need(x_i, wl_i)
-            if leave[2]:
-                wl_ref[...] = vin(wl_i)[...].T
-            need_for("far")
-
+        def leave_phase(x_ref, wl_ref, far_fill, near_fill):
             def two(k, block_a, block_b):
                 lhs = jnp.concatenate([part(x_ref, block_a, k)[...], part(x_ref, block_b, k)[...]], 0)
                 return nn(lhs, wl_ref[...])
@@ -479,11 +517,11 @@
                 def _():
                     push(k - 1)
 
-                fill(k, "far")
+                fill(k, far_fill)
                 return c
 
             lax.fori_loop(0, CHUNKS, out_far, 0)
-            need_for("near")
+            need_for(near_fill)
 
             def out_near(k, c):
                 p = two(k, me, sib)
@@ -495,83 +533,94 @@
                 def _():
                     push(CHUNKS - 1)
 
-                fill(k, "near")
+                fill(k, near_fill)
                 return c
 
             lax.fori_loop(0, CHUNKS, out_near, 0)
+
+        def leave_drain():
+            def drain(k, c):
+                pair_send(k).wait_send()
+                far_send(k).wait_send()
+                own_send(k).wait_send()
+                return c
+
+            lax.fori_loop(0, CHUNKS, drain, 0)
+
+        def join_phase(rule, has_leave, in_refs, outs, totals, gathers):
+            def join(k, c):
+                fill(k, "join")
+                branch = None
+                if has_leave:
+                    own_send(k).wait_recv()
+                    far_send(k).wait_recv()
+                    branch = part(own, 0, k)[...] + part(orv, 0, k)[...].astype(f32) + part(xr, 0, k)[...].astype(f32)
+                fresh = rule(
+                    branch, [part(r, 0, k)[...] for r in in_refs], t[gain_s], [part(vout(o), 0, k) for o in outs], [vout(o) for o in totals]
+                )
+                if gathers:
+                    part(all_ref, me, k)[...] = fresh
+                    all_far(k).start()
+                    all_sib(k).start()
+                for o in outs:
+                    if o[0] >= 0:
+                        store_rows(o, 0, k).start()
+                return c
+
+            lax.fori_loop(0, CHUNKS, join, 0)
+            for o in totals:
+                if o[0] >= 0:
+                    store_whole(o).start()
+
+        for o in s_o + ([tail_sum] if tail else []):
+            vout(o)[...] = jnp.zeros((8, width), f32)
+        meet()
+        if leave:
+            need(x_i, wl_i)
+        begin_loads(1)
+        for c in range(first_grad, len(chains)):
+            for p in range(chains[c][0]):
+                hop(c, 0, p).start()
+        if leave:
+            if leave[2]:
+                t[wl_s][...] = vin(wl_i)[...].T
+            need_for("far")
+            leave_phase(vin(x_i), t[wl_s] if leave[2] else vin(wl_i), "far", "near")
+        for c in range(first_grad, len(chains)):
+            keep(c).start()
         need(gains_i, *row_i)
         for i in range(5):
             t[gain_s][i : i + 1, :] = gain_row(vin(gains_i), i, width)
-        for a, b in dw_join:
-            need(a, b)
+        need_for("join")
         if enter and enter[1]:
             need(we_i)
             we_ref[...] = vin(we_i)[...].T
-
-        def join(k, c):
-            fill(k, "join")
-            branch = None
-            if leave:
-                own_send(k).wait_recv()
-                far_send(k).wait_recv()
-                branch = part(own, 0, k)[...] + part(orv, 0, k)[...].astype(f32) + part(xr, 0, k)[...].astype(f32)
-            fresh = junction(
-                branch, [part(vin(r), 0, k)[...] for r in row_i], t[gain_s], [part(vout(o[0]), 0, k) for o in r_o], [vout(o[0]) for o in s_o]
-            )
-            if enter:
-                part(all_ref, me, k)[...] = fresh
-                all_far(k).start()
-                all_sib(k).start()
-            for o in r_o:
-                store_rows(o, 0, k).start()
-            return c
-
-        lax.fori_loop(0, CHUNKS, join, 0)
-        for o in s_o:
-            store_whole(o).start()
-
+        join_phase(junction, bool(leave), [vin(r) for r in row_i], r_o, s_o, bool(enter))
+
+        lead = [c for c in range(first_grad) if tail and dws[[i for i, o in enumerate(dw_o) if o == c][0]][2] == "far"]
         if small:
-            need(*vector_i)
-            rows_ref = vout(small_o[0][0])
-            for i, v in enumerate([vout(s_o[0][0])] + [vin(i) for i in vector_i]):
+            partner = lambda at: (dp, sib) if at == "sib" else (dp, far) if at == "far" else (place(dp, at)[1], me)
+            need(*vector_i, table_i, taps_i)
+            rows_ref = vout(small_o[0])
+            rows_ref[...] = jnp.zeros((8, width), f32)
+            vectors = [vout(s_o[0])] + [vin(i) for i in vector_i]
+            for i, v in enumerate(vectors[:4]):
                 rows_ref[i : i + 1, :] = jnp.sum(v[...], 0, keepdims=True)
-            if table_in is not None:
-                need(table_i, taps_i)
-                both = vin(table_i)[...]
-                both = both + pltpu.roll(both, 64, 1)
-                left = lax.broadcasted_iota(jnp.int32, (TABLE_ROWS, 128), 1) < HEAD
-                vout(small_o[1][0])[...] = jnp.where(left, both[:TABLE_ROWS], both[TABLE_ROWS : 2 * TABLE_ROWS])
-                vout(small_o[2][0])[...] = vin(taps_i)[...]
-
-            def double(n):
-                at = course[n]
-                to = (dp, sib) if at == "sib" else (dp, far) if at == "far" else (place(dp, at)[1], me)
-                return [
-                    (
-                        pltpu.make_async_remote_copy(
-                            vout(o[0]), t[l].at[n], t[small_sems[0]].at[i, n], t[small_sems[1]].at[i, n],
-                            device_id=to, device_id_type=MESH,
-                        ),
-                        vout(o[0]),
-                        t[l].at[n],
-                    )
-                    for i, (o, l) in enumerate(zip(small_o, land_small))
-                    if i < 2 or not isinstance(at, str)
-                ]
-
-            def advance(n):
-                for cp, r, l in double(n):
-                    cp.wait()
-                    r[...] += l[...]
-                if n + 1 < len(course):
-                    for cp, _, _ in double(n + 1):
-                        cp.start()
-
-            for cp, _, _ in double(0):
-                cp.start()
-
-        lead = [c for c in range(first_grad) if len(chains[c][5]) == 2] if enter else []
+            for i, v in enumerate(vectors[4:]):
+                line = jnp.sum(v[...], 0, keepdims=True)
+                rows_ref[4:5, i * 128 : (i + 1) * 128] = functools.reduce(
+                    jnp.add, [line[:, j * 128 : (j + 1) * 128] for j in range(width // 128)]
+                )
+            both = vin(table_i)[...]
+            both = both + pltpu.roll(both, 64, 1)
+            left = lax.broadcasted_iota(jnp.int32, (TABLE_ROWS, 128), 1) < HEAD
+            vout(small_o[1])[...] = jnp.where(left, both[:TABLE_ROWS], both[TABLE_ROWS : 2 * TABLE_ROWS])
+            vout(small_o[2])[...] = vin(taps_i)[...]
+            wide = Doubling(courses[0], [vout(o) for o in small_o], [t[l] for l in small_l], [t[s] for s in small_sems[:2]], partner)
+            wide.start()
+
         if enter:
+            begin_loads(len(groups) - 1)
             need(we_i, *extra_i)
 
             def work(k, block_a, block_b):
@@ -579,9 +628,10 @@
                 h = nn(lhs, we_ref[...])
                 for i, block in enumerate((block_a, block_b)):
                     view = lambda ref: part(ref, block, k)
-                    enter[2](h[i * chunk : (i + 1) * chunk], [view(vin(r))[...] for r in extra_i], [view(vout(o[0])) for o in e_o])
+                    enter[2](h[i * chunk : (i + 1) * chunk], [view(vin(r))[...] for r in extra_i], [view(vout(o)) for o in e_o])
                     for o in [all_o] + e_o:
-                        store_rows(o, block, k).start()
+                        if o[0] >= 0:
+                            store_rows(o, block, k).start()
 
             def gather(k, c):
                 got_sib(k).wait_recv()
@@ -591,11 +641,10 @@
                 got_diag(k).wait_recv()
                 work(k, far, diag)
                 if small:
-                    for n in range(min(CHUNKS, len(course))):
-
-                        @pl.when(k == n)
-                        def _(n=n):
-                            advance(n)
+
+                    @pl.when(k == 1)
+                    def _():
+                        wide.advance(0)
 
                 if lead:
 
@@ -610,20 +659,48 @@
 
             lax.fori_loop(0, CHUNKS, gather, 0)
             if small:
-                for n in range(CHUNKS, len(course)):
-                    advance(n)
+                wide.done = 1
+
+        early = 0
+        if tail:
+            need_for("front")
+
+            def front(k, c):
+                fill(k, "front")
+                return c
+
+            lax.fori_loop(0, CHUNKS, front, 0)
+            wide.step()
+            early = 1
+            if lead and bits_all > 2:
+                early = 2
+                for ch in lead:
+                    for p in range(chains[ch][0]):
+                        settle(ch, 1, p)
+                        hop(ch, 2, p).start()
+            leave_drain()
+            need(tw_i, *tail_i)
+            t[tw_s][...] = vin(tw_i)[...].T
+            wide.step()
+            leave_phase(vin("out"), t[tw_s], None, "close")
+            wide.step()
+            join_phase(tail[1], True, [vout(r_o[0])] + [vin(r) for r in tail_i], tail_o, [tail_sum], False)
+            vout(lead_o)[...] = jnp.sum(vout(tail_sum)[...], 0, keepdims=True)
+            final = Doubling(courses[1], [vout(lead_o)], [t[l] for l in lead_l], [t[s] for s in small_sems[2:]], partner)
+            final.start()
+            while wide.done < len(courses[0]):
+                wide.step()
 
         pieces = [(c, p) for c in range(len(chains)) for p in range(chains[c][0])]
-        order = [x for x in pieces if x[0] >= first_grad] + [x for x in pieces if x[0] < first_grad]
+        order = [x for x in pieces if x[0] >= first_grad] + [x for x in pieces if x[0] in lead]
+        order += [x for x in pieces if x not in order]
         depth = lambda c: len(chains[c][5])
-        begin = lambda c: 1 if c in lead else 0
+        begin = lambda c: early if c in lead else 0
         deepest = max([depth(c) - begin(c) for c in range(len(chains))] + [0])
-        total_slots = max(len(order) + deepest - 1, len(course) if last else 0)
+        total_slots = len(order) + deepest - 1
         for slot in range(total_slots):
-            if last:
-                for n in range(len(course) - 1):
-                    if slot == (n if n < 2 else min(3 * n - 3, total_slots - 1)):
-                        advance(n)
+            if tail and (slot < 2 or slot % 3 == 0) and final.done < len(courses[1]) - 1:
+                final.step()
             for s in reversed(range(deepest)):
                 if 0 <= slot - s < len(order):
                     c, p = order[slot - s]
@@ -632,10 +709,10 @@
                         settle(c, step, p)
                         if step + 1 < depth(c):
                             hop(c, step + 1, p).start()
-        if last:
-            advance(len(course) - 1)
-        if small:
-            for o in small_o:
+        if tail:
+            while final.done < len(courses[1]):
+                final.step()
+            for o in small_o + [lead_o]:
                 store_whole(o).start()
         for c in range(len(chains)):
             for s in range(depth(c)):
@@ -645,29 +722,31 @@
             block = chains[c][5][-1][2]
             for p in range(chains[c][0]):
                 store_piece(out_o, p, PIECE, chains[c][1] and t[block].shape[2] % 128 == 0).wait()
+        if leave:
+            leave_drain()
 
         def drain(k, c):
-            if leave:
-                pair_send(k).wait_send()
-                far_send(k).wait_send()
-                own_send(k).wait_send()
             if enter:
                 all_far(k).wait_send()
                 all_sib(k).wait_send()
                 all_fwd(k).wait_send()
                 for block in range(4):
                     for o in [all_o] + e_o:
-                        store_rows(o, block, k).wait()
-            for o in r_o:
-                store_rows(o, 0, k).wait()
+                        if o[0] >= 0:
+                            store_rows(o, block, k).wait()
+            for o in r_o + (tail_o if tail else []):
+                if o[0] >= 0:
+                    store_rows(o, 0, k).wait()
             return c
 
         lax.fori_loop(0, CHUNKS, drain, 0)
-        for o in s_o + (small_o if small else []):
-            store_whole(o).wait()
-        for o in join_o:
-            for p in range(out_shape[o[0]].shape[0]):
-                store_piece(o, p, PIECE, False).wait()
+        for o in s_o + (small_o + [lead_o] if tail else []):
+            if o[0] >= 0:
+                store_whole(o).wait()
+        for d, o in zip(dws, dw_o):
+            if d[2] == "join":
+                for p in range(d[6]):
+                    store_piece(o, p, PIECE, False).wait()
 
     flops = 0
     if leave:
@@ -750,10 +829,11 @@
         small_out[5][:, TABLE_ROWS:] = turned[HEAD:, : rel - TABLE_ROWS]
         small_out[6][...] = tap[:-1]
         small_out[7][...] = tap[-1:]
-        square = jnp.sum(rows, -1, keepdims=True) / total
-        lane = lax.broadcasted_iota(jnp.int32, (rows.shape[0], 128), 1)
-        row = lax.broadcasted_iota(jnp.int32, (rows.shape[0], 128), 0)
-        root = jnp.sqrt(jnp.sum(jnp.where(row == lane + 4, square, 0.0), 0, keepdims=True))
+        lane = lax.broadcasted_iota(jnp.int32, (1, 128), 1)
+        mean = jnp.zeros((1, 128), f32)
+        for i in range(5):
+            mean = jnp.where(lane == i, jnp.sum(rows[4:5, i * 128 : (i + 1) * 128], -1, keepdims=True) / total, mean)
+        root = jnp.sqrt(mean)
         small_out[8][...] = root[:, :5]
         for i in range(m):
             for cp in loads[i]:
@@ -1416,22 +1496,21 @@
         qkv, turned_table, probs, dmixed, db2, mixed, [gb_in, ga_in, gconv_in, gconv_out], 9
     )
     dqkv = (dq, dk, dv)
-    db1, dh1, grad1, dga, (gqkv, gconv_in, gconv_out, gb_in), other_rows, table_end, taps_end = stage(
+    waiting = pending([gattn, gconv_in, gconv_out, ga_in, gb_in, gw2_out])
+    grad0, ends, other_rows, table_end, taps_end, lead_row = stage(
         "attn_back", 7, rows, width, dp_count, gains, leave=(dqkv, flat_qkv, True),
-        enter=(w1_out, True, slope_out, (slope1,), ((units, bf),)), dws=(weight(a2, dqkv, "far", False),), grads=(gconv_in, gconv_out, gb_in),
-        small=((dgc, dg2, dgf, sq1, sq2, sq3, sq4, sq5), dt, tap_sums),
+        enter=(w1_out, True, slope_out, (slope1,), ((units, bf),)),
+        dws=(
+            weight(a2, dqkv, "far", False),
+            weight("all", act1, "front", True),
+            weight(a1, "out", "close", False, pieces=units // PIECE),
+        ),
+        grads=waiting, small=((dgc, dg2, dgf, sq1, sq2, sq3, sq4, sq5), dt, tap_sums),
+        tail=(w1_in, backward(1.0, 0), (s0,)),
         junction=backward(0.5, 1), row_in=(grad2, s1), row_out=(f32,), sums=1,
     )
-    early = [gqkv, gattn, gconv_in, gconv_out, ga_in, gb_in, gw2_out]
-    waiting = pending(early)
-    grad0, dg1, ends, lead_row = stage(
-        "ffn1_back", 8, rows, width, dp_count, gains, leave=(dh1, w1_in, True),
-        dws=(weight(db1, act1, "front", True), weight(a1, dh1, "near", False)), grads=waiting,
-        small=((), None, None), last=True,
-        junction=backward(1.0, 0), row_in=(grad1, s0), row_out=(f32,), sums=1,
-    )
-    gw1_out, gw1_in = ends[:2]
-    for item, end in zip(waiting, ends[2:]):
+    gqkv, gw1_out, gw1_in = ends[:3]
+    for item, end in zip(waiting, ends[3:]):
         item.array = end.array
 
     def finish(item):

time: 441 us -> 449 us (1.018)
  Pallas kernels: 432 us -> 440 us
    pallas_call x9 -> x8, Pallas kernels: 340 us -> 347 us  [stage(): pl.pallas_call(kernel, in_specs=[in_hbm()] * n_in, out_specs=[in_hbm()] *...]
where the time goes in v7:
time: 449 us; the launch traced here: 448 us
  Pallas kernels  440 us (98%)
  local copies, waits for them, and re-layouts  6.89 us (2%)
    pallas_call x8, Pallas kernels, stage(): pl.pallas_call(kernel, in_specs=[in_hbm()] * n_in, out_specs=[in_hbm()] *...  347 us
    pallas_call x1, Pallas kernels, attn_bwd(): pl.pallas_call(functools.partial(bwd_kernel, riders), grid=(pairs, nb), i...  34.5 us
    pallas_call x1, Pallas kernels, attn_fwd(): pl.pallas_call(fwd_kernel, grid=(pairs, nb), in_specs=[pl.BlockSpec((BQ,...  22.2 us
    pallas_call x1, Pallas kernels, conv_mid_back(): pl.pallas_call(kernel, in_specs=[in_hbm()] * (9 + n), out_specs=[in_hbm()...  17.5 us
    pallas_call x1, Pallas kernels, conv_mid(): pl.pallas_call(kernel, in_specs=[in_hbm()] * 3, out_specs=[in_hbm()] * 4,...  12.6 us

profile of v7, /device:TPU:0, one launch (start us, length us, event | category | flops | bytes accessed | tf_op | source)
XLA Modules:
  0.0 448.0 jit_solution(16428444452544728746)
XLA Ops:
  0.7 0.7 constant_dynamic-update-slice_fusion.4
  1.3 0.7 constant_dynamic-update-slice_fusion.3
  2.0 0.7 constant_dynamic-update-slice_fusion.2
  2.7 0.7 constant_dynamic-update-slice_fusion.1
  3.4 0.7 constant_dynamic-update-slice_fusion
  4.1 0.8 dynamic-update-slice.5
  4.9 0.2 dynamic-update-slice.6
  5.1 0.6 bitcast_convert_fusion.refs_0_.refs_2_.g_h.refs_4_.refs_5_
  5.7 2.4 copy.37
  8.2 19.5 %ffn1_in.1 = (bf16[1024,1024]{1,0:T(8,128)(2,1)}, bf16[1024,1024]{1,0:T(8,128)(2,1)}, bf16[1024,1024]{1,0:T(8,128)(2,1)}) custom-call(f32[48,128]{1,0:T(8,128)} %bitcast_convert_fusion.refs_0_.refs_2_.g_h.refs_4_.refs_5_, bf16[256,1024]{1,0:T(8,128)(2,1)} %bitcast.26, bf16[1024,1024]{1,0:T(8,128)(2,1)} %refs_21_.1), custom_call_target="tpu_custom_call" | custom-call | flops 4294967296 | bytes 60000000 | tf_op jit(solution)/shard_map/ffn1_in/pallas_call | solution.py:757
  27.7 31.3 %ffn1_out.1 = (bf16[1024,1024]{1,0:T(8,128)(2,1)}, bf16[1024,768]{1,0:T(8,128)(2,1)}, f32[256,1024]{1,0:T(8,128)}, f32[8,1024]{1,0:T(8,128)}) custom-call(bf16[1024,1024]{1,0:T(8,128)(2,1)} %get-tuple-element.110.refs_0_.refs_20_, bf16[1024,1024]{1,0:T(8,128)(2,1)} %refs_8_.5, f32[48,128]{1,0:T(8,128)} %bitcast_convert_fusion.refs_0_.refs_2_.g_h.refs_4_.refs_5_, ...), custom_call_target="tpu_custom_call" | custom-call | flops 3758096384 | bytes 60000000 | tf_op jit(solution)/shard_map/ffn1_out/pallas_call | solution.py:757
  59.0 22.2 %attn_fwd.1 = (bf16[1024,256]{1,0:T(8,128)(2,1)}, bf16[2,2048,1024]{2,1,0:T(8,128)(2,1)}) custom-call(bf16[1024,768]{1,0:T(8,128)(2,1)} %get-tuple-element.111.q_ref.k_ref.v_ref.refs_0_.refs_1_.refs_2_, bf16[1024,768]{1,0:T(8,128)(2,1)} %get-tuple-element.111.q_ref.k_ref.v_ref.refs_0_.refs_1_.refs_2_, ...), custom_call_target="tpu_custom_call" | custom-call | tf_op jit(solution)/shard_map/attn_fwd/pallas_call | solution.py:1299
  81.2 29.9 %attn_out.1 = (bf16[1024,1024]{1,0:T(8,128)(2,1)}, f32[1024,256]{1,0:T(8,128)}, bf16[1024,256]{1,0:T(8,128)(2,1)}, bf16[1024,256]{1,0:T(8,128)(2,1)}, f32[256,1024]{1,0:T(8,128)}, /*index=5*/f32[8,1024]{1,0:T(8,128)}) custom-call(bf16[1024,256]{1,0:T(8,128)(2,1)} %get-tuple-element.112.refs_0_.refs_7_, bf16[256,1024]{1,0:T(8,128)(2,1)} %refs_8_.4, ...), custom_call_target="tpu_custom_call" | custom-call | flops 2147483648 | bytes 60000000 | tf_op jit(solution)/shard_map/attn_out/pallas_call | solution.py:757
  111.2 12.6 %conv_mid.1 = (bf16[1024,256]{1,0:T(8,128)(2,1)}, bf16[1024,256]{1,0:T(8,128)(2,1)}, f32[1024,256]{1,0:T(8,128)}, f32[8,1024]{1,0:T(8,128)}) custom-call(f32[1024,256]{1,0:T(8,128)} %get-tuple-element.114.glu_h.refs_6_, bf16[31,256]{1,0:T(8,128)(2,1)} %refs_4_.3, f32[48,128]{1,0:T(8,128)} %bitcast_convert_fusion.refs_0_.refs_2_.g_h.refs_4_.refs_5_), custom_call_target="tpu_custom_call" | custom-call | tf_op jit(solution)/shard_map/conv_mid/pallas_call | solution.py:991
  123.8 29.9 %conv_out.1 = (bf16[1024,1024]{1,0:T(8,128)(2,1)}, bf16[1024,1024]{1,0:T(8,128)(2,1)}, bf16[1024,1024]{1,0:T(8,128)(2,1)}, f32[256,1024]{1,0:T(8,128)}, f32[8,1024]{1,0:T(8,128)}) custom-call(bf16[1024,256]{1,0:T(8,128)(2,1)} %get-tuple-element.115.refs_0_.refs_4_, bf16[256,1024]{1,0:T(8,128)(2,1)} %refs_8_.3, ...), custom_call_target="tpu_custom_call" | custom-call | flops 4831838208 | bytes 60000000 | tf_op jit(solution)/shard_map/conv_out/pallas_call | solution.py:757
  153.7 31.8 %ffn2_out.1 = (bf16[1024,1024]{1,0:T(8,128)(2,1)}, bf16[1024,1024]{1,0:T(8,128)(2,1)}, f32[256,1024]{1,0:T(8,128)}, f32[256,1024]{1,0:T(8,128)}, f32[8,1024]{1,0...) custom-call(bf16[1024,1024]{1,0:T(8,128)(2,1)} %get-tuple-element.117.refs_0_.refs_3_, bf16[1024,1024]{1,0:T(8,128)(2,1)} %refs_1_.8, ...), custom_call_target="tpu_custom_call" | custom-call | flops 4294967296 | bytes 60000000 | tf_op jit(solution)/shard_map/ffn2_out/pallas_call | solution.py:757
  185.5 33.6 %ffn2_back.1 = (bf16[1024,1024]{1,0:T(8,128)(2,1)}, f32[1024,256]{1,0:T(8,128)}, f32[256,1024]{1,0:T(8,128)}, f32[8,1024]{1,0:T(8,128)}, bf16[2,4,2,128,256]{4,3...) custom-call(bf16[1024,1024]{1,0:T(8,128)(2,1)} %get-tuple-element.122.refs_0_, ...), custom_call_target="tpu_custom_call" | custom-call | flops 6979321856 | bytes 60000000 | tf_op jit(solution)/shard_map/ffn2_back/pallas_call | solution.py:757
  219.1 17.5 %conv_mid_back.1 = (bf16[1024,512]{1,0:T(8,128)(2,1)}, f32[32,256]{1,0:T(8,128)}, bf16[4,1,2,128,256]{4,3,2,1,0:T(8,128)(2,1)}, bf16[2,2,2,128,256]{4,3,2,1,0:T(8,128)(2,1)}) custom-call(f32[1024,256]{1,0:T(8,128)} %get-tuple-element.126.refs_0_, bf16[1024,256]{1,0:T(8,128)(2,1)} %get-tuple-element.127.refs_1_, f32[1024,256]{1,0:T(8,128)} %get-tuple-element.128.refs_2_, ...), custom_call_target="tpu_custom_call" | custom-call | tf_op jit(solution)/shard_map/conv_mid_back/pallas_call | solution.py:1116
  236.7 35.7 %conv_back.1 = (bf16[1024,1024]{1,0:T(8,128)(2,1)}, bf16[1024,256]{1,0:T(8,128)(2,1)}, f32[256,1024]{1,0:T(8,128)}, f32[8,1024]{1,0:T(8,128)}, bf16[2,2,2,128,25...) custom-call(bf16[1024,512]{1,0:T(8,128)(2,1)} %get-tuple-element.134, ...), custom_call_target="tpu_custom_call" | custom-call | flops 3221225472 | bytes 60000000 | tf_op jit(solution)/shard_map/conv_back/pallas_call | solution.py:757
  272.4 34.5 %attn_bwd.1 = (bf16[1024,256]{1,0:T(8,128)(2,1)}, bf16[1024,256]{1,0:T(8,128)(2,1)}, bf16[1024,256]{1,0:T(8,128)(2,1)}, f32[128,128]{1,0:T(8,128)}, bf16[1,2,2,1...) custom-call(bf16[1024,768]{1,0:T(8,128)(2,1)} %get-tuple-element.111, ...), custom_call_target="tpu_custom_call" | custom-call | flops 5368709120 | bytes 20000000 | tf_op jit(solution)/shard_map/attn_bwd/pallas_call | solution.py:1331
  306.8 135.6 %attn_back.1 = (f32[256,1024]{1,0:T(8,128)}, f32[128,768]{1,0:T(8,128)}, f32[1024,128]{1,0:T(8,128)}, f32[128,1024]{1,0:T(8,128)}, f32[256,128]{1,0:T(8,128)}, /...) custom-call(bf16[1024,256]{1,0:T(8,128)(2,1)} %get-tuple-element.147, ...), custom_call_target="tpu_custom_call" | custom-call | flops 9663676416 | bytes 60000000 | tf_op jit(solution)/shard_map/attn_back/pallas_call | solution.py:757
  442.4 5.4 %publish.1 = (f32[256,1,1024]{2,1,0:T(1,128)}, f32[256,1,1024]{2,1,0:T(1,128)}, f32[128,1024]{1,0:T(8,128)}, f32[1024,128]{1,0:T(8,128)}, f32[3,128,256]{2,1,0:T...) custom-call(f32[256,1024]{1,0:T(8,128)} %get-tuple-element.120.refs_, ...), custom_call_target="tpu_custom_call" | custom-call | tf_op jit(solution)/shard_map/publish/pallas_call | solution.py:852
  (1 shorter events, 0.0 us)

commit v8 on v7

--- a/solution.py
+++ b/solution.py
@@ -27,6 +27,8 @@
 MESH = pl.DeviceIdType.MESH
 CHUNKS = 4
 TABLE_ROWS = 40
+LAG = 2
+JOIN_SLOT = 3
 PIECE = 256
 VMEM_LIMIT = 58 << 20
 
@@ -339,7 +341,7 @@
         small_o = [add_out(s, f32, 1) for s in small_shapes]
         lead_o = add_out((1, width), f32, 1)
         downward = list(range(bits_all - 1, -1, -1))
-        courses = [downward + ["sib", "far"], ["sib", "far"] + downward]
+        courses = [downward[-1:] + downward[:-1] + ["sib", "far"], ["sib", "far"] + downward]
         small_l = [add_scratch(pltpu.VMEM((bits_all + 2,) + s, f32)) for s in small_shapes]
         lead_l = [add_scratch(pltpu.VMEM((bits_all + 2, 1, width), f32))]
         small_sems = [add_scratch(pltpu.SemaphoreType.DMA((3, bits_all + 2))) for _ in range(4)]
@@ -642,9 +644,11 @@
                 work(k, far, diag)
                 if small:
 
-                    @pl.when(k == 1)
-                    def _():
-                        wide.advance(0)
+                    for n, at in enumerate((1, CHUNKS - 1)):
+
+                        @pl.when(k == at)
+                        def _(n=n):
+                            wide.advance(n)
 
                 if lead:
 
@@ -659,7 +663,7 @@
 
             lax.fori_loop(0, CHUNKS, gather, 0)
             if small:
-                wide.done = 1
+                wide.done = 2
 
         early = 0
         if tail:
@@ -670,7 +674,6 @@
                 return c
 
             lax.fori_loop(0, CHUNKS, front, 0)
-            wide.step()
             early = 1
             if lead and bits_all > 2:
                 early = 2
@@ -681,34 +684,39 @@
             leave_drain()
             need(tw_i, *tail_i)
             t[tw_s][...] = vin(tw_i)[...].T
-            wide.step()
             leave_phase(vin("out"), t[tw_s], None, "close")
             wide.step()
+
+        def close_rows():
             join_phase(tail[1], True, [vout(r_o[0])] + [vin(r) for r in tail_i], tail_o, [tail_sum], False)
             vout(lead_o)[...] = jnp.sum(vout(tail_sum)[...], 0, keepdims=True)
             final = Doubling(courses[1], [vout(lead_o)], [t[l] for l in lead_l], [t[s] for s in small_sems[2:]], partner)
             final.start()
-            while wide.done < len(courses[0]):
-                wide.step()
-
-        pieces = [(c, p) for c in range(len(chains)) for p in range(chains[c][0])]
-        order = [x for x in pieces if x[0] >= first_grad] + [x for x in pieces if x[0] in lead]
-        order += [x for x in pieces if x not in order]
+            return final
+
         depth = lambda c: len(chains[c][5])
         begin = lambda c: early if c in lead else 0
-        deepest = max([depth(c) - begin(c) for c in range(len(chains))] + [0])
-        total_slots = len(order) + deepest - 1
-        for slot in range(total_slots):
-            if tail and (slot < 2 or slot % 3 == 0) and final.done < len(courses[1]) - 1:
+        agenda, fresh_slot = {}, 1
+        for c in range(len(chains)):
+            new = tail and c < first_grad and c not in lead
+            for p in range(chains[c][0]):
+                slot = fresh_slot if new else 0
+                fresh_slot += 1 if new else 0
+                for step in range(begin(c), depth(c)):
+                    agenda.setdefault(slot, []).append((step, c, p))
+                    slot += LAG
+        final = None
+        for slot in range(max(list(agenda) + [0]) + 1):
+            if tail and slot == JOIN_SLOT:
+                final = close_rows()
+            for step, c, p in sorted(agenda.get(slot, []), key=lambda x: -x[0]):
+                settle(c, step, p)
+                if step + 1 < depth(c):
+                    hop(c, step + 1, p).start()
+            if tail and wide.done < len(courses[0]):
+                wide.step()
+            elif final is not None and slot > JOIN_SLOT and final.done < len(courses[1]) - 1:
                 final.step()
-            for s in reversed(range(deepest)):
-                if 0 <= slot - s < len(order):
-                    c, p = order[slot - s]
-                    step = s + begin(c)
-                    if step < depth(c):
-                        settle(c, step, p)
-                        if step + 1 < depth(c):
-                            hop(c, step + 1, p).start()
         if tail:
             while final.done < len(courses[1]):
                 final.step()

time: 449 us -> 411 us (0.915)
  Pallas kernels: 440 us -> 402 us
    pallas_call x8, Pallas kernels: 347 us -> 310 us  [stage(): pl.pallas_call(kernel, in_specs=[in_hbm()] * n_in, out_specs=[in_hbm()] *...]
where the time goes in v8:
time: 411 us
  Pallas kernels  402 us (98%)
  local copies, waits for them, and re-layouts  6.89 us (2%)
    pallas_call x8, Pallas kernels, stage(): pl.pallas_call(kernel, in_specs=[in_hbm()] * n_in, out_specs=[in_hbm()] *...  310 us
    pallas_call x1, Pallas kernels, attn_bwd(): pl.pallas_call(functools.partial(bwd_kernel, riders), grid=(pairs, nb), i...  34.6 us
    pallas_call x1, Pallas kernels, attn_fwd(): pl.pallas_call(fwd_kernel, grid=(pairs, nb), in_specs=[pl.BlockSpec((BQ,...  22.2 us
    pallas_call x1, Pallas kernels, conv_mid_back(): pl.pallas_call(kernel, in_specs=[in_hbm()] * (9 + n), out_specs=[in_hbm()...  17.5 us
    pallas_call x1, Pallas kernels, conv_mid(): pl.pallas_call(kernel, in_specs=[in_hbm()] * 3, out_specs=[in_hbm()] * 4,...  12.6 us

profile of v8, /device:TPU:0, one launch (start us, length us, event | category | flops | bytes accessed | tf_op | source)
XLA Modules:
  0.0 410.9 jit_solution(8554858257876550757)
XLA Ops:
  0.7 0.7 constant_dynamic-update-slice_fusion.4
  1.3 0.7 constant_dynamic-update-slice_fusion.3
  2.0 0.7 constant_dynamic-update-slice_fusion.2
  2.7 0.7 constant_dynamic-update-slice_fusion.1
  3.4 0.7 constant_dynamic-update-slice_fusion
  4.1 0.8 dynamic-update-slice.5
  4.9 0.2 dynamic-update-slice.6
  5.1 0.6 bitcast_convert_fusion.refs_0_.refs_2_.g_h.refs_4_.refs_5_
  5.7 2.4 copy.37
  8.2 19.5 %ffn1_in.1 = (bf16[1024,1024]{1,0:T(8,128)(2,1)}, bf16[1024,1024]{1,0:T(8,128)(2,1)}, bf16[1024,1024]{1,0:T(8,128)(2,1)}) custom-call(f32[48,128]{1,0:T(8,128)} %bitcast_convert_fusion.refs_0_.refs_2_.g_h.refs_4_.refs_5_, bf16[256,1024]{1,0:T(8,128)(2,1)} %bitcast.26, bf16[1024,1024]{1,0:T(8,128)(2,1)} %refs_21_.1), custom_call_target="tpu_custom_call" | custom-call | flops 4294967296 | bytes 60000000 | tf_op jit(solution)/shard_map/ffn1_in/pallas_call | solution.py:765
  27.7 31.3 %ffn1_out.1 = (bf16[1024,1024]{1,0:T(8,128)(2,1)}, bf16[1024,768]{1,0:T(8,128)(2,1)}, f32[256,1024]{1,0:T(8,128)}, f32[8,1024]{1,0:T(8,128)}) custom-call(bf16[1024,1024]{1,0:T(8,128)(2,1)} %get-tuple-element.110.refs_0_.refs_20_, bf16[1024,1024]{1,0:T(8,128)(2,1)} %refs_8_.5, f32[48,128]{1,0:T(8,128)} %bitcast_convert_fusion.refs_0_.refs_2_.g_h.refs_4_.refs_5_, ...), custom_call_target="tpu_custom_call" | custom-call | flops 3758096384 | bytes 60000000 | tf_op jit(solution)/shard_map/ffn1_out/pallas_call | solution.py:765
  59.0 22.2 %attn_fwd.1 = (bf16[1024,256]{1,0:T(8,128)(2,1)}, bf16[2,2048,1024]{2,1,0:T(8,128)(2,1)}) custom-call(bf16[1024,768]{1,0:T(8,128)(2,1)} %get-tuple-element.111.q_ref.k_ref.v_ref.refs_0_.refs_1_.refs_2_, bf16[1024,768]{1,0:T(8,128)(2,1)} %get-tuple-element.111.q_ref.k_ref.v_ref.refs_0_.refs_1_.refs_2_, ...), custom_call_target="tpu_custom_call" | custom-call | tf_op jit(solution)/shard_map/attn_fwd/pallas_call | solution.py:1307
  81.2 29.9 %attn_out.1 = (bf16[1024,1024]{1,0:T(8,128)(2,1)}, f32[1024,256]{1,0:T(8,128)}, bf16[1024,256]{1,0:T(8,128)(2,1)}, bf16[1024,256]{1,0:T(8,128)(2,1)}, f32[256,1024]{1,0:T(8,128)}, /*index=5*/f32[8,1024]{1,0:T(8,128)}) custom-call(bf16[1024,256]{1,0:T(8,128)(2,1)} %get-tuple-element.112.refs_0_.refs_7_, bf16[256,1024]{1,0:T(8,128)(2,1)} %refs_8_.4, ...), custom_call_target="tpu_custom_call" | custom-call | flops 2147483648 | bytes 60000000 | tf_op jit(solution)/shard_map/attn_out/pallas_call | solution.py:765
  111.2 12.6 %conv_mid.1 = (bf16[1024,256]{1,0:T(8,128)(2,1)}, bf16[1024,256]{1,0:T(8,128)(2,1)}, f32[1024,256]{1,0:T(8,128)}, f32[8,1024]{1,0:T(8,128)}) custom-call(f32[1024,256]{1,0:T(8,128)} %get-tuple-element.114.glu_h.refs_6_, bf16[31,256]{1,0:T(8,128)(2,1)} %refs_4_.3, f32[48,128]{1,0:T(8,128)} %bitcast_convert_fusion.refs_0_.refs_2_.g_h.refs_4_.refs_5_), custom_call_target="tpu_custom_call" | custom-call | tf_op jit(solution)/shard_map/conv_mid/pallas_call | solution.py:999
  123.8 29.9 %conv_out.1 = (bf16[1024,1024]{1,0:T(8,128)(2,1)}, bf16[1024,1024]{1,0:T(8,128)(2,1)}, bf16[1024,1024]{1,0:T(8,128)(2,1)}, f32[256,1024]{1,0:T(8,128)}, f32[8,1024]{1,0:T(8,128)}) custom-call(bf16[1024,256]{1,0:T(8,128)(2,1)} %get-tuple-element.115.refs_0_.refs_4_, bf16[256,1024]{1,0:T(8,128)(2,1)} %refs_8_.3, ...), custom_call_target="tpu_custom_call" | custom-call | flops 4831838208 | bytes 60000000 | tf_op jit(solution)/shard_map/conv_out/pallas_call | solution.py:765
  153.7 31.8 %ffn2_out.1 = (bf16[1024,1024]{1,0:T(8,128)(2,1)}, bf16[1024,1024]{1,0:T(8,128)(2,1)}, f32[256,1024]{1,0:T(8,128)}, f32[256,1024]{1,0:T(8,128)}, f32[8,1024]{1,0...) custom-call(bf16[1024,1024]{1,0:T(8,128)(2,1)} %get-tuple-element.117.refs_0_.refs_3_, bf16[1024,1024]{1,0:T(8,128)(2,1)} %refs_1_.8, ...), custom_call_target="tpu_custom_call" | custom-call | flops 4294967296 | bytes 60000000 | tf_op jit(solution)/shard_map/ffn2_out/pallas_call | solution.py:765
  185.5 33.6 %ffn2_back.1 = (bf16[1024,1024]{1,0:T(8,128)(2,1)}, f32[1024,256]{1,0:T(8,128)}, f32[256,1024]{1,0:T(8,128)}, f32[8,1024]{1,0:T(8,128)}, bf16[2,4,2,128,256]{4,3...) custom-call(bf16[1024,1024]{1,0:T(8,128)(2,1)} %get-tuple-element.122.refs_0_, ...), custom_call_target="tpu_custom_call" | custom-call | flops 6979321856 | bytes 60000000 | tf_op jit(solution)/shard_map/ffn2_back/pallas_call | solution.py:765
  219.1 17.5 %conv_mid_back.1 = (bf16[1024,512]{1,0:T(8,128)(2,1)}, f32[32,256]{1,0:T(8,128)}, bf16[4,1,2,128,256]{4,3,2,1,0:T(8,128)(2,1)}, bf16[2,2,2,128,256]{4,3,2,1,0:T(8,128)(2,1)}) custom-call(f32[1024,256]{1,0:T(8,128)} %get-tuple-element.126.refs_0_, bf16[1024,256]{1,0:T(8,128)(2,1)} %get-tuple-element.127.refs_1_, f32[1024,256]{1,0:T(8,128)} %get-tuple-element.128.refs_2_, ...), custom_call_target="tpu_custom_call" | custom-call | tf_op jit(solution)/shard_map/conv_mid_back/pallas_call | solution.py:1124
  236.7 35.9 %conv_back.1 = (bf16[1024,1024]{1,0:T(8,128)(2,1)}, bf16[1024,256]{1,0:T(8,128)(2,1)}, f32[256,1024]{1,0:T(8,128)}, f32[8,1024]{1,0:T(8,128)}, bf16[2,2,2,128,25...) custom-call(bf16[1024,512]{1,0:T(8,128)(2,1)} %get-tuple-element.134, ...), custom_call_target="tpu_custom_call" | custom-call | flops 3221225472 | bytes 60000000 | tf_op jit(solution)/shard_map/conv_back/pallas_call | solution.py:765
  272.6 34.6 %attn_bwd.1 = (bf16[1024,256]{1,0:T(8,128)(2,1)}, bf16[1024,256]{1,0:T(8,128)(2,1)}, bf16[1024,256]{1,0:T(8,128)(2,1)}, f32[128,128]{1,0:T(8,128)}, bf16[1,2,2,1...) custom-call(bf16[1024,768]{1,0:T(8,128)(2,1)} %get-tuple-element.111, ...), custom_call_target="tpu_custom_call" | custom-call | flops 5368709120 | bytes 20000000 | tf_op jit(solution)/shard_map/attn_bwd/pallas_call | solution.py:1339
  307.2 98.1 %attn_back.1 = (f32[256,1024]{1,0:T(8,128)}, f32[128,768]{1,0:T(8,128)}, f32[1024,128]{1,0:T(8,128)}, f32[128,1024]{1,0:T(8,128)}, f32[256,128]{1,0:T(8,128)}, /...) custom-call(bf16[1024,256]{1,0:T(8,128)(2,1)} %get-tuple-element.147, ...), custom_call_target="tpu_custom_call" | custom-call | flops 9663676416 | bytes 60000000 | tf_op jit(solution)/shard_map/attn_back/pallas_call | solution.py:765
  405.3 5.4 %publish.1 = (f32[256,1,1024]{2,1,0:T(1,128)}, f32[256,1,1024]{2,1,0:T(1,128)}, f32[128,1024]{1,0:T(8,128)}, f32[1024,128]{1,0:T(8,128)}, f32[3,128,256]{2,1,0:T...) custom-call(f32[256,1024]{1,0:T(8,128)} %get-tuple-element.120.refs_, ...), custom_call_target="tpu_custom_call" | custom-call | tf_op jit(solution)/shard_map/publish/pallas_call | solution.py:860
  (1 shorter events, 0.0 us)

commit v9 on v8

--- a/solution.py
+++ b/solution.py
@@ -198,6 +198,111 @@
     return lambda: pl.semaphore_wait(barrier, len(targets))
 
 
+def split_pair(x):
+    left = lax.broadcasted_iota(jnp.int32, x.shape, 1) < HEAD
+    zero = jnp.zeros_like(x)
+    return jnp.concatenate([jnp.where(left, x, zero), jnp.where(left, zero, x)], 0)
+
+def join_pair(x):
+    rows = x.shape[0] // 2
+    left = lax.broadcasted_iota(jnp.int32, (rows, x.shape[1]), 1) < HEAD
+    return jnp.where(left, x[:rows], x[rows:])
+
+def spot_table(spots):
+    spot = lax.broadcasted_iota(jnp.int32, (spots, BQ), 0)
+    inner = jnp.clip(spot - REL_LEFT, 0, REL_LEFT + REL_RIGHT)
+    row = jnp.where(spot < 3 * BQ, inner, jnp.where(spot < 4 * BQ, 0, REL_LEFT + REL_RIGHT))
+    return (lax.broadcasted_iota(jnp.int32, (spots, BQ), 1) == row).astype(jnp.bfloat16)
+
+
+def wide_table(rel_ref, wide_ref):
+    wide_ref[...] = jnp.zeros_like(wide_ref)
+    turned = rel_ref[...].astype(jnp.float32)
+    cols = turned.shape[1]
+    wide_ref[0:HEAD, :cols] = turned
+    wide_ref[HEAD : 2 * HEAD, :cols] = turned
+    return wide_ref[...].T.astype(jnp.bfloat16)
+
+
+def fwd_kernel(q_ref, k_ref, v_ref, relt_ref, mixed_ref, probs_ref, bias_ref, rel_ref, wide_ref):
+    ib = pl.program_id(0)
+
+    @pl.when(ib == 0)
+    def _():
+        rel_ref[...] = nn(spot_table(5 * BQ), wide_table(relt_ref, wide_ref)).astype(jnp.bfloat16)
+
+    pairs = q_ref.shape[1] // 128
+    nkeys = k_ref.shape[0] // BQ
+    places = [pl.multiple_of(jnp.clip(jb - ib + 2, 0, 4) * BQ, BQ) for jb in range(nkeys)]
+    for pr in range(pairs):
+        cols = slice(pr * 128, (pr + 1) * 128)
+        qs = split_pair(q_ref[:, cols] * 0.125)
+        s = nt(qs, k_ref[:, cols])
+        b = nt(qs, rel_ref[...])
+        rows = b.shape[0] // 2
+        bias_ref[pr, :, 0:BQ] = b[:, 3 * BQ : 4 * BQ]
+        for h in range(2):
+            r = pltpu.roll(b[h * rows : (h + 1) * rows, :WIN], 0, 1, stride=1, stride_axis=0)
+            bias_ref[pr, h * rows : (h + 1) * rows, BQ : 4 * BQ] = r[:, : 3 * BQ]
+        bias_ref[pr, :, 4 * BQ :] = b[:, 4 * BQ :]
+        parts = [s[:, jb * BQ : (jb + 1) * BQ] + bias_ref[pr, :, pl.ds(places[jb], BQ)] for jb in range(nkeys)]
+        top = functools.reduce(jnp.maximum, parts)
+        m = jnp.max(top, -1, keepdims=True)
+        es = [jnp.exp(p - m) for p in parts]
+        tot = jnp.sum(functools.reduce(jnp.add, es), -1, keepdims=True)
+        inv = 1.0 / tot
+        for jb in range(nkeys):
+            probs_ref[pr, :, jb * BQ : (jb + 1) * BQ] = (es[jb] * inv).astype(jnp.bfloat16)
+        mixed_ref[:, cols] = join_pair(nn(probs_ref[pr], v_ref[:, cols])).astype(jnp.bfloat16)
+
+
+def attend_back_block(ib, qkv_ref, probs_ref, do_ref, dq_ref, tot_ref, dkt, dvt, dta, dz_ref, hot_ref, relb_ref):
+    frames, heads = qkv_ref.shape[0], qkv_ref.shape[1] // 3
+    at = pl.ds(pl.multiple_of(ib * BQ, BQ), BQ)
+    pairs = heads // 128
+    nkeys = frames // BQ
+    rows = BQ
+    r2 = lax.broadcasted_iota(jnp.int32, (2 * rows, 2 * rows), 0)
+    c2 = lax.broadcasted_iota(jnp.int32, (2 * rows, 2 * rows), 1)
+    mirror = (r2 + c2 == jnp.where(r2 < rows, rows - 1, 3 * rows - 1)).astype(jnp.bfloat16)
+    places = [pl.multiple_of(jnp.clip(jb - ib + 2, 0, 4) * BQ, BQ) for jb in range(nkeys)]
+    for pr in range(pairs):
+        cols = slice(pr * 128, (pr + 1) * 128)
+        keys = qkv_ref[:, heads + pr * 128 : heads + (pr + 1) * 128]
+        values = qkv_ref[:, 2 * heads + pr * 128 : 2 * heads + (pr + 1) * 128]
+        qs = split_pair(qkv_ref[at, cols] * 0.125)
+        dos = split_pair(do_ref[at, cols])
+        p = probs_ref[pr]
+        dprob = nt(dos, values)
+        dvt[pr] += tn(dos, p)
+        pf = p.astype(jnp.float32)
+        acc = functools.reduce(
+            jnp.add, [pf[:, jb * BQ : (jb + 1) * BQ] * dprob[:, jb * BQ : (jb + 1) * BQ] for jb in range(nkeys)]
+        )
+        inner = jnp.sum(acc, -1, keepdims=True)
+        tot_ref[pr] = jnp.zeros(tot_ref.shape[1:], jnp.float32)
+        for jb in range(nkeys):
+            sl = slice(jb * BQ, (jb + 1) * BQ)
+            dz = (pf[:, sl] * (dprob[:, sl] - inner)).astype(jnp.bfloat16)
+            dz_ref[pr, :, sl] = dz
+            tot_ref[pr, :, pl.ds(places[jb], BQ)] += dz.astype(jnp.float32)
+        w = jnp.concatenate([tot_ref[pr, :, BQ : 4 * BQ].astype(jnp.bfloat16), jnp.zeros((2 * rows, BQ), jnp.bfloat16)], 1)
+        w = nn(mirror, w)
+        outs = [pltpu.roll(w[h * rows : (h + 1) * rows], WIN - rows + 1, 1, stride=1, stride_axis=0) for h in range(2)]
+        d = nn(mirror, jnp.concatenate(outs, 0).astype(jnp.bfloat16)).astype(jnp.bfloat16)
+        drel = nn(d, hot_ref[...])
+        col = lax.broadcasted_iota(jnp.int32, drel.shape, 1)
+        low = jnp.sum(tot_ref[pr, :, :BQ], -1, keepdims=True)
+        high = jnp.sum(tot_ref[pr, :, 4 * BQ :], -1, keepdims=True)
+        drel = drel + jnp.where(col == 0, low, 0.0) + jnp.where(col == REL_LEFT + REL_RIGHT, high, 0.0)
+        drel = drel.astype(jnp.bfloat16)
+        dz = dz_ref[pr]
+        dq = nn(dz, keys) + nn(drel, relb_ref[...])
+        dq_ref[at, cols] = (join_pair(dq) * 0.125).astype(jnp.bfloat16)
+        dkt[pr] += tn(qs, dz)
+        dta[...] += tn(drel, qs)
+
+
 class Doubling:
     def __init__(self, course, refs, lands, sems, partner):
         self.course, self.items, self.sems, self.partner = course, list(zip(refs, lands)), sems, partner
@@ -234,7 +339,7 @@
             self.done += 1
 
 
-def stage(name, cid, rows, width, count, gains, *, leave=None, enter=None, dws=(), grads=(), small=None, tail=None, junction, row_in=(), row_out=(), sums=0):
+def stage(name, cid, rows, width, count, gains, *, leave=None, enter=None, dws=(), grads=(), small=None, tail=None, attend=None, junction, row_in=(), row_out=(), sums=0):
     chunk = rows // CHUNKS
     frames = rows * 4
     bits_all = count.bit_length() - 1
@@ -284,15 +389,32 @@
     if not leave:
         groups.append(len(vm_ins))
     add_dw(("near", "join"))
-    kept = not tail
+    kept = not (tail or attend)
+    kept_rows = not tail
     if enter:
         we_i = add_in(enter[0])
         extra_i = [add_in(e) for e in enter[3]]
         we_s = add_scratch(pltpu.VMEM(flat_shape(enter[0])[::-1], bf)) if enter[1] else None
         all_o = add_out((frames, width), bf, 4 * CHUNKS, kept)
         e_o = [add_out((frames, c), d, 4 * CHUNKS, kept) for c, d in enter[4]]
-    r_o = [add_out((rows, width), d, CHUNKS, kept) for d in row_out]
-    s_o = [add_out((8, width), f32, 1, kept) for _ in range(sums)]
+    r_o = [add_out((rows, width), d, CHUNKS, kept_rows) for d in row_out]
+    s_o = [add_out((8, width), f32, 1, kept_rows) for _ in range(sums)]
+    if attend:
+        qkv_i, probs_i, table_i = add_in(attend[0]), add_in(attend[1], True), add_in(attend[2])
+        add_dw(("post",))
+        heads = attend[0].shape[1] // 3
+        pairs = heads // 128
+        d_o = [add_out((frames, heads), bf, 4 * CHUNKS) for _ in range(3)] + [add_out((128, 128), f32, 1)]
+        attend_s = [
+            add_scratch(item)
+            for item in (
+                pltpu.VMEM((pairs, 2 * BQ, 5 * BQ), f32), pltpu.VMEM((pairs, 128, frames), f32), pltpu.VMEM((pairs, 128, frames), f32),
+                pltpu.VMEM((128, 128), f32), pltpu.VMEM((pairs, 2 * BQ, frames), bf), pltpu.VMEM((WIN, BQ), bf), pltpu.VMEM((128, 128), bf),
+            )
+        ]
+        wide_s = add_scratch(pltpu.VMEM((128, 128), f32))
+        probs_s = add_scratch(pltpu.VMEM((2, pairs, 2 * BQ, frames), bf))
+        probs_sem = add_scratch(pltpu.SemaphoreType.DMA((2,)))
     if small:
         vectors_in, table_in, taps_in = small
         vector_i = [add_in(v) for v in vectors_in]
@@ -314,13 +436,14 @@
         if d[2] == "join":
             dw_o.append(add_out(shape, bf, shape[0]))
         else:
-            plan.append((shape, 0, d[3], bits_all if tail else 1, add_scratch(pltpu.VMEM(shape, bf)), None, None))
+            plan.append((shape, 0, d[3], bits_all if tail else min(d[4], bits_all), add_scratch(pltpu.VMEM(shape, bf)), None, None))
             dw_o.append(len(plan) - 1)
     dw_in = [(add_in(d[0]), add_in(d[1])) for d in dws]
     first_grad = len(plan)
     for g in grads:
+        g, ahead = g if isinstance(g, tuple) else (g, 1)
         shape = g.array.shape
-        plan.append((shape, g.bit, g.turned, bits_all if tail else g.bit + 1, None, add_in(g.array, True), add_scratch(arriving(shape))))
+        plan.append((shape, g.bit, g.turned, bits_all if tail else min(g.bit + ahead, bits_all), None, add_in(g.array, True), add_scratch(arriving(shape))))
     chains = []
     slots = 0
     for shape, bit, turned, end, src_s, src_i, keep_s in plan:
@@ -621,6 +744,16 @@
             wide = Doubling(courses[0], [vout(o) for o in small_o], [t[l] for l in small_l], [t[s] for s in small_sems[:2]], partner)
             wide.start()
 
+        mid = set()
+
+        def hasten(which):
+            for c in which:
+                if len(chains[c][5]) > 1:
+                    mid.add(c)
+                    for p in range(chains[c][0]):
+                        settle(c, 0, p)
+                        hop(c, 1, p).start()
+
         if enter:
             begin_loads(len(groups) - 1)
             need(we_i, *extra_i)
@@ -635,11 +768,101 @@
                         if o[0] >= 0:
                             store_rows(o, block, k).start()
 
+        if attend:
+            tot_ref, dkt, dvt, dta, dz_ref, hot_ref, relb_ref = [t[s] for s in attend_s]
+            dq, dk, dv = [vout(o) for o in d_o[:3]]
+            need(qkv_i, table_i)
+            need_for("post")
+            for ref in (dkt, dvt, dta):
+                ref[...] = jnp.zeros(ref.shape, f32)
+            hot_ref[...] = spot_table(WIN)
+            relb_ref[...] = wide_table(vin(table_i), t[wide_s])
+
+            def block_of(j):
+                chip_j = chip + (j // 4) * (1 - 2 * chip)
+                core_j = core + (j % 2) * (1 - 2 * core)
+                return (chip_j * 2 + core_j) * 2 + (j // 2) % 2
+
+            def fetch(j):
+                at = pl.ds(pl.multiple_of(block_of(j) * 2 * BQ, 2 * BQ), 2 * BQ)
+                return pltpu.make_async_copy(hbm_in[probs_i].at[:, at, :], t[probs_s].at[j % 2], t[probs_sem].at[j % 2])
+
+            fetch(0).start()
+
+            def pass_on(*ks):
+                for k in ks:
+                    got_far(k).wait_recv()
+                    all_fwd(k).start()
+
+            def near(*ks):
+                for k in ks:
+                    got_sib(k).wait_recv()
+                    work(k, me, sib)
+
+            def distant(*ks):
+                for k in ks:
+                    got_diag(k).wait_recv()
+                    work(k, far, diag)
+
+            def before(n):
+                if n == 0:
+                    near(0, 1)
+                elif n == 1:
+                    pass_on(0)
+                elif n == 2:
+                    near(2, 3)
+                    pass_on(1)
+                elif n == 3:
+                    pass_on(2)
+                    hasten(range(first_grad, len(chains)))
+                elif n == 4:
+                    pass_on(3)
+                    distant(0, 1)
+                elif n == 5:
+                    hasten(range(first_grad))
+                elif n == 6:
+                    distant(2, 3)
+                    for k in range(CHUNKS):
+                        if any(d[2] == "post" and k < d[6] for d in dws):
+                            fill(k, "post")
+
+            def query_block(j, c):
+                for n in range(7):
+
+                    @pl.when(j == n)
+                    def _(n=n):
+                        before(n)
+
+                @pl.when(j < 7)
+                def _():
+                    fetch(j + 1).start()
+
+                fetch(j).wait()
+                attend_back_block(
+                    block_of(j), vin(qkv_i), t[probs_s].at[j % 2], vout(e_o[0]), dq, tot_ref, dkt, dvt, dta, dz_ref, hot_ref, relb_ref
+                )
+                return c
+
+            lax.fori_loop(0, 8, query_block, 0)
+            for pr in range(pairs):
+                dk[:, pr * 128 : (pr + 1) * 128] = dkt[pr].T.astype(bf)
+                dv[:, pr * 128 : (pr + 1) * 128] = dvt[pr].T.astype(bf)
+            vout(d_o[3])[...] = dta[...]
+            for o in d_o:
+                store_whole(o).start()
+        elif enter:
+            got_sib(0).wait_recv()
+            work(0, me, sib)
+
             def gather(k, c):
-                got_sib(k).wait_recv()
-                work(k, me, sib)
                 got_far(k).wait_recv()
                 all_fwd(k).start()
+
+                @pl.when(k + 1 < CHUNKS)
+                def _():
+                    got_sib(k + 1).wait_recv()
+                    work(k + 1, me, sib)
+
                 got_diag(k).wait_recv()
                 work(k, far, diag)
                 if small:
@@ -695,7 +918,7 @@
             return final
 
         depth = lambda c: len(chains[c][5])
-        begin = lambda c: early if c in lead else 0
+        begin = lambda c: early if c in lead else 1 if c in mid else 0
         agenda, fresh_slot = {}, 1
         for c in range(len(chains)):
             new = tail and c < first_grad and c not in lead
@@ -748,7 +971,7 @@
             return c
 
         lax.fori_loop(0, CHUNKS, drain, 0)
-        for o in s_o + (small_o + [lead_o] if tail else []):
+        for o in s_o + (small_o + [lead_o] if tail else []) + (d_o if attend else []):
             if o[0] >= 0:
                 store_whole(o).wait()
         for d, o in zip(dws, dw_o):
@@ -1140,229 +1363,32 @@
     return outs[0], outs[1], riders.results(outs[2:])
 
 
-def split_pair(x):
-    left = lax.broadcasted_iota(jnp.int32, x.shape, 1) < HEAD
-    zero = jnp.zeros_like(x)
-    return jnp.concatenate([jnp.where(left, x, zero), jnp.where(left, zero, x)], 0)
-
-def join_pair(x):
-    rows = x.shape[0] // 2
-    left = lax.broadcasted_iota(jnp.int32, (rows, x.shape[1]), 1) < HEAD
-    return jnp.where(left, x[:rows], x[rows:])
-
-def spot_table(spots):
-    spot = lax.broadcasted_iota(jnp.int32, (spots, BQ), 0)
-    inner = jnp.clip(spot - REL_LEFT, 0, REL_LEFT + REL_RIGHT)
-    row = jnp.where(spot < 3 * BQ, inner, jnp.where(spot < 4 * BQ, 0, REL_LEFT + REL_RIGHT))
-    return (lax.broadcasted_iota(jnp.int32, (spots, BQ), 1) == row).astype(jnp.bfloat16)
-
-
-def wide_table(rel_ref, wide_ref):
-    wide_ref[...] = jnp.zeros_like(wide_ref)
-    turned = rel_ref[...].astype(jnp.float32)
-    cols = turned.shape[1]
-    wide_ref[0:HEAD, :cols] = turned
-    wide_ref[HEAD : 2 * HEAD, :cols] = turned
-    return wide_ref[...].T.astype(jnp.bfloat16)
-
-
-def fwd_kernel(q_ref, k_ref, v_ref, relt_ref, mixed_ref, probs_ref, bias_ref, rel_ref, wide_ref):
-    ib = pl.program_id(1)
-
-    @pl.when((ib == 0) & (pl.program_id(0) == 0))
-    def _():
-        rel_ref[...] = nn(spot_table(5 * BQ), wide_table(relt_ref, wide_ref)).astype(jnp.bfloat16)
-
-    qs = split_pair(q_ref[...] * 0.125)
-    s = nt(qs, k_ref[...])
-    b = nt(qs, rel_ref[...])
-    rows = b.shape[0] // 2
-    bias_ref[:, 0:BQ] = b[:, 3 * BQ : 4 * BQ]
-    for h in range(2):
-        r = pltpu.roll(b[h * rows : (h + 1) * rows, :WIN], 0, 1, stride=1, stride_axis=0)
-        bias_ref[h * rows : (h + 1) * rows, BQ : 4 * BQ] = r[:, : 3 * BQ]
-    bias_ref[:, 4 * BQ :] = b[:, 4 * BQ :]
-    nkeys = s.shape[1] // BQ
-    parts = []
-    for jb in range(nkeys):
-        at = pl.multiple_of(jnp.clip(jb - ib + 2, 0, 4) * BQ, BQ)
-        parts.append(s[:, jb * BQ : (jb + 1) * BQ] + bias_ref[:, pl.ds(at, BQ)])
-    top = functools.reduce(jnp.maximum, parts)
-    m = jnp.max(top, -1, keepdims=True)
-    es = [jnp.exp(p - m) for p in parts]
-    tot = jnp.sum(functools.reduce(jnp.add, es), -1, keepdims=True)
-    inv = 1.0 / tot
-    for jb in range(nkeys):
-        probs_ref[0, :, jb * BQ : (jb + 1) * BQ] = (es[jb] * inv).astype(jnp.bfloat16)
-    mixed_ref[...] = join_pair(nn(probs_ref[0], v_ref[...])).astype(jnp.bfloat16)
-
-def bwd_kernel(riders, *refs):
-    n = len(riders.plan)
-    q_ref, k_ref, v_ref, relt_ref, probs_ref, do_ref, db_h, mix_h = refs[:8]
-    ride_in = refs[8 : 8 + n]
-    dq_ref, dk_ref, dv_ref, dt_ref, dw_h = refs[8 + n : 13 + n]
-    ride_out = refs[13 + n : 13 + 2 * n]
-    tot_ref, dkt, dvt, dta, dz_ref, hot_ref, db_v, mix_v, dw_v, dw_land, dw_half, relb_ref, wide_ref, osem, psem = refs[13 + 2 * n : 28 + 2 * n]
-    riders.bind(ride_in, ride_out, refs[28 + 2 * n :])
-    pr, ib, nb = pl.program_id(0), pl.program_id(1), pl.num_programs(1)
-    dp, mp = lax.axis_index("dp"), lax.axis_index("mp")
-    loads = [pltpu.make_async_copy(db_h, db_v, osem.at[0]), pltpu.make_async_copy(mix_h, mix_v, osem.at[1])]
-    pieces = dw_v.shape[0]
-    hops = [halving_copy(dw_v, dw_land, p, 0, psem.at[0], psem.at[1], p) for p in range(pieces)]
-    flip = dw_land.shape[2] % 128 == 0
-    stores = [
-        pltpu.make_async_copy(region(dw_half, p, PIECE, flip), region(dw_h, p, PIECE, flip), psem.at[2, p]) for p in range(pieces)
-    ]
-
-    @pl.when((ib == 0) & (pr == 0))
-    def _():
-        meet = greet(sorted_targets(riders, dp, mp))
-        for cp in loads:
-            cp.start()
-        hot_ref[...] = spot_table(WIN)
-        relb_ref[...] = wide_table(relt_ref, wide_ref)
-        meet()
-        riders.start()
-        for cp in loads:
-            cp.wait()
-        for p in range(pieces):
-            g = tn(db_v[...], mix_v[:, p * PIECE : (p + 1) * PIECE])
-            dw_v[p] = g.astype(jnp.bfloat16).reshape(dw_v.shape[1:])
-            hops[p].start()
-
-    @pl.when(ib == 0)
-    def _():
-        dkt[...] = jnp.zeros_like(dkt)
-        dvt[...] = jnp.zeros_like(dvt)
-    @pl.when((ib == 0) & (pr == 0))
-    def _():
-        dta[...] = jnp.zeros_like(dta)
-    qs = split_pair(q_ref[...] * 0.125)
-    dos = split_pair(do_ref[...])
-    p = probs_ref[0]
-    dp = nt(dos, v_ref[...])
-    nkeys = dp.shape[1] // BQ
-    dvt[...] += tn(dos, p)
-    pf = p.astype(jnp.float32)
-    acc = None
-    for jb in range(nkeys):
-        sl = slice(jb * BQ, (jb + 1) * BQ)
-        t = pf[:, sl] * dp[:, sl]
-        acc = t if acc is None else acc + t
-    inner = jnp.sum(acc, -1, keepdims=True)
-    tot_ref[...] = jnp.zeros_like(tot_ref)
-    for jb in range(nkeys):
-        sl = slice(jb * BQ, (jb + 1) * BQ)
-        dz = (pf[:, sl] * (dp[:, sl] - inner)).astype(jnp.bfloat16)
-        dz_ref[:, sl] = dz
-        at = pl.multiple_of(jnp.clip(jb - ib + 2, 0, 4) * BQ, BQ)
-        tot_ref[:, pl.ds(at, BQ)] += dz.astype(jnp.float32)
-    rows = BQ
-    r2 = lax.broadcasted_iota(jnp.int32, (2 * rows, 2 * rows), 0)
-    c2 = lax.broadcasted_iota(jnp.int32, (2 * rows, 2 * rows), 1)
-    mirror = (r2 + c2 == jnp.where(r2 < rows, rows - 1, 3 * rows - 1)).astype(jnp.bfloat16)
-    w = jnp.concatenate([tot_ref[:, BQ : 4 * BQ].astype(jnp.bfloat16), jnp.zeros((2 * rows, BQ), jnp.bfloat16)], 1)
-    w = nn(mirror, w)
-    outs = [pltpu.roll(w[h * rows : (h + 1) * rows], WIN - rows + 1, 1, stride=1, stride_axis=0) for h in range(2)]
-    d = nn(mirror, jnp.concatenate(outs, 0).astype(jnp.bfloat16)).astype(jnp.bfloat16)
-    drel = nn(d, hot_ref[...])
-    col = lax.broadcasted_iota(jnp.int32, drel.shape, 1)
-    low = jnp.sum(tot_ref[:, :BQ], -1, keepdims=True)
-    high = jnp.sum(tot_ref[:, 4 * BQ :], -1, keepdims=True)
-    drel = drel + jnp.where(col == 0, low, 0.0) + jnp.where(col == REL_LEFT + REL_RIGHT, high, 0.0)
-    drel = drel.astype(jnp.bfloat16)
-    dz = dz_ref[...]
-    dq = nn(dz, k_ref[...]) + nn(drel, relb_ref[...])
-    dq_ref[...] = (join_pair(dq) * 0.125).astype(jnp.bfloat16)
-    dkt[...] += tn(qs, dz)
-    dta[...] += tn(drel, qs)
-    @pl.when(ib == nb - 1)
-    def _():
-        dk_ref[...] = dkt[...].T.astype(jnp.bfloat16)
-        dv_ref[...] = dvt[...].T.astype(jnp.bfloat16)
-        dt_ref[...] = dta[...]
-
-    @pl.when((ib == nb - 1) & (pr == pl.num_programs(0) - 1))
-    def _():
-        own, _ = place(lax.axis_index("dp"), 0)
-        for p in range(pieces):
-            hops[p].wait_recv()
-            halving_add(lambda q, j: dw_v[q, j, own], dw_land, dw_half, p, True)
-            stores[p].start()
-        riders.finish()
-        for p in range(pieces):
-            hops[p].wait_send()
-            stores[p].wait()
-
-
-def sorted_targets(riders, dp, mp):
-    return [(place(dp, b)[1], mp) for b in sorted({0} | {x[1] for x in riders.plan})]
-
-
 def attn_fwd(qkv, rel):
     frames, cols = qkv.shape
-    pairs = cols // 3 // 128
+    heads = cols // 3
+    pairs = heads // 128
     nb = frames // BQ
     bf = jnp.bfloat16
     return pl.pallas_call(
         fwd_kernel,
-        grid=(pairs, nb),
+        grid=(nb,),
         in_specs=[
-            pl.BlockSpec((BQ, 128), lambda p, i: (i, p)),
-            pl.BlockSpec((frames, 128), lambda p, i: (0, pairs + p)),
-            pl.BlockSpec((frames, 128), lambda p, i: (0, 2 * pairs + p)),
-            pl.BlockSpec(rel.shape, lambda p, i: (0, 0)),
+            pl.BlockSpec((BQ, heads), lambda i: (i, 0)),
+            pl.BlockSpec((frames, heads), lambda i: (0, 1)),
+            pl.BlockSpec((frames, heads), lambda i: (0, 2)),
+            pl.BlockSpec(rel.shape, lambda i: (0, 0)),
         ],
         out_specs=[
-            pl.BlockSpec((BQ, 128), lambda p, i: (i, p)),
-            pl.BlockSpec((1, 2 * BQ, frames), lambda p, i: (p, i, 0)),
+            pl.BlockSpec((BQ, heads), lambda i: (i, 0)),
+            pl.BlockSpec((pairs, 2 * BQ, frames), lambda i: (0, i, 0)),
         ],
-        out_shape=[jax.ShapeDtypeStruct((frames, cols // 3), bf), jax.ShapeDtypeStruct((pairs, 2 * frames, frames), bf)],
-        scratch_shapes=[pltpu.VMEM((2 * BQ, 5 * BQ), jnp.float32), pltpu.VMEM((5 * BQ, 128), bf), pltpu.VMEM((128, 128), jnp.float32)],
+        out_shape=[jax.ShapeDtypeStruct((frames, heads), bf), jax.ShapeDtypeStruct((pairs, 2 * frames, frames), bf)],
+        scratch_shapes=[
+            pltpu.VMEM((pairs, 2 * BQ, 5 * BQ), jnp.float32), pltpu.VMEM((5 * BQ, 128), bf), pltpu.VMEM((128, 128), jnp.float32)
+        ],
         compiler_params=pltpu.CompilerParams(vmem_limit_bytes=VMEM_LIMIT),
         name="attn_fwd",
     )(qkv, qkv, qkv, rel)
-
-def attn_bwd(qkv, rel, probs, dmixed, grad_rows, mixed, grads, cid):
-    frames, cols = qkv.shape
-    pairs = cols // 3 // 128
-    nb = frames // BQ
-    bf = jnp.bfloat16
-    count = lax.axis_size("dp")
-    blk = pl.BlockSpec((BQ, 128), lambda p, i: (i, p))
-    full = pl.BlockSpec((frames, 128), lambda p, i: (0, p))
-    riders = Riders(grads)
-    width = grad_rows.shape[1]
-    shape = (mixed.shape[1] // PIECE, count // 2, 2, width // count, PIECE)
-    half = halved(shape, True)
-    vm = pltpu.VMEM
-    outs = pl.pallas_call(
-        functools.partial(bwd_kernel, riders),
-        grid=(pairs, nb),
-        in_specs=[
-            blk,
-            pl.BlockSpec((frames, 128), lambda p, i: (0, pairs + p)),
-            pl.BlockSpec((frames, 128), lambda p, i: (0, 2 * pairs + p)),
-            pl.BlockSpec(rel.shape, lambda p, i: (0, 0)),
-            pl.BlockSpec((1, 2 * BQ, frames), lambda p, i: (p, i, 0)),
-            blk,
-        ]
-        + [in_hbm()] * (2 + len(grads)),
-        out_specs=[blk, full, full, pl.BlockSpec((128, 128), lambda p, i: (0, 0))] + [in_hbm()] * (1 + len(grads)),
-        out_shape=[jax.ShapeDtypeStruct((frames, cols // 3), bf)] * 3 + [jax.ShapeDtypeStruct((128, 128), jnp.float32), half] + riders.after,
-        scratch_shapes=[
-            vm((2 * BQ, 5 * BQ), jnp.float32), vm((128, frames), jnp.float32), vm((128, frames), jnp.float32),
-            vm((128, 128), jnp.float32), vm((2 * BQ, frames), bf), vm((WIN, BQ), bf),
-            vm(grad_rows.shape, bf), vm(mixed.shape, bf), vm(shape, bf), arriving(shape), vm(half.shape, half.dtype),
-            vm((128, 128), bf), vm((128, 128), jnp.float32),
-            pltpu.SemaphoreType.DMA((2,)), pltpu.SemaphoreType.DMA((3, shape[0])),
-        ]
-        + riders.scratch,
-        compiler_params=pltpu.CompilerParams(vmem_limit_bytes=VMEM_LIMIT, collective_id=cid, has_side_effects=True),
-        cost_estimate=pl.CostEstimate(flops=20 * frames * frames * 128 * pairs, bytes_accessed=20_000_000, transcendentals=0),
-        name="attn_bwd",
-    )(qkv, qkv, qkv, rel, probs, dmixed, grad_rows, mixed, *riders.arrays)
-    return list(outs[:4]) + [[Grad(outs[4], 1, True)] + riders.results(outs[5:])]
 
 
 def body(
@@ -1495,13 +1521,16 @@
     dpaired, tap_sums, (gw2_out, ga_in) = conv_mid_back(
         de3, slope3, depth_unit, depth_stat, glu, sig, tail, w_depth, gains, width, 11, [gw2_out, ga_in]
     )
-    db2, dmixed, grad2, dgc, (gconv_in, gconv_out, gb_in, gw2_out, ga_in) = stage(
+    grad2, dgc, dq, dk, dv, dt, (gconv_in, gconv_out, gattn, gb_in, gw2_out, ga_in) = stage(
         "conv_back", 6, rows, width, dp_count, gains, leave=(dpaired, flat_conv, True),
-        enter=(w_attn_out, True, plain_out, (), ((w_attn_out.shape[0], bf),)), dws=(weight(a3, dpaired, "far", False), weight(db3, act3, "far", True)), grads=(gb_in, gw2_out, ga_in),
+        enter=(w_attn_out, True, plain_out, (), ((w_attn_out.shape[0], bf),)),
+        dws=(
+            weight(a3, dpaired, "far", False, 2),
+            weight(db3, act3, "far", True, 2),
+            weight("all", mixed, "post", True),
+        ),
+        grads=((gb_in, 2), gw2_out, (ga_in, 2)), attend=(qkv, probs, turned_table),
         junction=backward(1.0, 2), row_in=(grad3, s2), row_out=(f32,), sums=1,
-    )
-    dq, dk, dv, dt, (gattn, gb_in, ga_in, gconv_in, gconv_out) = attn_bwd(
-        qkv, turned_table, probs, dmixed, db2, mixed, [gb_in, ga_in, gconv_in, gconv_out], 9
     )
     dqkv = (dq, dk, dv)
     waiting = pending([gattn, gconv_in, gconv_out, ga_in, gb_in, gw2_out])

time: 411 us -> 405 us (0.985)
  Pallas kernels: 402 us -> 393 us
    pallas_call x2 -> x1, Pallas kernels: 56.8 us -> 20 us  [attn_fwd(): pl.pallas_call(fwd_kernel, grid=(nb,), in_specs=[pl.BlockSpec((BQ, heads)...]
    pallas_call x8, Pallas kernels: 310 us -> 337 us  [stage(): pl.pallas_call(kernel, in_specs=[in_hbm()] * n_in, out_specs=[in_hbm()] *...]
where the time goes in v9:
time: 405 us; the launch traced here: 401 us
  Pallas kernels  393 us (97%)
  local copies, waits for them, and re-layouts  6.89 us (2%)
    pallas_call x8, Pallas kernels, stage(): pl.pallas_call(kernel, in_specs=[in_hbm()] * n_in, out_specs=[in_hbm()] *...  337 us
    pallas_call x1, Pallas kernels, attn_fwd(): pl.pallas_call(fwd_kernel, grid=(nb,), in_specs=[pl.BlockSpec((BQ, heads)...  20 us
    pallas_call x1, Pallas kernels, conv_mid_back(): pl.pallas_call(kernel, in_specs=[in_hbm()] * (9 + n), out_specs=[in_hbm()...  17.6 us
    pallas_call x1, Pallas kernels, conv_mid(): pl.pallas_call(kernel, in_specs=[in_hbm()] * 3, out_specs=[in_hbm()] * 4,...  12.6 us

profile of v9, /device:TPU:0, one launch (start us, length us, event | category | flops | bytes accessed | tf_op | source)
XLA Modules:
  0.0 401.3 jit_solution(10869927820139954676)
XLA Ops:
  0.7 0.7 constant_dynamic-update-slice_fusion.4
  1.3 0.7 constant_dynamic-update-slice_fusion.3
  2.0 0.7 constant_dynamic-update-slice_fusion.2
  2.7 0.7 constant_dynamic-update-slice_fusion.1
  3.4 0.7 constant_dynamic-update-slice_fusion
  4.1 0.8 dynamic-update-slice.5
  4.9 0.2 dynamic-update-slice.6
  5.1 0.6 bitcast_convert_fusion.refs_0_.refs_2_.g_h.refs_4_.refs_5_
  5.7 2.4 copy.37
  8.2 19.0 %ffn1_in.1 = (bf16[1024,1024]{1,0:T(8,128)(2,1)}, bf16[1024,1024]{1,0:T(8,128)(2,1)}, bf16[1024,1024]{1,0:T(8,128)(2,1)}) custom-call(f32[48,128]{1,0:T(8,128)} %bitcast_convert_fusion.refs_0_.refs_2_.g_h.refs_4_.refs_5_, bf16[256,1024]{1,0:T(8,128)(2,1)} %bitcast.26, bf16[1024,1024]{1,0:T(8,128)(2,1)} %refs_21_.1), custom_call_target="tpu_custom_call" | custom-call | flops 4294967296 | bytes 60000000 | tf_op jit(solution)/shard_map/ffn1_in/pallas_call | solution.py:988
  27.2 30.8 %ffn1_out.1 = (bf16[1024,1024]{1,0:T(8,128)(2,1)}, bf16[1024,768]{1,0:T(8,128)(2,1)}, f32[256,1024]{1,0:T(8,128)}, f32[8,1024]{1,0:T(8,128)}) custom-call(bf16[1024,1024]{1,0:T(8,128)(2,1)} %get-tuple-element.104.refs_0_.refs_20_, bf16[1024,1024]{1,0:T(8,128)(2,1)} %refs_8_.5, f32[48,128]{1,0:T(8,128)} %bitcast_convert_fusion.refs_0_.refs_2_.g_h.refs_4_.refs_5_, ...), custom_call_target="tpu_custom_call" | custom-call | flops 3758096384 | bytes 60000000 | tf_op jit(solution)/shard_map/ffn1_out/pallas_call | solution.py:988
  58.0 20.0 %attn_fwd.1 = (bf16[1024,256]{1,0:T(8,128)(2,1)}, bf16[2,2048,1024]{2,1,0:T(8,128)(2,1)}) custom-call(bf16[1024,768]{1,0:T(8,128)(2,1)} %get-tuple-element.105.q_ref.k_ref.v_ref.refs_9_, bf16[1024,768]{1,0:T(8,128)(2,1)} %get-tuple-element.105.q_ref.k_ref.v_ref.refs_9_, bf16[1024,768]{1,0:T(8,128)(2,1)} %get-tuple-element.105.q_ref.k_ref.v_ref.refs_9_, ...), custom_call_target="tpu_custom_call" | custom-call | tf_op jit(solution)/shard_map/attn_fwd/pallas_call | solution.py:1372
  78.1 30.0 %attn_out.1 = (bf16[1024,1024]{1,0:T(8,128)(2,1)}, f32[1024,256]{1,0:T(8,128)}, bf16[1024,256]{1,0:T(8,128)(2,1)}, bf16[1024,256]{1,0:T(8,128)(2,1)}, f32[256,1024]{1,0:T(8,128)}, /*index=5*/f32[8,1024]{1,0:T(8,128)}) custom-call(bf16[1024,256]{1,0:T(8,128)(2,1)} %get-tuple-element.106.refs_0_.refs_12_, bf16[256,1024]{1,0:T(8,128)(2,1)} %refs_8_.4, ...), custom_call_target="tpu_custom_call" | custom-call | flops 2147483648 | bytes 60000000 | tf_op jit(solution)/shard_map/attn_out/pallas_call | solution.py:988
  108.1 12.6 %conv_mid.1 = (bf16[1024,256]{1,0:T(8,128)(2,1)}, bf16[1024,256]{1,0:T(8,128)(2,1)}, f32[1024,256]{1,0:T(8,128)}, f32[8,1024]{1,0:T(8,128)}) custom-call(f32[1024,256]{1,0:T(8,128)} %get-tuple-element.108.glu_h.refs_6_, bf16[31,256]{1,0:T(8,128)(2,1)} %refs_4_.3, f32[48,128]{1,0:T(8,128)} %bitcast_convert_fusion.refs_0_.refs_2_.g_h.refs_4_.refs_5_), custom_call_target="tpu_custom_call" | custom-call | tf_op jit(solution)/shard_map/conv_mid/pallas_call | solution.py:1222
  120.6 30.1 %conv_out.1 = (bf16[1024,1024]{1,0:T(8,128)(2,1)}, bf16[1024,1024]{1,0:T(8,128)(2,1)}, bf16[1024,1024]{1,0:T(8,128)(2,1)}, f32[256,1024]{1,0:T(8,128)}, f32[8,1024]{1,0:T(8,128)}) custom-call(bf16[1024,256]{1,0:T(8,128)(2,1)} %get-tuple-element.109.refs_0_.refs_4_, bf16[256,1024]{1,0:T(8,128)(2,1)} %refs_8_.3, ...), custom_call_target="tpu_custom_call" | custom-call | flops 4831838208 | bytes 60000000 | tf_op jit(solution)/shard_map/conv_out/pallas_call | solution.py:988
  150.8 31.1 %ffn2_out.1 = (bf16[1024,1024]{1,0:T(8,128)(2,1)}, bf16[1024,1024]{1,0:T(8,128)(2,1)}, f32[256,1024]{1,0:T(8,128)}, f32[256,1024]{1,0:T(8,128)}, f32[8,1024]{1,0...) custom-call(bf16[1024,1024]{1,0:T(8,128)(2,1)} %get-tuple-element.111.refs_0_.refs_3_, bf16[1024,1024]{1,0:T(8,128)(2,1)} %refs_1_.8, ...), custom_call_target="tpu_custom_call" | custom-call | flops 4294967296 | bytes 60000000 | tf_op jit(solution)/shard_map/ffn2_out/pallas_call | solution.py:988
  181.9 34.3 %ffn2_back.1 = (bf16[1024,1024]{1,0:T(8,128)(2,1)}, f32[1024,256]{1,0:T(8,128)}, f32[256,1024]{1,0:T(8,128)}, f32[8,1024]{1,0:T(8,128)}, bf16[2,4,2,128,256]{4,3...) custom-call(bf16[1024,1024]{1,0:T(8,128)(2,1)} %get-tuple-element.115.refs_0_, ...), custom_call_target="tpu_custom_call" | custom-call | flops 6979321856 | bytes 60000000 | tf_op jit(solution)/shard_map/ffn2_back/pallas_call | solution.py:988
  216.2 17.6 %conv_mid_back.1 = (bf16[1024,512]{1,0:T(8,128)(2,1)}, f32[32,256]{1,0:T(8,128)}, bf16[4,1,2,128,256]{4,3,2,1,0:T(8,128)(2,1)}, bf16[2,2,2,128,256]{4,3,2,1,0:T(8,128)(2,1)}) custom-call(f32[1024,256]{1,0:T(8,128)} %get-tuple-element.119.refs_0_, bf16[1024,256]{1,0:T(8,128)(2,1)} %get-tuple-element.120.refs_1_, f32[1024,256]{1,0:T(8,128)} %get-tuple-element.121.refs_2_, ...), custom_call_target="tpu_custom_call" | custom-call | tf_op jit(solution)/shard_map/conv_mid_back/pallas_call | solution.py:1347
  233.9 63.0 %conv_back.1 = (f32[256,1024]{1,0:T(8,128)}, f32[8,1024]{1,0:T(8,128)}, bf16[1024,256]{1,0:T(8,128)(2,1)}, bf16[1024,256]{1,0:T(8,128)(2,1)}, bf16[1024,256]{1,0...) custom-call(bf16[1024,512]{1,0:T(8,128)(2,1)} %get-tuple-element.127, ...), custom_call_target="tpu_custom_call" | custom-call | flops 3758096384 | bytes 60000000 | tf_op jit(solution)/shard_map/conv_back/pallas_call | solution.py:988
  296.9 98.7 %attn_back.1 = (f32[256,1024]{1,0:T(8,128)}, f32[128,768]{1,0:T(8,128)}, f32[1024,128]{1,0:T(8,128)}, f32[128,1024]{1,0:T(8,128)}, f32[256,128]{1,0:T(8,128)}, /...) custom-call(bf16[1024,256]{1,0:T(8,128)(2,1)} %get-tuple-element.135, ...), custom_call_target="tpu_custom_call" | custom-call | flops 9663676416 | bytes 60000000 | tf_op jit(solution)/shard_map/attn_back/pallas_call | solution.py:988
  395.6 5.4 %publish.1 = (f32[256,1,1024]{2,1,0:T(1,128)}, f32[256,1,1024]{2,1,0:T(1,128)}, f32[128,1024]{1,0:T(8,128)}, f32[1024,128]{1,0:T(8,128)}, f32[3,128,256]{2,1,0:T...) custom-call(f32[256,1024]{1,0:T(8,128)} %get-tuple-element.114.refs_, ...), custom_call_target="tpu_custom_call" | custom-call | tf_op jit(solution)/shard_map/publish/pallas_call | solution.py:1083
  (1 shorter events, 0.0 us)

commit v10 on v9

--- a/solution.py
+++ b/solution.py
@@ -794,40 +794,49 @@
                     got_far(k).wait_recv()
                     all_fwd(k).start()
 
-            def near(*ks):
-                for k in ks:
-                    got_sib(k).wait_recv()
-                    work(k, me, sib)
-
-            def distant(*ks):
-                for k in ks:
-                    got_diag(k).wait_recv()
-                    work(k, far, diag)
-
             def before(n):
-                if n == 0:
-                    near(0, 1)
-                elif n == 1:
-                    pass_on(0)
-                elif n == 2:
-                    near(2, 3)
-                    pass_on(1)
-                elif n == 3:
-                    pass_on(2)
+                if 0 < n < 5:
+                    pass_on(n - 1)
+                if n == 3:
                     hasten(range(first_grad, len(chains)))
-                elif n == 4:
-                    pass_on(3)
-                    distant(0, 1)
                 elif n == 5:
                     hasten(range(first_grad))
                 elif n == 6:
-                    distant(2, 3)
                     for k in range(CHUNKS):
                         if any(d[2] == "post" and k < d[6] for d in dws):
                             fill(k, "post")
 
+            def rows_for(j):
+                away = j // 4
+
+                def chunk_rows(k, c):
+                    @pl.when(away == 0)
+                    def _():
+                        got_sib(k).wait_recv()
+
+                    @pl.when(away == 1)
+                    def _():
+                        got_diag(k).wait_recv()
+
+                    there = chip + away * (1 - 2 * chip)
+                    work(k, there * 2 + core, there * 2 + 1 - core)
+                    return c
+
+                first = (j // 2) % 2 * 2
+                lax.fori_loop(first, first + 2, chunk_rows, 0)
+
             def query_block(j, c):
-                for n in range(7):
+                for n in (1, 2, 3, 4):
+
+                    @pl.when(j == n)
+                    def _(n=n):
+                        before(n)
+
+                @pl.when(j % 2 == 0)
+                def _():
+                    rows_for(j)
+
+                for n in (5, 6):
 
                     @pl.when(j == n)
                     def _(n=n):
@@ -851,18 +860,12 @@
             for o in d_o:
                 store_whole(o).start()
         elif enter:
-            got_sib(0).wait_recv()
-            work(0, me, sib)
 
             def gather(k, c):
+                got_sib(k).wait_recv()
+                work(k, me, sib)
                 got_far(k).wait_recv()
                 all_fwd(k).start()
-
-                @pl.when(k + 1 < CHUNKS)
-                def _():
-                    got_sib(k + 1).wait_recv()
-                    work(k + 1, me, sib)
-
                 got_diag(k).wait_recv()
                 work(k, far, diag)
                 if small:

time: 405 us -> 393 us (0.970)
  Pallas kernels: 393 us -> 384 us
    pallas_call x8, Pallas kernels: 337 us -> 328 us  [stage(): pl.pallas_call(kernel, in_specs=[in_hbm()] * n_in, out_specs=[in_hbm()] *...]
where the time goes in v10:
time: 393 us; the launch traced here: 392 us
  Pallas kernels  384 us (98%)
  local copies, waits for them, and re-layouts  6.89 us (2%)
    pallas_call x8, Pallas kernels, stage(): pl.pallas_call(kernel, in_specs=[in_hbm()] * n_in, out_specs=[in_hbm()] *...  328 us
    pallas_call x1, Pallas kernels, attn_fwd(): pl.pallas_call(fwd_kernel, grid=(nb,), in_specs=[pl.BlockSpec((BQ, heads)...  20 us
    pallas_call x1, Pallas kernels, conv_mid_back(): pl.pallas_call(kernel, in_specs=[in_hbm()] * (9 + n), out_specs=[in_hbm()...  17.6 us
    pallas_call x1, Pallas kernels, conv_mid(): pl.pallas_call(kernel, in_specs=[in_hbm()] * 3, out_specs=[in_hbm()] * 4,...  12.7 us

profile of v10, /device:TPU:0, one launch (start us, length us, event | category | flops | bytes accessed | tf_op | source)
XLA Modules:
  0.0 392.3 jit_solution(15356996902753461933)
XLA Ops:
  0.7 0.7 constant_dynamic-update-slice_fusion.4
  1.3 0.7 constant_dynamic-update-slice_fusion.3
  2.0 0.7 constant_dynamic-update-slice_fusion.2
  2.7 0.7 constant_dynamic-update-slice_fusion.1
  3.4 0.7 constant_dynamic-update-slice_fusion
  4.1 0.8 dynamic-update-slice.5
  4.9 0.2 dynamic-update-slice.6
  5.1 0.6 bitcast_convert_fusion.refs_0_.refs_2_.g_h.refs_4_.refs_5_
  5.7 2.4 copy.37
  8.2 19.5 %ffn1_in.1 = (bf16[1024,1024]{1,0:T(8,128)(2,1)}, bf16[1024,1024]{1,0:T(8,128)(2,1)}, bf16[1024,1024]{1,0:T(8,128)(2,1)}) custom-call(f32[48,128]{1,0:T(8,128)} %bitcast_convert_fusion.refs_0_.refs_2_.g_h.refs_4_.refs_5_, bf16[256,1024]{1,0:T(8,128)(2,1)} %bitcast.26, bf16[1024,1024]{1,0:T(8,128)(2,1)} %refs_21_.1), custom_call_target="tpu_custom_call" | custom-call | flops 4294967296 | bytes 60000000 | tf_op jit(solution)/shard_map/ffn1_in/pallas_call | solution.py:991
  27.7 31.3 %ffn1_out.1 = (bf16[1024,1024]{1,0:T(8,128)(2,1)}, bf16[1024,768]{1,0:T(8,128)(2,1)}, f32[256,1024]{1,0:T(8,128)}, f32[8,1024]{1,0:T(8,128)}) custom-call(bf16[1024,1024]{1,0:T(8,128)(2,1)} %get-tuple-element.104.refs_0_.refs_20_, bf16[1024,1024]{1,0:T(8,128)(2,1)} %refs_8_.5, f32[48,128]{1,0:T(8,128)} %bitcast_convert_fusion.refs_0_.refs_2_.g_h.refs_4_.refs_5_, ...), custom_call_target="tpu_custom_call" | custom-call | flops 3758096384 | bytes 60000000 | tf_op jit(solution)/shard_map/ffn1_out/pallas_call | solution.py:991
  59.0 20.0 %attn_fwd.1 = (bf16[1024,256]{1,0:T(8,128)(2,1)}, bf16[2,2048,1024]{2,1,0:T(8,128)(2,1)}) custom-call(bf16[1024,768]{1,0:T(8,128)(2,1)} %get-tuple-element.105.q_ref.k_ref.v_ref.refs_9_, bf16[1024,768]{1,0:T(8,128)(2,1)} %get-tuple-element.105.q_ref.k_ref.v_ref.refs_9_, bf16[1024,768]{1,0:T(8,128)(2,1)} %get-tuple-element.105.q_ref.k_ref.v_ref.refs_9_, ...), custom_call_target="tpu_custom_call" | custom-call | tf_op jit(solution)/shard_map/attn_fwd/pallas_call | solution.py:1375
  79.0 29.9 %attn_out.1 = (bf16[1024,1024]{1,0:T(8,128)(2,1)}, f32[1024,256]{1,0:T(8,128)}, bf16[1024,256]{1,0:T(8,128)(2,1)}, bf16[1024,256]{1,0:T(8,128)(2,1)}, f32[256,1024]{1,0:T(8,128)}, /*index=5*/f32[8,1024]{1,0:T(8,128)}) custom-call(bf16[1024,256]{1,0:T(8,128)(2,1)} %get-tuple-element.106.refs_0_.refs_12_, bf16[256,1024]{1,0:T(8,128)(2,1)} %refs_8_.4, ...), custom_call_target="tpu_custom_call" | custom-call | flops 2147483648 | bytes 60000000 | tf_op jit(solution)/shard_map/attn_out/pallas_call | solution.py:991
  108.9 12.7 %conv_mid.1 = (bf16[1024,256]{1,0:T(8,128)(2,1)}, bf16[1024,256]{1,0:T(8,128)(2,1)}, f32[1024,256]{1,0:T(8,128)}, f32[8,1024]{1,0:T(8,128)}) custom-call(f32[1024,256]{1,0:T(8,128)} %get-tuple-element.108.glu_h.refs_6_, bf16[31,256]{1,0:T(8,128)(2,1)} %refs_4_.3, f32[48,128]{1,0:T(8,128)} %bitcast_convert_fusion.refs_0_.refs_2_.g_h.refs_4_.refs_5_), custom_call_target="tpu_custom_call" | custom-call | tf_op jit(solution)/shard_map/conv_mid/pallas_call | solution.py:1225
  121.6 30.0 %conv_out.1 = (bf16[1024,1024]{1,0:T(8,128)(2,1)}, bf16[1024,1024]{1,0:T(8,128)(2,1)}, bf16[1024,1024]{1,0:T(8,128)(2,1)}, f32[256,1024]{1,0:T(8,128)}, f32[8,1024]{1,0:T(8,128)}) custom-call(bf16[1024,256]{1,0:T(8,128)(2,1)} %get-tuple-element.109.refs_0_.refs_4_, bf16[256,1024]{1,0:T(8,128)(2,1)} %refs_8_.3, ...), custom_call_target="tpu_custom_call" | custom-call | flops 4831838208 | bytes 60000000 | tf_op jit(solution)/shard_map/conv_out/pallas_call | solution.py:991
  151.6 31.7 %ffn2_out.1 = (bf16[1024,1024]{1,0:T(8,128)(2,1)}, bf16[1024,1024]{1,0:T(8,128)(2,1)}, f32[256,1024]{1,0:T(8,128)}, f32[256,1024]{1,0:T(8,128)}, f32[8,1024]{1,0...) custom-call(bf16[1024,1024]{1,0:T(8,128)(2,1)} %get-tuple-element.111.refs_0_.refs_3_, bf16[1024,1024]{1,0:T(8,128)(2,1)} %refs_1_.8, ...), custom_call_target="tpu_custom_call" | custom-call | flops 4294967296 | bytes 60000000 | tf_op jit(solution)/shard_map/ffn2_out/pallas_call | solution.py:991
  183.3 33.9 %ffn2_back.1 = (bf16[1024,1024]{1,0:T(8,128)(2,1)}, f32[1024,256]{1,0:T(8,128)}, f32[256,1024]{1,0:T(8,128)}, f32[8,1024]{1,0:T(8,128)}, bf16[2,4,2,128,256]{4,3...) custom-call(bf16[1024,1024]{1,0:T(8,128)(2,1)} %get-tuple-element.115.refs_0_, ...), custom_call_target="tpu_custom_call" | custom-call | flops 6979321856 | bytes 60000000 | tf_op jit(solution)/shard_map/ffn2_back/pallas_call | solution.py:991
  217.3 17.6 %conv_mid_back.1 = (bf16[1024,512]{1,0:T(8,128)(2,1)}, f32[32,256]{1,0:T(8,128)}, bf16[4,1,2,128,256]{4,3,2,1,0:T(8,128)(2,1)}, bf16[2,2,2,128,256]{4,3,2,1,0:T(8,128)(2,1)}) custom-call(f32[1024,256]{1,0:T(8,128)} %get-tuple-element.119.refs_0_, bf16[1024,256]{1,0:T(8,128)(2,1)} %get-tuple-element.120.refs_1_, f32[1024,256]{1,0:T(8,128)} %get-tuple-element.121.refs_2_, ...), custom_call_target="tpu_custom_call" | custom-call | tf_op jit(solution)/shard_map/conv_mid_back/pallas_call | solution.py:1350
  234.9 53.3 %conv_back.1 = (f32[256,1024]{1,0:T(8,128)}, f32[8,1024]{1,0:T(8,128)}, bf16[1024,256]{1,0:T(8,128)(2,1)}, bf16[1024,256]{1,0:T(8,128)(2,1)}, bf16[1024,256]{1,0...) custom-call(bf16[1024,512]{1,0:T(8,128)(2,1)} %get-tuple-element.127, ...), custom_call_target="tpu_custom_call" | custom-call | flops 3758096384 | bytes 60000000 | tf_op jit(solution)/shard_map/conv_back/pallas_call | solution.py:991
  288.2 98.5 %attn_back.1 = (f32[256,1024]{1,0:T(8,128)}, f32[128,768]{1,0:T(8,128)}, f32[1024,128]{1,0:T(8,128)}, f32[128,1024]{1,0:T(8,128)}, f32[256,128]{1,0:T(8,128)}, /...) custom-call(bf16[1024,256]{1,0:T(8,128)(2,1)} %get-tuple-element.135, ...), custom_call_target="tpu_custom_call" | custom-call | flops 9663676416 | bytes 60000000 | tf_op jit(solution)/shard_map/attn_back/pallas_call | solution.py:991
  386.7 5.4 %publish.1 = (f32[256,1,1024]{2,1,0:T(1,128)}, f32[256,1,1024]{2,1,0:T(1,128)}, f32[128,1024]{1,0:T(8,128)}, f32[1024,128]{1,0:T(8,128)}, f32[3,128,256]{2,1,0:T...) custom-call(f32[256,1024]{1,0:T(8,128)} %get-tuple-element.114.refs_, ...), custom_call_target="tpu_custom_call" | custom-call | tf_op jit(solution)/shard_map/publish/pallas_call | solution.py:1086
  (1 shorter events, 0.0 us)

commit v11 on v10

--- a/solution.py
+++ b/solution.py
@@ -139,6 +139,23 @@
 def gain_row(ref, i, width):
     first = i * width // 128
     return jnp.concatenate([ref[first + j : first + j + 1, :] for j in range(width // 128)], 1)
+
+
+def pack_gains(gains, width):
+    step = width // 128
+
+    def kernel(*refs):
+        out = refs[-1]
+        out[...] = jnp.zeros_like(out)
+        for i, ref in enumerate(refs[:-1]):
+            rows = ref.shape[0] // 128
+            out[i * step : i * step + rows, :] = ref[...].astype(jnp.float32).reshape(rows, 128)
+
+    return pl.pallas_call(
+        kernel,
+        out_shape=jax.ShapeDtypeStruct((len(gains) * step, 128), jnp.float32),
+        name="pack_gains",
+    )(*gains)
 
 
 class Riders:
@@ -224,20 +241,18 @@
     return wide_ref[...].T.astype(jnp.bfloat16)
 
 
-def fwd_kernel(q_ref, k_ref, v_ref, relt_ref, mixed_ref, probs_ref, bias_ref, rel_ref, wide_ref):
-    ib = pl.program_id(0)
-
-    @pl.when(ib == 0)
-    def _():
-        rel_ref[...] = nn(spot_table(5 * BQ), wide_table(relt_ref, wide_ref)).astype(jnp.bfloat16)
-
-    pairs = q_ref.shape[1] // 128
-    nkeys = k_ref.shape[0] // BQ
+def attend_block(ib, qkv_ref, probs_ref, mixed_ref, bias_ref, rel_ref):
+    frames, heads = qkv_ref.shape[0], qkv_ref.shape[1] // 3
+    at = pl.ds(pl.multiple_of(ib * BQ, BQ), BQ)
+    pairs = heads // 128
+    nkeys = frames // BQ
     places = [pl.multiple_of(jnp.clip(jb - ib + 2, 0, 4) * BQ, BQ) for jb in range(nkeys)]
     for pr in range(pairs):
         cols = slice(pr * 128, (pr + 1) * 128)
-        qs = split_pair(q_ref[:, cols] * 0.125)
-        s = nt(qs, k_ref[:, cols])
+        keys = qkv_ref[:, heads + pr * 128 : heads + (pr + 1) * 128]
+        values = qkv_ref[:, 2 * heads + pr * 128 : 2 * heads + (pr + 1) * 128]
+        qs = split_pair(qkv_ref[at, cols] * 0.125)
+        s = nt(qs, keys)
         b = nt(qs, rel_ref[...])
         rows = b.shape[0] // 2
         bias_ref[pr, :, 0:BQ] = b[:, 3 * BQ : 4 * BQ]
@@ -253,7 +268,7 @@
         inv = 1.0 / tot
         for jb in range(nkeys):
             probs_ref[pr, :, jb * BQ : (jb + 1) * BQ] = (es[jb] * inv).astype(jnp.bfloat16)
-        mixed_ref[:, cols] = join_pair(nn(probs_ref[pr], v_ref[:, cols])).astype(jnp.bfloat16)
+        mixed_ref[at, cols] = join_pair(nn(probs_ref[pr], values)).astype(jnp.bfloat16)
 
 
 def attend_back_block(ib, qkv_ref, probs_ref, do_ref, dq_ref, tot_ref, dkt, dvt, dta, dz_ref, hot_ref, relb_ref):
@@ -339,7 +354,7 @@
             self.done += 1
 
 
-def stage(name, cid, rows, width, count, gains, *, leave=None, enter=None, dws=(), grads=(), small=None, tail=None, attend=None, junction, row_in=(), row_out=(), sums=0):
+def stage(name, cid, rows, width, count, gains, *, leave=None, enter=None, dws=(), grads=(), small=None, tail=None, attend=None, mix=None, junction, row_in=(), row_out=(), sums=0):
     chunk = rows // CHUNKS
     frames = rows * 4
     bits_all = count.bit_length() - 1
@@ -377,7 +392,21 @@
     add_dw = lambda where: [(add_in(d[0]), add_in(d[1])) if d[2] in where else None for d in dws]
     groups = []
     if leave:
-        x_i, wl_i = add_in(leave[0]), add_in(leave[1])
+        if mix:
+            heads = mix[0].shape[1] // 3
+            pairs = heads // 128
+            mix_i = [add_in(m) for m in mix]
+            mixed_o = add_out((frames, heads), bf, 1)
+            probs_o = add_out((pairs, 2 * frames, frames), bf, 2)
+            mix_s = [
+                add_scratch(item)
+                for item in (
+                    pltpu.VMEM((2, pairs, 2 * BQ, frames), bf), pltpu.VMEM((pairs, 2 * BQ, 5 * BQ), f32),
+                    pltpu.VMEM((5 * BQ, 128), bf), pltpu.VMEM((128, 128), f32),
+                )
+            ]
+        x_i = None if mix else add_in(leave[0])
+        wl_i = add_in(leave[1])
         leave_s = [add_scratch(pltpu.VMEM((rows, width), f32)) for _ in range(2)]
         leave_s += [add_scratch(pltpu.VMEM((rows, width), bf)) for _ in range(6)]
         wl_s = add_scratch(pltpu.VMEM(flat_shape(leave[1])[::-1], bf)) if leave[2] else None
@@ -475,7 +504,7 @@
     store_sem = add_scratch(pltpu.SemaphoreType.DMA((out_slots[0],)))
     n_in, n_out = len(ins), len(out_shape)
     vm_at = [add_scratch(item[2]) for item in vm_ins]
-    vo_at = [add_scratch(pltpu.VMEM(o.shape, o.dtype)) for o in out_shape]
+    vo_at = [None if mix and i == probs_o[0] else add_scratch(pltpu.VMEM(o.shape, o.dtype)) for i, o in enumerate(out_shape)]
 
     def kernel(*refs):
         hbm_in, hbm_out, t = refs[:n_in], refs[n_in : n_in + n_out], refs[n_in + n_out :]
@@ -637,31 +666,79 @@
                 part(px, 0, k)[...] = p[:chunk]
                 part(sb, 0, k)[...] = p[chunk:].astype(bf)
                 pair_send(k).start()
-
-                @pl.when(k > 0)
-                def _():
-                    push(k - 1)
+                if not mix:
+
+                    @pl.when(k > 0)
+                    def _():
+                        push(k - 1)
 
                 fill(k, far_fill)
                 return c
 
-            lax.fori_loop(0, CHUNKS, out_far, 0)
-            need_for(near_fill)
+            if not mix:
+                lax.fori_loop(0, CHUNKS, out_far, 0)
+                need_for(near_fill)
 
             def out_near(k, c):
                 p = two(k, me, sib)
                 part(own, 0, k)[...] = p[:chunk]
                 part(ob, 0, k)[...] = p[chunk:].astype(bf)
                 own_send(k).start()
-
-                @pl.when(k == 0)
-                def _():
-                    push(CHUNKS - 1)
+                if not mix:
+
+                    @pl.when(k == 0)
+                    def _():
+                        push(CHUNKS - 1)
 
                 fill(k, near_fill)
                 return c
 
-            lax.fori_loop(0, CHUNKS, out_near, 0)
+            if not mix:
+                lax.fori_loop(0, CHUNKS, out_near, 0)
+                return
+            probs_v, bias_v, rel_v, wide_v = [t[n] for n in mix_s]
+            rel_v[...] = nn(spot_table(5 * BQ), wide_table(vin(mix_i[1]), wide_v)).astype(bf)
+
+            def spot(n):
+                there = chip + (1 - n // 4) * (1 - 2 * chip)
+                return (there * 2 + core + (n % 2) * (1 - 2 * core)) * 2 + (n // 2) % 2
+
+            def store_probs(n):
+                at = pl.ds(pl.multiple_of(spot(n) * 2 * BQ, 2 * BQ), 2 * BQ)
+                return pltpu.make_async_copy(
+                    probs_v.at[n % 2], hbm_out[probs_o[0]].at[:, at, :], t[store_sem].at[probs_o[1] + n % 2]
+                )
+
+            def quarter(s, c):
+                def one(b, c):
+                    n = s * 2 + b
+
+                    @pl.when(n > 1)
+                    def _():
+                        store_probs(n - 2).wait()
+
+                    attend_block(spot(n), vin(mix_i[0]), probs_v.at[n % 2], x_ref, bias_v, rel_v)
+                    store_probs(n).start()
+                    return c
+
+                lax.fori_loop(0, 2, one, 0)
+                first = s % 2 * 2
+
+                @pl.when(s < 2)
+                def _():
+                    lax.fori_loop(first, first + 2, out_far, 0)
+                    push(first)
+                    push(first + 1)
+
+                @pl.when(s > 1)
+                def _():
+                    lax.fori_loop(first, first + 2, out_near, 0)
+
+                return c
+
+            lax.fori_loop(0, 4, quarter, 0)
+            store_probs(6).wait()
+            store_probs(7).wait()
 
         def leave_drain():
             def drain(k, c):
@@ -701,7 +778,7 @@
             vout(o)[...] = jnp.zeros((8, width), f32)
         meet()
         if leave:
-            need(x_i, wl_i)
+            need(*(mix_i if mix else [x_i]), wl_i)
         begin_loads(1)
         for c in range(first_grad, len(chains)):
             for p in range(chains[c][0]):
@@ -710,7 +787,9 @@
             if leave[2]:
                 t[wl_s][...] = vin(wl_i)[...].T
             need_for("far")
-            leave_phase(vin(x_i), t[wl_s] if leave[2] else vin(wl_i), "far", "near")
+            leave_phase(vout(mixed_o) if mix else vin(x_i), t[wl_s] if leave[2] else vin(wl_i), "far", "near")
+            if mix:
+                store_whole(mixed_o).start()
         for c in range(first_grad, len(chains)):
             keep(c).start()
         need(gains_i, *row_i)
@@ -974,7 +1053,7 @@
             return c
 
         lax.fori_loop(0, CHUNKS, drain, 0)
-        for o in s_o + (small_o + [lead_o] if tail else []) + (d_o if attend else []):
+        for o in s_o + (small_o + [lead_o] if tail else []) + (d_o if attend else []) + ([mixed_o] if mix else []):
             if o[0] >= 0:
                 store_whole(o).wait()
         for d, o in zip(dws, dw_o):
@@ -1366,34 +1445,6 @@
     return outs[0], outs[1], riders.results(outs[2:])
 
 
-def attn_fwd(qkv, rel):
-    frames, cols = qkv.shape
-    heads = cols // 3
-    pairs = heads // 128
-    nb = frames // BQ
-    bf = jnp.bfloat16
-    return pl.pallas_call(
-        fwd_kernel,
-        grid=(nb,),
-        in_specs=[
-            pl.BlockSpec((BQ, heads), lambda i: (i, 0)),
-            pl.BlockSpec((frames, heads), lambda i: (0, 1)),
-            pl.BlockSpec((frames, heads), lambda i: (0, 2)),
-            pl.BlockSpec(rel.shape, lambda i: (0, 0)),
-        ],
-        out_specs=[
-            pl.BlockSpec((BQ, heads), lambda i: (i, 0)),
-            pl.BlockSpec((pairs, 2 * BQ, frames), lambda i: (0, i, 0)),
-        ],
-        out_shape=[jax.ShapeDtypeStruct((frames, heads), bf), jax.ShapeDtypeStruct((pairs, 2 * frames, frames), bf)],
-        scratch_shapes=[
-            pltpu.VMEM((pairs, 2 * BQ, 5 * BQ), jnp.float32), pltpu.VMEM((5 * BQ, 128), bf), pltpu.VMEM((128, 128), jnp.float32)
-        ],
-        compiler_params=pltpu.CompilerParams(vmem_limit_bytes=VMEM_LIMIT),
-        name="attn_fwd",
-    )(qkv, qkv, qkv, rel)
-
-
 def body(
     features,
     w1_in,
@@ -1419,9 +1470,7 @@
     f32, bf = jnp.float32, jnp.bfloat16
     s0 = features.reshape(rows, width)
     seed = cotangent.reshape(rows, width)
-    spare = jnp.zeros((width - gain_depth.shape[0],), bf)
-    gains = jnp.concatenate([gain_ffn1, gain_attn, gain_conv, gain_ffn2, gain_final, gain_depth, spare])
-    gains = gains.astype(f32).reshape(-1, 128)
+    gains = pack_gains((gain_ffn1, gain_attn, gain_conv, gain_ffn2, gain_final, gain_depth), width)
     flat_qkv = w_qkv.transpose(1, 0, 2)
     flat_conv = w_conv_in.reshape(width, -1)
     units = w1_in.shape[1]
@@ -1495,9 +1544,8 @@
         junction=forward(0.5, 1), row_in=(s0,), row_out=(f32,), sums=1,
     )
     turned_table = rel_table.T
-    mixed, probs = attn_fwd(qkv, turned_table)
-    a3, glu, sig, tail, s2, sq2, _ = stage(
-        "attn_out", 2, rows, width, dp_count, gains, leave=(mixed, w_attn_out, False),
+    mixed, probs, a3, glu, sig, tail, s2, sq2, _ = stage(
+        "attn_out", 2, rows, width, dp_count, gains, leave=(None, w_attn_out, False), mix=(qkv, turned_table),
         enter=(flat_conv, False, glu_out, (), ((chans, f32), (chans, bf), (chans, bf))),
         junction=forward(1.0, 2), row_in=(s1,), row_out=(f32,), sums=1,
     )

time: 393 us -> 380 us (0.967)
  Pallas kernels: 384 us -> 376 us
  local copies, waits for them, and re-layouts: 6.89 us -> 2.42 us
    pallas_call x1, Pallas kernels: 20 us -> 1.38 us  [pack_gains(): pl.pallas_call(kernel, out_shape=jax.ShapeDtypeStruct((len(gains) * step,...]
    pallas_call x8, Pallas kernels: 328 us -> 339 us  [stage(): pl.pallas_call(kernel, in_specs=[in_hbm()] * n_in, out_specs=[in_hbm()] *...]
    unnamed x7 -> x1, local copies, waits for them, and re-layouts: 6.68 us -> 2.42 us
where the time goes in v11:
time: 380 us; the launch traced here: 379 us
  Pallas kernels  376 us (99%)
    pallas_call x8, Pallas kernels, stage(): pl.pallas_call(kernel, in_specs=[in_hbm()] * n_in, out_specs=[in_hbm()] *...  339 us
    pallas_call x1, Pallas kernels, conv_mid_back(): pl.pallas_call(kernel, in_specs=[in_hbm()] * (9 + n), out_specs=[in_hbm()...  17.6 us
    pallas_call x1, Pallas kernels, conv_mid(): pl.pallas_call(kernel, in_specs=[in_hbm()] * 3, out_specs=[in_hbm()] * 4,...  12.4 us

profile of v11, /device:TPU:0, one launch (start us, length us, event | category | flops | bytes accessed | tf_op | source)
XLA Modules:
  0.0 379.2 jit_solution(4730584651317494914)
XLA Ops:
  0.7 1.4 pack_gains.1.refs_0_.refs_2_.refs_3_.g_h.refs_4_.refs_5_
  2.0 2.4 copy.37
  4.5 19.5 %ffn1_in.1 = (bf16[1024,1024]{1,0:T(8,128)(2,1)}, bf16[1024,1024]{1,0:T(8,128)(2,1)}, bf16[1024,1024]{1,0:T(8,128)(2,1)}) custom-call(f32[48,128]{1,0:T(8,128)} %pack_gains.1.refs_0_.refs_2_.refs_3_.g_h.refs_4_.refs_5_, bf16[256,1024]{1,0:T(8,128)(2,1)} %bitcast.23, bf16[1024,1024]{1,0:T(8,128)(2,1)} %refs_21_.1), custom_call_target="tpu_custom_call" | custom-call | flops 4294967296 | bytes 60000000 | tf_op jit(solution)/shard_map/ffn1_in/pallas_call | solution.py:1070
  24.0 31.3 %ffn1_out.1 = (bf16[1024,1024]{1,0:T(8,128)(2,1)}, bf16[1024,768]{1,0:T(8,128)(2,1)}, f32[256,1024]{1,0:T(8,128)}, f32[8,1024]{1,0:T(8,128)}) custom-call(bf16[1024,1024]{1,0:T(8,128)(2,1)} %get-tuple-element.104.refs_0_.refs_20_, bf16[1024,1024]{1,0:T(8,128)(2,1)} %refs_8_.5, f32[48,128]{1,0:T(8,128)} %pack_gains.1.refs_0_.refs_2_.refs_3_.g_h.refs_4_.refs_5_, ...), custom_call_target="tpu_custom_call" | custom-call | flops 3758096384 | bytes 60000000 | tf_op jit(solution)/shard_map/ffn1_out/pallas_call | solution.py:1070
  55.3 40.4 %attn_out.1 = (bf16[1024,256]{1,0:T(8,128)(2,1)}, bf16[2,2048,1024]{2,1,0:T(8,128)(2,1)}, bf16[1024,1024]{1,0:T(8,128)(2,1)}, f32[1024,256]{1,0:T(8,128)}, bf16[...) custom-call(bf16[1024,768]{1,0:T(8,128)(2,1)} %get-tuple-element.105.refs_0_.refs_9_,, ...), custom_call_target="tpu_custom_call" | custom-call | flops 2147483648 | bytes 60000000 | tf_op jit(solution)/shard_map/attn_out/pallas_call | solution.py:1070
  95.8 12.4 %conv_mid.1 = (bf16[1024,256]{1,0:T(8,128)(2,1)}, bf16[1024,256]{1,0:T(8,128)(2,1)}, f32[1024,256]{1,0:T(8,128)}, f32[8,1024]{1,0:T(8,128)}) custom-call(f32[1024,256]{1,0:T(8,128)} %get-tuple-element.107.glu_h.refs_6_, bf16[31,256]{1,0:T(8,128)(2,1)} %refs_4_.5, f32[48,128]{1,0:T(8,128)} %pack_gains.1.refs_0_.refs_2_.refs_3_.g_h.refs_4_.refs_5_), custom_call_target="tpu_custom_call" | custom-call | tf_op jit(solution)/shard_map/conv_mid/pallas_call | solution.py:1304
  108.2 30.0 %conv_out.1 = (bf16[1024,1024]{1,0:T(8,128)(2,1)}, bf16[1024,1024]{1,0:T(8,128)(2,1)}, bf16[1024,1024]{1,0:T(8,128)(2,1)}, f32[256,1024]{1,0:T(8,128)}, f32[8,1024]{1,0:T(8,128)}) custom-call(bf16[1024,256]{1,0:T(8,128)(2,1)} %get-tuple-element.108.refs_0_.refs_4_, bf16[256,1024]{1,0:T(8,128)(2,1)} %refs_8_.3, ...), custom_call_target="tpu_custom_call" | custom-call | flops 4831838208 | bytes 60000000 | tf_op jit(solution)/shard_map/conv_out/pallas_call | solution.py:1070
  138.2 31.7 %ffn2_out.1 = (bf16[1024,1024]{1,0:T(8,128)(2,1)}, bf16[1024,1024]{1,0:T(8,128)(2,1)}, f32[256,1024]{1,0:T(8,128)}, f32[256,1024]{1,0:T(8,128)}, f32[8,1024]{1,0...) custom-call(bf16[1024,1024]{1,0:T(8,128)(2,1)} %get-tuple-element.110.refs_0_.refs_3_, bf16[1024,1024]{1,0:T(8,128)(2,1)} %refs_1_.8, ...), custom_call_target="tpu_custom_call" | custom-call | flops 4294967296 | bytes 60000000 | tf_op jit(solution)/shard_map/ffn2_out/pallas_call | solution.py:1070
  169.9 33.8 %ffn2_back.1 = (bf16[1024,1024]{1,0:T(8,128)(2,1)}, f32[1024,256]{1,0:T(8,128)}, f32[256,1024]{1,0:T(8,128)}, f32[8,1024]{1,0:T(8,128)}, bf16[2,4,2,128,256]{4,3...) custom-call(bf16[1024,1024]{1,0:T(8,128)(2,1)} %get-tuple-element.114.refs_0_, ...), custom_call_target="tpu_custom_call" | custom-call | flops 6979321856 | bytes 60000000 | tf_op jit(solution)/shard_map/ffn2_back/pallas_call | solution.py:1070
  203.7 17.6 %conv_mid_back.1 = (bf16[1024,512]{1,0:T(8,128)(2,1)}, f32[32,256]{1,0:T(8,128)}, bf16[4,1,2,128,256]{4,3,2,1,0:T(8,128)(2,1)}, bf16[2,2,2,128,256]{4,3,2,1,0:T(8,128)(2,1)}) custom-call(f32[1024,256]{1,0:T(8,128)} %get-tuple-element.118.refs_0_, bf16[1024,256]{1,0:T(8,128)(2,1)} %get-tuple-element.119.refs_1_, f32[1024,256]{1,0:T(8,128)} %get-tuple-element.120.refs_2_, ...), custom_call_target="tpu_custom_call" | custom-call | tf_op jit(solution)/shard_map/conv_mid_back/pallas_call | solution.py:1429
  221.3 53.5 %conv_back.1 = (f32[256,1024]{1,0:T(8,128)}, f32[8,1024]{1,0:T(8,128)}, bf16[1024,256]{1,0:T(8,128)(2,1)}, bf16[1024,256]{1,0:T(8,128)(2,1)}, bf16[1024,256]{1,0...) custom-call(bf16[1024,512]{1,0:T(8,128)(2,1)} %get-tuple-element.126, ...), custom_call_target="tpu_custom_call" | custom-call | flops 3758096384 | bytes 60000000 | tf_op jit(solution)/shard_map/conv_back/pallas_call | solution.py:1070
  274.8 98.8 %attn_back.1 = (f32[256,1024]{1,0:T(8,128)}, f32[128,768]{1,0:T(8,128)}, f32[1024,128]{1,0:T(8,128)}, f32[128,1024]{1,0:T(8,128)}, f32[256,128]{1,0:T(8,128)}, /...) custom-call(bf16[1024,256]{1,0:T(8,128)(2,1)} %get-tuple-element.135, ...), custom_call_target="tpu_custom_call" | custom-call | flops 9663676416 | bytes 60000000 | tf_op jit(solution)/shard_map/attn_back/pallas_call | solution.py:1070
  373.6 5.4 %publish.1 = (f32[256,1,1024]{2,1,0:T(1,128)}, f32[256,1,1024]{2,1,0:T(1,128)}, f32[128,1024]{1,0:T(8,128)}, f32[1024,128]{1,0:T(8,128)}, f32[3,128,256]{2,1,0:T...) custom-call(f32[256,1024]{1,0:T(8,128)} %get-tuple-element.113.refs_, ...), custom_call_target="tpu_custom_call" | custom-call | tf_op jit(solution)/shard_map/publish/pallas_call | solution.py:1165

commit v12 on v11

--- a/solution.py
+++ b/solution.py
@@ -122,10 +122,10 @@
     lax.fori_loop(0, pairs, add, 0)
 
 
-def weight(lhs, rhs, where, turned, deep=1, lo=0, pieces=None):
+def weight(lhs, rhs, where, turned, deep=1, lo=0, pieces=None, order=None):
     if pieces is None:
         pieces = (sum(r.shape[1] for r in rhs) if isinstance(rhs, tuple) else rhs.shape[1]) // PIECE
-    return lhs, rhs, where, turned, deep, lo, pieces
+    return lhs, rhs, where, turned, deep, lo, pieces, order
 
 
 def flat_shape(array):
@@ -354,7 +354,7 @@
             self.done += 1
 
 
-def stage(name, cid, rows, width, count, gains, *, leave=None, enter=None, dws=(), grads=(), small=None, tail=None, attend=None, mix=None, junction, row_in=(), row_out=(), sums=0):
+def stage(name, cid, rows, width, count, gains, *, leave=None, enter=None, dws=(), grads=(), small=None, tail=None, attend=None, mix=None, pre=None, junction, row_in=(), row_out=(), sums=0):
     chunk = rows // CHUNKS
     frames = rows * 4
     bits_all = count.bit_length() - 1
@@ -405,7 +405,11 @@
                     pltpu.VMEM((5 * BQ, 128), bf), pltpu.VMEM((128, 128), f32),
                 )
             ]
-        x_i = None if mix else add_in(leave[0])
+        if pre:
+            pre_i = [add_in(a, True) for a in pre[0]]
+            pre_o = [add_out(o.shape, o.dtype, 0) for o in pre[1]]
+            pre_s = [add_scratch(item) for item in pre[2]]
+        x_i = None if mix or pre else add_in(leave[0])
         wl_i = add_in(leave[1])
         leave_s = [add_scratch(pltpu.VMEM((rows, width), f32)) for _ in range(2)]
         leave_s += [add_scratch(pltpu.VMEM((rows, width), bf)) for _ in range(6)]
@@ -465,7 +469,7 @@
         if d[2] == "join":
             dw_o.append(add_out(shape, bf, shape[0]))
         else:
-            plan.append((shape, 0, d[3], bits_all if tail else min(d[4], bits_all), add_scratch(pltpu.VMEM(shape, bf)), None, None))
+            plan.append((shape, d[7] or 0, d[3], bits_all if tail else min(d[4], bits_all), add_scratch(pltpu.VMEM(shape, bf)), None, None))
             dw_o.append(len(plan) - 1)
     dw_in = [(add_in(d[0]), add_in(d[1])) for d in dws]
     first_grad = len(plan)
@@ -478,10 +482,11 @@
     for shape, bit, turned, end, src_s, src_i, keep_s in plan:
         links = []
         pieces = shape[0]
-        for b in range(bit, end):
+        course = bit if isinstance(bit, tuple) else tuple(range(bit, end))
+        for b in course:
             nxt = halved(shape, turned)
             land_s = add_scratch(arriving(shape))
-            if b == end - 1:
+            if b == course[-1]:
                 links.append((b, slots, land_s, None, add_out(nxt.shape, nxt.dtype, pieces)))
             else:
                 links.append((b, slots, land_s, add_scratch(pltpu.VMEM(nxt.shape, nxt.dtype)), None))
@@ -504,7 +509,7 @@
     store_sem = add_scratch(pltpu.SemaphoreType.DMA((out_slots[0],)))
     n_in, n_out = len(ins), len(out_shape)
     vm_at = [add_scratch(item[2]) for item in vm_ins]
-    vo_at = [None if mix and i == probs_o[0] else add_scratch(pltpu.VMEM(o.shape, o.dtype)) for i, o in enumerate(out_shape)]
+    vo_at = [None if (mix and i == probs_o[0]) or (pre and i < len(pre[1])) else add_scratch(pltpu.VMEM(o.shape, o.dtype)) for i, o in enumerate(out_shape)]
 
     def kernel(*refs):
         hbm_in, hbm_out, t = refs[:n_in], refs[n_in : n_in + n_out], refs[n_in + n_out :]
@@ -557,7 +562,7 @@
         far = (1 - chip) * 2 + core
         diag = (1 - chip) * 2 + 1 - core
         bits = sorted({link[0] for ch in chains for link in ch[5]} | set(range(bits_all) if small else ()))
-        meet = greet([(dp, sib), (dp, far)] + [(place(dp, b)[1], me) for b in bits])
+        meet = greet([(dp, sib), (dp, far)] + ([(dp, diag)] if pre else []) + [(place(dp, b)[1], me) for b in bits])
         begin_loads(0)
 
         def part(ref, block, k):
@@ -638,9 +643,15 @@
                 dw = vout(o) if chain is None else t[chains[o][2]]
 
                 @pl.when(k < dw.shape[0])
-                def _(a=a, b=b, dw=dw, chain=chain, o=o, lo=d[5]):
-                    g = tn(vin(a)[...], vin(b)[:, pl.ds(pl.multiple_of((lo + k) * PIECE, PIECE), PIECE)])
-                    dw[k] = g.astype(bf).reshape(dw.shape[1:])
+                def _(a=a, b=b, dw=dw, chain=chain, o=o, lo=d[5], order=d[7]):
+                    g = tn(vin(a)[...], vin(b)[:, pl.ds(pl.multiple_of((lo + k) * PIECE, PIECE), PIECE)]).astype(bf)
+                    if order:
+                        size = width // count
+                        for blk in range(count):
+                            at = sum((blk >> bit & 1) << n for n, bit in enumerate(order))
+                            dw[k, at // 2, at % 2] = g[blk * size : (blk + 1) * size]
+                    else:
+                        dw[k] = g.reshape(dw.shape[1:])
                     if chain is None:
                         store_piece(o, k, PIECE, False).start()
                     else:
@@ -776,9 +787,14 @@
 
         for o in s_o + ([tail_sum] if tail else []):
             vout(o)[...] = jnp.zeros((8, width), f32)
+        if pre:
+            steps = pre[3](*[hbm_in[i] for i in pre_i], *[hbm_out[o[0]] for o in pre_o], *[t[n] for n in pre_s])
+            next(steps)
         meet()
+        if pre:
+            pre_x = next(steps)
         if leave:
-            need(*(mix_i if mix else [x_i]), wl_i)
+            need(*(mix_i if mix else [] if pre else [x_i]), wl_i)
         begin_loads(1)
         for c in range(first_grad, len(chains)):
             for p in range(chains[c][0]):
@@ -787,7 +803,7 @@
             if leave[2]:
                 t[wl_s][...] = vin(wl_i)[...].T
             need_for("far")
-            leave_phase(vout(mixed_o) if mix else vin(x_i), t[wl_s] if leave[2] else vin(wl_i), "far", "near")
+            leave_phase(vout(mixed_o) if mix else pre_x if pre else vin(x_i), t[wl_s] if leave[2] else vin(wl_i), "far", "near")
             if mix:
                 store_whole(mixed_o).start()
         for c in range(first_grad, len(chains)):
@@ -1001,9 +1017,15 @@
 
         depth = lambda c: len(chains[c][5])
         begin = lambda c: early if c in lead else 1 if c in mid else 0
-        agenda, fresh_slot = {}, 1
+        agenda, fresh_slot, late = {}, 1, []
         for c in range(len(chains)):
             new = tail and c < first_grad and c not in lead
+            if isinstance(plan[c][1], tuple):
+                for p in range(chains[c][0]):
+                    for step in range(depth(c) - 1):
+                        agenda.setdefault(1 + LAG * step, []).append((step, c, p))
+                    late.append((depth(c) - 1, c, p))
+                continue
             for p in range(chains[c][0]):
                 slot = fresh_slot if new else 0
                 fresh_slot += 1 if new else 0
@@ -1011,6 +1033,7 @@
                     agenda.setdefault(slot, []).append((step, c, p))
                     slot += LAG
         final = None
+        agenda.setdefault(max(list(agenda) + [0]), []).extend(late)
         for slot in range(max(list(agenda) + [0]) + 1):
             if tail and slot == JOIN_SLOT:
                 final = close_rows()
@@ -1037,6 +1060,8 @@
                 store_piece(out_o, p, PIECE, chains[c][1] and t[block].shape[2] % 128 == 0).wait()
         if leave:
             leave_drain()
+        if pre:
+            next(steps)
 
         def drain(k, c):
             if enter:
@@ -1215,7 +1240,7 @@
     return jnp.concatenate([ref[first + j : first + j + 1, :] for j in range(chans // 128)], 1)
 
 
-def conv_mid(glu, w_depth, gains, width, cid):
+def conv_mid(glu, w_depth, gains, width):
     frames, chans = glu.shape
     taps = w_depth.shape[0]
     reach = taps - 1
@@ -1223,8 +1248,7 @@
     f32, bf = jnp.float32, jnp.bfloat16
     tiles, lanes = frames // SPAN, chans // 128
 
-    def kernel(glu_h, w_h, g_h, act_h, slope_h, unit_h, stat_h, pad, w_raw, g_raw, w_v, g_v, act, slope, unit, stat, sendbuf, landing, lsem, ssem, send, recv):
-        meet = greet(group_targets())
+    def run(glu_h, w_h, g_h, act_h, slope_h, unit_h, stat_h, pad, w_raw, g_raw, w_v, g_v, act, slope, unit, stat, sendbuf, landing, lsem, ssem, send, recv):
         loads = [
             pltpu.make_async_copy(glu_h, pad.at[pl.ds(edge, frames)], lsem.at[0]),
             pltpu.make_async_copy(w_h, w_raw, lsem.at[1]),
@@ -1233,6 +1257,7 @@
         for cp in loads:
             cp.start()
         pad[:edge, :] = jnp.zeros((edge, chans), f32)
+        yield None
         for cp in loads:
             cp.wait()
         w_v[...] = w_raw[...].astype(f32)
@@ -1258,7 +1283,6 @@
             return c
 
         lax.fori_loop(0, tiles, tile, 0)
-        meet()
         copies = exchange(sendbuf, landing, send, recv)
         for cp in copies:
             cp.start()
@@ -1291,30 +1315,25 @@
         lax.fori_loop(0, tiles, finish, 0)
         last = pltpu.make_async_copy(stat, stat_h, lsem.at[0])
         last.start()
+        yield act
         for cp in copies:
             cp.wait_send()
         for i in range(tiles):
             for n in range(3):
                 store(i, n).wait()
         last.wait()
+        yield None
 
     S = jax.ShapeDtypeStruct
     out_shape = [S((frames, chans), bf), S((frames, chans), bf), S((frames, chans), f32), S((8, frames), f32)]
     vm = pltpu.VMEM
-    return pl.pallas_call(
-        kernel,
-        in_specs=[in_hbm()] * 3,
-        out_specs=[in_hbm()] * 4,
-        out_shape=out_shape,
-        scratch_shapes=[
-            vm((frames + edge, chans), f32), vm(w_depth.shape, bf), vm(gains.shape, f32), vm(w_depth.shape, f32), vm((1, chans), f32),
-            vm((frames, chans), bf), vm((frames, chans), bf), vm((frames, chans), f32), vm((8, frames), f32),
-            vm((8, frames), f32), vm((3, 8, frames), f32),
-            pltpu.SemaphoreType.DMA((3,)), pltpu.SemaphoreType.DMA((3, tiles)), pltpu.SemaphoreType.DMA((3,)), pltpu.SemaphoreType.DMA((3,)),
-        ],
-        compiler_params=pltpu.CompilerParams(collective_id=cid, has_side_effects=True, vmem_limit_bytes=VMEM_LIMIT),
-        name="conv_mid",
-    )(glu, w_depth, gains)
+    scratch = [
+        vm((frames + edge, chans), f32), vm(w_depth.shape, bf), vm(gains.shape, f32), vm(w_depth.shape, f32), vm((1, chans), f32),
+        vm((frames, chans), bf), vm((frames, chans), bf), vm((frames, chans), f32), vm((8, frames), f32),
+        vm((8, frames), f32), vm((3, 8, frames), f32),
+        pltpu.SemaphoreType.DMA((3,)), pltpu.SemaphoreType.DMA((3, tiles)), pltpu.SemaphoreType.DMA((3,)), pltpu.SemaphoreType.DMA((3,)),
+    ]
+    return [glu, w_depth, gains], out_shape, scratch, run
 
 
 def conv_mid_back(grad, slope, unit, stat, glu, sig, tail, w_depth, gains, width, cid, grads):
@@ -1549,9 +1568,8 @@
         enter=(flat_conv, False, glu_out, (), ((chans, f32), (chans, bf), (chans, bf))),
         junction=forward(1.0, 2), row_in=(s1,), row_out=(f32,), sums=1,
     )
-    act3, slope3, depth_unit, depth_stat = conv_mid(glu, w_depth, gains, width, 10)
-    a4, act2, slope2, s3, sq3, _ = stage(
-        "conv_out", 3, rows, width, dp_count, gains, leave=(act3, w_conv_out, False),
+    act3, slope3, depth_unit, depth_stat, a4, act2, slope2, s3, sq3, _ = stage(
+        "conv_out", 3, rows, width, dp_count, gains, leave=(None, w_conv_out, False), pre=conv_mid(glu, w_depth, gains, width),
         enter=(w2_in, False, swish_out, (), ((units, bf), (units, bf))),
         junction=forward(1.0, 3), row_in=(s2,), row_out=(f32,), sums=1,
     )
@@ -1590,15 +1608,16 @@
         enter=(w1_out, True, slope_out, (slope1,), ((units, bf),)),
         dws=(
             weight(a2, dqkv, "far", False),
-            weight("all", act1, "front", True),
+            weight("all", act1, "front", True, 1, 0, 1, tuple(range(1, done)) + (0,)),
+            weight("all", act1, "front", True, 1, 1, units // PIECE - 1),
             weight(a1, "out", "close", False, pieces=units // PIECE),
         ),
         grads=waiting, small=((dgc, dg2, dgf, sq1, sq2, sq3, sq4, sq5), dt, tap_sums),
         tail=(w1_in, backward(1.0, 0), (s0,)),
         junction=backward(0.5, 1), row_in=(grad2, s1), row_out=(f32,), sums=1,
     )
-    gqkv, gw1_out, gw1_in = ends[:3]
-    for item, end in zip(waiting, ends[3:]):
+    gqkv, gw1_head, gw1_out, gw1_in = ends[:4]
+    for item, end in zip(waiting, ends[4:]):
         item.array = end.array
 
     def finish(item):
@@ -1610,7 +1629,7 @@
         ([output], 1),
         ([grad0], 1),
         ([finish(gw1_in)], 0),
-        ([finish(gw1_out)], 0),
+        ([finish(gw1_head), finish(gw1_out)], 0),
         ([finish(gqkv)], -3),
         ([finish(gattn)], 0),
         ([finish(gconv_in)], 2),
@@ -1618,7 +1637,7 @@
         ([finish(ga_in), finish(gb_in)], 0),
         ([finish(gw2_out)], 0),
     ]
-    done_ends = publish(ends, [lead_row, other_rows, table_end, taps_end], {8: False}, rel_table.shape[0], float(token_total * width))
+    done_ends = publish(ends, [lead_row, other_rows, table_end, taps_end], {3: True, 8: False}, rel_table.shape[0], float(token_total * width))
     (output, grad0, gw1_in, gw1_out, gqkv, gattn, gconv_in, gconv_out, gw2_in, gw2_out) = done_ends[:10]
     *gain_sums, table_sum, depth_sum, depth_gain_sum, rms_stats = done_ends[10:]
     gain_sums = [g[0] for g in gain_sums]

time: 380 us -> 374 us (0.984)
  Pallas kernels: 376 us -> 370 us
    pallas_call x1 -> x0, Pallas kernels: 12.4 us -> none  [conv_mid(): pl.pallas_call(kernel, in_specs=[in_hbm()] * 3, out_specs=[in_hbm()] * 4,...]
    pallas_call x8, Pallas kernels: 339 us -> 346 us  [stage(): pl.pallas_call(kernel, in_specs=[in_hbm()] * n_in, out_specs=[in_hbm()] *...]
where the time goes in v12:
time: 374 us
  Pallas kernels  370 us (99%)
    pallas_call x8, Pallas kernels, stage(): pl.pallas_call(kernel, in_specs=[in_hbm()] * n_in, out_specs=[in_hbm()] *...  346 us
    pallas_call x1, Pallas kernels, conv_mid_back(): pl.pallas_call(kernel, in_specs=[in_hbm()] * (9 + n), out_specs=[in_hbm()...  17.5 us

profile of v12, /device:TPU:0, one launch (start us, length us, event | category | flops | bytes accessed | tf_op | source)
XLA Modules:
  0.0 373.7 jit_solution(513656854793656700)
XLA Ops:
  0.7 1.4 pack_gains.1.refs_0_.refs_2_.refs_3_.refs_4_.refs_5_
  2.0 2.4 copy.37
  4.5 19.5 %ffn1_in.1 = (bf16[1024,1024]{1,0:T(8,128)(2,1)}, bf16[1024,1024]{1,0:T(8,128)(2,1)}, bf16[1024,1024]{1,0:T(8,128)(2,1)}) custom-call(f32[48,128]{1,0:T(8,128)} %pack_gains.1.refs_0_.refs_2_.refs_3_.refs_4_.refs_5_, bf16[256,1024]{1,0:T(8,128)(2,1)} %bitcast.23, bf16[1024,1024]{1,0:T(8,128)(2,1)} %refs_21_.1), custom_call_target="tpu_custom_call" | custom-call | flops 4294967296 | bytes 60000000 | tf_op jit(solution)/shard_map/ffn1_in/pallas_call | solution.py:1095
  24.0 31.3 %ffn1_out.1 = (bf16[1024,1024]{1,0:T(8,128)(2,1)}, bf16[1024,768]{1,0:T(8,128)(2,1)}, f32[256,1024]{1,0:T(8,128)}, f32[8,1024]{1,0:T(8,128)}) custom-call(bf16[1024,1024]{1,0:T(8,128)(2,1)} %get-tuple-element.105.refs_0_.refs_20_, bf16[1024,1024]{1,0:T(8,128)(2,1)} %refs_8_.5, f32[48,128]{1,0:T(8,128)} %pack_gains.1.refs_0_.refs_2_.refs_3_.refs_4_.refs_5_, ...), custom_call_target="tpu_custom_call" | custom-call | flops 3758096384 | bytes 60000000 | tf_op jit(solution)/shard_map/ffn1_out/pallas_call | solution.py:1095
  55.3 40.5 %attn_out.1 = (bf16[1024,256]{1,0:T(8,128)(2,1)}, bf16[2,2048,1024]{2,1,0:T(8,128)(2,1)}, bf16[1024,1024]{1,0:T(8,128)(2,1)}, f32[1024,256]{1,0:T(8,128)}, bf16[...) custom-call(bf16[1024,768]{1,0:T(8,128)(2,1)} %get-tuple-element.106.refs_0_.refs_9_,, ...), custom_call_target="tpu_custom_call" | custom-call | flops 2147483648 | bytes 60000000 | tf_op jit(solution)/shard_map/attn_out/pallas_call | solution.py:1095
  95.8 40.3 %conv_out.1 = (bf16[1024,256]{1,0:T(8,128)(2,1)}, bf16[1024,256]{1,0:T(8,128)(2,1)}, f32[1024,256]{1,0:T(8,128)}, f32[8,1024]{1,0:T(8,128)}, bf16[1024,1024]{1,0...) custom-call(f32[1024,256]{1,0:T(8,128)} %get-tuple-element.108.refs_, ...), custom_call_target="tpu_custom_call" | custom-call | flops 4831838208 | bytes 60000000 | tf_op jit(solution)/shard_map/conv_out/pallas_call | solution.py:1095
  136.1 31.7 %ffn2_out.1 = (bf16[1024,1024]{1,0:T(8,128)(2,1)}, bf16[1024,1024]{1,0:T(8,128)(2,1)}, f32[256,1024]{1,0:T(8,128)}, f32[256,1024]{1,0:T(8,128)}, f32[8,1024]{1,0...) custom-call(bf16[1024,1024]{1,0:T(8,128)(2,1)} %get-tuple-element.110.refs_0_.refs_3_, bf16[1024,1024]{1,0:T(8,128)(2,1)} %refs_1_.8, ...), custom_call_target="tpu_custom_call" | custom-call | flops 4294967296 | bytes 60000000 | tf_op jit(solution)/shard_map/ffn2_out/pallas_call | solution.py:1095
  167.8 33.8 %ffn2_back.1 = (bf16[1024,1024]{1,0:T(8,128)(2,1)}, f32[1024,256]{1,0:T(8,128)}, f32[256,1024]{1,0:T(8,128)}, f32[8,1024]{1,0:T(8,128)}, bf16[2,4,2,128,256]{4,3...) custom-call(bf16[1024,1024]{1,0:T(8,128)(2,1)} %get-tuple-element.114.refs_0_, ...), custom_call_target="tpu_custom_call" | custom-call | flops 6979321856 | bytes 60000000 | tf_op jit(solution)/shard_map/ffn2_back/pallas_call | solution.py:1095
  201.6 17.5 %conv_mid_back.1 = (bf16[1024,512]{1,0:T(8,128)(2,1)}, f32[32,256]{1,0:T(8,128)}, bf16[4,1,2,128,256]{4,3,2,1,0:T(8,128)(2,1)}, bf16[2,2,2,128,256]{4,3,2,1,0:T(8,128)(2,1)}) custom-call(f32[1024,256]{1,0:T(8,128)} %get-tuple-element.118.refs_0_, bf16[1024,256]{1,0:T(8,128)(2,1)} %get-tuple-element.119.refs_1_, f32[1024,256]{1,0:T(8,128)} %get-tuple-element.120.refs_2_, ...), custom_call_target="tpu_custom_call" | custom-call | tf_op jit(solution)/shard_map/conv_mid_back/pallas_call | solution.py:1448
  219.1 53.3 %conv_back.1 = (f32[256,1024]{1,0:T(8,128)}, f32[8,1024]{1,0:T(8,128)}, bf16[1024,256]{1,0:T(8,128)(2,1)}, bf16[1024,256]{1,0:T(8,128)(2,1)}, bf16[1024,256]{1,0...) custom-call(bf16[1024,512]{1,0:T(8,128)(2,1)} %get-tuple-element.126, ...), custom_call_target="tpu_custom_call" | custom-call | flops 3758096384 | bytes 60000000 | tf_op jit(solution)/shard_map/conv_back/pallas_call | solution.py:1095
  272.4 95.7 %attn_back.1 = (f32[256,1024]{1,0:T(8,128)}, f32[128,768]{1,0:T(8,128)}, f32[256,128]{1,0:T(8,128)}, f32[768,128]{1,0:T(8,128)}, f32[128,1024]{1,0:T(8,128)}, /*...) custom-call(bf16[1024,256]{1,0:T(8,128)(2,1)} %get-tuple-element.136, ...), custom_call_target="tpu_custom_call" | custom-call | flops 9663676416 | bytes 60000000 | tf_op jit(solution)/shard_map/attn_back/pallas_call | solution.py:1095
  368.1 5.4 %publish.1 = (f32[256,1,1024]{2,1,0:T(1,128)}, f32[256,1,1024]{2,1,0:T(1,128)}, f32[128,1024]{1,0:T(8,128)}, f32[1024,128]{1,0:T(8,128)}, f32[3,128,256]{2,1,0:T...) custom-call(f32[256,1024]{1,0:T(8,128)} %get-tuple-element.113.refs_, ...), custom_call_target="tpu_custom_call" | custom-call | tf_op jit(solution)/shard_map/publish/pallas_call | solution.py:1190
